TPU v7x, 32 devices: a whole 2x2x4 slice. The times are simulated.
32 devices in a mesh: groups: 2 (over y), tok: 4 (over z), rep: 2 (over x), head: 2 (over core).
Axes of the slice: x: 2, y: 2, z: 4, core: 2. Of those that a mesh axis runs over, the one named last changes fastest.
Arguments:
- query_rows: float32 [4, 2, 1024, 512], P(('groups', 'rep'), 'head', 'tok'), parts along dimension 0, may hold values from -6 to 6
- key_rows: float32 [4, 2, 1024, 512], P(('groups', 'rep'), 'head', 'tok'), parts along dimension 0, may hold values from -6 to 6
- value_rows: float32 [4, 2, 1024, 512], P(('groups', 'rep'), 'head', 'tok'), parts along dimension 0, may hold values from -6 to 6
- step_logits: float32 [4, 2, 1024], P(('groups', 'rep'), 'head', 'tok'), parts along dimension 0, may hold values from -3 to 3
- read_cotangent: float32 [4, 2, 1024, 512], P(('groups', 'rep'), 'head', 'tok'), parts along dimension 0, may hold values from -6 to 6
- fast_gate: float32 [2, 512, 512], P('head', ('tok', 'rep')), may hold values from -0.25 to 0.25
- fast_up: float32 [2, 512, 512], P('head', ('tok', 'rep')), may hold values from -0.25 to 0.25
- fast_down: float32 [2, 512, 512], P('head', ('tok', 'rep')), may hold values from -0.25 to 0.25
Outputs:
- query_grad: float32 [4, 2, 1024, 512], P(('groups', 'rep'), 'head', 'tok'), parts along dimension 0
- key_grad: float32 [4, 2, 1024, 512], P(('groups', 'rep'), 'head', 'tok'), parts along dimension 0
- value_grad: float32 [4, 2, 1024, 512], P(('groups', 'rep'), 'head', 'tok'), parts along dimension 0
- logit_grad: float32 [4, 2, 1024], P(('groups', 'rep'), 'head', 'tok'), parts along dimension 0
- gate_grad: float32 [4, 512, 512], P(('groups', 'head'), ('tok', 'rep')), parts along dimension 0
- up_grad: float32 [4, 512, 512], P(('groups', 'head'), ('tok', 'rep')), parts along dimension 0
- down_grad: float32 [4, 512, 512], P(('groups', 'head'), ('tok', 'rep')), parts along dimension 0
There are 2 independent parts, one for each index of `groups`. A program takes and returns all parts, laid end to end along the dimension named above; an argument that names none is the same for every part. Nothing has to cross between parts.
All inputs are finite; a program needn't handle non-finite values.
Results may differ from a plain program's by a relative error of at most 0.00023.
Values sent between devices are 32-bit elements; how exact they have to be, the bound alone decides.
No kernel may reach another device: no remote copies, remote signals or barrier semaphores. Data moves between devices by JAX's collectives and lax.ppermute only.
A program may use at most 64 MiB of HBM per device.

v0:
```python
import math

import jax
import jax.numpy as jnp
from jax import lax
from jax.sharding import PartitionSpec as P

EPSILON = 1e-06


def contract(form, left, right):
    return jnp.einsum(form, left, right, precision=lax.Precision.HIGHEST)


def silu_slope(pre):
    sigma = jax.nn.sigmoid(pre)
    return sigma * (1.0 + pre * (1.0 - sigma))


def inner_gradient(key_head, value_head, logit_head, gate_head, up_head, down_head, factor):
    step = jax.nn.softplus(logit_head) * factor
    gate_pre = contract("td,df->tf", key_head, gate_head)
    up_pre = contract("td,df->tf", key_head, up_head)
    hidden = jax.nn.silu(gate_pre) * up_pre
    target = -step[:, None] * value_head
    back = contract("td,df->tf", target, down_head)
    down_step = contract("td,tf->df", target, hidden)
    gate_back = back * up_pre * silu_slope(gate_pre)
    up_back = back * jax.nn.silu(gate_pre)
    return (
        contract("td,tf->df", key_head, gate_back),
        contract("td,tf->df", key_head, up_back),
        down_step,
    )


def renormalize(weight, step):
    moved = weight - step
    ratio = jnp.sqrt(jnp.mean(weight * weight, axis=-2, keepdims=True) + EPSILON) / jnp.sqrt(
        jnp.mean(moved * moved, axis=-2, keepdims=True) + EPSILON
    )
    return moved * ratio


def renorm_three(weights, steps):
    return (
        renormalize(weights[0], steps[0]),
        renormalize(weights[1], steps[1]),
        renormalize(weights[2], steps[2]),
    )


def read_backward(queries, cotangent, new_weights):
    gate_new, up_new, down_new = new_weights
    gate_pre = contract("htd,hdf->htf", queries, gate_new)
    up_pre = contract("htd,hdf->htf", queries, up_new)
    gate_act = jax.nn.silu(gate_pre)
    hidden = gate_act * up_pre
    hidden_back = contract("htd,hdf->htf", cotangent, down_new)
    gate_back = hidden_back * up_pre * silu_slope(gate_pre)
    up_back = hidden_back * gate_act
    parts = (
        contract("htd,htf->hdf", queries, gate_back),
        contract("htd,htf->hdf", queries, up_back),
        contract("htd,htf->hdf", cotangent, hidden),
    )
    query_grad = contract("htf,hdf->htd", gate_back, gate_new) + contract(
        "htf,hdf->htd", up_back, up_new
    )
    return (parts, query_grad)


def per_device(
    query_rows, key_rows, value_rows, step_logits, read_cotangent, fast_gate, fast_up, fast_down
):
    tokens_here = key_rows.shape[2]
    factor = 1.0 / (8.0 * math.sqrt(tokens_here * lax.axis_size("tok")))
    queries = query_rows[0]
    keys_local = key_rows[0]
    values_local = value_rows[0]
    logits_local = step_logits[0]
    cotangent = read_cotangent[0]
    whole = (
        lax.all_gather(fast_gate, ("tok", "rep"), axis=1, tiled=True),
        lax.all_gather(fast_up, ("tok", "rep"), axis=1, tiled=True),
        lax.all_gather(fast_down, ("tok", "rep"), axis=1, tiled=True),
    )

    def local_update(key_head, value_head, logit_head, gate_head, up_head, down_head):
        return inner_gradient(
            key_head, value_head, logit_head, gate_head, up_head, down_head, factor
        )

    partials, update_back = jax.vjp(
        jax.vmap(local_update), keys_local, values_local, logits_local, whole[0], whole[1], whole[2]
    )
    sums = lax.psum((partials[0], partials[1], partials[2]), "tok")
    new_weights, norm_back = jax.vjp(renorm_three, whole, sums)
    read_parts, query_grad = read_backward(queries, cotangent, new_weights)
    read_total = lax.psum((read_parts[0], read_parts[1], read_parts[2]), "tok")
    direct, step_cot = norm_back(read_total)
    back_terms = update_back(step_cot)
    first_tok = lax.axis_index("tok") == 0
    weight_terms = (
        back_terms[3] + jnp.where(first_tok, direct[0], 0.0),
        back_terms[4] + jnp.where(first_tok, direct[1], 0.0),
        back_terms[5] + jnp.where(first_tok, direct[2], 0.0),
    )
    sectioned = (
        lax.psum_scatter(weight_terms[0], "tok", scatter_dimension=1, tiled=True),
        lax.psum_scatter(weight_terms[1], "tok", scatter_dimension=1, tiled=True),
        lax.psum_scatter(weight_terms[2], "tok", scatter_dimension=1, tiled=True),
    )
    owned = (
        lax.psum_scatter(sectioned[0], "rep", scatter_dimension=1, tiled=True),
        lax.psum_scatter(sectioned[1], "rep", scatter_dimension=1, tiled=True),
        lax.psum_scatter(sectioned[2], "rep", scatter_dimension=1, tiled=True),
    )
    return (
        query_grad[None],
        back_terms[0][None],
        back_terms[1][None],
        back_terms[2][None],
        owned[0],
        owned[1],
        owned[2],
    )


def solution(mesh):
    return jax.shard_map(
        per_device,
        mesh=mesh,
        in_specs=(
            P(("groups", "rep"), "head", "tok", None),
            P(("groups", "rep"), "head", "tok", None),
            P(("groups", "rep"), "head", "tok", None),
            P(("groups", "rep"), "head", "tok"),
            P(("groups", "rep"), "head", "tok", None),
            P("head", ("tok", "rep"), None),
            P("head", ("tok", "rep"), None),
            P("head", ("tok", "rep"), None),
        ),
        out_specs=(
            P(("groups", "rep"), "head", "tok", None),
            P(("groups", "rep"), "head", "tok", None),
            P(("groups", "rep"), "head", "tok", None),
            P(("groups", "rep"), "head", "tok"),
            P(("groups", "head"), ("tok", "rep"), None),
            P(("groups", "head"), ("tok", "rep"), None),
            P(("groups", "head"), ("tok", "rep"), None),
        ),
        check_vma=False,
    )
```

profile of v0, /device:TPU:22, one launch (start us, length us, event | category | flops | bytes accessed | tf_op | source)
XLA Modules:
  0.0 555.1 jit_solution(18374811547471461724)
XLA Ops:
  7.2 0.7 all-gather.8.cloned.1.call-update
  8.0 0.7 all-gather.6.cloned.1.call-update
  8.7 0.7 all-gather.4.cloned.1.call-update
  9.5 0.6 copy-done.47
  10.1 38.6 %all-gather.8.cloned.1.call-done = f32[1,512,512]{2,1,0:T(8,128)} async-done(((f32[1,64,512]{2,1,0:T(8,128)}), f32[1,512,512]{2,1,0:T(8,128)}) %all-gather.8.cloned.1.call-update) | async-done | bytes 1048592 | tf_op jit(solution)/shard_map/all_gather | solution.py:85
  48.7 2.3 fusion.26
  51.0 38.8 %all-gather.6.cloned.1.call-done = f32[1,512,512]{2,1,0:T(8,128)} async-done(((f32[1,64,512]{2,1,0:T(8,128)}), f32[1,512,512]{2,1,0:T(8,128)}) %all-gather.6.cloned.1.call-update) | async-done | bytes 1048592 | tf_op jit(solution)/shard_map/all_gather | solution.py:84
  89.7 2.3 fusion.29
  92.0 2.2 convolution_bitcast_fusion.8
  94.2 36.6 %all-gather.4.cloned.1.call-done = f32[1,512,512]{2,1,0:T(8,128)} async-done(((f32[1,64,512]{2,1,0:T(8,128)}), f32[1,512,512]{2,1,0:T(8,128)}) %all-gather.4.cloned.1.call-update) | async-done | bytes 1048592 | tf_op jit(solution)/shard_map/all_gather | solution.py:86
  130.8 2.3 fusion.22
  133.1 0.8 copy-done.25
  133.9 2.3 convolution_bitcast_fusion.6
  136.4 0.9 copy-done.26
  137.3 2.2 convolution_bitcast_fusion.7
  139.5 84.2 %all-reduce.11.cloned.1.call-done = (f32[1,512,512]{2,1,0:T(8,128)}, f32[1,512,512]{2,1,0:T(8,128)}) async-done(((f32[1,512,512]{2,1,0:T(8,128)}, f32[1,512,512]{2,1,0:T(8,128)}), (f32[1,512,512]{2,1,0:T(8,128)}, f32[1,512,512]{2,1,0:T(8,128)})) %all-reduce.11.cloned.1.call-update) | async-done | bytes 2097168 | tf_op jit(solution)/shard_map/psum | solution.py:97
  223.6 2.4 multiply_reduce_fusion.3
  226.2 1.1 convolution_bitcast_fusion.16
  227.6 1.1 convolution_bitcast_fusion.18
  228.8 0.8 copy-done.32
  229.5 2.2 convolution_bitcast_fusion.5
  231.8 0.2 all-reduce.7.cloned.1.call-start
  232.0 85.9 %all-reduce.9.cloned.1.call-done = (f32[1,512,512]{2,1,0:T(8,128)}, f32[1,512,512]{2,1,0:T(8,128)}) async-done(((f32[1,512,512]{2,1,0:T(8,128)}, f32[1,512,512]{2,1,0:T(8,128)}), (f32[1,512,512]{2,1,0:T(8,128)}, f32[1,512,512]{2,1,0:T(8,128)})) %all-reduce.9.cloned.1.call-update) | async-done | bytes 2097168 | tf_op jit(solution)/shard_map/psum | solution.py:97
  317.9 1.9 multiply_reduce_fusion.2
  319.9 1.2 convolution_bitcast_fusion.17
  321.1 0.2 copy-done.30
  321.4 2.3 convolution_bitcast_fusion.4
  323.7 2.2 convolution_bitcast_fusion.3
  326.0 1.5 add_add_fusion.2
  327.4 1.0 copy-done.15
  328.4 1.9 convolution_bitcast_fusion.12
  330.4 81.7 %all-reduce.7.cloned.1.call-done = (f32[1,512,512]{2,1,0:T(8,128)}, f32[1,512,512]{2,1,0:T(8,128)}) async-done(((f32[1,512,512]{2,1,0:T(8,128)}, f32[1,512,512]{2,1,0:T(8,128)}), (f32[1,512,512]{2,1,0:T(8,128)}, f32[1,512,512]{2,1,0:T(8,128)})) %all-reduce.7.cloned.1.call-update) | async-done | bytes 2097168 | tf_op jit(solution)/shard_map/psum | solution.py:100
  412.1 1.5 multiply_reduce_fusion
  413.6 0.3 copy-done.36
  414.0 0.2 add_add_fusion
  414.2 1.1 convolution_bitcast_fusion.14
  415.4 0.3 copy-done.35
  415.7 0.3 multiply_reduce_fusion.1
  416.1 0.2 add_add_fusion.1
  416.4 0.8 copy-done.18
  417.6 2.7 fusion.55
  420.3 0.8 copy-done.41
  421.1 2.2 fusion
  423.4 3.6 fusion.1
  427.0 0.3 reduce-scatter.15.cloned.1.call-start
  427.3 3.6 fusion.2
  430.9 1.0 copy.29
  431.9 3.6 fusion.14
  435.6 2.1 fusion.16
  437.6 11.9 %reduce-scatter.7.cloned.1.call-done = f32[1,128,512]{2,1,0:T(8,128)} async-done(((f32[1,512,512]{2,1,0:T(8,128)}), f32[1,128,512]{2,1,0:T(8,128)}) %reduce-scatter.7.cloned.1.call-update) | async-done | bytes 262160 | tf_op jit(solution)/shard_map/reduce_scatter | solution.py:110
  449.6 3.6 fusion.4
  453.2 1.8 convolution_bitcast_fusion.11
  455.1 1.8 convolution_bitcast_fusion.9
  456.9 20.8 %reduce-scatter.11.cloned.1.call-done = f32[1,128,512]{2,1,0:T(8,128)} async-done(((f32[1,512,512]{2,1,0:T(8,128)}), f32[1,128,512]{2,1,0:T(8,128)}) %reduce-scatter.11.cloned.1.call-update) | async-done | bytes 262160 | tf_op jit(solution)/shard_map/reduce_scatter | solution.py:111
  477.8 3.4 fusion.52
  481.2 1.2 fusion.3
  482.4 23.5 %reduce-scatter.15.cloned.1.call-done = f32[1,128,512]{2,1,0:T(8,128)} async-done(((f32[1,512,512]{2,1,0:T(8,128)}), f32[1,128,512]{2,1,0:T(8,128)}) %reduce-scatter.15.cloned.1.call-update) | async-done | bytes 262160 | tf_op jit(solution)/shard_map/reduce_scatter | solution.py:112
  505.9 2.2 fusion.7
  508.1 1.0 copy.33
  509.2 1.0 copy.34
  510.2 0.6 exponential_multiply_fusion
  510.8 8.6 %reduce-scatter.9.cloned.1.call-done = f32[1,64,512]{2,1,0:T(8,128)} async-done(((f32[1,128,512]{2,1,0:T(8,128)}), f32[1,64,512]{2,1,0:T(8,128)}) %reduce-scatter.9.cloned.1.call-update) | async-done | bytes 131088 | tf_op jit(solution)/shard_map/reduce_scatter | solution.py:115
  519.3 14.6 %reduce-scatter.13.cloned.1.call-done = f32[1,64,512]{2,1,0:T(8,128)} async-done(((f32[1,128,512]{2,1,0:T(8,128)}), f32[1,64,512]{2,1,0:T(8,128)}) %reduce-scatter.13.cloned.1.call-update) | async-done | bytes 131088 | tf_op jit(solution)/shard_map/reduce_scatter | solution.py:116
  533.9 14.4 %reduce-scatter.17.cloned.1.call-done = f32[1,64,512]{2,1,0:T(8,128)} async-done(((f32[1,128,512]{2,1,0:T(8,128)}), f32[1,64,512]{2,1,0:T(8,128)}) %reduce-scatter.17.cloned.1.call-update) | async-done | bytes 131088 | tf_op jit(solution)/shard_map/reduce_scatter | solution.py:117
  (112 shorter events, 1.8 us)
Async XLA Ops:
  7.2 41.5 %copy-start = (f32[1,1,256,512]{3,2,1,0:T(8,128)S(1)}, f32[1,1,256,512]{3,2,1,0:T(8,128)}, u32[]{:S(2)}) copy-start(f32[1,1,256,512]{3,2,1,0:T(8,128)} %param.9) | copy-start | bytes 1572868
  7.2 41.5 %all-gather.8.cloned.1.call-start = ((), (), s32[]{:S(2)}) async-start(), calls=%async_computation.8 | async-start | bytes 1179648 | tf_op jit(solution)/shard_map/all_gather | solution.py:85
  7.9 81.8 %all-gather.6.cloned.1.call-start = ((), (), s32[]{:S(2)}) async-start(), calls=%async_computation.7 | async-start | bytes 1179648 | tf_op jit(solution)/shard_map/all_gather | solution.py:84
  8.7 122.2 %all-gather.4.cloned.1.call-start = ((), (), s32[]{:S(2)}) async-start(), calls=%async_computation.6 | async-start | bytes 1179648 | tf_op jit(solution)/shard_map/all_gather | solution.py:86
  9.4 0.7 copy-start.47
  9.4 214.2 %all-reduce.11.cloned.1.call-start = ((), (), s32[]{:S(2)}) async-start(), calls=%async_computation.17 | async-start | bytes 4194304 | tf_op jit(solution)/shard_map/psum | solution.py:97
  51.0 82.2 %copy-start.17 = (f32[256,512]{1,0:T(8,128)}, f32[256,512]{1,0:T(8,128)S(1)}, u32[]{:S(2)}) copy-start(f32[256,512]{1,0:T(8,128)S(1)} %fusion.26) | copy-start | bytes 1572868
  51.0 41.1 %copy-start.16 = (f32[1,1,256,512]{3,2,1,0:T(8,128)S(1)}, f32[1,1,256,512]{3,2,1,0:T(8,128)}, u32[]{:S(2)}) copy-start(f32[1,1,256,512]{3,2,1,0:T(8,128)} %param.10) | copy-start | bytes 1572868
  92.0 44.3 %copy-start.20 = (f32[256,512]{1,0:T(8,128)}, f32[256,512]{1,0:T(8,128)S(1)}, u32[]{:S(2)}) copy-start(f32[256,512]{1,0:T(8,128)S(1)} %fusion.29) | copy-start | bytes 1572868
  133.1 0.8 copy-start.25
  136.3 1.0 copy-start.26
  136.3 87.3 %copy-start.3 = (f32[1,512,512]{2,1,0:T(8,128)S(1)}, f32[1,512,512]{2,1,0:T(8,128)}, u32[]{:S(2)}) copy-start(f32[1,512,512]{2,1,0:T(8,128)} %all-gather.4.cloned.1.call-done) | copy-start | bytes 3145732
  136.3 181.6 %all-reduce.9.cloned.1.call-start = ((), (), s32[]{:S(2)}) async-start(), calls=%async_computation.16 | async-start | bytes 4194304 | tf_op jit(solution)/shard_map/psum | solution.py:97
  223.6 2.5 copy-start.23
  226.1 1.2 copy-start.5
  226.1 1.4 copy-start.8
  226.2 1.4 copy-start.43
  227.3 1.4 copy-start.29
  228.7 0.8 copy-start.32
  231.7 86.2 %copy-start.1 = (f32[1,512,512]{2,1,0:T(8,128)S(1)}, f32[1,512,512]{2,1,0:T(8,128)}, u32[]{:S(2)}) copy-start(f32[1,512,512]{2,1,0:T(8,128)} %all-gather.8.cloned.1.call-done) | copy-start | bytes 3145732
  231.8 180.3 %all-reduce.7.cloned.1.call-start = ((), (), s32[]{:S(2)}) async-start(), calls=%async_computation.15 | async-start | bytes 4194304 | tf_op jit(solution)/shard_map/psum | solution.py:100
  317.9 1.9 copy-start.24
  319.8 6.1 %copy-start.2 = (f32[1,512,512]{2,1,0:T(8,128)}, f32[1,512,512]{2,1,0:T(8,128)S(1)}, u32[]{:S(2)}) copy-start(f32[1,512,512]{2,1,0:T(8,128)S(1)} %get-tuple-element.22) | copy-start | bytes 3145732
  319.9 1.4 copy-start.30
  319.9 1.5 copy-start.33
  321.4 2.3 copy-start.38
  321.4 2.3 copy-start.44
  325.9 123.6 %reduce-scatter.7.cloned.1.call-start = ((), (), s32[]{:S(2)}) async-start(), calls=%async_computation.9 | async-start | bytes 1310720 | tf_op jit(solution)/shard_map/reduce_scatter | solution.py:110
  327.4 1.0 copy-start.15
  328.4 83.7 %copy-start.9 = (f32[1,512,512]{2,1,0:T(8,128)S(1)}, f32[1,512,512]{2,1,0:T(8,128)}, u32[]{:S(2)}) copy-start(f32[1,512,512]{2,1,0:T(8,128)} %copy-done.8) | copy-start | bytes 3145732
  412.1 1.5 copy-start.10
  412.1 1.9 copy-start.36
  414.2 1.2 copy-start.6
  414.2 1.5 copy-start.35
  416.1 1.0 copy-start.18
  416.1 1.2 copy-start.21
  416.1 1.3 copy-start.27
  416.1 1.5 copy-start.46
  417.6 2.7 copy-start.13
  417.6 3.5 copy-start.11
  420.3 0.8 copy-start.41
  423.3 54.3 %reduce-scatter.11.cloned.1.call-start = ((), (), s32[]{:S(2)}) async-start(), calls=%async_computation.11 | async-start | bytes 1310720 | tf_op jit(solution)/shard_map/reduce_scatter | solution.py:111
  427.0 78.8 %reduce-scatter.15.cloned.1.call-start = ((), (), s32[]{:S(2)}) async-start(), calls=%async_computation.13 | async-start | bytes 1310720 | tf_op jit(solution)/shard_map/reduce_scatter | solution.py:112
  430.9 88.4 %reduce-scatter.9.cloned.1.call-start = ((), (), s32[]{:S(2)}) async-start(), calls=%async_computation.10 | async-start | bytes 393216 | tf_op jit(solution)/shard_map/reduce_scatter | solution.py:115
  431.9 3.6 copy-start.7
  431.9 3.6 copy-start.31
  431.9 3.6 copy-start.34
  431.9 3.6 copy-start.39
  449.5 84.4 %reduce-scatter.13.cloned.1.call-start = ((), (), s32[]{:S(2)}) async-start(), calls=%async_computation.12 | async-start | bytes 393216 | tf_op jit(solution)/shard_map/reduce_scatter | solution.py:116
  449.6 3.6 copy-start.12
  449.6 3.6 copy-start.42
  453.2 1.8 copy-start.4
  453.2 1.8 copy-start.40
  455.1 22.7 %copy-start.19 = (f32[256,512]{1,0:T(8,128)S(1)}, f32[256,512]{1,0:T(8,128)}, u32[]{:S(2)}) copy-start(f32[256,512]{1,0:T(8,128)} %copy-done.17) | copy-start | bytes 1572868
  477.7 70.6 %reduce-scatter.17.cloned.1.call-start = ((), (), s32[]{:S(2)}) async-start(), calls=%async_computation.14 | async-start | bytes 393216 | tf_op jit(solution)/shard_map/reduce_scatter | solution.py:117
  477.7 3.5 copy-start.14
  477.7 3.5 copy-start.22
  477.7 3.4 copy-start.28
  477.7 3.4 copy-start.45
  508.1 1.0 copy-start.37
Sparse Core Ops, SparseCore 0:
  10.1 38.4 all-gather.7
  50.8 38.8 all-gather.5
  91.9 38.8 all-gather.3
  136.4 87.1 all-reduce.10
  231.9 86.0 all-reduce.8
  326.0 86.0 all-reduce.6
  423.5 26.0 reduce-scatter.6
  451.8 25.7 reduce-scatter.10
  480.0 25.7 reduce-scatter.14
  508.5 10.7 reduce-scatter.8
  522.2 11.6 reduce-scatter.12
  536.6 11.6 reduce-scatter.16
where the time goes:
time: 558 us; the launch traced here: 555 us
  waiting for transfers between devices  462 us (83%)
  matrix products  58.4 us (10%)
  between operations  14.7 us (3%)
  local copies, waits for them, and re-layouts  10.7 us (2%)
  other arithmetic  8.8 us (2%)
    psum x2, waiting for transfers between devices, per_device(): sums = lax.psum((partials[0], partials[1], partials[2]), 'tok')  170 us
    psum x1, waiting for transfers between devices, per_device(): read_total = lax.psum((read_parts[0], read_parts[1], read_parts[2]), 'tok')  81.7 us
    dot_general x26, matrix products, contract(): return jnp.einsum(form, left, right, precision=lax.Precision.HIGHEST)  58.4 us
    all_gather x1, waiting for transfers between devices, per_device(): lax.all_gather(fast_gate, ('tok', 'rep'), axis=1, tiled=True)  38.8 us
    all_gather x1, waiting for transfers between devices, per_device(): lax.all_gather(fast_up, ('tok', 'rep'), axis=1, tiled=True)  38.6 us
    all_gather x1, waiting for transfers between devices, per_device(): lax.all_gather(fast_down, ('tok', 'rep'), axis=1, tiled=True)  36.6 us
    reduce_scatter x1, waiting for transfers between devices, per_device(): lax.psum_scatter(weight_terms[2], 'tok', scatter_dimension=1, tiled=True)  23.5 us
    reduce_scatter x1, waiting for transfers between devices, per_device(): lax.psum_scatter(weight_terms[1], 'tok', scatter_dimension=1, tiled=True)  20.8 us
  transfers between devices with their start and end apart: 12, of which 12 were waited for; matrix products, arithmetic and copies ran while one was open for 8% of the time, Pallas kernels for 0%

commit v1 on v0

v1 whole, which is shorter than its diff:
```python
import math

import jax
import jax.numpy as jnp
from jax import lax
from jax.sharding import PartitionSpec as P

EPSILON = 1e-06
CELL = 4
ROUNDS = CELL - 1
PLACE = ("tok", "head")
SWAP = [(0, 1), (1, 0)]


def home_of(head):
    return (CELL - 1) // 2 + head


def source_of(head, turn):
    return (home_of(head) + 1 + turn % ROUNDS) % CELL


def routes(cells):
    rounds = []
    for turn in range(ROUNDS):
        pairs = []
        for cell in range(cells):
            for head in range(2):
                for core in range(2):
                    origin = cell * CELL + source_of(head, turn + core)
                    home = cell * CELL + home_of(head)
                    pairs.append((origin * 2 + head, home * 2 + core))
        rounds.append(pairs)
    return rounds


def local_routes(cells):
    pairs = []
    for cell in range(cells):
        for head in range(2):
            home = cell * CELL + home_of(head)
            pairs.append((home * 2 + head, home * 2 + 1 - head))
    return pairs


def flipped(pairs):
    return [(second, first) for first, second in pairs]


def contract(form, left, right):
    return jnp.einsum(form, left, right, precision=lax.Precision.HIGH)


def per_device(
    query_rows, key_rows, value_rows, step_logits, read_cotangent, fast_gate, fast_up, fast_down
):
    tokens_here = key_rows.shape[2]
    half = tokens_here // 2
    tok_size = lax.axis_size("tok")
    rep_size = lax.axis_size("rep")
    cells = tok_size // CELL
    assert tok_size % CELL == 0 and lax.axis_size("head") == 2
    factor = 1.0 / (8.0 * math.sqrt(tokens_here * tok_size))
    pairs = routes(cells)
    local_pairs = local_routes(cells)
    place = lax.axis_index("tok") % CELL
    core = lax.axis_index("head")
    rep = lax.axis_index("rep")
    cell_groups = [[cell * CELL + spot for cell in range(cells)] for spot in range(CELL)]
    turn0 = jnp.mod(place - core - home_of(0) - 1, CELL)
    turn1 = jnp.mod(turn0 + ROUNDS - 1, ROUNDS)
    at_home = place == home_of(0) + core
    owner = core == place - home_of(0)

    step = jax.nn.softplus(step_logits[0, 0]) * factor
    target = -step[:, None] * value_rows[0, 0]
    keys = key_rows[0, 0]
    queries = query_rows[0, 0]
    cotangent = read_cotangent[0, 0]
    weights_own = jnp.stack((fast_gate[0], fast_up[0], fast_down[0]))
    rows = weights_own.shape[1]
    width = weights_own.shape[2]
    cols = width // 2

    def start_of(turn):
        return jnp.where(turn1 == turn, 1, 0)

    sent = []
    for turn in range(ROUNDS):
        piece = lax.dynamic_slice_in_dim(weights_own, start_of(turn) * cols, cols, axis=2)
        sent.append(lax.ppermute(piece, PLACE, pairs[turn]))
    mine = lax.dynamic_slice_in_dim(weights_own, core * cols, cols, axis=2)
    other = lax.dynamic_slice_in_dim(weights_own, (1 - core) * cols, cols, axis=2)
    sent.append(jnp.where(owner, mine, lax.ppermute(other, PLACE, local_pairs)))
    came = [
        jnp.mod(place + 1 + jnp.mod(turn + core, ROUNDS), CELL) for turn in range(ROUNDS)
    ] + [place]

    def pick(pieces, keys_of, wanted):
        out = pieces[-1]
        for piece, key in zip(pieces[:-1], keys_of[:-1]):
            out = jnp.where(key == wanted, piece, out)
        return out

    ordered = jnp.stack([pick(sent, came, spot) for spot in range(CELL)], axis=1)
    if rep_size == 2:
        across = lax.ppermute(ordered, "rep", SWAP)
        ordered = jnp.stack(
            (jnp.where(rep == 0, ordered, across), jnp.where(rep == 0, across, ordered)), axis=2
        )
    else:
        ordered = lax.all_gather(ordered, "rep", axis=2)
    ordered = ordered[:, None]
    if cells > 1:
        ordered = lax.all_gather(ordered, "tok", axis=1, tiled=True, axis_index_groups=cell_groups)
    weights = ordered.reshape(3, cells * CELL * rep_size * rows, cols)

    def gather(first, second):
        near, far = [], []
        for turn in range(ROUNDS):
            begin = start_of(turn) * half
            piece = jnp.stack(
                (
                    lax.dynamic_slice_in_dim(first, begin, half),
                    lax.dynamic_slice_in_dim(second, begin, half),
                )
            )
            near.append(lax.ppermute(piece, PLACE, pairs[turn]))
        for turn in range(ROUNDS):
            far.append(lax.ppermute(near[turn], "head", SWAP))
        whole = jnp.stack((first, second))
        local = jnp.where(owner, whole, lax.ppermute(whole, PLACE, local_pairs))
        return jnp.concatenate(near + far + [local], axis=1)

    def scatter(grads):
        near = grads[:, : ROUNDS * half]
        far = grads[:, ROUNDS * half : 2 * ROUNDS * half]
        local = grads[:, 2 * ROUNDS * half :]
        total = near + lax.ppermute(far, "head", SWAP)
        back = [
            lax.ppermute(total[:, turn * half : (turn + 1) * half], PLACE, flipped(pairs[turn]))
            for turn in range(ROUNDS)
        ]
        local = local + lax.ppermute(local, PLACE, flipped(local_pairs))

        def choose(turn):
            return jnp.where(turn == 0, back[0], jnp.where(turn == 1, back[1], back[2]))

        remote = jnp.concatenate((choose(turn0), choose(turn1)), axis=1)
        return jnp.where(at_home, local, remote)

    gathered = gather(keys, target)
    keys_all, target_all = gathered[0], gathered[1]
    gathered = gather(queries, cotangent)
    query_all, cot_all = gathered[0], gathered[1]

    gate, up, down = weights[0], weights[1], weights[2]
    gate_pre = contract("td,df->tf", keys_all, gate)
    up_pre = contract("td,df->tf", keys_all, up)
    back = contract("td,df->tf", target_all, down)
    sigma = jax.nn.sigmoid(gate_pre)
    slope = sigma * (1.0 + gate_pre * (1.0 - sigma))
    act = gate_pre * sigma
    hidden = act * up_pre
    gate_back = back * up_pre * slope
    up_back = back * act
    steps = jnp.stack(
        (
            contract("td,tf->df", keys_all, gate_back),
            contract("td,tf->df", keys_all, up_back),
            contract("td,tf->df", target_all, hidden),
        )
    )
    if cells > 1:
        steps = lax.psum(steps, "tok", axis_index_groups=cell_groups)
    moved = weights - steps
    norm_old = jnp.mean(weights * weights, axis=1, keepdims=True) + EPSILON
    norm_new = jnp.mean(moved * moved, axis=1, keepdims=True) + EPSILON
    ratio = jnp.sqrt(norm_old) / jnp.sqrt(norm_new)
    renewed = moved * ratio

    gate_new, up_new, down_new = renewed[0], renewed[1], renewed[2]
    read_gate = contract("td,df->tf", query_all, gate_new)
    read_up = contract("td,df->tf", query_all, up_new)
    hidden_back = contract("td,df->tf", cot_all, down_new)
    read_sigma = jax.nn.sigmoid(read_gate)
    read_slope = read_sigma * (1.0 + read_gate * (1.0 - read_sigma))
    read_act = read_gate * read_sigma
    read_gate_back = hidden_back * read_up * read_slope
    read_up_back = hidden_back * read_act
    totals = jnp.stack(
        (
            contract("td,tf->df", query_all, read_gate_back),
            contract("td,tf->df", query_all, read_up_back),
            contract("td,tf->df", cot_all, read_act * read_up),
        )
    )
    query_part = contract("tf,df->td", read_gate_back, gate_new) + contract(
        "tf,df->td", read_up_back, up_new
    )
    query_grad = scatter(query_part[None])
    if cells > 1:
        totals = lax.psum(totals, "tok", axis_index_groups=cell_groups)

    ratio_cot = jnp.sum(totals * moved, axis=1, keepdims=True)
    moved_cot = ratio * (totals - moved * (ratio_cot / (width * norm_new)))
    direct = moved_cot + weights * (ratio_cot * ratio / (width * norm_old))
    step_cot = -moved_cot

    gate_back_cot = contract("td,df->tf", keys_all, step_cot[0])
    up_back_cot = contract("td,df->tf", keys_all, step_cot[1])
    hidden_cot = contract("td,df->tf", target_all, step_cot[2])
    bend = sigma * (1.0 - sigma) * (2.0 + gate_pre * (1.0 - 2.0 * sigma))
    back_cot = gate_back_cot * up_pre * slope + up_back_cot * act
    up_cot = gate_back_cot * back * slope + hidden_cot * act
    gate_cot = (
        gate_back_cot * back * up_pre * bend + (up_back_cot * back + hidden_cot * up_pre) * slope
    )
    grads = jnp.stack(
        (
            contract("td,tf->df", keys_all, gate_cot),
            contract("td,tf->df", keys_all, up_cot),
            contract("td,tf->df", target_all, back_cot),
        )
    )
    if cells > 1:
        direct = jnp.where(lax.axis_index("tok") < CELL, direct, 0.0)
    grads = grads + direct

    shaped = grads.reshape(3, cells, CELL, rep_size, rows, cols)
    if cells > 1:
        shaped = lax.psum_scatter(
            shaped, "tok", scatter_dimension=1, tiled=True, axis_index_groups=cell_groups
        )
    shaped = shaped[:, 0]
    if rep_size == 2:
        keep = jnp.where(rep == 0, shaped[:, :, 0], shaped[:, :, 1])
        give = jnp.where(rep == 0, shaped[:, :, 1], shaped[:, :, 0])
        shaped = keep + lax.ppermute(give, "rep", SWAP)
    else:
        shaped = lax.psum_scatter(shaped, "rep", scatter_dimension=2)
    spots = [shaped[:, spot] for spot in range(CELL)]
    returned = [
        lax.ppermute(pick(spots, list(range(CELL)), came[turn]), PLACE, flipped(pairs[turn]))
        for turn in range(ROUNDS)
    ]
    home_piece = pick(spots, list(range(CELL)), place)
    home_other = lax.ppermute(home_piece, PLACE, flipped(local_pairs))

    def choose(turn):
        return jnp.where(turn == 0, returned[0], jnp.where(turn == 1, returned[1], returned[2]))

    low = jnp.where(at_home, jnp.where(core == 0, home_piece, home_other), choose(turn0))
    high = jnp.where(at_home, jnp.where(core == 0, home_other, home_piece), choose(turn1))
    owned = jnp.concatenate((low, high), axis=2)

    key_part = (
        contract("tf,df->td", gate_back, step_cot[0])
        + contract("tf,df->td", up_back, step_cot[1])
        + contract("tf,df->td", gate_cot, gate)
        + contract("tf,df->td", up_cot, up)
    )
    target_part = contract("tf,df->td", hidden, step_cot[2]) + contract(
        "tf,df->td", back_cot, down
    )
    settled = scatter(jnp.stack((key_part, target_part)))
    key_grad, target_grad = settled[0], settled[1]
    value_grad = -step[:, None] * target_grad
    step_grad = -jnp.sum(value_rows[0, 0] * target_grad, axis=1)
    logit_grad = step_grad * factor * jax.nn.sigmoid(step_logits[0, 0])
    return (
        query_grad[0][None, None],
        key_grad[None, None],
        value_grad[None, None],
        logit_grad[None, None],
        owned[0][None],
        owned[1][None],
        owned[2][None],
    )


def solution(mesh):
    tokens = P(("groups", "rep"), "head", "tok", None)
    logits = P(("groups", "rep"), "head", "tok")
    weight = P("head", ("tok", "rep"), None)
    grad = P(("groups", "head"), ("tok", "rep"), None)
    return jax.shard_map(
        per_device,
        mesh=mesh,
        in_specs=(tokens, tokens, tokens, logits, tokens, weight, weight, weight),
        out_specs=(tokens, tokens, tokens, logits, grad, grad, grad),
        check_vma=False,
    )
```

time: 558 us -> 224 us (0.40)
  the two profiles are of different devices: /device:TPU:22 before, /device:TPU:1 now
where the time goes in v1:
time: 224 us; the launch traced here: 220 us
  waiting for transfers between devices  74.8 us (33%)
  matrix products  49.3 us (22%)
  starting transfers between devices  43.1 us (19%)
  local copies, waits for them, and re-layouts  31 us (14%)
  other arithmetic  19.6 us (9%)
    dot_general x26, matrix products, contract(): return jnp.einsum(form, left, right, precision=lax.Precision.HIGH)  49.3 us
    ppermute x6, waiting for transfers between devices, scatter(): lax.ppermute(total[:, turn * half:(turn + 1) * half], PLACE, flipped(pair...  33.4 us
    ppermute x6, waiting for transfers between devices, gather(): near.append(lax.ppermute(piece, PLACE, pairs[turn]))  20.8 us
    unnamed x101, local copies, waits for them, and re-layouts  14.7 us
    ppermute x1, waiting for transfers between devices, per_device(): shaped = keep + lax.ppermute(give, 'rep', SWAP)  12.8 us
    ppermute x6, starting transfers between devices, gather(): near.append(lax.ppermute(piece, PLACE, pairs[turn]))  12 us
    ppermute x3, starting transfers between devices, per_device(): sent.append(lax.ppermute(piece, PLACE, pairs[turn]))  11.1 us
    dot_general x3, local copies, waits for them, and re-layouts, contract(): return jnp.einsum(form, left, right, precision=lax.Precision.HIGH)  8.39 us
  transfers between devices with their start and end apart: 34, of which 9 were waited for; matrix products, arithmetic and copies ran while one was open for 27% of the time, Pallas kernels for 0%

profile of v1, /device:TPU:1, one launch (start us, length us, event | category | flops | bytes accessed | tf_op | source)
XLA Modules:
  0.0 220.0 jit_solution(14142509405324060167)
XLA Ops:
  4.5 1.3 collective-permute-start.10
  5.8 7.6 %collective-permute-start.9 = (f32[3,64,256]{2,1,0:T(8,128)}, f32[3,64,256]{2,1,0:T(8,128)}, u32[]{:S(2)}, u32[]{:S(2)}) collective-permute-start(f32[3,64,256]{2,1,0:T(8,128)} %get-tuple-element.69), channel_id=1, source_target_pairs={{8,4},{12,5},{13,8},{1,9},{10,6},{14,7},{15,10},{3,11},{24,20},{28... | collective-permute-start | bytes 589832 | tf_op jit(solution)/shard_map/ppermute | solution.py:91
  13.4 2.1 collective-permute-start.8
  15.5 1.3 collective-permute-start.7
  19.8 2.1 collective-permute-start.12
  22.0 1.2 copy.43
  23.2 1.8 pad_maximum_fusion.11
  25.0 1.1 pad_maximum_fusion.5
  29.6 1.1 pad_maximum_fusion.4
  30.6 3.6 %collective-permute-start.13 = (f32[2,128,512]{2,1,0:T(8,128)}, f32[2,128,512]{2,1,0:T(8,128)}, u32[]{:S(2)}, u32[]{:S(2)}) collective-permute-start(f32[2,128,512]{2,1,0:T(8,128)} %pad_maximum_fusion.11), channel_id=1, source_target_pairs={{12,4},{0,5},{1,8},{5,9},{14,6},{2,7},{3,10},{7,11},{28,20},{16,21... | collective-permute-start | bytes 1572872 | tf_op jit(solution)/shard_map/ppermute | solution.py:128
  34.2 2.1 collective-permute-start
  36.3 2.1 collective-permute-start.1
  38.5 1.5 collective-permute-start.2
  39.9 1.0 select_bitcast_fusion.7
  41.0 1.2 select_bitcast_fusion.6
  42.2 1.3 collective-permute-start.11
  44.3 12.4 %collective-permute-done = f32[2,128,512]{2,1,0:T(8,128)} collective-permute-done((f32[2,128,512]{2,1,0:T(8,128)}, f32[2,128,512]{2,1,0:T(8,128)}, u32[]{:S(2)}, u32[]{:S(2)}) %collective-permute-start) | collective-permute-done | bytes 524320 | tf_op jit(solution)/shard_map/ppermute | solution.py:128
  57.4 1.1 constant_dynamic-update-slice_fusion.5
  58.5 1.1 constant_dynamic-update-slice_fusion.14
  59.6 8.4 %collective-permute-done.1 = f32[2,128,512]{2,1,0:T(8,128)} collective-permute-done((f32[2,128,512]{2,1,0:T(8,128)}, f32[2,128,512]{2,1,0:T(8,128)}, u32[]{:S(2)}, u32[]{:S(2)}) %collective-permute-start.1) | collective-permute-done | bytes 524320 | tf_op jit(solution)/shard_map/ppermute | solution.py:128
  68.7 1.1 constant_dynamic-update-slice_fusion.4
  70.7 1.1 constant_dynamic-update-slice_fusion.3
  71.9 1.1 constant_dynamic-update-slice_fusion.13
  74.5 1.3 select_bitcast_fusion.1
  80.7 1.8 fusion.10
  82.5 1.8 fusion.12
  84.4 1.8 fusion.2
  88.1 1.0 fusion.22
  89.1 1.4 fusion.19
  91.6 1.9 fusion.20
  93.5 1.9 fusion.21
  95.4 1.9 fusion.18
  98.5 2.0 fusion.6
  100.5 2.0 fusion.8
  102.4 1.2 fusion.53
  103.7 1.1 add_bitcast_fusion.2
  107.2 2.4 %slice_bitcast_fusion.9 = (f32[512,1024]{0,1:T(8,128)}, f32[512,1024]{0,1:T(8,128)}) fusion(f32[2,1024,512]{2,1,0:T(8,128)S(1)} %select_dynamic-update-slice_fusion), kind=kLoop, calls=%fused_computation.59 | loop fusion | bytes 8388608 | tf_op jit(solution)/shard_map/td,tf->df/dot_general | solution.py:51
  109.7 2.5 %fusion.56 = f32[1024,512]{0,1:T(8,128)} fusion(f32[3,512,256]{2,1,0:T(8,128)S(1)} %fusion.28, f32[1024,256]{1,0:T(8,128)S(1)} %fusion.16, f32[1024,256]{1,0:T(8,128)S(1)} %fusion.14), kind=kOutput, calls=%fused_computation.124 | convolution fusion | flops 806617088 | bytes 4718592 | tf_op jit(solution)/shard_map/tf,df->td/dot_general | solution.py:51
  112.2 2.7 %fusion.54 = f32[1024,512]{0,1:T(8,128)} fusion(f32[3,512,256]{2,1,0:T(8,128)S(1)} %fusion.28, f32[1024,256]{1,0:T(8,128)S(1)} %fusion.4, f32[1024,256]{1,0:T(8,128)S(1)} %fusion.16, f32[1024,256]{1,0:T(8,128)S(1)} %fusion.14), kind=kOutput, calls=%fused_computation.122 | convolution fusion | flops 807665664 | bytes 5767168 | tf_op jit(solution)/shard_map/tf,df->td/dot_general | solution.py:51
  114.9 2.7 %fusion.55 = f32[1024,512]{0,1:T(8,128)} fusion(f32[3,512,256]{2,1,0:T(8,128)S(1)} %fusion.28, f32[1024,256]{1,0:T(8,128)S(1)} %fusion.4, f32[1024,256]{1,0:T(8,128)S(1)} %fusion.14), kind=kOutput, calls=%fused_computation.123 | convolution fusion | flops 806617088 | bytes 4718592 | tf_op jit(solution)/shard_map/tf,df->td/dot_general | solution.py:51
  117.6 3.0 %copy.45 = f32[512,1024]{1,0:T(8,128)} copy(f32[512,1024]{0,1:T(8,128)} %get-tuple-element.25) | data formatting | bytes 4194304 | tf_op jit(solution)/shard_map/td,tf->df/dot_general | solution.py:51
  120.6 6.1 %multiply_add_fusion.1 = (f32[1024,256]{1,0:T(8,128)S(1)}, f32[1024,256]{1,0:T(8,128)S(1)}, f32[1024,256]{1,0:T(8,128)}) fusion(f32[1024,256]{1,0:T(8,128)} %fusion.8, f32[1024,256]{1,0:T(8,128)} %copy-done.35, f32[1024,256]{1,0:T(8,128)} %copy-done.34, f32[1024,256]{1,0:T(8,128)} %copy-done.36, f32[1024,256]{1,0:T(8,128)} %fusion.6, ...), kind=kOutput, calls=%fused_computation.77 | convolution fusion | flops 812908544 | bytes 11010048 | tf_op jit(solution)/shard_map/td,df->tf/dot_general | solution.py:51
  126.7 2.3 %fusion.85 = f32[1024,512]{0,1:T(8,128)} fusion(f32[1024,256]{1,0:T(8,128)S(1)} %get-tuple-element.28, f32[512,256]{1,0:T(8,128)S(1)} %bitcast.281), kind=kOutput, calls=%fused_computation.201 | convolution fusion | flops 805306368 | bytes 3670016 | tf_op jit(solution)/shard_map/tf,df->td/dot_general | solution.py:51
  129.1 1.9 convolution_bitcast_fusion.2
  130.9 1.8 convolution_bitcast_fusion.1
  132.8 2.9 %copy.46 = f32[512,1024]{1,0:T(8,128)} copy(f32[512,1024]{0,1:T(8,128)} %get-tuple-element.26) | data formatting | bytes 4194304 | tf_op jit(solution)/shard_map/td,tf->df/dot_general | solution.py:51
  135.7 3.0 %convolution_bitcast_fusion = f32[1,4,2,64,256]{4,3,2,1,0:T(8,128)S(1)} fusion(f32[4,2,64,1024]{3,2,1,0:T(8,128)} %bitcast.271, f32[1024,256]{1,0:T(8,128)} %get-tuple-element.29), kind=kOutput, calls=%fused_computation.61 | convolution fusion | flops 805306368 | bytes 3670016 | tf_op jit(solution)/shard_map/td,tf->df/dot_general | solution.py:51
  139.7 1.3 collective-permute-start.29
  141.3 1.1 add_bitcast_fusion
  143.3 1.5 add_bitcast_fusion.1
  145.6 12.8 %collective-permute-done.29 = f32[3,4,64,256]{3,2,1,0:T(8,128)S(1)} collective-permute-done((f32[3,4,64,256]{3,2,1,0:T(8,128)S(1)}, f32[3,4,64,256]{3,2,1,0:T(8,128)S(1)}, u32[]{:S(2)}, u32[]{:S(2)}) %collective-permute-start.29) | collective-permute-done | bytes 786464 | tf_op jit(solution)/shard_map/ppermute | solution.py:239
  158.6 1.4 collective-permute-start.32
  161.6 1.4 collective-permute-start.31
  163.0 1.3 slice_add_fusion
  164.3 6.4 %collective-permute-done.32 = f32[3,64,256]{2,1,0:T(8,128)S(1)} collective-permute-done((f32[3,64,256]{2,1,0:T(8,128)S(1)}, f32[3,64,256]{2,1,0:T(8,128)S(1)}, u32[]{:S(2)}, u32[]{:S(2)}) %collective-permute-start.32) | collective-permute-done | bytes 196640 | tf_op jit(solution)/shard_map/ppermute | solution.py:244
  172.8 1.5 collective-permute-done.31
  174.4 1.3 collective-permute-start.22
  175.7 1.3 collective-permute-start.21
  178.1 13.9 %collective-permute-done.22 = f32[1,128,512]{2,1,0:T(8,128)S(1)} collective-permute-done((f32[1,128,512]{2,1,0:T(8,128)S(1)}, f32[1,128,512]{2,1,0:T(8,128)S(1)}, u32[]{:S(2)}, u32[]{:S(2)}) %collective-permute-start.22) | collective-permute-done | bytes 262176 | tf_op jit(solution)/shard_map/ppermute | solution.py:141
  192.0 1.3 collective-permute-start.27
  193.3 1.5 collective-permute-done.21
  194.8 1.3 collective-permute-start.26
  197.8 16.6 %collective-permute-done.27 = f32[2,128,512]{1,2,0:T(8,128)S(1)} collective-permute-done((f32[2,128,512]{1,2,0:T(8,128)S(1)}, f32[2,128,512]{1,2,0:T(8,128)S(1)}, u32[]{:S(2)}, u32[]{:S(2)}) %collective-permute-start.27) | collective-permute-done | bytes 524320 | tf_op jit(solution)/shard_map/ppermute | solution.py:141
  214.4 1.4 collective-permute-done.26
  (191 shorter events, 39.9 us)
Async XLA Ops:
  0.6 16.2 %copy-start.41 = (f32[1,1,256]{2,1,0:T(1,128)S(1)}, f32[1,1,256]{2,1,0:T(1,128)}, u32[]{:S(2)}) copy-start(f32[1,1,256]{2,1,0:T(1,128)} %param.11) | copy-start | bytes 3076
  0.6 16.2 %copy-start.32 = (f32[1,1,256,512]{3,2,1,0:T(8,128)S(1)}, f32[1,1,256,512]{3,2,1,0:T(8,128)}, u32[]{:S(2)}) copy-start(f32[1,1,256,512]{3,2,1,0:T(8,128)} %param.10) | copy-start | bytes 1572868
  4.5 26.2 %collective-permute-start.10 = (f32[3,64,256]{2,1,0:T(8,128)}, f32[3,64,256]{2,1,0:T(8,128)}, u32[]{:S(2)}, u32[]{:S(2)}) collective-permute-start(f32[3,64,256]{2,1,0:T(8,128)} %get-tuple-element.68), channel_id=1, source_target_pairs={{4,5},{9,8},{6,7},{11,10},{20,21},{25,24},{22,23},{27,26}} | collective-permute-start | bytes 589832 | tf_op jit(solution)/shard_map/ppermute | solution.py:94
  5.8 28.4 %collective-permute-start.9 = (f32[3,64,256]{2,1,0:T(8,128)}, f32[3,64,256]{2,1,0:T(8,128)}, u32[]{:S(2)}, u32[]{:S(2)}) collective-permute-start(f32[3,64,256]{2,1,0:T(8,128)} %get-tuple-element.69), channel_id=1, source_target_pairs={{8,4},{12,5},{13,8},{1,9},{10,6},{14,7},{15,10},{3,11},{24,20},{28... | collective-permute-start | bytes 589832 | tf_op jit(solution)/shard_map/ppermute | solution.py:91
  13.4 22.9 %collective-permute-start.8 = (f32[3,64,256]{2,1,0:T(8,128)}, f32[3,64,256]{2,1,0:T(8,128)}, u32[]{:S(2)}, u32[]{:S(2)}) collective-permute-start(f32[3,64,256]{2,1,0:T(8,128)} %get-tuple-element.70), channel_id=1, source_target_pairs={{12,4},{0,5},{1,8},{5,9},{14,6},{2,7},{3,10},{7,11},{28,20},{16,21... | collective-permute-start | bytes 589832 | tf_op jit(solution)/shard_map/ppermute | solution.py:91
  15.5 23.0 %collective-permute-start.7 = (f32[3,64,256]{2,1,0:T(8,128)}, f32[3,64,256]{2,1,0:T(8,128)}, u32[]{:S(2)}, u32[]{:S(2)}) collective-permute-start(f32[3,64,256]{2,1,0:T(8,128)} %get-tuple-element.71), channel_id=1, source_target_pairs={{0,4},{8,5},{5,8},{13,9},{2,6},{10,7},{7,10},{15,11},{16,20},{24,2... | collective-permute-start | bytes 589832 | tf_op jit(solution)/shard_map/ppermute | solution.py:91
  19.8 22.4 %collective-permute-start.12 = (f32[2,128,512]{2,1,0:T(8,128)}, f32[2,128,512]{2,1,0:T(8,128)}, u32[]{:S(2)}, u32[]{:S(2)}) collective-permute-start(f32[2,128,512]{2,1,0:T(8,128)} %pad_maximum_fusion.10), channel_id=1, source_target_pairs={{8,4},{12,5},{13,8},{1,9},{10,6},{14,7},{15,10},{3,11},{24,20},{28... | collective-permute-start | bytes 1572872 | tf_op jit(solution)/shard_map/ppermute | solution.py:128
  22.0 4.0 %copy-start.6 = (f32[1,1,256,512]{3,2,1,0:T(8,128)S(1)}, f32[1,1,256,512]{3,2,1,0:T(8,128)}, u32[]{:S(2)}) copy-start(f32[1,1,256,512]{3,2,1,0:T(8,128)} %param.12) | copy-start | bytes 1572868
  22.0 4.0 %copy-start.8 = (f32[1,1,256,512]{3,2,1,0:T(8,128)S(1)}, f32[1,1,256,512]{3,2,1,0:T(8,128)}, u32[]{:S(2)}) copy-start(f32[1,1,256,512]{3,2,1,0:T(8,128)} %param.8) | copy-start | bytes 1572868
  30.6 12.9 %copy-start.37 = (f32[1,128,512]{2,1,0:T(8,128)S(1)}, f32[1,128,512]{2,1,0:T(8,128)}, u32[]{:S(2)}) copy-start(f32[1,128,512]{2,1,0:T(8,128)} %get-tuple-element.59) | copy-start | bytes 786436
  30.6 12.9 %copy-start.38 = (f32[128,512]{1,0:T(8,128)S(1)}, f32[128,512]{1,0:T(8,128)}, u32[]{:S(2)}) copy-start(f32[128,512]{1,0:T(8,128)} %copy.44) | copy-start | bytes 786436
  30.6 41.1 %collective-permute-start.13 = (f32[2,128,512]{2,1,0:T(8,128)}, f32[2,128,512]{2,1,0:T(8,128)}, u32[]{:S(2)}, u32[]{:S(2)}) collective-permute-start(f32[2,128,512]{2,1,0:T(8,128)} %pad_maximum_fusion.11), channel_id=1, source_target_pairs={{12,4},{0,5},{1,8},{5,9},{14,6},{2,7},{3,10},{7,11},{28,20},{16,21... | collective-permute-start | bytes 1572872 | tf_op jit(solution)/shard_map/ppermute | solution.py:128
  34.2 22.5 %collective-permute-start = (f32[2,128,512]{2,1,0:T(8,128)}, f32[2,128,512]{2,1,0:T(8,128)}, u32[]{:S(2)}, u32[]{:S(2)}) collective-permute-start(f32[2,128,512]{2,1,0:T(8,128)} %pad_maximum_fusion.7), channel_id=1, source_target_pairs={{8,4},{12,5},{13,8},{1,9},{10,6},{14,7},{15,10},{3,11},{24,20},{28... | collective-permute-start | bytes 1572872 | tf_op jit(solution)/shard_map/ppermute | solution.py:128
  36.3 31.6 %collective-permute-start.1 = (f32[2,128,512]{2,1,0:T(8,128)}, f32[2,128,512]{2,1,0:T(8,128)}, u32[]{:S(2)}, u32[]{:S(2)}) collective-permute-start(f32[2,128,512]{2,1,0:T(8,128)} %pad_maximum_fusion.8), channel_id=1, source_target_pairs={{12,4},{0,5},{1,8},{5,9},{14,6},{2,7},{3,10},{7,11},{28,20},{16,21... | collective-permute-start | bytes 1572872 | tf_op jit(solution)/shard_map/ppermute | solution.py:128
  38.5 31.3 %collective-permute-start.2 = (f32[2,128,512]{2,1,0:T(8,128)}, f32[2,128,512]{2,1,0:T(8,128)}, u32[]{:S(2)}, u32[]{:S(2)}) collective-permute-start(f32[2,128,512]{2,1,0:T(8,128)} %pad_maximum_fusion.9), channel_id=1, source_target_pairs={{0,4},{8,5},{5,8},{13,9},{2,6},{10,7},{7,10},{15,11},{16,20},{24,2... | collective-permute-start | bytes 1572872 | tf_op jit(solution)/shard_map/ppermute | solution.py:128
  42.2 31.3 %collective-permute-start.11 = (f32[3,4,64,256]{3,2,1,0:T(8,128)S(1)}, f32[3,4,64,256]{3,2,1,0:T(8,128)S(1)}, u32[]{:S(2)}, u32[]{:S(2)}) collective-permute-start(f32[3,4,64,256]{3,2,1,0:T(8,128)S(1)} %pad_maximum_fusion.6), channel_id=1, source_target_pairs={{0,2},{2,0},{1,3},{3,1},{4,6},{6,4},{5,7},{7,5},{8,10},{10,8},{9,1... | collective-permute-start | bytes 2359304 | tf_op jit(solution)/shard_map/ppermute | solution.py:107
  56.7 16.2 %collective-permute-start.14 = (f32[2,128,512]{2,1,0:T(8,128)}, f32[2,128,512]{2,1,0:T(8,128)S(1)}, u32[]{:S(2)}, u32[]{:S(2)}) collective-permute-start(f32[2,128,512]{2,1,0:T(8,128)} %pad_maximum_fusion.12), channel_id=1, source_target_pairs={{0,4},{8,5},{5,8},{13,9},{2,6},{10,7},{7,10},{15,11},{16,20},{24,2... | collective-permute-start | bytes 1572872 | tf_op jit(solution)/shard_map/ppermute | solution.py:128
  68.0 18.9 %collective-permute-start.6 = (f32[2,256,512]{2,1,0:T(8,128)}, f32[2,256,512]{2,1,0:T(8,128)S(1)}, u32[]{:S(2)}, u32[]{:S(2)}) collective-permute-start(f32[2,256,512]{2,1,0:T(8,128)} %pad_maximum_fusion.4), channel_id=1, source_target_pairs={{4,5},{9,8},{6,7},{11,10},{20,21},{25,24},{22,23},{27,26}} | collective-permute-start | bytes 3145736 | tf_op jit(solution)/shard_map/ppermute | solution.py:132
  69.8 7.5 %collective-permute-start.18 = (f32[2,256,512]{2,1,0:T(8,128)}, f32[2,256,512]{2,1,0:T(8,128)S(1)}, u32[]{:S(2)}, u32[]{:S(2)}) collective-permute-start(f32[2,256,512]{2,1,0:T(8,128)} %pad_maximum_fusion.5), channel_id=1, source_target_pairs={{4,5},{9,8},{6,7},{11,10},{20,21},{25,24},{22,23},{27,26}} | collective-permute-start | bytes 3145736 | tf_op jit(solution)/shard_map/ppermute | solution.py:132
  71.8 4.2 %collective-permute-start.15 = (f32[2,128,512]{2,1,0:T(8,128)}, f32[2,128,512]{2,1,0:T(8,128)S(1)}, u32[]{:S(2)}, u32[]{:S(2)}) collective-permute-start(f32[2,128,512]{2,1,0:T(8,128)} %collective-permute-done.12), channel_id=1, source_target_pairs={{0,1},{1,0},{2,3},{3,2},{4,5},{5,4},{6,7},{7,6},{8,9},{9,8},{10,11... | collective-permute-start | bytes 1572872 | tf_op jit(solution)/shard_map/ppermute | solution.py:130
  73.0 3.6 %collective-permute-start.16 = (f32[2,128,512]{2,1,0:T(8,128)}, f32[2,128,512]{2,1,0:T(8,128)S(1)}, u32[]{:S(2)}, u32[]{:S(2)}) collective-permute-start(f32[2,128,512]{2,1,0:T(8,128)} %collective-permute-done.13), channel_id=1, source_target_pairs={{0,1},{1,0},{2,3},{3,2},{4,5},{5,4},{6,7},{7,6},{8,9},{9,8},{10,11... | collective-permute-start | bytes 1572872 | tf_op jit(solution)/shard_map/ppermute | solution.py:130
  74.5 2.2 %collective-permute-start.17 = (f32[2,128,512]{2,1,0:T(8,128)S(1)}, f32[2,128,512]{2,1,0:T(8,128)S(1)}, u32[]{:S(2)}, u32[]{:S(2)}) collective-permute-start(f32[2,128,512]{2,1,0:T(8,128)S(1)} %collective-permute-done.14), channel_id=1, source_target_pairs={{0,1},{1,0},{2,3},{3,2},{4,5},{5,4},{6,7},{7,6},{8,9},{9,8},{10,11... | collective-permute-start | bytes 1572872 | tf_op jit(solution)/shard_map/ppermute | solution.py:130
  75.9 2.6 %copy-start.22 = (f32[1,4,2,64,256]{4,3,2,1,0:T(8,128)}, f32[1,4,2,64,256]{4,3,2,1,0:T(8,128)S(1)}, u32[]{:S(2)}) copy-start(f32[1,4,2,64,256]{4,3,2,1,0:T(8,128)S(1)} %get-tuple-element.36) | copy-start | bytes 1572868
  76.0 3.6 %copy-start.12 = (f32[1,4,2,64,256]{4,3,2,1,0:T(8,128)}, f32[1,4,2,64,256]{4,3,2,1,0:T(8,128)S(1)}, u32[]{:S(2)}) copy-start(f32[1,4,2,64,256]{4,3,2,1,0:T(8,128)S(1)} %get-tuple-element.37) | copy-start | bytes 1572868
  76.0 4.6 %collective-permute-start.3 = (f32[2,128,512]{2,1,0:T(8,128)}, f32[2,128,512]{2,1,0:T(8,128)S(1)}, u32[]{:S(2)}, u32[]{:S(2)}) collective-permute-start(f32[2,128,512]{2,1,0:T(8,128)} %collective-permute-done), channel_id=1, source_target_pairs={{0,1},{1,0},{2,3},{3,2},{4,5},{5,4},{6,7},{7,6},{8,9},{9,8},{10,11... | collective-permute-start | bytes 1572872 | tf_op jit(solution)/shard_map/ppermute | solution.py:130
  76.6 5.9 %collective-permute-start.4 = (f32[2,128,512]{2,1,0:T(8,128)}, f32[2,128,512]{2,1,0:T(8,128)S(1)}, u32[]{:S(2)}, u32[]{:S(2)}) collective-permute-start(f32[2,128,512]{2,1,0:T(8,128)} %collective-permute-done.1), channel_id=1, source_target_pairs={{0,1},{1,0},{2,3},{3,2},{4,5},{5,4},{6,7},{7,6},{8,9},{9,8},{10,11... | collective-permute-start | bytes 1572872 | tf_op jit(solution)/shard_map/ppermute | solution.py:130
  76.7 7.7 %collective-permute-start.5 = (f32[2,128,512]{2,1,0:T(8,128)}, f32[2,128,512]{2,1,0:T(8,128)S(1)}, u32[]{:S(2)}, u32[]{:S(2)}) collective-permute-start(f32[2,128,512]{2,1,0:T(8,128)} %collective-permute-done.2), channel_id=1, source_target_pairs={{0,1},{1,0},{2,3},{3,2},{4,5},{5,4},{6,7},{7,6},{8,9},{9,8},{10,11... | collective-permute-start | bytes 1572872 | tf_op jit(solution)/shard_map/ppermute | solution.py:130
  77.5 29.7 %copy-start = (f32[2,1024,512]{2,1,0:T(8,128)}, f32[2,1024,512]{2,1,0:T(8,128)S(1)}, u32[]{:S(2)}) copy-start(f32[2,1024,512]{2,1,0:T(8,128)S(1)} %select_dynamic-update-slice_fusion) | copy-start | bytes 12582916
  78.6 36.3 %copy-start.34 = (f32[1024,256]{1,0:T(8,128)}, f32[1024,256]{1,0:T(8,128)S(1)}, u32[]{:S(2)}) copy-start(f32[1024,256]{1,0:T(8,128)S(1)} %fusion.14) | copy-start | bytes 3145732
  79.6 35.3 %copy-start.35 = (f32[1024,256]{1,0:T(8,128)}, f32[1024,256]{1,0:T(8,128)S(1)}, u32[]{:S(2)}) copy-start(f32[1024,256]{1,0:T(8,128)S(1)} %fusion.4) | copy-start | bytes 3145732
  80.6 31.6 %copy-start.36 = (f32[1024,256]{1,0:T(8,128)}, f32[1024,256]{1,0:T(8,128)S(1)}, u32[]{:S(2)}) copy-start(f32[1024,256]{1,0:T(8,128)S(1)} %fusion.16) | copy-start | bytes 3145732
  93.5 4.3 %copy-start.16 = (f32[512,256]{1,0:T(8,128)}, f32[512,256]{1,0:T(8,128)S(1)}, u32[]{:S(2)}) copy-start(f32[512,256]{1,0:T(8,128)S(1)} %fusion.20) | copy-start | bytes 1572868
  95.4 2.3 %copy-start.18 = (f32[512,256]{1,0:T(8,128)}, f32[512,256]{1,0:T(8,128)S(1)}, u32[]{:S(2)}) copy-start(f32[512,256]{1,0:T(8,128)S(1)} %fusion.21) | copy-start | bytes 1572868
  98.4 16.4 %copy-start.24 = (f32[3,512,256]{2,1,0:T(8,128)}, f32[3,512,256]{2,1,0:T(8,128)S(1)}, u32[]{:S(2)}) copy-start(f32[3,512,256]{2,1,0:T(8,128)S(1)} %fusion.28) | copy-start | bytes 4718596
  117.5 44.0 %collective-permute-start.20 = (f32[1,384,512]{2,1,0:T(8,128)}, f32[1,384,512]{2,1,0:T(8,128)}, u32[]{:S(2)}, u32[]{:S(2)}) collective-permute-start(f32[1,384,512]{2,1,0:T(8,128)} %slice.167), channel_id=1, source_target_pairs={{0,1},{1,0},{2,3},{3,2},{4,5},{5,4},{6,7},{7,6},{8,9},{9,8},{10,11... | collective-permute-start | bytes 2359304 | tf_op jit(solution)/shard_map/ppermute | solution.py:139
  120.6 6.1 %copy-start.15 = (f32[1,4,2,64,256]{4,3,2,1,0:T(8,128)S(1)}, f32[1,4,2,64,256]{4,3,2,1,0:T(8,128)}, u32[]{:S(2)}) copy-start(f32[1,4,2,64,256]{4,3,2,1,0:T(8,128)} %copy-done.14) | copy-start | bytes 1572868
  126.7 4.2 %copy-start.25 = (f32[1024,256]{1,0:T(8,128)}, f32[1024,256]{1,0:T(8,128)S(1)}, u32[]{:S(2)}) copy-start(f32[1024,256]{1,0:T(8,128)S(1)} %get-tuple-element.27) | copy-start | bytes 3145732
  126.7 2.3 %copy-start.1 = (f32[512,1024]{1,0:T(8,128)S(1)}, f32[512,1024]{1,0:T(8,128)}, u32[]{:S(2)}) copy-start(f32[512,1024]{1,0:T(8,128)} %copy.45) | copy-start | bytes 6291460
  135.7 3.0 %copy-start.17 = (f32[512,256]{1,0:T(8,128)S(1)}, f32[512,256]{1,0:T(8,128)}, u32[]{:S(2)}) copy-start(f32[512,256]{1,0:T(8,128)} %copy-done.16) | copy-start | bytes 1572868
  135.7 3.0 %copy-start.19 = (f32[512,256]{1,0:T(8,128)S(1)}, f32[512,256]{1,0:T(8,128)}, u32[]{:S(2)}) copy-start(f32[512,256]{1,0:T(8,128)} %copy-done.18) | copy-start | bytes 1572868
  135.7 3.1 %copy-start.21 = (f32[512,256]{1,0:T(8,128)S(1)}, f32[512,256]{1,0:T(8,128)}, u32[]{:S(2)}) copy-start(f32[512,256]{1,0:T(8,128)} %copy-done.20) | copy-start | bytes 1572868
  135.7 3.1 %copy-start.30 = (f32[1,4,2,64,256]{4,3,2,1,0:T(8,128)S(1)}, f32[1,4,2,64,256]{4,3,2,1,0:T(8,128)}, u32[]{:S(2)}) copy-start(f32[1,4,2,64,256]{4,3,2,1,0:T(8,128)} %convolution_bitcast_fusion.2) | copy-start | bytes 1572868
  135.7 3.1 %copy-start.31 = (f32[1,4,2,64,256]{4,3,2,1,0:T(8,128)S(1)}, f32[1,4,2,64,256]{4,3,2,1,0:T(8,128)}, u32[]{:S(2)}) copy-start(f32[1,4,2,64,256]{4,3,2,1,0:T(8,128)} %convolution_bitcast_fusion.1) | copy-start | bytes 1572868
  138.8 3.6 %copy-start.29 = (f32[1024,512]{0,1:T(8,128)S(1)}, f32[1024,512]{0,1:T(8,128)}, u32[]{:S(2)}) copy-start(f32[1024,512]{0,1:T(8,128)} %fusion.55) | copy-start | bytes 6291460
  139.7 2.7 %copy-start.4 = (f32[1024,512]{0,1:T(8,128)S(1)}, f32[1024,512]{0,1:T(8,128)}, u32[]{:S(2)}) copy-start(f32[1024,512]{0,1:T(8,128)} %fusion.85) | copy-start | bytes 6291460
  139.7 2.7 %copy-start.13 = (f32[1,4,2,64,256]{4,3,2,1,0:T(8,128)S(1)}, f32[1,4,2,64,256]{4,3,2,1,0:T(8,128)}, u32[]{:S(2)}) copy-start(f32[1,4,2,64,256]{4,3,2,1,0:T(8,128)} %copy-done.12) | copy-start | bytes 1572868
  139.7 3.0 %copy-start.26 = (f32[1024,256]{1,0:T(8,128)S(1)}, f32[1024,256]{1,0:T(8,128)}, u32[]{:S(2)}) copy-start(f32[1024,256]{1,0:T(8,128)} %copy-done.25) | copy-start | bytes 3145732
  139.7 3.6 %copy-start.28 = (f32[1024,512]{0,1:T(8,128)S(1)}, f32[1024,512]{0,1:T(8,128)}, u32[]{:S(2)}) copy-start(f32[1024,512]{0,1:T(8,128)} %fusion.54) | copy-start | bytes 6291460
  139.7 18.7 %collective-permute-start.29 = (f32[3,4,64,256]{3,2,1,0:T(8,128)S(1)}, f32[3,4,64,256]{3,2,1,0:T(8,128)S(1)}, u32[]{:S(2)}, u32[]{:S(2)}) collective-permute-start(f32[3,4,64,256]{3,2,1,0:T(8,128)S(1)} %select_bitcast_fusion), channel_id=1, source_target_pairs={{0,2},{2,0},{1,3},{3,1},{4,6},{6,4},{5,7},{7,5},{8,10},{10,8},{9,1... | collective-permute-start | bytes 2359304 | tf_op jit(solution)/shard_map/ppermute | solution.py:239
  145.0 30.8 %collective-permute-start.25 = (f32[2,384,512]{1,2,0:T(8,128)S(1)}, f32[2,384,512]{1,2,0:T(8,128)S(1)}, u32[]{:S(2)}, u32[]{:S(2)}) collective-permute-start(f32[2,384,512]{1,2,0:T(8,128)S(1)} %pad_maximum_fusion.1), channel_id=1, source_target_pairs={{0,1},{1,0},{2,3},{3,2},{4,5},{5,4},{6,7},{7,6},{8,9},{9,8},{10,11... | collective-permute-start | bytes 4718600 | tf_op jit(solution)/shard_map/ppermute | solution.py:139
  158.6 4.4 %copy-start.3 = (f32[1,1024,512]{2,1,0:T(8,128)S(1)}, f32[1,1024,512]{2,1,0:T(8,128)}, u32[]{:S(2)}) copy-start(f32[1,1024,512]{2,1,0:T(8,128)} %copy-done.2) | copy-start | bytes 6291460
  158.6 12.1 %collective-permute-start.32 = (f32[3,64,256]{2,1,0:T(8,128)S(1)}, f32[3,64,256]{2,1,0:T(8,128)S(1)}, u32[]{:S(2)}, u32[]{:S(2)}) collective-permute-start(f32[3,64,256]{2,1,0:T(8,128)S(1)} %get-tuple-element.44), channel_id=1, source_target_pairs={{4,12},{5,0},{8,1},{9,5},{6,14},{7,2},{10,3},{11,7},{20,28},{21,16... | collective-permute-start | bytes 589832 | tf_op jit(solution)/shard_map/ppermute | solution.py:244
  160.1 11.3 %collective-permute-start.30 = (f32[3,64,256]{2,1,0:T(8,128)S(1)}, f32[3,64,256]{2,1,0:T(8,128)S(1)}, u32[]{:S(2)}, u32[]{:S(2)}) collective-permute-start(f32[3,64,256]{2,1,0:T(8,128)S(1)} %get-tuple-element.43), channel_id=1, source_target_pairs={{5,4},{8,9},{7,6},{10,11},{21,20},{24,25},{23,22},{26,27}} | collective-permute-start | bytes 589832 | tf_op jit(solution)/shard_map/ppermute | solution.py:248
  160.8 11.3 %collective-permute-start.33 = (f32[3,64,256]{2,1,0:T(8,128)S(1)}, f32[3,64,256]{2,1,0:T(8,128)S(1)}, u32[]{:S(2)}, u32[]{:S(2)}) collective-permute-start(f32[3,64,256]{2,1,0:T(8,128)S(1)} %select_bitcast_fusion.3), channel_id=1, source_target_pairs={{4,0},{5,8},{8,5},{9,13},{6,2},{7,10},{10,7},{11,15},{20,16},{21,2... | collective-permute-start | bytes 589832 | tf_op jit(solution)/shard_map/ppermute | solution.py:244
  161.5 9.2 %copy-start.40 = (f32[1,256,512]{2,1,0:T(8,128)S(1)}, f32[1,256,512]{2,1,0:T(8,128)}, u32[]{:S(2)}) copy-start(f32[1,256,512]{2,1,0:T(8,128)} %slice.165) | copy-start | bytes 1572868
  161.6 12.8 %collective-permute-start.31 = (f32[3,64,256]{2,1,0:T(8,128)S(1)}, f32[3,64,256]{2,1,0:T(8,128)S(1)}, u32[]{:S(2)}, u32[]{:S(2)}) collective-permute-start(f32[3,64,256]{2,1,0:T(8,128)S(1)} %fusion.64), channel_id=1, source_target_pairs={{4,8},{5,12},{8,13},{9,1},{6,10},{7,14},{10,15},{11,3},{20,24},{21... | collective-permute-start | bytes 589832 | tf_op jit(solution)/shard_map/ppermute | solution.py:244
  170.7 26.2 %collective-permute-start.19 = (f32[1,256,512]{2,1,0:T(8,128)S(1)}, f32[1,256,512]{2,1,0:T(8,128)S(1)}, u32[]{:S(2)}, u32[]{:S(2)}) collective-permute-start(f32[1,256,512]{2,1,0:T(8,128)S(1)} %copy-done.40), channel_id=1, source_target_pairs={{5,4},{8,9},{7,6},{10,11},{21,20},{24,25},{23,22},{26,27}} | collective-permute-start | bytes 1572872 | tf_op jit(solution)/shard_map/ppermute | solution.py:144
  171.4 44.5 %collective-permute-start.24 = (f32[2,256,512]{1,2,0:T(8,128)S(1)}, f32[2,256,512]{1,2,0:T(8,128)S(1)}, u32[]{:S(2)}, u32[]{:S(2)}) collective-permute-start(f32[2,256,512]{1,2,0:T(8,128)S(1)} %pad_maximum_fusion.3), channel_id=1, source_target_pairs={{5,4},{8,9},{7,6},{10,11},{21,20},{24,25},{23,22},{26,27}} | collective-permute-start | bytes 3145736 | tf_op jit(solution)/shard_map/ppermute | solution.py:144
  172.2 5.2 %collective-permute-start.23 = (f32[1,128,512]{2,1,0:T(8,128)S(1)}, f32[1,128,512]{2,1,0:T(8,128)S(1)}, u32[]{:S(2)}, u32[]{:S(2)}) collective-permute-start(f32[1,128,512]{2,1,0:T(8,128)S(1)} %get-tuple-element.47), channel_id=1, source_target_pairs={{4,0},{5,8},{8,5},{9,13},{6,2},{7,10},{10,7},{11,15},{20,16},{21,2... | collective-permute-start | bytes 786440 | tf_op jit(solution)/shard_map/ppermute | solution.py:141
  174.4 17.6 %collective-permute-start.22 = (f32[1,128,512]{2,1,0:T(8,128)S(1)}, f32[1,128,512]{2,1,0:T(8,128)S(1)}, u32[]{:S(2)}, u32[]{:S(2)}) collective-permute-start(f32[1,128,512]{2,1,0:T(8,128)S(1)} %get-tuple-element.48), channel_id=1, source_target_pairs={{4,12},{5,0},{8,1},{9,5},{6,14},{7,2},{10,3},{11,7},{20,28},{21,16... | collective-permute-start | bytes 786440 | tf_op jit(solution)/shard_map/ppermute | solution.py:141
  175.7 19.0 %collective-permute-start.21 = (f32[1,128,512]{2,1,0:T(8,128)S(1)}, f32[1,128,512]{2,1,0:T(8,128)S(1)}, u32[]{:S(2)}, u32[]{:S(2)}) collective-permute-start(f32[1,128,512]{2,1,0:T(8,128)S(1)} %get-tuple-element.49), channel_id=1, source_target_pairs={{4,8},{5,12},{8,13},{9,1},{6,10},{7,14},{10,15},{11,3},{20,24},{21... | collective-permute-start | bytes 786440 | tf_op jit(solution)/shard_map/ppermute | solution.py:141
  177.4 20.4 %collective-permute-start.28 = (f32[2,128,512]{1,2,0:T(8,128)S(1)}, f32[2,128,512]{1,2,0:T(8,128)S(1)}, u32[]{:S(2)}, u32[]{:S(2)}) collective-permute-start(f32[2,128,512]{1,2,0:T(8,128)S(1)} %get-tuple-element.32), channel_id=1, source_target_pairs={{4,0},{5,8},{8,5},{9,13},{6,2},{7,10},{10,7},{11,15},{20,16},{21,2... | collective-permute-start | bytes 1572872 | tf_op jit(solution)/shard_map/ppermute | solution.py:141
  192.0 22.4 %collective-permute-start.27 = (f32[2,128,512]{1,2,0:T(8,128)S(1)}, f32[2,128,512]{1,2,0:T(8,128)S(1)}, u32[]{:S(2)}, u32[]{:S(2)}) collective-permute-start(f32[2,128,512]{1,2,0:T(8,128)S(1)} %get-tuple-element.33), channel_id=1, source_target_pairs={{4,12},{5,0},{8,1},{9,5},{6,14},{7,2},{10,3},{11,7},{20,28},{21,16... | collective-permute-start | bytes 1572872 | tf_op jit(solution)/shard_map/ppermute | solution.py:141
  194.8 21.1 %collective-permute-start.26 = (f32[2,128,512]{1,2,0:T(8,128)S(1)}, f32[2,128,512]{1,2,0:T(8,128)S(1)}, u32[]{:S(2)}, u32[]{:S(2)}) collective-permute-start(f32[2,128,512]{1,2,0:T(8,128)S(1)} %get-tuple-element.34), channel_id=1, source_target_pairs={{4,8},{5,12},{8,13},{9,1},{6,10},{7,14},{10,15},{11,3},{20,24},{21... | collective-permute-start | bytes 1572872 | tf_op jit(solution)/shard_map/ppermute | solution.py:141
  (12 other events, 16.7 us)

commit v2 on v0

v2 whole, which is shorter than its diff:
```python
import functools
import math

import jax
import jax.numpy as jnp
from jax import lax
from jax.experimental import pallas as pl
from jax.experimental.pallas import tpu as pltpu
from jax.sharding import PartitionSpec as P

EPSILON = 1e-06
CELL = 4
ROUNDS = CELL - 1
PLACE = ("tok", "head")
SWAP = [(0, 1), (1, 0)]
F32 = jnp.float32
BF16 = jnp.bfloat16
NN = ((1,), (0,))
NT = ((1,), (1,))
ANY = pl.BlockSpec(memory_space=pl.ANY)
VMEM = pl.BlockSpec(memory_space=pltpu.VMEM)


def home_of(head):
    return (CELL - 1) // 2 + head


def source_of(head, turn):
    return (home_of(head) + 1 + (turn + 2 * (1 - head)) % ROUNDS) % CELL


def routes(cells):
    rounds = []
    for turn in range(ROUNDS):
        pairs = []
        for cell in range(cells):
            here = []
            for head in range(2):
                for core in range(2):
                    origin = cell * CELL + source_of(head, turn + core)
                    home = cell * CELL + home_of(head)
                    here.append((origin * 2 + head, home * 2 + core))
            everyone = range(cell * CELL * 2, (cell + 1) * CELL * 2)
            idle = sorted(set(everyone) - {first for first, _ in here})
            free = sorted(set(everyone) - {second for _, second in here})
            pairs += here + list(zip(idle, free))
        rounds.append(pairs)
    return rounds


def flipped(pairs):
    return [(second, first) for first, second in pairs]


def split(value):
    high = value.astype(BF16)
    return high, (value - high.astype(F32)).astype(BF16)


def dot3(left, right, form):
    def one(first, second):
        return lax.dot_general(first, second, (form, ((), ())), preferred_element_type=F32)

    return one(left[0], right[0]) + (one(left[0], right[1]) + one(left[1], right[0]))


def position():
    place = lax.rem(lax.axis_index("tok"), CELL)
    core = lax.axis_index("head")
    return place, core


def spot_of(place, core, slot):
    if slot == ROUNDS:
        return place
    head = place - home_of(0)
    return lax.rem(place + 1 + lax.rem(slot + core + 2 * (1 - head) + ROUNDS, ROUNDS), CELL)


def halves_sent(place, core):
    ahead = lax.rem(place - home_of(0) - core - 1 + 2 * CELL, CELL)
    turn0 = lax.rem(ahead + 1 - core, ROUNDS)
    turn1 = lax.rem(turn0 + ROUNDS - 1, ROUNDS)
    return turn0, turn1


def run_copies(copies):
    for copy in copies:
        copy.start()
    for copy in copies:
        copy.wait()


def pack_weights_kernel(gate, up, down, *rest):
    outs, sems = rest[:-1], rest[-1]
    place, core = position()
    _, turn1 = halves_sent(place, core)
    cols = outs[0].shape[2]
    copies = []
    for piece, out in enumerate(outs):
        if piece < ROUNDS:
            part = jnp.where(turn1 == piece, 1, 0)
        else:
            part = core if piece == ROUNDS else 1 - core
        begin = pl.multiple_of(part * cols, cols)
        for which, ref in enumerate((gate, up, down)):
            copies.append(
                pltpu.make_async_copy(
                    ref.at[:, pl.ds(begin, cols)], out.at[which], sems.at[piece, which]
                )
            )
    run_copies(copies)


def pack_rows_kernel(scaled, half, *refs):
    if scaled:
        first, second, scale, *rest = refs
        *outs, held, sems, load_sem = rest
        load = pltpu.make_async_copy(second, held, load_sem)
        load.start()
    else:
        first, second, *rest = refs
        *outs, sems = rest
    place, core = position()
    _, turn1 = halves_sent(place, core)

    def copies_of(which, ref):
        copies = []
        for piece in range(ROUNDS):
            begin = pl.multiple_of(jnp.where(turn1 == piece, half, 0), half)
            copies.append(
                pltpu.make_async_copy(
                    ref.at[pl.ds(begin, half)],
                    outs[piece].at[pl.ds(which * half, half)],
                    sems.at[piece, which],
                )
            )
        copies.append(
            pltpu.make_async_copy(
                ref, outs[ROUNDS].at[pl.ds(which * 2 * half, 2 * half)], sems.at[ROUNDS, which]
            )
        )
        return copies

    early = copies_of(0, first)
    for copy in early:
        copy.start()
    if scaled:
        load.wait()
        held[...] = held[...] * scale[...]
        late = copies_of(1, held)
    else:
        late = copies_of(1, second)
    for copy in late:
        copy.start()
    for copy in early + late:
        copy.wait()


def fetch_rows(near, far, own, got, buffers, sems):
    half = near[0].shape[0] // 2
    place, core = position()
    mine = core == place - home_of(0)
    for block in range(ROUNDS):
        for which in range(2):
            rows = pl.ds(which * half, half)
            for side, group in enumerate((near, far)):
                pltpu.make_async_copy(
                    group[block].at[rows],
                    buffers[which].at[block, pl.ds(side * half, half)],
                    sems.at[block, which * 2 + side],
                ).start()

    def local(source):
        for which in range(2):
            for side in range(2):
                pltpu.make_async_copy(
                    source.at[pl.ds((which * 2 + side) * half, half)],
                    buffers[which].at[ROUNDS, pl.ds(side * half, half)],
                    sems.at[ROUNDS, which * 2 + side],
                ).start()

    @pl.when(mine)
    def _():
        local(own)

    @pl.when(jnp.logical_not(mine))
    def _():
        local(got)


def wait_rows(buffers, block, sems):
    half = buffers[0].shape[1] // 2
    for part in range(4):
        view = buffers[part // 2].at[block, pl.ds((part % 2) * half, half)]
        pltpu.make_async_copy(view, view, sems.at[block, part]).wait()


def row_starts(cells, reps, rows):
    place, core = position()
    rep = lax.axis_index("rep")
    starts = {}
    for cell in range(cells):
        for shift in range(reps):
            owner_rep = lax.rem(rep - shift + reps, reps)
            for slot in range(CELL):
                spot = spot_of(place, core, slot)
                begin = ((cell * CELL + spot) * reps + owner_rep) * rows
                starts[cell, shift, slot] = pl.multiple_of(begin, rows)
    return starts


def silu_parts(pre):
    sigma = jax.nn.sigmoid(pre)
    rest = 1.0 - sigma
    return sigma, pre * sigma, sigma * (1.0 + pre * rest)


def store_split(ref, index, value):
    high, low = split(value)
    ref[(0,) + index] = high
    ref[(1,) + index] = low


def pair_of(ref, *index):
    return ref[(0,) + index], ref[(1,) + index]


def inner_kernel(cells, reps, *refs):
    pieces = CELL * reps if cells == 1 else 1
    parts, refs = refs[:pieces], refs[pieces:]
    near, far, (own, got), refs = refs[:3], refs[3:6], refs[6:8], refs[8:]
    weights, gates, ups, backs, steps, *scratch = refs
    keys, targets, wide, turned, acts, row_sems, weight_sems = scratch
    rows = parts[0].shape[-2]
    starts = row_starts(cells, reps, rows)
    copies = []
    for number, ((cell, shift, slot), begin) in enumerate(starts.items()):
        source = parts[shift * CELL + slot] if cells == 1 else parts[0].at[cell, shift * CELL + slot]
        copies.append(
            pltpu.make_async_copy(
                source, weights.at[:, pl.ds(begin, rows)], weight_sems.at[number]
            )
        )
    for copy in copies:
        copy.start()
    fetch_rows(near, far, own, got, (keys, targets), row_sems)
    for copy in copies:
        copy.wait()
    for which in range(3):
        store_split(wide, (which,), weights[which])
    size = keys.shape[1]

    @pl.loop(0, CELL)
    def _(block):
        wait_rows((keys, targets), block, row_sems)
        where = pl.ds(pl.multiple_of(block * size, size), size)
        key, target = split(keys[block]), split(targets[block])
        gate_pre = dot3(key, pair_of(wide, 0), NN)
        up_pre = dot3(key, pair_of(wide, 1), NN)
        back = dot3(target, pair_of(wide, 2), NN)
        gates[where] = gate_pre
        ups[where] = up_pre
        backs[where] = back
        _, act, slope = silu_parts(gate_pre)
        store_split(acts, (0, where), back * up_pre * slope)
        store_split(acts, (1, where), back * act)
        store_split(acts, (2, where), act * up_pre)
        for part in range(2):
            turned[part, 0, :, where] = key[part].T
            turned[part, 1, :, where] = target[part].T

    for which in range(3):
        steps[which] = dot3(pair_of(turned, which // 2), pair_of(acts, which), NN)


def renew_kernel(weights, steps, high, low):
    for which in range(3):
        weight = weights[which]
        moved = weight - steps[which]
        old = jnp.mean(weight * weight, axis=0, keepdims=True) + EPSILON
        new = jnp.mean(moved * moved, axis=0, keepdims=True) + EPSILON
        high[which], low[which] = split(moved * (jnp.sqrt(old) / jnp.sqrt(new)))


def read_kernel(*refs):
    near, far, (own, got, high, low), refs = refs[:3], refs[3:6], refs[6:10], refs[10:]
    (totals, near_out, far_out, local_out), scratch = (
        (refs[0], refs[1:4], refs[4:7], refs[7]),
        refs[8:],
    )
    queries, cots, turned, acts, sent, row_sems, out_sems = scratch
    fetch_rows(near, far, own, got, (queries, cots), row_sems)
    size = queries.shape[1]
    half = size // 2

    def weight(which):
        return high[which], low[which]

    def outgoing(block):
        if block < ROUNDS:
            return [
                (sent.at[block, pl.ds(0, half)], near_out[block]),
                (sent.at[block, pl.ds(half, half)], far_out[block]),
            ]
        return [(sent.at[block], local_out)]

    @pl.loop(0, CELL)
    def _(block):
        wait_rows((queries, cots), block, row_sems)
        where = pl.ds(pl.multiple_of(block * size, size), size)
        query, cot = split(queries[block]), split(cots[block])
        gate_pre = dot3(query, weight(0), NN)
        up_pre = dot3(query, weight(1), NN)
        back = dot3(cot, weight(2), NN)
        _, act, slope = silu_parts(gate_pre)
        gate_back = split(back * up_pre * slope)
        up_back = split(back * act)
        for part in range(2):
            acts[part, 0, where] = gate_back[part]
            acts[part, 1, where] = up_back[part]
            turned[part, 0, :, where] = query[part].T
            turned[part, 1, :, where] = cot[part].T
        store_split(acts, (2, where), act * up_pre)
        sent[block] = dot3(gate_back, weight(0), NT) + dot3(up_back, weight(1), NT)
        for number in range(CELL):

            @pl.when(block == number)
            def _():
                for side, (source, out) in enumerate(outgoing(number)):
                    pltpu.make_async_copy(source, out, out_sems.at[number, side]).start()

    for which in range(3):
        totals[which] = dot3(pair_of(turned, which // 2), pair_of(acts, which), NN)
    for block in range(CELL):
        for side, (source, out) in enumerate(outgoing(block)):
            pltpu.make_async_copy(source, out, out_sems.at[block, side]).wait()


def backward_kernel(cells, reps, *refs):
    near, far, (own, got), refs = refs[:3], refs[3:6], refs[6:8], refs[8:]
    (weights, steps, totals, gates, ups, backs), refs = refs[:6], refs[6:]
    near_out, far_out, local_out, refs = refs[:3], refs[3:6], refs[6], refs[7:]
    pieces, scratch = refs[:reps], refs[reps:]
    keys, targets, wide, cots, turned, acts, grads, sent, row_sems, out_sems, grad_sems = scratch
    fetch_rows(near, far, own, got, (keys, targets), row_sems)
    size = keys.shape[1]
    half = size // 2
    width = weights.shape[1]
    scale = 1.0 / width
    for which in range(3):
        weight, total = weights[which], totals[which]
        moved = weight - steps[which]
        old = jnp.mean(weight * weight, axis=0, keepdims=True) + EPSILON
        new = jnp.mean(moved * moved, axis=0, keepdims=True) + EPSILON
        ratio = jnp.sqrt(old) / jnp.sqrt(new)
        ratio_cot = jnp.sum(total * moved, axis=0, keepdims=True) * scale
        moved_cot = ratio * (total - moved * (ratio_cot / new))
        direct = moved_cot + weight * (ratio_cot * ratio / old)
        if cells > 1:
            direct = direct * jnp.where(lax.axis_index("tok") < CELL, 1.0, 0.0)
        grads[which] = direct
        store_split(wide, (which,), weight)
        store_split(cots, (which,), -moved_cot)

    def outgoing(block):
        if block < ROUNDS:
            return [
                (sent.at[which, block, pl.ds(side * half, half)],
                 (near_out, far_out)[side][block].at[pl.ds(which * half, half)])
                for which in range(2)
                for side in range(2)
            ]
        return [
            (sent.at[which, block], local_out.at[pl.ds(which * size, size)]) for which in range(2)
        ]

    @pl.loop(0, CELL)
    def _(block):
        wait_rows((keys, targets), block, row_sems)
        where = pl.ds(pl.multiple_of(block * size, size), size)
        key, target = split(keys[block]), split(targets[block])
        gate_back_cot = dot3(key, pair_of(cots, 0), NN)
        up_back_cot = dot3(key, pair_of(cots, 1), NN)
        hidden_cot = dot3(target, pair_of(cots, 2), NN)
        gate_pre, up_pre, back = gates[where], ups[where], backs[where]
        sigma, act, slope = silu_parts(gate_pre)
        bend = sigma * (1.0 - sigma) * (2.0 + gate_pre * (1.0 - 2.0 * sigma))
        mixed = gate_back_cot * slope
        back_cot = split(mixed * up_pre + up_back_cot * act)
        up_cot = split(mixed * back + hidden_cot * act)
        gate_cot = split(
            gate_back_cot * back * up_pre * bend
            + (up_back_cot * back + hidden_cot * up_pre) * slope
        )
        for part in range(2):
            acts[part, 0, where] = gate_cot[part]
            acts[part, 1, where] = up_cot[part]
            acts[part, 2, where] = back_cot[part]
            turned[part, 0, :, where] = key[part].T
            turned[part, 1, :, where] = target[part].T
        sent[0, block] = (
            dot3(gate_cot, pair_of(wide, 0), NT)
            + dot3(up_cot, pair_of(wide, 1), NT)
            + dot3(split(back * up_pre * slope), pair_of(cots, 0), NT)
            + dot3(split(back * act), pair_of(cots, 1), NT)
        )
        sent[1, block] = dot3(back_cot, pair_of(wide, 2), NT) + dot3(
            split(act * up_pre), pair_of(cots, 2), NT
        )
        for number in range(CELL):

            @pl.when(block == number)
            def _():
                for side, (source, out) in enumerate(outgoing(number)):
                    pltpu.make_async_copy(source, out, out_sems.at[number, side]).start()

    for which in range(3):
        grads[which] += dot3(pair_of(turned, which // 2), pair_of(acts, which), NN)
    rows = pieces[0].shape[-2]
    copies = []
    place, core = position()
    rep = lax.axis_index("rep")
    number = 0
    for cell in range(cells):
        for shift in range(reps):
            owner_rep = lax.rem(rep + shift, reps)
            for slot in range(CELL):
                spot = spot_of(place, core, slot)
                begin = pl.multiple_of(((cell * CELL + spot) * reps + owner_rep) * rows, rows)
                copies.append(
                    pltpu.make_async_copy(
                        grads.at[:, pl.ds(begin, rows)],
                        pieces[shift].at[cell, slot],
                        grad_sems.at[number],
                    )
                )
                number += 1
    run_copies(copies)
    for block in range(CELL):
        for side, (source, out) in enumerate(outgoing(block)):
            pltpu.make_async_copy(source, out, out_sems.at[block, side]).wait()


def call(kernel, inputs, in_specs, outs, out_specs, scratch, flops=0):
    moved = sum(math.prod(value.shape) * value.dtype.itemsize for value in list(inputs) + list(outs))
    return pl.pallas_call(
        kernel,
        out_shape=outs,
        in_specs=in_specs,
        out_specs=out_specs,
        scratch_shapes=scratch,
        cost_estimate=pl.CostEstimate(flops=flops, bytes_accessed=moved, transcendentals=0),
        compiler_params=pltpu.CompilerParams(vmem_limit_bytes=48 << 20),
    )(*inputs)


def per_device(
    query_rows, key_rows, value_rows, step_logits, read_cotangent, fast_gate, fast_up, fast_down
):
    tokens_here, depth = key_rows.shape[2:]
    half = tokens_here // 2
    tok_size = lax.axis_size("tok")
    reps = lax.axis_size("rep")
    cells = tok_size // CELL
    assert tok_size % CELL == 0 and lax.axis_size("head") == 2
    factor = 1.0 / (8.0 * math.sqrt(tokens_here * tok_size))
    pairs = routes(cells)
    place, core = position()
    turn0, turn1 = halves_sent(place, core)
    at_home = place == home_of(0) + core
    cell_groups = [[cell * CELL + spot for cell in range(cells)] for spot in range(CELL)]
    rows, width = fast_gate.shape[1:]
    cols = width // 2
    shape = jax.ShapeDtypeStruct
    dma = pltpu.SemaphoreType.DMA

    def shifted(shift, sign):
        return [(rep, (rep + sign * shift) % reps) for rep in range(reps)]

    step = jax.nn.softplus(step_logits[0, 0]) * factor

    packed = call(
        pack_weights_kernel,
        (fast_gate[0], fast_up[0], fast_down[0]),
        [ANY] * 3,
        [shape((3, rows, cols), F32)] * (ROUNDS + 2),
        [ANY] * (ROUNDS + 2),
        [dma((ROUNDS + 2, 3))],
    )
    slots = [lax.ppermute(packed[turn], PLACE, pairs[turn]) for turn in range(ROUNDS)]
    other = lax.ppermute(packed[ROUNDS + 1], "head", SWAP)
    owner = core == place - home_of(0)
    slots.append(jnp.where(owner, packed[ROUNDS], other))
    parts = list(slots)
    for shift in range(1, reps):
        parts += [lax.ppermute(piece, "rep", shifted(shift, 1)) for piece in slots]
    if cells > 1:
        parts = [lax.all_gather(jnp.stack(parts), "tok", axis_index_groups=cell_groups)]

    def gather(first, second, scale):
        outs = [shape((2 * half, depth), F32)] * ROUNDS + [shape((4 * half, depth), F32)]
        scratch = [dma((CELL, 2))]
        inputs, specs = [first, second], [ANY, ANY]
        if scale is not None:
            inputs, specs = inputs + [scale], specs + [VMEM]
            scratch = [pltpu.VMEM((2 * half, depth), F32)] + scratch + [dma]
        packed = call(
            functools.partial(pack_rows_kernel, scale is not None, half),
            inputs,
            specs,
            outs,
            [ANY] * CELL,
            scratch,
        )
        near = [lax.ppermute(packed[turn], PLACE, pairs[turn]) for turn in range(ROUNDS)]
        got = lax.ppermute(packed[ROUNDS], "head", SWAP)
        far = [lax.ppermute(piece, "head", SWAP) for piece in near]
        return near + far + [packed[ROUNDS], got]

    def scatter(near, far, local):
        back = []
        for turn in range(ROUNDS):
            total = near[turn] + lax.ppermute(far[turn], "head", SWAP)
            back.append(lax.ppermute(total, PLACE, flipped(pairs[turn])))
        local = local + lax.ppermute(local, "head", SWAP)

        def choose(turn):
            return jnp.where(turn == 0, back[0], jnp.where(turn == 1, back[1], back[2]))

        low, high = choose(turn0), choose(turn1)
        found = []
        for which in range(low.shape[0] // half):
            span = slice(which * half, (which + 1) * half)
            remote = jnp.concatenate((low[span], high[span]))
            here = local[which * 2 * half : (which + 1) * 2 * half]
            found.append(jnp.where(at_home, here, remote))
        return found

    inner_rows = gather(key_rows[0, 0], value_rows[0, 0], -step[:, None])
    read_rows = gather(query_rows[0, 0], read_cotangent[0, 0], None)

    size = 2 * half
    count = CELL * size
    square = shape((3, width, cols), F32)
    tall = shape((count, cols), F32)
    product = 6 * count * width * cols
    buffers = [pltpu.VMEM((CELL, size, depth), F32)] * 2
    turned = pltpu.VMEM((2, 2, depth, count), BF16)
    acts = pltpu.VMEM((2, 3, count, cols), BF16)
    split_square = pltpu.VMEM((2, 3, width, cols), BF16)
    weights, gates, ups, backs, steps = call(
        functools.partial(inner_kernel, cells, reps),
        parts + inner_rows,
        [ANY] * (len(parts) + 8),
        [square, tall, tall, tall, square],
        [VMEM] * 5,
        buffers
        + [split_square, turned, acts, dma((CELL, 4)), dma((cells * reps * CELL,))],
        6 * product,
    )
    if cells > 1:
        steps = lax.psum(steps, "tok", axis_index_groups=cell_groups)
    narrow = shape((3, width, cols), BF16)
    high, low = call(
        renew_kernel, (weights, steps), [VMEM] * 2, [narrow, narrow], [VMEM] * 2, []
    )
    piece = shape((half, depth), F32)
    read = call(
        read_kernel,
        read_rows + [high, low],
        [ANY] * 8 + [VMEM] * 2,
        [square] + [piece] * 6 + [shape((size, depth), F32)],
        [VMEM] + [ANY] * 7,
        buffers
        + [turned, acts, pltpu.VMEM((CELL, size, depth), F32), dma((CELL, 4)), dma((CELL, 2))],
        8 * product,
    )
    totals = read[0]
    if cells > 1:
        totals = lax.psum(totals, "tok", axis_index_groups=cell_groups)
    piece = shape((size, depth), F32)
    final = call(
        functools.partial(backward_kernel, cells, reps),
        inner_rows + [weights, steps, totals, gates, ups, backs],
        [ANY] * 8 + [VMEM] * 6,
        [piece] * 6
        + [shape((2 * size, depth), F32)]
        + [shape((cells, CELL, 3, rows, cols), F32)] * reps,
        [ANY] * (7 + reps),
        buffers
        + [
            split_square,
            split_square,
            turned,
            acts,
            pltpu.VMEM((3, width, cols), F32),
            pltpu.VMEM((2, CELL, size, depth), F32),
            dma((CELL, 4)),
            dma((CELL, 4)),
            dma((cells * reps * CELL,)),
        ],
        12 * product,
    )
    (query_grad,) = scatter(read[1:4], read[4:7], read[7])
    key_grad, target_grad = scatter(final[0:3], final[3:6], final[6])

    given = list(final[7:])
    if cells > 1:
        given = [
            lax.psum_scatter(value, "tok", scatter_dimension=0, tiled=True, axis_index_groups=cell_groups)
            for value in given
        ]
    total = given[0][0]
    for shift in range(1, reps):
        total = total + lax.ppermute(given[shift][0], "rep", shifted(shift, 1))
    returned = [
        lax.ppermute(total[turn], PLACE, flipped(pairs[turn])) for turn in range(ROUNDS)
    ]
    home_piece = total[ROUNDS]
    home_other = lax.ppermute(home_piece, "head", SWAP)

    def choose(turn):
        return jnp.where(turn == 0, returned[0], jnp.where(turn == 1, returned[1], returned[2]))

    left = jnp.where(at_home, jnp.where(core == 0, home_piece, home_other), choose(turn0))
    right = jnp.where(at_home, jnp.where(core == 0, home_other, home_piece), choose(turn1))
    owned = jnp.concatenate((left, right), axis=2)

    value_grad = -step[:, None] * target_grad
    step_grad = -jnp.sum(value_rows[0, 0] * target_grad, axis=1)
    logit_grad = step_grad * factor * jax.nn.sigmoid(step_logits[0, 0])
    return (
        query_grad[None, None],
        key_grad[None, None],
        value_grad[None, None],
        logit_grad[None, None],
        owned[0][None],
        owned[1][None],
        owned[2][None],
    )


def solution(mesh):
    tokens = P(("groups", "rep"), "head", "tok", None)
    logits = P(("groups", "rep"), "head", "tok")
    weight = P("head", ("tok", "rep"), None)
    grad = P(("groups", "head"), ("tok", "rep"), None)
    return jax.shard_map(
        per_device,
        mesh=mesh,
        in_specs=(tokens, tokens, tokens, logits, tokens, weight, weight, weight),
        out_specs=(tokens, tokens, tokens, logits, grad, grad, grad),
        check_vma=False,
    )
```

time: 558 us -> 203 us (0.36)
  the two profiles are of different devices: /device:TPU:22 before, /device:TPU:1 now
where the time goes in v2:
time: 203 us
  waiting for transfers between devices  67.4 us (33%)
  starting transfers between devices  58.1 us (29%)
  Pallas kernels  47.3 us (23%)
  local copies, waits for them, and re-layouts  15.8 us (8%)
  other arithmetic  12.7 us (6%)
    pallas_call x7, Pallas kernels, call(): pl.pallas_call(kernel, out_shape=outs, in_specs=in_specs, out_specs=out_s...  47.3 us
    ppermute x3, waiting for transfers between devices, per_device(): lax.ppermute(total[turn], PLACE, flipped(pairs[turn]))  21.6 us
    ppermute x6, starting transfers between devices, scatter(): back.append(lax.ppermute(total, PLACE, flipped(pairs[turn])))  17 us
    ppermute x3, waiting for transfers between devices, per_device(): lax.ppermute(packed[turn], PLACE, pairs[turn])  16.3 us
    ppermute x6, waiting for transfers between devices, gather(): lax.ppermute(packed[turn], PLACE, pairs[turn])  15.4 us
    unnamed x58, local copies, waits for them, and re-layouts  14.9 us
    ppermute x6, starting transfers between devices, gather(): lax.ppermute(packed[turn], PLACE, pairs[turn])  13.8 us
    ppermute x4, waiting for transfers between devices, per_device(): parts += [lax.ppermute(piece, 'rep', shifted(shift, 1)) for piece in slots]  11.1 us
  transfers between devices with their start and end apart: 41, of which 14 were waited for; matrix products, arithmetic and copies ran while one was open for 6% of the time, Pallas kernels for 16%

profile of v2, /device:TPU:1, one launch (start us, length us, event | category | flops | bytes accessed | tf_op | source)
XLA Modules:
  0.0 202.5 jit_solution(6636374690948849923)
XLA Ops:
  0.7 1.0 copy-done.7
  1.6 0.9 copy-done.8
  2.5 0.9 copy-done.9
  3.4 0.9 shard_map.136
  4.4 0.7 copy-done.18
  5.1 0.8 copy.20
  6.1 1.0 copy-done
  7.1 1.0 copy-done.4
  8.2 1.1 shard_map.137
  9.3 0.8 copy-done.15
  10.1 3.7 %collective-permute-start.15 = (f32[256,512]{1,0:T(8,128)}, f32[256,512]{1,0:T(8,128)S(1)}, u32[]{:S(2)}, u32[]{:S(2)}) collective-permute-start(f32[256,512]{1,0:T(8,128)} %get-tuple-element.53), channel_id=1, source_target_pairs={{0,4},{8,5},{13,8},{1,9},{4,0},{5,1},{9,12},{12,13},{2,6},{10,7},{... | collective-permute-start | bytes 1572872 | tf_op jit(solution)/shard_map/ppermute | solution.py:516
  13.8 2.3 %collective-permute-start.16 = (f32[256,512]{1,0:T(8,128)}, f32[256,512]{1,0:T(8,128)S(1)}, u32[]{:S(2)}, u32[]{:S(2)}) collective-permute-start(f32[256,512]{1,0:T(8,128)} %get-tuple-element.54), channel_id=1, source_target_pairs={{8,4},{12,5},{1,8},{5,9},{0,0},{4,1},{9,12},{13,13},{10,6},{14,7},... | collective-permute-start | bytes 1572872 | tf_op jit(solution)/shard_map/ppermute | solution.py:516
  16.1 1.3 collective-permute-start.7
  17.4 3.1 %collective-permute-start.8 = (f32[3,64,256]{2,1,0:T(8,128)}, f32[3,64,256]{2,1,0:T(8,128)}, u32[]{:S(2)}, u32[]{:S(2)}) collective-permute-start(f32[3,64,256]{2,1,0:T(8,128)} %copy-done.18), channel_id=1, source_target_pairs={{8,4},{12,5},{1,8},{5,9},{0,0},{4,1},{9,12},{13,13},{10,6},{14,7},... | collective-permute-start | bytes 589832 | tf_op jit(solution)/shard_map/ppermute | solution.py:491
  20.9 1.0 broadcast_select_fusion.refs_3_
  21.8 15.4 %collective-permute-done.7.refs_0_ = f32[3,64,256]{2,1,0:T(8,128)} collective-permute-done((f32[3,64,256]{2,1,0:T(8,128)}, f32[3,64,256]{2,1,0:T(8,128)}, u32[]{:S(2)}, u32[]{:S(2)}) %collective-permute-start.7) | collective-permute-done | bytes 196640 | tf_op jit(solution)/shard_map/ppermute | solution.py:491
  37.3 1.2 collective-permute-start.14
  38.5 0.9 collective-permute-done.8.refs_1_
  39.4 1.2 collective-permute-start.11
  40.9 3.3 %collective-permute-done.14.refs_7_ = f32[3,64,256]{2,1,0:T(8,128)S(1)} collective-permute-done((f32[3,64,256]{2,1,0:T(8,128)S(1)}, f32[3,64,256]{2,1,0:T(8,128)S(1)}, u32[]{:S(2)}, u32[]{:S(2)}) %collective-permute-start.14) | collective-permute-done | bytes 196640 | tf_op jit(solution)/shard_map/ppermute | solution.py:497
  44.2 1.2 collective-permute-start.13
  45.7 2.7 %collective-permute-done.11.refs_4_ = f32[3,64,256]{2,1,0:T(8,128)S(1)} collective-permute-done((f32[3,64,256]{2,1,0:T(8,128)}, f32[3,64,256]{2,1,0:T(8,128)S(1)}, u32[]{:S(2)}, u32[]{:S(2)}) %collective-permute-start.11) | collective-permute-done | bytes 196640 | tf_op jit(solution)/shard_map/ppermute | solution.py:497
  48.4 4.2 %collective-permute-done.12.refs_5_ = f32[3,64,256]{2,1,0:T(8,128)S(1)} collective-permute-done((f32[3,64,256]{2,1,0:T(8,128)}, f32[3,64,256]{2,1,0:T(8,128)S(1)}, u32[]{:S(2)}, u32[]{:S(2)}) %collective-permute-start.12) | collective-permute-done | bytes 196640 | tf_op jit(solution)/shard_map/ppermute | solution.py:497
  52.6 2.0 collective-permute-start
  54.7 0.9 collective-permute-done.13.refs_6_
  55.5 5.6 %collective-permute-start.1 = (f32[256,512]{1,0:T(8,128)S(1)}, f32[256,512]{1,0:T(8,128)S(1)}, u32[]{:S(2)}, u32[]{:S(2)}) collective-permute-start(f32[256,512]{1,0:T(8,128)S(1)} %get-tuple-element.45), channel_id=1, source_target_pairs={{8,4},{12,5},{1,8},{5,9},{0,0},{4,1},{9,12},{13,13},{10,6},{14,7},... | collective-permute-start | bytes 1572872 | tf_op jit(solution)/shard_map/ppermute | solution.py:516
  61.8 4.8 %collective-permute-done.refs_0_ = f32[256,512]{1,0:T(8,128)S(1)} collective-permute-done((f32[256,512]{1,0:T(8,128)S(1)}, f32[256,512]{1,0:T(8,128)S(1)}, u32[]{:S(2)}, u32[]{:S(2)}) %collective-permute-start) | collective-permute-done | bytes 524320 | tf_op jit(solution)/shard_map/ppermute | solution.py:516
  66.6 2.3 %collective-permute-start.19 = (f32[256,512]{1,0:T(8,128)S(1)}, f32[256,512]{1,0:T(8,128)S(1)}, u32[]{:S(2)}, u32[]{:S(2)}) collective-permute-start(f32[256,512]{1,0:T(8,128)S(1)} %collective-permute-done.16.refs_9_.refs_1_), channel_id=1, source_target_pairs={{0,1},{1,0},{2,3},{3,2},{4,5},{5,4},{6,7},{7,6},{8,9},{9,8},{10,11... | collective-permute-start | bytes 1572872 | tf_op jit(solution)/shard_map/ppermute | solution.py:518
  69.0 8.6 %collective-permute-done.1.refs_1_ = f32[256,512]{1,0:T(8,128)S(1)} collective-permute-done((f32[256,512]{1,0:T(8,128)S(1)}, f32[256,512]{1,0:T(8,128)S(1)}, u32[]{:S(2)}, u32[]{:S(2)}) %collective-permute-start.1) | collective-permute-done | bytes 524320 | tf_op jit(solution)/shard_map/ppermute | solution.py:516
  77.5 2.0 collective-permute-done.2.refs_2_
  80.5 1.0 copy-done.27
  81.5 9.0 %shard_map.138 = (f32[3,512,256]{2,1,0:T(8,128)}, f32[1024,256]{1,0:T(8,128)S(1)}, f32[1024,256]{1,0:T(8,128)}, f32[1024,256]{1,0:T(8,128)}, f32[3,512,256]{2,1,0:T(8,128)}) custom-call(f32[3,64,256]{2,1,0:T(8,128)} %collective-permute-done.7.refs_0_, f32[3,64,256]{2,1,0:T(8,128)} %collective-permute-done.8.refs_1_, ...), custom_call_target="tpu_custom_call" | custom-call | flops 4831838208 | bytes 13107200 | tf_op jit(solution)/shard_map/pallas_call | solution.py:447
  90.5 1.0 copy-done.20
  91.5 1.4 copy-done.2
  92.9 1.4 copy-done.3
  94.3 0.6 shard_map.139
  95.0 0.9 copy-done.12
  95.9 1.0 copy-done.28
  96.9 14.0 %shard_map.140 = (f32[3,512,256]{2,1,0:T(8,128)}, f32[128,512]{1,0:T(8,128)S(1)}, f32[128,512]{1,0:T(8,128)S(1)}, f32[128,512]{1,0:T(8,128)S(1)}, f32[128,512]{1...) custom-call(f32[256,512]{1,0:T(8,128)S(1)} %collective-permute-done.refs_0_, ...), custom_call_target="tpu_custom_call" | custom-call | flops 6442450944 | bytes 10485760 | tf_op jit(solution)/shard_map/pallas_call | solution.py:447
  111.1 21.4 %shard_map.141 = (f32[256,512]{1,0:T(8,128)S(1)}, f32[256,512]{1,0:T(8,128)S(1)}, f32[256,512]{1,0:T(8,128)S(1)}, f32[256,512]{1,0:T(8,128)}, f32[256,512]{1,0:T...) custom-call(f32[256,512]{1,0:T(8,128)S(1)} %collective-permute-done., ...), custom_call_target="tpu_custom_call" | custom-call | flops 9663676416 | bytes 18874368 | tf_op jit(solution)/shard_map/pallas_call | solution.py:447
  132.5 1.2 collective-permute-start.36
  133.8 0.6 collective-permute-start.25
  135.0 0.9 collective-permute-done.25
  135.9 0.7 copy-done.25
  137.0 1.1 add.69
  138.1 1.0 add.68
  139.3 1.0 add.67
  141.1 1.1 add.73
  142.2 7.4 %collective-permute-start.28 = (f32[128,512]{1,0:T(8,128)S(1)}, f32[128,512]{1,0:T(8,128)S(1)}, u32[]{:S(2)}, u32[]{:S(2)}) collective-permute-start(f32[128,512]{1,0:T(8,128)S(1)} %add.69), channel_id=1, source_target_pairs={{4,12},{5,0},{8,5},{9,13},{0,1},{1,4},{12,8},{13,9},{6,14},{7,2},{... | collective-permute-start | bytes 786440 | tf_op jit(solution)/shard_map/ppermute | solution.py:525
  149.6 1.2 add.72
  150.8 2.2 %collective-permute-start.26 = (f32[128,512]{1,0:T(8,128)S(1)}, f32[128,512]{1,0:T(8,128)S(1)}, u32[]{:S(2)}, u32[]{:S(2)}) collective-permute-start(f32[128,512]{1,0:T(8,128)S(1)} %add.68), channel_id=1, source_target_pairs={{4,8},{5,12},{8,1},{9,5},{0,0},{1,4},{12,9},{13,13},{6,10},{7,14},... | collective-permute-start | bytes 786440 | tf_op jit(solution)/shard_map/ppermute | solution.py:525
  153.0 1.1 add.71
  154.2 5.3 %collective-permute-start.24 = (f32[128,512]{1,0:T(8,128)S(1)}, f32[128,512]{1,0:T(8,128)S(1)}, u32[]{:S(2)}, u32[]{:S(2)}) collective-permute-start(f32[128,512]{1,0:T(8,128)S(1)} %add.67), channel_id=1, source_target_pairs={{4,0},{5,8},{8,13},{9,1},{0,4},{1,5},{12,9},{13,12},{6,2},{7,10},{... | collective-permute-start | bytes 786440 | tf_op jit(solution)/shard_map/ppermute | solution.py:525
  159.5 1.2 bitcast_add_fusion
  160.8 1.3 collective-permute-start.37
  162.4 1.7 collective-permute-done.24
  164.1 7.3 %collective-permute-start.39 = (f32[3,64,256]{2,1,0:T(8,128)S(1)}, f32[3,64,256]{2,1,0:T(8,128)S(1)}, u32[]{:S(2)}, u32[]{:S(2)}) collective-permute-start(f32[3,64,256]{2,1,0:T(8,128)S(1)} %get-tuple-element.90), channel_id=1, source_target_pairs={{4,8},{5,12},{8,1},{9,5},{0,0},{1,4},{12,9},{13,13},{6,10},{7,14},... | collective-permute-start | bytes 589832 | tf_op jit(solution)/shard_map/ppermute | solution.py:618
  171.6 1.9 collective-permute-start.33
  174.1 2.5 %collective-permute-start.40 = (f32[3,64,256]{2,1,0:T(8,128)S(1)}, f32[3,64,256]{2,1,0:T(8,128)S(1)}, u32[]{:S(2)}, u32[]{:S(2)}) collective-permute-start(f32[3,64,256]{2,1,0:T(8,128)S(1)} %get-tuple-element.89), channel_id=1, source_target_pairs={{4,12},{5,0},{8,5},{9,13},{0,1},{1,4},{12,8},{13,9},{6,14},{7,2},{... | collective-permute-start | bytes 589832 | tf_op jit(solution)/shard_map/ppermute | solution.py:618
  176.5 0.9 fusion.1
  177.5 21.2 %collective-permute-done.40 = f32[3,64,256]{2,1,0:T(8,128)S(1)} collective-permute-done((f32[3,64,256]{2,1,0:T(8,128)S(1)}, f32[3,64,256]{2,1,0:T(8,128)S(1)}, u32[]{:S(2)}, u32[]{:S(2)}) %collective-permute-start.40) | collective-permute-done | bytes 196640 | tf_op jit(solution)/shard_map/ppermute | solution.py:618
  198.7 0.8 pad_maximum_fusion
  200.0 0.8 copy-done.1
  200.8 1.2 multiply_reduce_fusion
  (105 shorter events, 7.0 us)
Async XLA Ops:
  0.6 44.8 %copy-start.5 = (f32[1,1,256,512]{3,2,1,0:T(8,128)S(1)}, f32[1,1,256,512]{3,2,1,0:T(8,128)}, u32[]{:S(2)}) copy-start(f32[1,1,256,512]{3,2,1,0:T(8,128)} %param.8) | copy-start | bytes 1572868
  0.6 1.0 copy-start.7
  1.6 0.9 copy-start.8
  5.1 1.0 copy-start.19
  5.1 15.5 %collective-permute-start.10 = (f32[3,64,256]{2,1,0:T(8,128)}, f32[3,64,256]{2,1,0:T(8,128)}, u32[]{:S(2)}, u32[]{:S(2)}) collective-permute-start(f32[3,64,256]{2,1,0:T(8,128)} %get-tuple-element.52), channel_id=1, source_target_pairs={{0,1},{1,0},{2,3},{3,2},{4,5},{5,4},{6,7},{7,6},{8,9},{9,8},{10,11... | collective-permute-start | bytes 589832 | tf_op jit(solution)/shard_map/ppermute | solution.py:492
  6.1 1.0 copy-start
  7.1 1.0 copy-start.4
  8.1 37.2 %copy-start.6 = (f32[1,1,256,512]{3,2,1,0:T(8,128)S(1)}, f32[1,1,256,512]{3,2,1,0:T(8,128)}, u32[]{:S(2)}) copy-start(f32[1,1,256,512]{3,2,1,0:T(8,128)} %param.12) | copy-start | bytes 1572868
  10.1 70.5 %copy-start.10 = (f32[512,512]{1,0:T(8,128)}, f32[512,512]{1,0:T(8,128)S(1)}, u32[]{:S(2)}) copy-start(f32[512,512]{1,0:T(8,128)S(1)} %get-tuple-element.56.refs_14_.refs_6_) | copy-start | bytes 3145732
  10.1 51.1 %collective-permute-start.15 = (f32[256,512]{1,0:T(8,128)}, f32[256,512]{1,0:T(8,128)S(1)}, u32[]{:S(2)}, u32[]{:S(2)}) collective-permute-start(f32[256,512]{1,0:T(8,128)} %get-tuple-element.53), channel_id=1, source_target_pairs={{0,4},{8,5},{13,8},{1,9},{4,0},{5,1},{9,12},{12,13},{2,6},{10,7},{... | collective-permute-start | bytes 1572872 | tf_op jit(solution)/shard_map/ppermute | solution.py:516
  13.8 47.4 %collective-permute-start.16 = (f32[256,512]{1,0:T(8,128)}, f32[256,512]{1,0:T(8,128)S(1)}, u32[]{:S(2)}, u32[]{:S(2)}) collective-permute-start(f32[256,512]{1,0:T(8,128)} %get-tuple-element.54), channel_id=1, source_target_pairs={{8,4},{12,5},{1,8},{5,9},{0,0},{4,1},{9,12},{13,13},{10,6},{14,7},... | collective-permute-start | bytes 1572872 | tf_op jit(solution)/shard_map/ppermute | solution.py:516
  16.1 21.1 %collective-permute-start.7 = (f32[3,64,256]{2,1,0:T(8,128)}, f32[3,64,256]{2,1,0:T(8,128)}, u32[]{:S(2)}, u32[]{:S(2)}) collective-permute-start(f32[3,64,256]{2,1,0:T(8,128)} %copy-done.19), channel_id=1, source_target_pairs={{0,4},{8,5},{13,8},{1,9},{4,0},{5,1},{9,12},{12,13},{2,6},{10,7},{... | collective-permute-start | bytes 589832 | tf_op jit(solution)/shard_map/ppermute | solution.py:491
  17.4 21.9 %collective-permute-start.8 = (f32[3,64,256]{2,1,0:T(8,128)}, f32[3,64,256]{2,1,0:T(8,128)}, u32[]{:S(2)}, u32[]{:S(2)}) collective-permute-start(f32[3,64,256]{2,1,0:T(8,128)} %copy-done.18), channel_id=1, source_target_pairs={{8,4},{12,5},{1,8},{5,9},{0,0},{4,1},{9,12},{13,13},{10,6},{14,7},... | collective-permute-start | bytes 589832 | tf_op jit(solution)/shard_map/ppermute | solution.py:491
  20.6 27.8 %copy-start.16 = (f32[256,512]{1,0:T(8,128)S(1)}, f32[256,512]{1,0:T(8,128)}, u32[]{:S(2)}) copy-start(f32[256,512]{1,0:T(8,128)} %copy-done.15) | copy-start | bytes 1572868
  20.6 20.0 %collective-permute-start.9 = (f32[3,64,256]{2,1,0:T(8,128)S(1)}, f32[3,64,256]{2,1,0:T(8,128)S(1)}, u32[]{:S(2)}, u32[]{:S(2)}) collective-permute-start(f32[3,64,256]{2,1,0:T(8,128)S(1)} %get-tuple-element.50), channel_id=1, source_target_pairs={{12,4},{0,5},{5,8},{13,9},{1,0},{4,1},{8,12},{9,13},{14,6},{2,7},{... | collective-permute-start | bytes 589832 | tf_op jit(solution)/shard_map/ppermute | solution.py:491
  37.3 6.9 %collective-permute-start.14 = (f32[3,64,256]{2,1,0:T(8,128)S(1)}, f32[3,64,256]{2,1,0:T(8,128)S(1)}, u32[]{:S(2)}, u32[]{:S(2)}) collective-permute-start(f32[3,64,256]{2,1,0:T(8,128)S(1)} %broadcast_select_fusion.refs_3_), channel_id=1, source_target_pairs={{0,2},{2,0},{1,3},{3,1},{4,6},{6,4},{5,7},{7,5},{8,10},{10,8},{9,1... | collective-permute-start | bytes 589832 | tf_op jit(solution)/shard_map/ppermute | solution.py:497
  39.4 9.0 %collective-permute-start.11 = (f32[3,64,256]{2,1,0:T(8,128)}, f32[3,64,256]{2,1,0:T(8,128)S(1)}, u32[]{:S(2)}, u32[]{:S(2)}) collective-permute-start(f32[3,64,256]{2,1,0:T(8,128)} %collective-permute-done.7.refs_0_), channel_id=1, source_target_pairs={{0,2},{2,0},{1,3},{3,1},{4,6},{6,4},{5,7},{7,5},{8,10},{10,8},{9,1... | collective-permute-start | bytes 589832 | tf_op jit(solution)/shard_map/ppermute | solution.py:497
  40.6 12.0 %collective-permute-start.12 = (f32[3,64,256]{2,1,0:T(8,128)}, f32[3,64,256]{2,1,0:T(8,128)S(1)}, u32[]{:S(2)}, u32[]{:S(2)}) collective-permute-start(f32[3,64,256]{2,1,0:T(8,128)} %collective-permute-done.8.refs_1_), channel_id=1, source_target_pairs={{0,2},{2,0},{1,3},{3,1},{4,6},{6,4},{5,7},{7,5},{8,10},{10,8},{9,1... | collective-permute-start | bytes 589832 | tf_op jit(solution)/shard_map/ppermute | solution.py:497
  44.2 11.3 %collective-permute-start.13 = (f32[3,64,256]{2,1,0:T(8,128)S(1)}, f32[3,64,256]{2,1,0:T(8,128)S(1)}, u32[]{:S(2)}, u32[]{:S(2)}) collective-permute-start(f32[3,64,256]{2,1,0:T(8,128)S(1)} %collective-permute-done.9.refs_2_), channel_id=1, source_target_pairs={{0,2},{2,0},{1,3},{3,1},{4,6},{6,4},{5,7},{7,5},{8,10},{10,8},{9,1... | collective-permute-start | bytes 589832 | tf_op jit(solution)/shard_map/ppermute | solution.py:497
  45.7 44.8 %copy-start.11 = (f32[512,512]{1,0:T(8,128)}, f32[512,512]{1,0:T(8,128)S(1)}, u32[]{:S(2)}) copy-start(f32[512,512]{1,0:T(8,128)S(1)} %get-tuple-element.47.refs_6_) | copy-start | bytes 3145732
  48.4 13.1 %collective-permute-start.17 = (f32[256,512]{1,0:T(8,128)S(1)}, f32[256,512]{1,0:T(8,128)S(1)}, u32[]{:S(2)}, u32[]{:S(2)}) collective-permute-start(f32[256,512]{1,0:T(8,128)S(1)} %copy-done.16), channel_id=1, source_target_pairs={{12,4},{0,5},{5,8},{13,9},{1,0},{4,1},{8,12},{9,13},{14,6},{2,7},{... | collective-permute-start | bytes 1572872 | tf_op jit(solution)/shard_map/ppermute | solution.py:516
  52.6 14.0 %collective-permute-start = (f32[256,512]{1,0:T(8,128)S(1)}, f32[256,512]{1,0:T(8,128)S(1)}, u32[]{:S(2)}, u32[]{:S(2)}) collective-permute-start(f32[256,512]{1,0:T(8,128)S(1)} %get-tuple-element.44), channel_id=1, source_target_pairs={{0,4},{8,5},{13,8},{1,9},{4,0},{5,1},{9,12},{12,13},{2,6},{10,7},{... | collective-permute-start | bytes 1572872 | tf_op jit(solution)/shard_map/ppermute | solution.py:516
  55.5 22.0 %collective-permute-start.1 = (f32[256,512]{1,0:T(8,128)S(1)}, f32[256,512]{1,0:T(8,128)S(1)}, u32[]{:S(2)}, u32[]{:S(2)}) collective-permute-start(f32[256,512]{1,0:T(8,128)S(1)} %get-tuple-element.45), channel_id=1, source_target_pairs={{8,4},{12,5},{1,8},{5,9},{0,0},{4,1},{9,12},{13,13},{10,6},{14,7},... | collective-permute-start | bytes 1572872 | tf_op jit(solution)/shard_map/ppermute | solution.py:516
  61.1 18.4 %collective-permute-start.2 = (f32[256,512]{1,0:T(8,128)S(1)}, f32[256,512]{1,0:T(8,128)S(1)}, u32[]{:S(2)}, u32[]{:S(2)}) collective-permute-start(f32[256,512]{1,0:T(8,128)S(1)} %get-tuple-element.46), channel_id=1, source_target_pairs={{12,4},{0,5},{5,8},{13,9},{1,0},{4,1},{8,12},{9,13},{14,6},{2,7},{... | collective-permute-start | bytes 1572872 | tf_op jit(solution)/shard_map/ppermute | solution.py:516
  61.2 29.3 %copy-start.13 = (f32[256,512]{1,0:T(8,128)}, f32[256,512]{1,0:T(8,128)S(1)}, u32[]{:S(2)}) copy-start(f32[256,512]{1,0:T(8,128)S(1)} %collective-permute-done.16.refs_9_.refs_1_) | copy-start | bytes 1572868
  61.2 19.3 %collective-permute-start.21 = (f32[512,512]{1,0:T(8,128)S(1)}, f32[512,512]{1,0:T(8,128)S(1)}, u32[]{:S(2)}, u32[]{:S(2)}) collective-permute-start(f32[512,512]{1,0:T(8,128)S(1)} %get-tuple-element.56.refs_14_.refs_6_), channel_id=1, source_target_pairs={{0,1},{1,0},{2,3},{3,2},{4,5},{5,4},{6,7},{7,6},{8,9},{9,8},{10,11... | collective-permute-start | bytes 3145736 | tf_op jit(solution)/shard_map/ppermute | solution.py:517
  61.5 18.0 %collective-permute-start.18 = (f32[256,512]{1,0:T(8,128)S(1)}, f32[256,512]{1,0:T(8,128)S(1)}, u32[]{:S(2)}, u32[]{:S(2)}) collective-permute-start(f32[256,512]{1,0:T(8,128)S(1)} %collective-permute-done.15.refs_8_.refs_0_), channel_id=1, source_target_pairs={{0,1},{1,0},{2,3},{3,2},{4,5},{5,4},{6,7},{7,6},{8,9},{9,8},{10,11... | collective-permute-start | bytes 1572872 | tf_op jit(solution)/shard_map/ppermute | solution.py:518
  66.6 13.4 %collective-permute-start.19 = (f32[256,512]{1,0:T(8,128)S(1)}, f32[256,512]{1,0:T(8,128)S(1)}, u32[]{:S(2)}, u32[]{:S(2)}) collective-permute-start(f32[256,512]{1,0:T(8,128)S(1)} %collective-permute-done.16.refs_9_.refs_1_), channel_id=1, source_target_pairs={{0,1},{1,0},{2,3},{3,2},{4,5},{5,4},{6,7},{7,6},{8,9},{9,8},{10,11... | collective-permute-start | bytes 1572872 | tf_op jit(solution)/shard_map/ppermute | solution.py:518
  77.5 2.6 %collective-permute-start.20 = (f32[256,512]{1,0:T(8,128)S(1)}, f32[256,512]{1,0:T(8,128)S(1)}, u32[]{:S(2)}, u32[]{:S(2)}) collective-permute-start(f32[256,512]{1,0:T(8,128)S(1)} %collective-permute-done.17.refs_10_.refs_2_), channel_id=1, source_target_pairs={{0,1},{1,0},{2,3},{3,2},{4,5},{5,4},{6,7},{7,6},{8,9},{9,8},{10,11... | collective-permute-start | bytes 1572872 | tf_op jit(solution)/shard_map/ppermute | solution.py:518
  79.5 16.4 %collective-permute-start.6 = (f32[512,512]{1,0:T(8,128)S(1)}, f32[512,512]{1,0:T(8,128)S(1)}, u32[]{:S(2)}, u32[]{:S(2)}) collective-permute-start(f32[512,512]{1,0:T(8,128)S(1)} %get-tuple-element.47.refs_6_), channel_id=1, source_target_pairs={{0,1},{1,0},{2,3},{3,2},{4,5},{5,4},{6,7},{7,6},{8,9},{9,8},{10,11... | collective-permute-start | bytes 3145736 | tf_op jit(solution)/shard_map/ppermute | solution.py:517
  79.5 16.3 %collective-permute-start.3 = (f32[256,512]{1,0:T(8,128)S(1)}, f32[256,512]{1,0:T(8,128)S(1)}, u32[]{:S(2)}, u32[]{:S(2)}) collective-permute-start(f32[256,512]{1,0:T(8,128)S(1)} %collective-permute-done.refs_0_), channel_id=1, source_target_pairs={{0,1},{1,0},{2,3},{3,2},{4,5},{5,4},{6,7},{7,6},{8,9},{9,8},{10,11... | collective-permute-start | bytes 1572872 | tf_op jit(solution)/shard_map/ppermute | solution.py:518
  80.0 15.8 %collective-permute-start.4 = (f32[256,512]{1,0:T(8,128)S(1)}, f32[256,512]{1,0:T(8,128)S(1)}, u32[]{:S(2)}, u32[]{:S(2)}) collective-permute-start(f32[256,512]{1,0:T(8,128)S(1)} %collective-permute-done.1.refs_1_), channel_id=1, source_target_pairs={{0,1},{1,0},{2,3},{3,2},{4,5},{5,4},{6,7},{7,6},{8,9},{9,8},{10,11... | collective-permute-start | bytes 1572872 | tf_op jit(solution)/shard_map/ppermute | solution.py:518
  80.1 10.4 %copy-start.17 = (f32[256,512]{1,0:T(8,128)}, f32[256,512]{1,0:T(8,128)S(1)}, u32[]{:S(2)}) copy-start(f32[256,512]{1,0:T(8,128)S(1)} %collective-permute-done.20.refs_13_.refs_5_) | copy-start | bytes 1572868
  80.1 15.8 %collective-permute-start.5 = (f32[256,512]{1,0:T(8,128)S(1)}, f32[256,512]{1,0:T(8,128)S(1)}, u32[]{:S(2)}, u32[]{:S(2)}) collective-permute-start(f32[256,512]{1,0:T(8,128)S(1)} %collective-permute-done.2.refs_2_), channel_id=1, source_target_pairs={{0,1},{1,0},{2,3},{3,2},{4,5},{5,4},{6,7},{7,6},{8,9},{9,8},{10,11... | collective-permute-start | bytes 1572872 | tf_op jit(solution)/shard_map/ppermute | solution.py:518
  80.5 1.0 copy-start.27
  90.5 1.0 copy-start.20
  91.5 1.4 copy-start.2
  92.9 1.4 copy-start.3
  95.9 1.0 copy-start.28
  96.9 14.2 %copy-start.14 = (f32[256,512]{1,0:T(8,128)S(1)}, f32[256,512]{1,0:T(8,128)}, u32[]{:S(2)}) copy-start(f32[256,512]{1,0:T(8,128)} %copy-done.13) | copy-start | bytes 1572868
  110.9 24.0 %collective-permute-start.27 = (f32[128,512]{1,0:T(8,128)S(1)}, f32[128,512]{1,0:T(8,128)S(1)}, u32[]{:S(2)}, u32[]{:S(2)}) collective-permute-start(f32[128,512]{1,0:T(8,128)S(1)} %get-tuple-element.67), channel_id=1, source_target_pairs={{0,1},{1,0},{2,3},{3,2},{4,5},{5,4},{6,7},{7,6},{8,9},{9,8},{10,11... | collective-permute-start | bytes 786440 | tf_op jit(solution)/shard_map/ppermute | solution.py:524
  111.1 25.9 %copy-start.26 = (f32[1,1,256]{2,1,0:T(1,128)S(1)}, f32[1,1,256]{2,1,0:T(1,128)}, u32[]{:S(2)}) copy-start(f32[1,1,256]{2,1,0:T(1,128)} %param.11) | copy-start | bytes 3076
  132.5 21.7 %collective-permute-start.36 = (f32[4,3,64,256]{3,2,1,0:T(8,128)}, f32[4,3,64,256]{3,2,1,0:T(8,128)}, u32[]{:S(2)}, u32[]{:S(2)}) collective-permute-start(f32[4,3,64,256]{3,2,1,0:T(8,128)} %bitcast.42), channel_id=1, source_target_pairs={{0,2},{2,0},{1,3},{3,1},{4,6},{6,4},{5,7},{7,5},{8,10},{10,8},{9,1... | collective-permute-start | bytes 2359304 | tf_op jit(solution)/shard_map/ppermute | solution.py:616
  133.8 2.1 %collective-permute-start.25 = (f32[128,512]{1,0:T(8,128)S(1)}, f32[128,512]{1,0:T(8,128)S(1)}, u32[]{:S(2)}, u32[]{:S(2)}) collective-permute-start(f32[128,512]{1,0:T(8,128)S(1)} %get-tuple-element.65), channel_id=1, source_target_pairs={{0,1},{1,0},{2,3},{3,2},{4,5},{5,4},{6,7},{7,6},{8,9},{9,8},{10,11... | collective-permute-start | bytes 786440 | tf_op jit(solution)/shard_map/ppermute | solution.py:524
  134.4 5.9 %collective-permute-start.34 = (f32[256,512]{1,0:T(8,128)}, f32[256,512]{1,0:T(8,128)S(1)}, u32[]{:S(2)}, u32[]{:S(2)}) collective-permute-start(f32[256,512]{1,0:T(8,128)} %get-tuple-element.78), channel_id=1, source_target_pairs={{0,1},{1,0},{2,3},{3,2},{4,5},{5,4},{6,7},{7,6},{8,9},{9,8},{10,11... | collective-permute-start | bytes 1572872 | tf_op jit(solution)/shard_map/ppermute | solution.py:524
  134.4 7.8 %collective-permute-start.32 = (f32[256,512]{1,0:T(8,128)}, f32[256,512]{1,0:T(8,128)}, u32[]{:S(2)}, u32[]{:S(2)}) collective-permute-start(f32[256,512]{1,0:T(8,128)} %get-tuple-element.76), channel_id=1, source_target_pairs={{0,1},{1,0},{2,3},{3,2},{4,5},{5,4},{6,7},{7,6},{8,9},{9,8},{10,11... | collective-permute-start | bytes 1572872 | tf_op jit(solution)/shard_map/ppermute | solution.py:524
  134.9 1.0 copy-start.24
  134.9 15.9 %collective-permute-start.30 = (f32[256,512]{1,0:T(8,128)}, f32[256,512]{1,0:T(8,128)}, u32[]{:S(2)}, u32[]{:S(2)}) collective-permute-start(f32[256,512]{1,0:T(8,128)} %get-tuple-element.74), channel_id=1, source_target_pairs={{0,1},{1,0},{2,3},{3,2},{4,5},{5,4},{6,7},{7,6},{8,9},{9,8},{10,11... | collective-permute-start | bytes 1572872 | tf_op jit(solution)/shard_map/ppermute | solution.py:524
  136.6 2.5 %collective-permute-start.23 = (f32[128,512]{1,0:T(8,128)}, f32[128,512]{1,0:T(8,128)}, u32[]{:S(2)}, u32[]{:S(2)}) collective-permute-start(f32[128,512]{1,0:T(8,128)} %get-tuple-element.63), channel_id=1, source_target_pairs={{0,1},{1,0},{2,3},{3,2},{4,5},{5,4},{6,7},{7,6},{8,9},{9,8},{10,11... | collective-permute-start | bytes 786440 | tf_op jit(solution)/shard_map/ppermute | solution.py:524
  137.0 2.1 %copy-start.21 = (f32[512,512]{1,0:T(8,128)S(1)}, f32[512,512]{1,0:T(8,128)}, u32[]{:S(2)}) copy-start(f32[512,512]{1,0:T(8,128)} %get-tuple-element.72) | copy-start | bytes 3145732
  139.1 60.7 %collective-permute-start.29 = (f32[512,512]{1,0:T(8,128)S(1)}, f32[512,512]{1,0:T(8,128)S(1)}, u32[]{:S(2)}, u32[]{:S(2)}) collective-permute-start(f32[512,512]{1,0:T(8,128)S(1)} %copy-done.21), channel_id=1, source_target_pairs={{0,1},{1,0},{2,3},{3,2},{4,5},{5,4},{6,7},{7,6},{8,9},{9,8},{10,11... | collective-permute-start | bytes 3145736 | tf_op jit(solution)/shard_map/ppermute | solution.py:526
  140.3 31.2 %collective-permute-start.22 = (f32[256,512]{1,0:T(8,128)S(1)}, f32[256,512]{1,0:T(8,128)S(1)}, u32[]{:S(2)}, u32[]{:S(2)}) collective-permute-start(f32[256,512]{1,0:T(8,128)S(1)} %get-tuple-element.61), channel_id=1, source_target_pairs={{0,1},{1,0},{2,3},{3,2},{4,5},{5,4},{6,7},{7,6},{8,9},{9,8},{10,11... | collective-permute-start | bytes 1572872 | tf_op jit(solution)/shard_map/ppermute | solution.py:526
  142.2 18.6 %collective-permute-start.28 = (f32[128,512]{1,0:T(8,128)S(1)}, f32[128,512]{1,0:T(8,128)S(1)}, u32[]{:S(2)}, u32[]{:S(2)}) collective-permute-start(f32[128,512]{1,0:T(8,128)S(1)} %add.69), channel_id=1, source_target_pairs={{4,12},{5,0},{8,5},{9,13},{0,1},{1,4},{12,8},{13,9},{6,14},{7,2},{... | collective-permute-start | bytes 786440 | tf_op jit(solution)/shard_map/ppermute | solution.py:525
  149.6 9.9 %copy-start.22 = (f32[1,4,3,64,256]{4,3,2,1,0:T(8,128)S(1)}, f32[1,4,3,64,256]{4,3,2,1,0:T(8,128)}, u32[]{:S(2)}) copy-start(f32[1,4,3,64,256]{4,3,2,1,0:T(8,128)} %get-tuple-element.79) | copy-start | bytes 2359300
  150.8 11.5 %collective-permute-start.26 = (f32[128,512]{1,0:T(8,128)S(1)}, f32[128,512]{1,0:T(8,128)S(1)}, u32[]{:S(2)}, u32[]{:S(2)}) collective-permute-start(f32[128,512]{1,0:T(8,128)S(1)} %add.68), channel_id=1, source_target_pairs={{4,8},{5,12},{8,1},{9,5},{0,0},{1,4},{12,9},{13,13},{6,10},{7,14},... | collective-permute-start | bytes 786440 | tf_op jit(solution)/shard_map/ppermute | solution.py:525
  154.2 9.9 %collective-permute-start.24 = (f32[128,512]{1,0:T(8,128)S(1)}, f32[128,512]{1,0:T(8,128)S(1)}, u32[]{:S(2)}, u32[]{:S(2)}) collective-permute-start(f32[128,512]{1,0:T(8,128)S(1)} %add.67), channel_id=1, source_target_pairs={{4,0},{5,8},{8,13},{9,1},{0,4},{1,5},{12,9},{13,12},{6,2},{7,10},{... | collective-permute-start | bytes 786440 | tf_op jit(solution)/shard_map/ppermute | solution.py:525
  160.8 10.8 %collective-permute-start.37 = (f32[3,64,256]{2,1,0:T(8,128)S(1)}, f32[3,64,256]{2,1,0:T(8,128)S(1)}, u32[]{:S(2)}, u32[]{:S(2)}) collective-permute-start(f32[3,64,256]{2,1,0:T(8,128)S(1)} %get-tuple-element.88), channel_id=1, source_target_pairs={{0,1},{1,0},{2,3},{3,2},{4,5},{5,4},{6,7},{7,6},{8,9},{9,8},{10,11... | collective-permute-start | bytes 589832 | tf_op jit(solution)/shard_map/ppermute | solution.py:621
  162.4 11.2 %collective-permute-start.38 = (f32[3,64,256]{2,1,0:T(8,128)S(1)}, f32[3,64,256]{2,1,0:T(8,128)S(1)}, u32[]{:S(2)}, u32[]{:S(2)}) collective-permute-start(f32[3,64,256]{2,1,0:T(8,128)S(1)} %get-tuple-element.91), channel_id=1, source_target_pairs={{4,0},{5,8},{8,13},{9,1},{0,4},{1,5},{12,9},{13,12},{6,2},{7,10},{... | collective-permute-start | bytes 589832 | tf_op jit(solution)/shard_map/ppermute | solution.py:618
  164.1 9.9 %collective-permute-start.39 = (f32[3,64,256]{2,1,0:T(8,128)S(1)}, f32[3,64,256]{2,1,0:T(8,128)S(1)}, u32[]{:S(2)}, u32[]{:S(2)}) collective-permute-start(f32[3,64,256]{2,1,0:T(8,128)S(1)} %get-tuple-element.90), channel_id=1, source_target_pairs={{4,8},{5,12},{8,1},{9,5},{0,0},{1,4},{12,9},{13,13},{6,10},{7,14},... | collective-permute-start | bytes 589832 | tf_op jit(solution)/shard_map/ppermute | solution.py:618
  171.5 27.9 %collective-permute-start.35 = (f32[256,512]{1,0:T(8,128)S(1)}, f32[256,512]{1,0:T(8,128)S(1)}, u32[]{:S(2)}, u32[]{:S(2)}) collective-permute-start(f32[256,512]{1,0:T(8,128)S(1)} %add.73), channel_id=1, source_target_pairs={{4,12},{5,0},{8,5},{9,13},{0,1},{1,4},{12,8},{13,9},{6,14},{7,2},{... | collective-permute-start | bytes 1572872 | tf_op jit(solution)/shard_map/ppermute | solution.py:525
  171.6 27.8 %collective-permute-start.33 = (f32[256,512]{1,0:T(8,128)S(1)}, f32[256,512]{1,0:T(8,128)S(1)}, u32[]{:S(2)}, u32[]{:S(2)}) collective-permute-start(f32[256,512]{1,0:T(8,128)S(1)} %add.72), channel_id=1, source_target_pairs={{4,8},{5,12},{8,1},{9,5},{0,0},{1,4},{12,9},{13,13},{6,10},{7,14},... | collective-permute-start | bytes 1572872 | tf_op jit(solution)/shard_map/ppermute | solution.py:525
  173.6 25.9 %collective-permute-start.31 = (f32[256,512]{1,0:T(8,128)S(1)}, f32[256,512]{1,0:T(8,128)S(1)}, u32[]{:S(2)}, u32[]{:S(2)}) collective-permute-start(f32[256,512]{1,0:T(8,128)S(1)} %add.71), channel_id=1, source_target_pairs={{4,0},{5,8},{8,13},{9,1},{0,4},{1,5},{12,9},{13,12},{6,2},{7,10},{... | collective-permute-start | bytes 1572872 | tf_op jit(solution)/shard_map/ppermute | solution.py:525
  174.1 24.6 %collective-permute-start.40 = (f32[3,64,256]{2,1,0:T(8,128)S(1)}, f32[3,64,256]{2,1,0:T(8,128)S(1)}, u32[]{:S(2)}, u32[]{:S(2)}) collective-permute-start(f32[3,64,256]{2,1,0:T(8,128)S(1)} %get-tuple-element.89), channel_id=1, source_target_pairs={{4,12},{5,0},{8,5},{9,13},{0,1},{1,4},{12,8},{13,9},{6,14},{7,2},{... | collective-permute-start | bytes 589832 | tf_op jit(solution)/shard_map/ppermute | solution.py:618
  199.7 1.0 copy-start.1
  (6 other events, 4.8 us)

commit v3 on v2

--- a/solution.py
+++ b/solution.py
@@ -17,7 +17,7 @@
 BF16 = jnp.bfloat16
 NN = ((1,), (0,))
 NT = ((1,), (1,))
-ANY = pl.BlockSpec(memory_space=pl.ANY)
+HBM = pl.BlockSpec(memory_space=pltpu.MemorySpace.HBM)
 VMEM = pl.BlockSpec(memory_space=pltpu.VMEM)
 
 
@@ -112,6 +112,29 @@
     run_copies(copies)
 
 
+def collect_kernel(first, second, third, own, got, out, sems):
+    place, core = position()
+    mine = core == place - home_of(0)
+    copies = [
+        pltpu.make_async_copy(piece, out.at[slot], sems.at[slot])
+        for slot, piece in enumerate((first, second, third))
+    ]
+    for copy in copies:
+        copy.start()
+
+    @pl.when(mine)
+    def _():
+        pltpu.make_async_copy(own, out.at[ROUNDS], sems.at[ROUNDS]).start()
+
+    @pl.when(jnp.logical_not(mine))
+    def _():
+        pltpu.make_async_copy(got, out.at[ROUNDS], sems.at[ROUNDS]).start()
+
+    for copy in copies:
+        copy.wait()
+    pltpu.make_async_copy(own, out.at[ROUNDS], sems.at[ROUNDS]).wait()
+
+
 def pack_rows_kernel(scaled, half, *refs):
     if scaled:
         first, second, scale, *rest = refs
@@ -227,7 +250,7 @@
 
 
 def inner_kernel(cells, reps, *refs):
-    pieces = CELL * reps if cells == 1 else 1
+    pieces = reps if cells == 1 else 1
     parts, refs = refs[:pieces], refs[pieces:]
     near, far, (own, got), refs = refs[:3], refs[3:6], refs[6:8], refs[8:]
     weights, gates, ups, backs, steps, *scratch = refs
@@ -236,7 +259,7 @@
     starts = row_starts(cells, reps, rows)
     copies = []
     for number, ((cell, shift, slot), begin) in enumerate(starts.items()):
-        source = parts[shift * CELL + slot] if cells == 1 else parts[0].at[cell, shift * CELL + slot]
+        source = parts[shift].at[slot] if cells == 1 else parts[0].at[cell, shift, slot]
         copies.append(
             pltpu.make_async_copy(
                 source, weights.at[:, pl.ds(begin, rows)], weight_sems.at[number]
@@ -285,10 +308,7 @@
 
 def read_kernel(*refs):
     near, far, (own, got, high, low), refs = refs[:3], refs[3:6], refs[6:10], refs[10:]
-    (totals, near_out, far_out, local_out), scratch = (
-        (refs[0], refs[1:4], refs[4:7], refs[7]),
-        refs[8:],
-    )
+    totals, near_out, far_out, scratch = refs[0], refs[1:4], refs[4], refs[5:]
     queries, cots, turned, acts, sent, row_sems, out_sems = scratch
     fetch_rows(near, far, own, got, (queries, cots), row_sems)
     size = queries.shape[1]
@@ -301,9 +321,9 @@
         if block < ROUNDS:
             return [
                 (sent.at[block, pl.ds(0, half)], near_out[block]),
-                (sent.at[block, pl.ds(half, half)], far_out[block]),
+                (sent.at[block, pl.ds(half, half)], far_out.at[pl.ds(block * half, half)]),
             ]
-        return [(sent.at[block], local_out)]
+        return [(sent.at[block], far_out.at[pl.ds(ROUNDS * half, size)])]
 
     @pl.loop(0, CELL)
     def _(block):
@@ -337,17 +357,14 @@
             pltpu.make_async_copy(source, out, out_sems.at[block, side]).wait()
 
 
-def backward_kernel(cells, reps, *refs):
+def weight_grad_kernel(cells, reps, *refs):
     near, far, (own, got), refs = refs[:3], refs[3:6], refs[6:8], refs[8:]
     (weights, steps, totals, gates, ups, backs), refs = refs[:6], refs[6:]
-    near_out, far_out, local_out, refs = refs[:3], refs[3:6], refs[6], refs[7:]
-    pieces, scratch = refs[:reps], refs[reps:]
-    keys, targets, wide, cots, turned, acts, grads, sent, row_sems, out_sems, grad_sems = scratch
+    (cots, acts), pieces, scratch = refs[:2], refs[2 : 2 + reps], refs[2 + reps :]
+    keys, targets, turned, grads, row_sems, grad_sems = scratch
     fetch_rows(near, far, own, got, (keys, targets), row_sems)
     size = keys.shape[1]
-    half = size // 2
-    width = weights.shape[1]
-    scale = 1.0 / width
+    scale = 1.0 / weights.shape[1]
     for which in range(3):
         weight, total = weights[which], totals[which]
         moved = weight - steps[which]
@@ -360,20 +377,7 @@
         if cells > 1:
             direct = direct * jnp.where(lax.axis_index("tok") < CELL, 1.0, 0.0)
         grads[which] = direct
-        store_split(wide, (which,), weight)
         store_split(cots, (which,), -moved_cot)
-
-    def outgoing(block):
-        if block < ROUNDS:
-            return [
-                (sent.at[which, block, pl.ds(side * half, half)],
-                 (near_out, far_out)[side][block].at[pl.ds(which * half, half)])
-                for which in range(2)
-                for side in range(2)
-            ]
-        return [
-            (sent.at[which, block], local_out.at[pl.ds(which * size, size)]) for which in range(2)
-        ]
 
     @pl.loop(0, CELL)
     def _(block):
@@ -387,33 +391,17 @@
         sigma, act, slope = silu_parts(gate_pre)
         bend = sigma * (1.0 - sigma) * (2.0 + gate_pre * (1.0 - 2.0 * sigma))
         mixed = gate_back_cot * slope
-        back_cot = split(mixed * up_pre + up_back_cot * act)
-        up_cot = split(mixed * back + hidden_cot * act)
-        gate_cot = split(
+        store_split(
+            acts,
+            (0, where),
             gate_back_cot * back * up_pre * bend
-            + (up_back_cot * back + hidden_cot * up_pre) * slope
+            + (up_back_cot * back + hidden_cot * up_pre) * slope,
         )
+        store_split(acts, (1, where), mixed * back + hidden_cot * act)
+        store_split(acts, (2, where), mixed * up_pre + up_back_cot * act)
         for part in range(2):
-            acts[part, 0, where] = gate_cot[part]
-            acts[part, 1, where] = up_cot[part]
-            acts[part, 2, where] = back_cot[part]
             turned[part, 0, :, where] = key[part].T
             turned[part, 1, :, where] = target[part].T
-        sent[0, block] = (
-            dot3(gate_cot, pair_of(wide, 0), NT)
-            + dot3(up_cot, pair_of(wide, 1), NT)
-            + dot3(split(back * up_pre * slope), pair_of(cots, 0), NT)
-            + dot3(split(back * act), pair_of(cots, 1), NT)
-        )
-        sent[1, block] = dot3(back_cot, pair_of(wide, 2), NT) + dot3(
-            split(act * up_pre), pair_of(cots, 2), NT
-        )
-        for number in range(CELL):
-
-            @pl.when(block == number)
-            def _():
-                for side, (source, out) in enumerate(outgoing(number)):
-                    pltpu.make_async_copy(source, out, out_sems.at[number, side]).start()
 
     for which in range(3):
         grads[which] += dot3(pair_of(turned, which // 2), pair_of(acts, which), NN)
@@ -421,7 +409,6 @@
     copies = []
     place, core = position()
     rep = lax.axis_index("rep")
-    number = 0
     for cell in range(cells):
         for shift in range(reps):
             owner_rep = lax.rem(rep + shift, reps)
@@ -432,14 +419,64 @@
                     pltpu.make_async_copy(
                         grads.at[:, pl.ds(begin, rows)],
                         pieces[shift].at[cell, slot],
-                        grad_sems.at[number],
+                        grad_sems.at[len(copies)],
                     )
                 )
-                number += 1
     run_copies(copies)
-    for block in range(CELL):
-        for side, (source, out) in enumerate(outgoing(block)):
-            pltpu.make_async_copy(source, out, out_sems.at[block, side]).wait()
+
+
+def token_grad_kernel(first, last, *refs):
+    (weights, cots, acts, gates, ups, backs), refs = refs[:6], refs[6:]
+    rounds = min(last, ROUNDS) - first
+    near_out, far_out, (wide, sent, out_sems) = refs[:rounds], refs[rounds], refs[rounds + 1 :]
+    size = sent.shape[2]
+    half = size // 2
+    for which in range(3):
+        store_split(wide, (which,), weights[which])
+
+    def outgoing(number):
+        if number < rounds:
+            near = [
+                (sent.at[which, number, pl.ds(0, half)], near_out[number].at[pl.ds(which * half, half)])
+                for which in range(2)
+            ]
+            far = [
+                (
+                    sent.at[which, number, pl.ds(half, half)],
+                    far_out.at[pl.ds(number * size + which * half, half)],
+                )
+                for which in range(2)
+            ]
+            return near + far
+        return [
+            (sent.at[which, number], far_out.at[pl.ds((rounds + which) * size, size)])
+            for which in range(2)
+        ]
+
+    @pl.loop(0, last - first)
+    def _(number):
+        where = pl.ds(pl.multiple_of((first + number) * size, size), size)
+        gate_pre, up_pre, back = gates[where], ups[where], backs[where]
+        _, act, slope = silu_parts(gate_pre)
+        sent[0, number] = (
+            dot3(pair_of(acts, 0, where), pair_of(wide, 0), NT)
+            + dot3(pair_of(acts, 1, where), pair_of(wide, 1), NT)
+            + dot3(split(back * up_pre * slope), pair_of(cots, 0), NT)
+            + dot3(split(back * act), pair_of(cots, 1), NT)
+        )
+        sent[1, number] = dot3(pair_of(acts, 2, where), pair_of(wide, 2), NT) + dot3(
+            split(act * up_pre), pair_of(cots, 2), NT
+        )
+        for each in range(last - first):
+
+            @pl.when(number == each)
+            def _():
+                for side, (source, out) in enumerate(outgoing(each)):
+                    pltpu.make_async_copy(source, out, out_sems.at[each, side]).start()
+
+    for each in range(last - first):
+        for side, (source, out) in enumerate(outgoing(each)):
+            pltpu.make_async_copy(source, out, out_sems.at[each, side]).wait()
 
 
 def call(kernel, inputs, in_specs, outs, out_specs, scratch, flops=0):
@@ -451,7 +488,7 @@
         out_specs=out_specs,
         scratch_shapes=scratch,
         cost_estimate=pl.CostEstimate(flops=flops, bytes_accessed=moved, transcendentals=0),
-        compiler_params=pltpu.CompilerParams(vmem_limit_bytes=48 << 20),
+        compiler_params=pltpu.CompilerParams(vmem_limit_bytes=26 << 20),
     )(*inputs)
 
 
@@ -483,25 +520,31 @@
     packed = call(
         pack_weights_kernel,
         (fast_gate[0], fast_up[0], fast_down[0]),
-        [ANY] * 3,
+        [HBM] * 3,
         [shape((3, rows, cols), F32)] * (ROUNDS + 2),
-        [ANY] * (ROUNDS + 2),
+        [HBM] * (ROUNDS + 2),
         [dma((ROUNDS + 2, 3))],
     )
     slots = [lax.ppermute(packed[turn], PLACE, pairs[turn]) for turn in range(ROUNDS)]
     other = lax.ppermute(packed[ROUNDS + 1], "head", SWAP)
-    owner = core == place - home_of(0)
-    slots.append(jnp.where(owner, packed[ROUNDS], other))
-    parts = list(slots)
+    (together,) = call(
+        collect_kernel,
+        slots + [packed[ROUNDS], other],
+        [HBM] * 5,
+        [shape((CELL, 3, rows, cols), F32)],
+        [HBM],
+        [dma((CELL,))],
+    )
+    parts = [together]
     for shift in range(1, reps):
-        parts += [lax.ppermute(piece, "rep", shifted(shift, 1)) for piece in slots]
+        parts.append(lax.ppermute(together, "rep", shifted(shift, 1)))
     if cells > 1:
         parts = [lax.all_gather(jnp.stack(parts), "tok", axis_index_groups=cell_groups)]
 
     def gather(first, second, scale):
         outs = [shape((2 * half, depth), F32)] * ROUNDS + [shape((4 * half, depth), F32)]
         scratch = [dma((CELL, 2))]
-        inputs, specs = [first, second], [ANY, ANY]
+        inputs, specs = [first, second], [HBM, HBM]
         if scale is not None:
             inputs, specs = inputs + [scale], specs + [VMEM]
             scratch = [pltpu.VMEM((2 * half, depth), F32)] + scratch + [dma]
@@ -510,21 +553,26 @@
             inputs,
             specs,
             outs,
-            [ANY] * CELL,
+            [HBM] * CELL,
             scratch,
         )
         near = [lax.ppermute(packed[turn], PLACE, pairs[turn]) for turn in range(ROUNDS)]
         got = lax.ppermute(packed[ROUNDS], "head", SWAP)
-        far = [lax.ppermute(piece, "head", SWAP) for piece in near]
-        return near + far + [packed[ROUNDS], got]
-
-    def scatter(near, far, local):
+        return near, [packed[ROUNDS], got]
+
+    def spread(near, local):
+        return near + [lax.ppermute(piece, "head", SWAP) for piece in near] + local
+
+    def hand_back(near, far, first):
+        across = lax.ppermute(far, "head", SWAP)
+        length = near[0].shape[0]
         back = []
-        for turn in range(ROUNDS):
-            total = near[turn] + lax.ppermute(far[turn], "head", SWAP)
-            back.append(lax.ppermute(total, PLACE, flipped(pairs[turn])))
-        local = local + lax.ppermute(local, "head", SWAP)
-
+        for number, part in enumerate(near):
+            total = part + across[number * length : (number + 1) * length]
+            back.append(lax.ppermute(total, PLACE, flipped(pairs[first + number])))
+        return back, far[len(near) * length :] + across[len(near) * length :]
+
+    def settle(back, local):
         def choose(turn):
             return jnp.where(turn == 0, back[0], jnp.where(turn == 1, back[1], back[2]))
 
@@ -537,8 +585,9 @@
             found.append(jnp.where(at_home, here, remote))
         return found
 
-    inner_rows = gather(key_rows[0, 0], value_rows[0, 0], -step[:, None])
-    read_rows = gather(query_rows[0, 0], read_cotangent[0, 0], None)
+    inner_near, inner_local = gather(key_rows[0, 0], value_rows[0, 0], -step[:, None])
+    read_near, read_local = gather(query_rows[0, 0], read_cotangent[0, 0], None)
+    inner_rows = spread(inner_near, inner_local)
 
     size = 2 * half
     count = CELL * size
@@ -552,7 +601,7 @@
     weights, gates, ups, backs, steps = call(
         functools.partial(inner_kernel, cells, reps),
         parts + inner_rows,
-        [ANY] * (len(parts) + 8),
+        [HBM] * (len(parts) + 8),
         [square, tall, tall, tall, square],
         [VMEM] * 5,
         buffers
@@ -565,13 +614,15 @@
     high, low = call(
         renew_kernel, (weights, steps), [VMEM] * 2, [narrow, narrow], [VMEM] * 2, []
     )
+    *read_near, high = lax.optimization_barrier((*read_near, high))
+    read_rows = spread(list(read_near), read_local)
     piece = shape((half, depth), F32)
     read = call(
         read_kernel,
         read_rows + [high, low],
-        [ANY] * 8 + [VMEM] * 2,
-        [square] + [piece] * 6 + [shape((size, depth), F32)],
-        [VMEM] + [ANY] * 7,
+        [HBM] * 8 + [VMEM] * 2,
+        [square] + [piece] * ROUNDS + [shape((ROUNDS * half + size, depth), F32)],
+        [VMEM] + [HBM] * (ROUNDS + 1),
         buffers
         + [turned, acts, pltpu.VMEM((CELL, size, depth), F32), dma((CELL, 4)), dma((CELL, 2))],
         8 * product,
@@ -579,33 +630,43 @@
     totals = read[0]
     if cells > 1:
         totals = lax.psum(totals, "tok", axis_index_groups=cell_groups)
-    piece = shape((size, depth), F32)
-    final = call(
-        functools.partial(backward_kernel, cells, reps),
+    cots, acts_cot, *given = call(
+        functools.partial(weight_grad_kernel, cells, reps),
         inner_rows + [weights, steps, totals, gates, ups, backs],
-        [ANY] * 8 + [VMEM] * 6,
-        [piece] * 6
-        + [shape((2 * size, depth), F32)]
+        [HBM] * 8 + [VMEM] * 6,
+        [shape((2, 3, width, cols), BF16), shape((2, 3, count, cols), BF16)]
         + [shape((cells, CELL, 3, rows, cols), F32)] * reps,
-        [ANY] * (7 + reps),
+        [VMEM] * 2 + [HBM] * reps,
         buffers
         + [
-            split_square,
-            split_square,
             turned,
-            acts,
             pltpu.VMEM((3, width, cols), F32),
-            pltpu.VMEM((2, CELL, size, depth), F32),
-            dma((CELL, 4)),
             dma((CELL, 4)),
             dma((cells * reps * CELL,)),
         ],
-        12 * product,
+        6 * product,
     )
-    (query_grad,) = scatter(read[1:4], read[4:7], read[7])
-    key_grad, target_grad = scatter(final[0:3], final[3:6], final[6])
-
-    given = list(final[7:])
+    query_back, query_local = hand_back(read[1:4], read[4], 0)
+    middle = 2
+    piece = shape((size, depth), F32)
+    back = []
+    for first, last in ((0, middle), (middle, CELL)):
+        rounds = min(last, ROUNDS) - first
+        over = size * (2 * (last - first) - rounds)
+        out = call(
+            functools.partial(token_grad_kernel, first, last),
+            [weights, cots, acts_cot, gates, ups, backs],
+            [VMEM] * 6,
+            [piece] * rounds + [shape((over, depth), F32)],
+            [HBM] * (rounds + 1),
+            [split_square, pltpu.VMEM((2, last - first, size, depth), F32), dma((last - first, 4))],
+            6 * product * (last - first) // CELL,
+        )
+        returned, local = hand_back(out[:rounds], out[rounds], first)
+        back += returned
+    (query_grad,) = settle(query_back, query_local)
+    key_grad, target_grad = settle(back, local)
+
     if cells > 1:
         given = [
             lax.psum_scatter(value, "tok", scatter_dimension=0, tiled=True, axis_index_groups=cell_groups)

time: 203 us -> 174 us (0.86)
  the two profiles are of different devices: /device:TPU:1 before, /device:TPU:22 now
where the time goes in v3:
time: 174 us; the launch traced here: 171 us
  waiting for transfers between devices  82.5 us (47%)
  Pallas kernels  38.9 us (22%)
  starting transfers between devices  28.7 us (16%)
  other arithmetic  11.5 us (7%)
  local copies, waits for them, and re-layouts  8.41 us (5%)
    pallas_call x10, Pallas kernels, call(): pl.pallas_call(kernel, out_shape=outs, in_specs=in_specs, out_specs=out_s...  38.9 us
    ppermute x6, waiting for transfers between devices, gather(): lax.ppermute(packed[turn], PLACE, pairs[turn])  32.3 us
    ppermute x6, waiting for transfers between devices, hand_back(): back.append(lax.ppermute(total, PLACE, flipped(pairs[first + number])))  23.8 us
    ppermute x1, waiting for transfers between devices, per_device(): total = total + lax.ppermute(given[shift][0], 'rep', shifted(shift, 1))  10.9 us
    ppermute x6, starting transfers between devices, gather(): lax.ppermute(packed[turn], PLACE, pairs[turn])  8.75 us
    ppermute x6, starting transfers between devices, hand_back(): back.append(lax.ppermute(total, PLACE, flipped(pairs[first + number])))  8.62 us
    ppermute x3, waiting for transfers between devices, per_device(): lax.ppermute(total[turn], PLACE, flipped(pairs[turn]))  8.14 us
    unnamed x28, local copies, waits for them, and re-layouts  6.64 us
  transfers between devices with their start and end apart: 33, of which 18 were waited for; matrix products, arithmetic and copies ran while one was open for 7% of the time, Pallas kernels for 10%

profile of v3, /device:TPU:22, one launch (start us, length us, event | category | flops | bytes accessed | tf_op | source)
XLA Modules:
  0.0 171.0 jit_solution(9441007613924295711)
XLA Ops:
  0.6 0.9 copy-done.9
  1.5 0.9 copy-done.10
  2.4 0.9 copy-done.11
  3.3 0.3 shard_map.136
  3.8 2.8 %collective-permute-start.4 = (f32[3,64,256]{2,1,0:T(8,128)S(1)}, f32[3,64,256]{2,1,0:T(8,128)S(1)}, u32[]{:S(2)}, u32[]{:S(2)}) collective-permute-start(f32[3,64,256]{2,1,0:T(8,128)S(1)} %get-tuple-element.49), channel_id=1, source_target_pairs={{8,4},{12,5},{1,8},{5,9},{0,0},{4,1},{9,12},{13,13},{10,6},{14,7},... | collective-permute-start | bytes 589832 | tf_op jit(solution)/shard_map/ppermute | solution.py:528
  6.5 0.8 collective-permute-start.5
  7.3 0.8 copy.20
  8.2 1.0 copy-done
  9.3 1.0 copy-done.2
  10.3 0.4 shard_map.138
  10.8 1.5 collective-permute-start.8
  12.3 3.9 %collective-permute-start.9 = (f32[256,512]{1,0:T(8,128)S(1)}, f32[256,512]{1,0:T(8,128)S(1)}, u32[]{:S(2)}, u32[]{:S(2)}) collective-permute-start(f32[256,512]{1,0:T(8,128)S(1)} %get-tuple-element.54), channel_id=1, source_target_pairs={{8,4},{12,5},{1,8},{5,9},{0,0},{4,1},{9,12},{13,13},{10,6},{14,7},... | collective-permute-start | bytes 1572872 | tf_op jit(solution)/shard_map/ppermute | solution.py:559
  16.4 2.4 %collective-permute-done.5.third = f32[3,64,256]{2,1,0:T(8,128)S(1)} collective-permute-done((f32[3,64,256]{2,1,0:T(8,128)S(1)}, f32[3,64,256]{2,1,0:T(8,128)S(1)}, u32[]{:S(2)}, u32[]{:S(2)}) %collective-permute-start.5) | collective-permute-done | bytes 196640 | tf_op jit(solution)/shard_map/ppermute | solution.py:528
  18.8 1.1 shard_map.137.refs_0_
  19.8 0.6 collective-permute-start.7
  20.4 4.0 %collective-permute-done.8.refs_2_.refs_0_ = f32[256,512]{1,0:T(8,128)S(1)} collective-permute-done((f32[256,512]{1,0:T(8,128)S(1)}, f32[256,512]{1,0:T(8,128)S(1)}, u32[]{:S(2)}, u32[]{:S(2)}) %collective-permute-start.8) | collective-permute-done | bytes 524320 | tf_op jit(solution)/shard_map/ppermute | solution.py:559
  24.4 1.6 collective-permute-start.11
  26.0 11.4 %collective-permute-done.9.refs_3_.refs_1_ = f32[256,512]{1,0:T(8,128)S(1)} collective-permute-done((f32[256,512]{1,0:T(8,128)S(1)}, f32[256,512]{1,0:T(8,128)S(1)}, u32[]{:S(2)}, u32[]{:S(2)}) %collective-permute-start.9) | collective-permute-done | bytes 524320 | tf_op jit(solution)/shard_map/ppermute | solution.py:559
  37.4 1.9 %collective-permute-done.10.refs_4_.refs_2_ = f32[256,512]{1,0:T(8,128)S(1)} collective-permute-done((f32[256,512]{1,0:T(8,128)S(1)}, f32[256,512]{1,0:T(8,128)S(1)}, u32[]{:S(2)}, u32[]{:S(2)}) %collective-permute-start.10) | collective-permute-done | bytes 524320 | tf_op jit(solution)/shard_map/ppermute | solution.py:559
  39.3 0.3 shard_map.135
  39.7 0.2 collective-permute-done.7.refs_1_
  39.8 3.0 %collective-permute-start.1 = (f32[256,512]{1,0:T(8,128)S(1)}, f32[256,512]{1,0:T(8,128)S(1)}, u32[]{:S(2)}, u32[]{:S(2)}) collective-permute-start(f32[256,512]{1,0:T(8,128)S(1)} %get-tuple-element.46), channel_id=1, source_target_pairs={{8,4},{12,5},{1,8},{5,9},{0,0},{4,1},{9,12},{13,13},{10,6},{14,7},... | collective-permute-start | bytes 1572872 | tf_op jit(solution)/shard_map/ppermute | solution.py:559
  42.8 0.3 collective-permute-start.2
  43.1 7.8 %shard_map.139 = (f32[3,512,256]{2,1,0:T(8,128)S(1)}, f32[1024,256]{1,0:T(8,128)S(1)}, f32[1024,256]{1,0:T(8,128)S(1)}, f32[1024,256]{1,0:T(8,128)S(1)}, f32[3,512,256]{2,1,0:T(8,128)S(1)}) custom-call(f32[4,3,64,256]{3,2,1,0:T(8,128)S(1)} %shard_map.137.refs_0_, f32[4,3,64,256]{3,2,1,0:T(8,128)S(1)} %collective-permute-done.7.refs_1_, ...), custom_call_target="tpu_custom_call" | custom-call | flops 4831838208 | bytes 13107200 | tf_op jit(solution)/shard_map/pallas_call | solution.py:484
  51.0 0.6 shard_map.140
  51.6 0.6 collective-permute-done.refs_0_
  52.2 13.8 %collective-permute-done.1.refs_1_ = f32[256,512]{1,0:T(8,128)S(1)} collective-permute-done((f32[256,512]{1,0:T(8,128)S(1)}, f32[256,512]{1,0:T(8,128)S(1)}, u32[]{:S(2)}, u32[]{:S(2)}) %collective-permute-start.1) | collective-permute-done | bytes 524320 | tf_op jit(solution)/shard_map/ppermute | solution.py:559
  66.0 0.7 collective-permute-done.2.refs_2_
  66.7 0.5 collective-permute-start.16
  67.2 1.4 collective-permute-done.15.refs_3_
  68.6 0.7 collective-permute-done.16.refs_4_
  69.3 0.7 collective-permute-done.17.refs_5_
  70.1 11.6 %shard_map.141 = (f32[3,512,256]{2,1,0:T(8,128)S(1)}, f32[128,512]{1,0:T(8,128)S(1)}, f32[128,512]{1,0:T(8,128)S(1)}, f32[128,512]{1,0:T(8,128)S(1)}, f32[640,512]{1,0:T(8,128)}) custom-call(f32[256,512]{1,0:T(8,128)S(1)} %collective-permute-done.refs_0_, f32[256,512]{1,0:T(8,128)S(1)} %collective-permute-done.1.refs_1_, ...), custom_call_target="tpu_custom_call" | custom-call | flops 6442450944 | bytes 10485760 | tf_op jit(solution)/shard_map/pallas_call | solution.py:484
  81.7 9.3 %shard_map.142 = (bf16[2,3,512,256]{3,2,1,0:T(8,128)(2,1)S(1)}, bf16[2,3,1024,256]{3,2,1,0:T(8,128)(2,1)S(1)}, f32[1,4,3,64,256]{4,3,2,1,0:T(8,128)S(1)}, f32[1,4,3,64,256]{4,3,2,1,0:T(8,128)S(1)}) custom-call(f32[256,512]{1,0:T(8,128)S(1)} %collective-permute-done.8.refs_2_.refs_0_, f32[256,512]{1,0:T(8,128)S(1)} %collective-permute-done.9.refs_3_.refs_1_, ...), custom_call_target="tpu_custom_call" | custom-call | flops 4831838208 | bytes 19398656 | tf_op jit(solution)/shard_map/pallas_call | solution.py:484
  91.0 0.6 collective-permute-start.28
  91.6 3.3 %shard_map.143 = (f32[256,512]{1,0:T(8,128)S(1)}, f32[768,512]{1,0:T(8,128)S(1)}) custom-call(f32[3,512,256]{2,1,0:T(8,128)S(1)} %get-tuple-element.57.weights.refs_8_.refs_0_, bf16[2,3,512,256]{3,2,1,0:T(8,128)(2,1)S(1)} %get-tuple-element.74.refs_1_, bf16[2,3,1024,256]{3,2,1,0:T(8,128)(2,1)S(1)} %get-tuple-element.75.refs_2_, ...), custom_call_target="tpu_custom_call" | custom-call | flops 2415919104 | bytes 11534336 | tf_op jit(solution)/shard_map/pallas_call | solution.py:484
  95.1 4.1 %shard_map.144 = (f32[256,512]{1,0:T(8,128)S(1)}, f32[256,512]{1,0:T(8,128)S(1)}, f32[512,512]{1,0:T(8,128)}) custom-call(f32[3,512,256]{2,1,0:T(8,128)S(1)} %get-tuple-element.57.weights.refs_8_.refs_0_, bf16[2,3,512,256]{3,2,1,0:T(8,128)(2,1)S(1)} %get-tuple-element.74.refs_1_, bf16[2,3,1024,256]{3,2,1,0:T(8,128)(2,1)S(1)} %get-tuple-element.75.refs_2_, ...), custom_call_target="tpu_custom_call" | custom-call | flops 2415919104 | bytes 11534336 | tf_op jit(solution)/shard_map/pallas_call | solution.py:484
  99.1 0.6 collective-permute-start.24
  99.8 10.9 %collective-permute-done.28 = f32[4,3,64,256]{3,2,1,0:T(8,128)S(1)} collective-permute-done((f32[4,3,64,256]{3,2,1,0:T(8,128)S(1)}, f32[4,3,64,256]{3,2,1,0:T(8,128)S(1)}, u32[]{:S(2)}, u32[]{:S(2)}) %collective-permute-start.28) | collective-permute-done | bytes 786464 | tf_op jit(solution)/shard_map/ppermute | solution.py:677
  110.7 0.1 bitcast_add_fusion
  110.8 0.9 copy-done.12
  111.7 0.9 slice_bitcast_fusion.3
  112.6 1.8 %collective-permute-done.29 = f32[3,64,256]{2,1,0:T(8,128)} collective-permute-done((f32[3,64,256]{2,1,0:T(8,128)}, f32[3,64,256]{2,1,0:T(8,128)}, u32[]{:S(2)}, u32[]{:S(2)}) %collective-permute-start.29) | collective-permute-done | bytes 196640 | tf_op jit(solution)/shard_map/ppermute | solution.py:682
  114.4 1.9 %collective-permute-start.31 = (f32[3,64,256]{2,1,0:T(8,128)}, f32[3,64,256]{2,1,0:T(8,128)S(1)}, u32[]{:S(2)}, u32[]{:S(2)}) collective-permute-start(f32[3,64,256]{2,1,0:T(8,128)} %get-tuple-element.97), channel_id=1, source_target_pairs={{4,8},{5,12},{8,1},{9,5},{0,0},{1,4},{12,9},{13,13},{6,10},{7,14},... | collective-permute-start | bytes 589832 | tf_op jit(solution)/shard_map/ppermute | solution.py:679
  116.3 1.7 %collective-permute-done.30 = f32[3,64,256]{2,1,0:T(8,128)} collective-permute-done((f32[3,64,256]{2,1,0:T(8,128)}, f32[3,64,256]{2,1,0:T(8,128)}, u32[]{:S(2)}, u32[]{:S(2)}) %collective-permute-start.30) | collective-permute-done | bytes 196640 | tf_op jit(solution)/shard_map/ppermute | solution.py:679
  118.0 1.6 collective-permute-start.32
  119.6 3.8 %collective-permute-done.31 = f32[3,64,256]{2,1,0:T(8,128)S(1)} collective-permute-done((f32[3,64,256]{2,1,0:T(8,128)}, f32[3,64,256]{2,1,0:T(8,128)S(1)}, u32[]{:S(2)}, u32[]{:S(2)}) %collective-permute-start.31) | collective-permute-done | bytes 196640 | tf_op jit(solution)/shard_map/ppermute | solution.py:679
  123.4 2.6 %collective-permute-done.32 = f32[3,64,256]{2,1,0:T(8,128)S(1)} collective-permute-done((f32[3,64,256]{2,1,0:T(8,128)}, f32[3,64,256]{2,1,0:T(8,128)S(1)}, u32[]{:S(2)}, u32[]{:S(2)}) %collective-permute-start.32) | collective-permute-done | bytes 196640 | tf_op jit(solution)/shard_map/ppermute | solution.py:679
  126.1 1.2 select_select_fusion.4
  127.3 0.8 pad_maximum_fusion
  128.0 1.5 slice_add_fusion.2
  129.6 2.5 %collective-permute-start.26 = (f32[256,512]{1,0:T(8,128)S(1)}, f32[256,512]{1,0:T(8,128)S(1)}, u32[]{:S(2)}, u32[]{:S(2)}) collective-permute-start(f32[256,512]{1,0:T(8,128)S(1)} %get-tuple-element.93), channel_id=1, source_target_pairs={{4,8},{5,12},{8,1},{9,5},{0,0},{1,4},{12,9},{13,13},{6,10},{7,14},... | collective-permute-start | bytes 1572872 | tf_op jit(solution)/shard_map/ppermute | solution.py:572
  132.1 1.3 slice_add_fusion.5
  133.4 4.9 %collective-permute-start.21 = (f32[128,512]{1,0:T(8,128)S(1)}, f32[128,512]{1,0:T(8,128)S(1)}, u32[]{:S(2)}, u32[]{:S(2)}) collective-permute-start(f32[128,512]{1,0:T(8,128)S(1)} %get-tuple-element.90), channel_id=1, source_target_pairs={{4,8},{5,12},{8,1},{9,5},{0,0},{1,4},{12,9},{13,13},{6,10},{7,14},... | collective-permute-start | bytes 786440 | tf_op jit(solution)/shard_map/ppermute | solution.py:572
  138.3 1.1 collective-permute-start.22
  139.4 1.1 slice_add_fusion.1
  140.6 17.3 %collective-permute-done.20 = f32[128,512]{1,0:T(8,128)S(1)} collective-permute-done((f32[128,512]{1,0:T(8,128)S(1)}, f32[128,512]{1,0:T(8,128)S(1)}, u32[]{:S(2)}, u32[]{:S(2)}) %collective-permute-start.20) | collective-permute-done | bytes 262176 | tf_op jit(solution)/shard_map/ppermute | solution.py:572
  157.9 2.1 %fusion.2 = f32[1,1,256,512]{3,2,1,0:T(8,128)} fusion(f32[640,512]{1,0:T(8,128)} %collective-permute-done.19, f32[128,512]{1,0:T(8,128)S(1)} %get-tuple-element.100, f32[128,512]{1,0:T(8,128)S(1)} %get-tuple-element.99, f32[640,512]{1,0:T(8,128)} %get-tuple-element.66, pred[]{:T(512)S(6)} %eq.12), kind=kLoop, calls=%fused_computation.10 | loop fusion | flops 393216 | bytes 2097153 | tf_op jit(solution)/shard_map/broadcast_in_dim | solution.py:695
  160.0 1.4 slice_add_fusion
  161.5 6.5 %collective-permute-done.27 = f32[256,512]{1,0:T(8,128)S(1)} collective-permute-done((f32[256,512]{1,0:T(8,128)S(1)}, f32[256,512]{1,0:T(8,128)S(1)}, u32[]{:S(2)}, u32[]{:S(2)}) %collective-permute-start.27) | collective-permute-done | bytes 524320 | tf_op jit(solution)/shard_map/ppermute | solution.py:572
  168.0 0.2 select_select_fusion.1
  168.3 1.0 copy-done.1
  169.3 1.2 multiply_reduce_fusion
  170.4 0.6 divide_multiply_fusion
  (58 shorter events, 0.8 us)
Async XLA Ops:
  0.6 0.9 copy-start.9
  1.5 0.9 copy-start.10
  2.4 0.9 copy-start.11
  3.7 12.5 %collective-permute-start.3 = (f32[3,64,256]{2,1,0:T(8,128)S(1)}, f32[3,64,256]{2,1,0:T(8,128)S(1)}, u32[]{:S(2)}, u32[]{:S(2)}) collective-permute-start(f32[3,64,256]{2,1,0:T(8,128)S(1)} %get-tuple-element.48), channel_id=1, source_target_pairs={{0,4},{8,5},{13,8},{1,9},{4,0},{5,1},{9,12},{12,13},{2,6},{10,7},{... | collective-permute-start | bytes 589832 | tf_op jit(solution)/shard_map/ppermute | solution.py:528
  3.8 12.5 %collective-permute-start.4 = (f32[3,64,256]{2,1,0:T(8,128)S(1)}, f32[3,64,256]{2,1,0:T(8,128)S(1)}, u32[]{:S(2)}, u32[]{:S(2)}) collective-permute-start(f32[3,64,256]{2,1,0:T(8,128)S(1)} %get-tuple-element.49), channel_id=1, source_target_pairs={{8,4},{12,5},{1,8},{5,9},{0,0},{4,1},{9,12},{13,13},{10,6},{14,7},... | collective-permute-start | bytes 589832 | tf_op jit(solution)/shard_map/ppermute | solution.py:528
  6.5 12.2 %collective-permute-start.5 = (f32[3,64,256]{2,1,0:T(8,128)S(1)}, f32[3,64,256]{2,1,0:T(8,128)S(1)}, u32[]{:S(2)}, u32[]{:S(2)}) collective-permute-start(f32[3,64,256]{2,1,0:T(8,128)S(1)} %get-tuple-element.50), channel_id=1, source_target_pairs={{12,4},{0,5},{5,8},{13,9},{1,0},{4,1},{8,12},{9,13},{14,6},{2,7},{... | collective-permute-start | bytes 589832 | tf_op jit(solution)/shard_map/ppermute | solution.py:528
  8.2 1.0 copy-start
  9.3 1.0 copy-start.2
  10.3 29.0 %copy-start.3 = (f32[1,1,256,512]{3,2,1,0:T(8,128)S(1)}, f32[1,1,256,512]{3,2,1,0:T(8,128)}, u32[]{:S(2)}) copy-start(f32[1,1,256,512]{3,2,1,0:T(8,128)} %param.8) | copy-start | bytes 1572868
  10.3 29.0 %copy-start.4 = (f32[1,1,256,512]{3,2,1,0:T(8,128)S(1)}, f32[1,1,256,512]{3,2,1,0:T(8,128)}, u32[]{:S(2)}) copy-start(f32[1,1,256,512]{3,2,1,0:T(8,128)} %param.12) | copy-start | bytes 1572868
  10.8 13.6 %collective-permute-start.8 = (f32[256,512]{1,0:T(8,128)S(1)}, f32[256,512]{1,0:T(8,128)S(1)}, u32[]{:S(2)}, u32[]{:S(2)}) collective-permute-start(f32[256,512]{1,0:T(8,128)S(1)} %get-tuple-element.53), channel_id=1, source_target_pairs={{0,4},{8,5},{13,8},{1,9},{4,0},{5,1},{9,12},{12,13},{2,6},{10,7},{... | collective-permute-start | bytes 1572872 | tf_op jit(solution)/shard_map/ppermute | solution.py:559
  12.3 25.2 %collective-permute-start.9 = (f32[256,512]{1,0:T(8,128)S(1)}, f32[256,512]{1,0:T(8,128)S(1)}, u32[]{:S(2)}, u32[]{:S(2)}) collective-permute-start(f32[256,512]{1,0:T(8,128)S(1)} %get-tuple-element.54), channel_id=1, source_target_pairs={{8,4},{12,5},{1,8},{5,9},{0,0},{4,1},{9,12},{13,13},{10,6},{14,7},... | collective-permute-start | bytes 1572872 | tf_op jit(solution)/shard_map/ppermute | solution.py:559
  16.2 23.1 %collective-permute-start.10 = (f32[256,512]{1,0:T(8,128)S(1)}, f32[256,512]{1,0:T(8,128)S(1)}, u32[]{:S(2)}, u32[]{:S(2)}) collective-permute-start(f32[256,512]{1,0:T(8,128)S(1)} %get-tuple-element.55), channel_id=1, source_target_pairs={{12,4},{0,5},{5,8},{13,9},{1,0},{4,1},{8,12},{9,13},{14,6},{2,7},{... | collective-permute-start | bytes 1572872 | tf_op jit(solution)/shard_map/ppermute | solution.py:559
  16.3 2.5 %collective-permute-start.6 = (f32[3,64,256]{2,1,0:T(8,128)S(1)}, f32[3,64,256]{2,1,0:T(8,128)S(1)}, u32[]{:S(2)}, u32[]{:S(2)}) collective-permute-start(f32[3,64,256]{2,1,0:T(8,128)S(1)} %get-tuple-element.52), channel_id=1, source_target_pairs={{0,1},{1,0},{2,3},{3,2},{4,5},{5,4},{6,7},{7,6},{8,9},{9,8},{10,11... | collective-permute-start | bytes 589832 | tf_op jit(solution)/shard_map/ppermute | solution.py:529
  18.8 24.4 %collective-permute-start.14 = (f32[512,512]{1,0:T(8,128)S(1)}, f32[512,512]{1,0:T(8,128)S(1)}, u32[]{:S(2)}, u32[]{:S(2)}) collective-permute-start(f32[512,512]{1,0:T(8,128)S(1)} %get-tuple-element.56.refs_8_.refs_6_), channel_id=1, source_target_pairs={{0,1},{1,0},{2,3},{3,2},{4,5},{5,4},{6,7},{7,6},{8,9},{9,8},{10,11... | collective-permute-start | bytes 3145736 | tf_op jit(solution)/shard_map/ppermute | solution.py:560
  19.8 20.0 %collective-permute-start.7 = (f32[4,3,64,256]{3,2,1,0:T(8,128)S(1)}, f32[4,3,64,256]{3,2,1,0:T(8,128)S(1)}, u32[]{:S(2)}, u32[]{:S(2)}) collective-permute-start(f32[4,3,64,256]{3,2,1,0:T(8,128)S(1)} %shard_map.137.refs_0_), channel_id=1, source_target_pairs={{0,2},{2,0},{1,3},{3,1},{4,6},{6,4},{5,7},{7,5},{8,10},{10,8},{9,1... | collective-permute-start | bytes 2359304 | tf_op jit(solution)/shard_map/ppermute | solution.py:540
  24.4 15.4 %collective-permute-start.11 = (f32[256,512]{1,0:T(8,128)S(1)}, f32[256,512]{1,0:T(8,128)S(1)}, u32[]{:S(2)}, u32[]{:S(2)}) collective-permute-start(f32[256,512]{1,0:T(8,128)S(1)} %collective-permute-done.8.refs_2_.refs_0_), channel_id=1, source_target_pairs={{0,1},{1,0},{2,3},{3,2},{4,5},{5,4},{6,7},{7,6},{8,9},{9,8},{10,11... | collective-permute-start | bytes 1572872 | tf_op jit(solution)/shard_map/ppermute | solution.py:564
  37.4 5.4 %collective-permute-start.12 = (f32[256,512]{1,0:T(8,128)S(1)}, f32[256,512]{1,0:T(8,128)S(1)}, u32[]{:S(2)}, u32[]{:S(2)}) collective-permute-start(f32[256,512]{1,0:T(8,128)S(1)} %collective-permute-done.9.refs_3_.refs_1_), channel_id=1, source_target_pairs={{0,1},{1,0},{2,3},{3,2},{4,5},{5,4},{6,7},{7,6},{8,9},{9,8},{10,11... | collective-permute-start | bytes 1572872 | tf_op jit(solution)/shard_map/ppermute | solution.py:564
  39.3 3.8 %collective-permute-start.13 = (f32[256,512]{1,0:T(8,128)S(1)}, f32[256,512]{1,0:T(8,128)S(1)}, u32[]{:S(2)}, u32[]{:S(2)}) collective-permute-start(f32[256,512]{1,0:T(8,128)S(1)} %collective-permute-done.10.refs_4_.refs_2_), channel_id=1, source_target_pairs={{0,1},{1,0},{2,3},{3,2},{4,5},{5,4},{6,7},{7,6},{8,9},{9,8},{10,11... | collective-permute-start | bytes 1572872 | tf_op jit(solution)/shard_map/ppermute | solution.py:564
  39.8 12.4 %collective-permute-start = (f32[256,512]{1,0:T(8,128)S(1)}, f32[256,512]{1,0:T(8,128)S(1)}, u32[]{:S(2)}, u32[]{:S(2)}) collective-permute-start(f32[256,512]{1,0:T(8,128)S(1)} %get-tuple-element.45), channel_id=1, source_target_pairs={{0,4},{8,5},{13,8},{1,9},{4,0},{5,1},{9,12},{12,13},{2,6},{10,7},{... | collective-permute-start | bytes 1572872 | tf_op jit(solution)/shard_map/ppermute | solution.py:559
  39.8 26.1 %collective-permute-start.1 = (f32[256,512]{1,0:T(8,128)S(1)}, f32[256,512]{1,0:T(8,128)S(1)}, u32[]{:S(2)}, u32[]{:S(2)}) collective-permute-start(f32[256,512]{1,0:T(8,128)S(1)} %get-tuple-element.46), channel_id=1, source_target_pairs={{8,4},{12,5},{1,8},{5,9},{0,0},{4,1},{9,12},{13,13},{10,6},{14,7},... | collective-permute-start | bytes 1572872 | tf_op jit(solution)/shard_map/ppermute | solution.py:559
  42.8 23.8 %collective-permute-start.2 = (f32[256,512]{1,0:T(8,128)S(1)}, f32[256,512]{1,0:T(8,128)S(1)}, u32[]{:S(2)}, u32[]{:S(2)}) collective-permute-start(f32[256,512]{1,0:T(8,128)S(1)} %get-tuple-element.47), channel_id=1, source_target_pairs={{12,4},{0,5},{5,8},{13,9},{1,0},{4,1},{8,12},{9,13},{14,6},{2,7},{... | collective-permute-start | bytes 1572872 | tf_op jit(solution)/shard_map/ppermute | solution.py:559
  43.1 24.1 %collective-permute-start.18 = (f32[512,512]{1,0:T(8,128)S(1)}, f32[512,512]{1,0:T(8,128)S(1)}, u32[]{:S(2)}, u32[]{:S(2)}) collective-permute-start(f32[512,512]{1,0:T(8,128)S(1)} %get-tuple-element.63.refs_6_), channel_id=1, source_target_pairs={{0,1},{1,0},{2,3},{3,2},{4,5},{5,4},{6,7},{7,6},{8,9},{9,8},{10,11... | collective-permute-start | bytes 3145736 | tf_op jit(solution)/shard_map/ppermute | solution.py:560
  66.7 1.9 %collective-permute-start.15 = (f32[256,512]{1,0:T(8,128)S(1)}, f32[256,512]{1,0:T(8,128)S(1)}, u32[]{:S(2)}, u32[]{:S(2)}) collective-permute-start(f32[256,512]{1,0:T(8,128)S(1)} %collective-permute-done.refs_0_), channel_id=1, source_target_pairs={{0,1},{1,0},{2,3},{3,2},{4,5},{5,4},{6,7},{7,6},{8,9},{9,8},{10,11... | collective-permute-start | bytes 1572872 | tf_op jit(solution)/shard_map/ppermute | solution.py:564
  66.7 2.7 %collective-permute-start.16 = (f32[256,512]{1,0:T(8,128)S(1)}, f32[256,512]{1,0:T(8,128)S(1)}, u32[]{:S(2)}, u32[]{:S(2)}) collective-permute-start(f32[256,512]{1,0:T(8,128)S(1)} %collective-permute-done.1.refs_1_), channel_id=1, source_target_pairs={{0,1},{1,0},{2,3},{3,2},{4,5},{5,4},{6,7},{7,6},{8,9},{9,8},{10,11... | collective-permute-start | bytes 1572872 | tf_op jit(solution)/shard_map/ppermute | solution.py:564
  67.2 2.9 %collective-permute-start.17 = (f32[256,512]{1,0:T(8,128)S(1)}, f32[256,512]{1,0:T(8,128)S(1)}, u32[]{:S(2)}, u32[]{:S(2)}) collective-permute-start(f32[256,512]{1,0:T(8,128)S(1)} %collective-permute-done.2.refs_2_), channel_id=1, source_target_pairs={{0,1},{1,0},{2,3},{3,2},{4,5},{5,4},{6,7},{7,6},{8,9},{9,8},{10,11... | collective-permute-start | bytes 1572872 | tf_op jit(solution)/shard_map/ppermute | solution.py:564
  81.6 9.4 %copy-start.5 = (f32[128,512]{1,0:T(8,128)}, f32[128,512]{1,0:T(8,128)S(1)}, u32[]{:S(2)}) copy-start(f32[128,512]{1,0:T(8,128)S(1)} %get-tuple-element.68) | copy-start | bytes 786436
  81.7 9.4 %copy-start.7 = (f32[128,512]{1,0:T(8,128)}, f32[128,512]{1,0:T(8,128)S(1)}, u32[]{:S(2)}) copy-start(f32[128,512]{1,0:T(8,128)S(1)} %get-tuple-element.69) | copy-start | bytes 786436
  91.0 19.7 %collective-permute-start.28 = (f32[4,3,64,256]{3,2,1,0:T(8,128)S(1)}, f32[4,3,64,256]{3,2,1,0:T(8,128)S(1)}, u32[]{:S(2)}, u32[]{:S(2)}) collective-permute-start(f32[4,3,64,256]{3,2,1,0:T(8,128)S(1)} %bitcast.39), channel_id=1, source_target_pairs={{0,2},{2,0},{1,3},{3,1},{4,6},{6,4},{5,7},{7,5},{8,10},{10,8},{9,1... | collective-permute-start | bytes 2359304 | tf_op jit(solution)/shard_map/ppermute | solution.py:677
  95.0 43.3 %collective-permute-start.23 = (f32[768,512]{1,0:T(8,128)S(1)}, f32[768,512]{1,0:T(8,128)}, u32[]{:S(2)}, u32[]{:S(2)}) collective-permute-start(f32[768,512]{1,0:T(8,128)S(1)} %get-tuple-element.76), channel_id=1, source_target_pairs={{0,1},{1,0},{2,3},{3,2},{4,5},{5,4},{6,7},{7,6},{8,9},{9,8},{10,11... | collective-permute-start | bytes 4718600 | tf_op jit(solution)/shard_map/ppermute | solution.py:567
  99.1 28.9 %collective-permute-start.24 = (f32[512,512]{1,0:T(8,128)}, f32[512,512]{1,0:T(8,128)}, u32[]{:S(2)}, u32[]{:S(2)}) collective-permute-start(f32[512,512]{1,0:T(8,128)} %get-tuple-element.78), channel_id=1, source_target_pairs={{0,1},{1,0},{2,3},{3,2},{4,5},{5,4},{6,7},{7,6},{8,9},{9,8},{10,11... | collective-permute-start | bytes 3145736 | tf_op jit(solution)/shard_map/ppermute | solution.py:567
  99.7 32.4 %collective-permute-start.19 = (f32[640,512]{1,0:T(8,128)}, f32[640,512]{1,0:T(8,128)}, u32[]{:S(2)}, u32[]{:S(2)}) collective-permute-start(f32[640,512]{1,0:T(8,128)} %get-tuple-element.66), channel_id=1, source_target_pairs={{0,1},{1,0},{2,3},{3,2},{4,5},{5,4},{6,7},{7,6},{8,9},{9,8},{10,11... | collective-permute-start | bytes 3932168 | tf_op jit(solution)/shard_map/ppermute | solution.py:567
  110.7 8.9 %copy-start.13 = (f32[1,1,256]{2,1,0:T(1,128)S(1)}, f32[1,1,256]{2,1,0:T(1,128)}, u32[]{:S(2)}) copy-start(f32[1,1,256]{2,1,0:T(1,128)} %param.11) | copy-start | bytes 3076
  110.8 0.9 copy-start.12
  112.6 1.8 %collective-permute-start.29 = (f32[3,64,256]{2,1,0:T(8,128)}, f32[3,64,256]{2,1,0:T(8,128)}, u32[]{:S(2)}, u32[]{:S(2)}) collective-permute-start(f32[3,64,256]{2,1,0:T(8,128)} %get-tuple-element.95), channel_id=1, source_target_pairs={{0,1},{1,0},{2,3},{3,2},{4,5},{5,4},{6,7},{7,6},{8,9},{9,8},{10,11... | collective-permute-start | bytes 589832 | tf_op jit(solution)/shard_map/ppermute | solution.py:682
  112.6 5.4 %collective-permute-start.30 = (f32[3,64,256]{2,1,0:T(8,128)}, f32[3,64,256]{2,1,0:T(8,128)}, u32[]{:S(2)}, u32[]{:S(2)}) collective-permute-start(f32[3,64,256]{2,1,0:T(8,128)} %get-tuple-element.98), channel_id=1, source_target_pairs={{4,0},{5,8},{8,13},{9,1},{0,4},{1,5},{12,9},{13,12},{6,2},{7,10},{... | collective-permute-start | bytes 589832 | tf_op jit(solution)/shard_map/ppermute | solution.py:679
  114.4 9.1 %collective-permute-start.31 = (f32[3,64,256]{2,1,0:T(8,128)}, f32[3,64,256]{2,1,0:T(8,128)S(1)}, u32[]{:S(2)}, u32[]{:S(2)}) collective-permute-start(f32[3,64,256]{2,1,0:T(8,128)} %get-tuple-element.97), channel_id=1, source_target_pairs={{4,8},{5,12},{8,1},{9,5},{0,0},{1,4},{12,9},{13,13},{6,10},{7,14},... | collective-permute-start | bytes 589832 | tf_op jit(solution)/shard_map/ppermute | solution.py:679
  118.0 8.1 %collective-permute-start.32 = (f32[3,64,256]{2,1,0:T(8,128)}, f32[3,64,256]{2,1,0:T(8,128)S(1)}, u32[]{:S(2)}, u32[]{:S(2)}) collective-permute-start(f32[3,64,256]{2,1,0:T(8,128)} %get-tuple-element.96), channel_id=1, source_target_pairs={{4,12},{5,0},{8,5},{9,13},{0,1},{1,4},{12,8},{13,9},{6,14},{7,2},{... | collective-permute-start | bytes 589832 | tf_op jit(solution)/shard_map/ppermute | solution.py:679
  128.0 4.1 %copy-start.6 = (f32[128,512]{1,0:T(8,128)S(1)}, f32[128,512]{1,0:T(8,128)}, u32[]{:S(2)}) copy-start(f32[128,512]{1,0:T(8,128)} %copy-done.5) | copy-start | bytes 786436
  128.0 4.1 %copy-start.8 = (f32[128,512]{1,0:T(8,128)S(1)}, f32[128,512]{1,0:T(8,128)}, u32[]{:S(2)}) copy-start(f32[128,512]{1,0:T(8,128)} %copy-done.7) | copy-start | bytes 786436
  129.5 32.0 %collective-permute-start.25 = (f32[256,512]{1,0:T(8,128)S(1)}, f32[256,512]{1,0:T(8,128)S(1)}, u32[]{:S(2)}, u32[]{:S(2)}) collective-permute-start(f32[256,512]{1,0:T(8,128)S(1)} %get-tuple-element.94), channel_id=1, source_target_pairs={{4,0},{5,8},{8,13},{9,1},{0,4},{1,5},{12,9},{13,12},{6,2},{7,10},{... | collective-permute-start | bytes 1572872 | tf_op jit(solution)/shard_map/ppermute | solution.py:572
  129.6 31.9 %collective-permute-start.26 = (f32[256,512]{1,0:T(8,128)S(1)}, f32[256,512]{1,0:T(8,128)S(1)}, u32[]{:S(2)}, u32[]{:S(2)}) collective-permute-start(f32[256,512]{1,0:T(8,128)S(1)} %get-tuple-element.93), channel_id=1, source_target_pairs={{4,8},{5,12},{8,1},{9,5},{0,0},{1,4},{12,9},{13,13},{6,10},{7,14},... | collective-permute-start | bytes 1572872 | tf_op jit(solution)/shard_map/ppermute | solution.py:572
  133.4 24.5 %collective-permute-start.20 = (f32[128,512]{1,0:T(8,128)S(1)}, f32[128,512]{1,0:T(8,128)S(1)}, u32[]{:S(2)}, u32[]{:S(2)}) collective-permute-start(f32[128,512]{1,0:T(8,128)S(1)} %get-tuple-element.91), channel_id=1, source_target_pairs={{4,0},{5,8},{8,13},{9,1},{0,4},{1,5},{12,9},{13,12},{6,2},{7,10},{... | collective-permute-start | bytes 786440 | tf_op jit(solution)/shard_map/ppermute | solution.py:572
  133.4 24.4 %collective-permute-start.21 = (f32[128,512]{1,0:T(8,128)S(1)}, f32[128,512]{1,0:T(8,128)S(1)}, u32[]{:S(2)}, u32[]{:S(2)}) collective-permute-start(f32[128,512]{1,0:T(8,128)S(1)} %get-tuple-element.90), channel_id=1, source_target_pairs={{4,8},{5,12},{8,1},{9,5},{0,0},{1,4},{12,9},{13,13},{6,10},{7,14},... | collective-permute-start | bytes 786440 | tf_op jit(solution)/shard_map/ppermute | solution.py:572
  138.3 19.5 %collective-permute-start.22 = (f32[128,512]{1,0:T(8,128)S(1)}, f32[128,512]{1,0:T(8,128)S(1)}, u32[]{:S(2)}, u32[]{:S(2)}) collective-permute-start(f32[128,512]{1,0:T(8,128)S(1)} %get-tuple-element.89), channel_id=1, source_target_pairs={{4,12},{5,0},{8,5},{9,13},{0,1},{1,4},{12,8},{13,9},{6,14},{7,2},{... | collective-permute-start | bytes 786440 | tf_op jit(solution)/shard_map/ppermute | solution.py:572
  157.8 10.2 %collective-permute-start.27 = (f32[256,512]{1,0:T(8,128)S(1)}, f32[256,512]{1,0:T(8,128)S(1)}, u32[]{:S(2)}, u32[]{:S(2)}) collective-permute-start(f32[256,512]{1,0:T(8,128)S(1)} %slice_add_fusion.1), channel_id=1, source_target_pairs={{4,12},{5,0},{8,5},{9,13},{0,1},{1,4},{12,8},{13,9},{6,14},{7,2},{... | collective-permute-start | bytes 1572872 | tf_op jit(solution)/shard_map/ppermute | solution.py:572
  168.2 1.0 copy-start.1

commit v4 on v3

--- a/solution.py
+++ b/solution.py
@@ -181,10 +181,11 @@
 
 
 def fetch_rows(near, far, own, got, buffers, sems):
-    half = near[0].shape[0] // 2
+    half = buffers[0].shape[1] // 2
     place, core = position()
     mine = core == place - home_of(0)
-    for block in range(ROUNDS):
+    last = len(near)
+    for block in range(last):
         for which in range(2):
             rows = pl.ds(which * half, half)
             for side, group in enumerate((near, far)):
@@ -199,9 +200,12 @@
             for side in range(2):
                 pltpu.make_async_copy(
                     source.at[pl.ds((which * 2 + side) * half, half)],
-                    buffers[which].at[ROUNDS, pl.ds(side * half, half)],
-                    sems.at[ROUNDS, which * 2 + side],
+                    buffers[which].at[last, pl.ds(side * half, half)],
+                    sems.at[last, which * 2 + side],
                 ).start()
+
+    if own is None:
+        return
 
     @pl.when(mine)
     def _():
@@ -253,8 +257,8 @@
     pieces = reps if cells == 1 else 1
     parts, refs = refs[:pieces], refs[pieces:]
     near, far, (own, got), refs = refs[:3], refs[3:6], refs[6:8], refs[8:]
-    weights, gates, ups, backs, steps, *scratch = refs
-    keys, targets, wide, turned, acts, row_sems, weight_sems = scratch
+    weights, gates, ups, backs, turned, steps, *scratch = refs
+    keys, targets, wide, acts, row_sems, weight_sems = scratch
     rows = parts[0].shape[-2]
     starts = row_starts(cells, reps, rows)
     copies = []
@@ -357,13 +361,7 @@
             pltpu.make_async_copy(source, out, out_sems.at[block, side]).wait()
 
 
-def weight_grad_kernel(cells, reps, *refs):
-    near, far, (own, got), refs = refs[:3], refs[3:6], refs[6:8], refs[8:]
-    (weights, steps, totals, gates, ups, backs), refs = refs[:6], refs[6:]
-    (cots, acts), pieces, scratch = refs[:2], refs[2 : 2 + reps], refs[2 + reps :]
-    keys, targets, turned, grads, row_sems, grad_sems = scratch
-    fetch_rows(near, far, own, got, (keys, targets), row_sems)
-    size = keys.shape[1]
+def renew_back_kernel(cells, weights, steps, totals, cots, direct):
     scale = 1.0 / weights.shape[1]
     for which in range(3):
         weight, total = weights[which], totals[which]
@@ -373,17 +371,53 @@
         ratio = jnp.sqrt(old) / jnp.sqrt(new)
         ratio_cot = jnp.sum(total * moved, axis=0, keepdims=True) * scale
         moved_cot = ratio * (total - moved * (ratio_cot / new))
-        direct = moved_cot + weight * (ratio_cot * ratio / old)
+        grad = moved_cot + weight * (ratio_cot * ratio / old)
         if cells > 1:
-            direct = direct * jnp.where(lax.axis_index("tok") < CELL, 1.0, 0.0)
-        grads[which] = direct
+            grad = grad * jnp.where(lax.axis_index("tok") < CELL, 1.0, 0.0)
+        direct[which] = grad
         store_split(cots, (which,), -moved_cot)
 
-    @pl.loop(0, CELL)
-    def _(block):
-        wait_rows((keys, targets), block, row_sems)
-        where = pl.ds(pl.multiple_of(block * size, size), size)
-        key, target = split(keys[block]), split(targets[block])
+
+def token_grad_kernel(first, last, *refs):
+    rounds = min(last, ROUNDS) - first
+    near, far, refs = refs[:rounds], refs[rounds : 2 * rounds], refs[2 * rounds :]
+    own, got = None, None
+    if last > ROUNDS:
+        (own, got), refs = refs[:2], refs[2:]
+    (weights, cots, gates, ups, backs), refs = refs[:5], refs[5:]
+    acts, near_out, far_out, scratch = refs[0], refs[1 : 1 + rounds], refs[1 + rounds], refs[2 + rounds :]
+    keys, targets, wide, sent, row_sems, out_sems = scratch
+    fetch_rows(near, far, own, got, (keys, targets), row_sems)
+    size = sent.shape[2]
+    half = size // 2
+    for which in range(3):
+        store_split(wide, (which,), weights[which])
+
+    def outgoing(number):
+        if number < rounds:
+            near = [
+                (sent.at[which, number, pl.ds(0, half)], near_out[number].at[pl.ds(which * half, half)])
+                for which in range(2)
+            ]
+            far = [
+                (
+                    sent.at[which, number, pl.ds(half, half)],
+                    far_out.at[pl.ds(number * size + which * half, half)],
+                )
+                for which in range(2)
+            ]
+            return near + far
+        return [
+            (sent.at[which, number], far_out.at[pl.ds((rounds + which) * size, size)])
+            for which in range(2)
+        ]
+
+    @pl.loop(0, last - first)
+    def _(number):
+        wait_rows((keys, targets), number, row_sems)
+        where = pl.ds(pl.multiple_of((first + number) * size, size), size)
+        here = pl.ds(pl.multiple_of(number * size, size), size)
+        key, target = split(keys[number]), split(targets[number])
         gate_back_cot = dot3(key, pair_of(cots, 0), NN)
         up_back_cot = dot3(key, pair_of(cots, 1), NN)
         hidden_cot = dot3(target, pair_of(cots, 2), NN)
@@ -391,20 +425,48 @@
         sigma, act, slope = silu_parts(gate_pre)
         bend = sigma * (1.0 - sigma) * (2.0 + gate_pre * (1.0 - 2.0 * sigma))
         mixed = gate_back_cot * slope
-        store_split(
-            acts,
-            (0, where),
+        gate_cot = split(
             gate_back_cot * back * up_pre * bend
-            + (up_back_cot * back + hidden_cot * up_pre) * slope,
+            + (up_back_cot * back + hidden_cot * up_pre) * slope
         )
-        store_split(acts, (1, where), mixed * back + hidden_cot * act)
-        store_split(acts, (2, where), mixed * up_pre + up_back_cot * act)
+        up_cot = split(mixed * back + hidden_cot * act)
+        back_cot = split(mixed * up_pre + up_back_cot * act)
         for part in range(2):
-            turned[part, 0, :, where] = key[part].T
-            turned[part, 1, :, where] = target[part].T
-
+            acts[part, 0, here] = gate_cot[part]
+            acts[part, 1, here] = up_cot[part]
+            acts[part, 2, here] = back_cot[part]
+        sent[0, number] = (
+            dot3(gate_cot, pair_of(wide, 0), NT)
+            + dot3(up_cot, pair_of(wide, 1), NT)
+            + dot3(split(back * up_pre * slope), pair_of(cots, 0), NT)
+            + dot3(split(back * act), pair_of(cots, 1), NT)
+        )
+        sent[1, number] = dot3(back_cot, pair_of(wide, 2), NT) + dot3(
+            split(act * up_pre), pair_of(cots, 2), NT
+        )
+        for each in range(last - first):
+
+            @pl.when(number == each)
+            def _():
+                for side, (source, out) in enumerate(outgoing(each)):
+                    pltpu.make_async_copy(source, out, out_sems.at[each, side]).start()
+
+    for each in range(last - first):
+        for side, (source, out) in enumerate(outgoing(each)):
+            pltpu.make_async_copy(source, out, out_sems.at[each, side]).wait()
+
+
+def weight_grad_kernel(cells, reps, turned, direct, *refs):
+    parts, pieces, (grads, grad_sems) = refs[: -reps - 2], refs[-reps - 2 : -2], refs[-2:]
     for which in range(3):
-        grads[which] += dot3(pair_of(turned, which // 2), pair_of(acts, which), NN)
+        total = direct[which]
+        begin = 0
+        for acts in parts:
+            span = pl.ds(begin, acts.shape[2])
+            begin += acts.shape[2]
+            left = turned[0, which // 2, :, span], turned[1, which // 2, :, span]
+            total = total + dot3(left, pair_of(acts, which), NN)
+        grads[which] = total
     rows = pieces[0].shape[-2]
     copies = []
     place, core = position()
@@ -425,61 +487,7 @@
     run_copies(copies)
 
 
-def token_grad_kernel(first, last, *refs):
-    (weights, cots, acts, gates, ups, backs), refs = refs[:6], refs[6:]
-    rounds = min(last, ROUNDS) - first
-    near_out, far_out, (wide, sent, out_sems) = refs[:rounds], refs[rounds], refs[rounds + 1 :]
-    size = sent.shape[2]
-    half = size // 2
-    for which in range(3):
-        store_split(wide, (which,), weights[which])
-
-    def outgoing(number):
-        if number < rounds:
-            near = [
-                (sent.at[which, number, pl.ds(0, half)], near_out[number].at[pl.ds(which * half, half)])
-                for which in range(2)
-            ]
-            far = [
-                (
-                    sent.at[which, number, pl.ds(half, half)],
-                    far_out.at[pl.ds(number * size + which * half, half)],
-                )
-                for which in range(2)
-            ]
-            return near + far
-        return [
-            (sent.at[which, number], far_out.at[pl.ds((rounds + which) * size, size)])
-            for which in range(2)
-        ]
-
-    @pl.loop(0, last - first)
-    def _(number):
-        where = pl.ds(pl.multiple_of((first + number) * size, size), size)
-        gate_pre, up_pre, back = gates[where], ups[where], backs[where]
-        _, act, slope = silu_parts(gate_pre)
-        sent[0, number] = (
-            dot3(pair_of(acts, 0, where), pair_of(wide, 0), NT)
-            + dot3(pair_of(acts, 1, where), pair_of(wide, 1), NT)
-            + dot3(split(back * up_pre * slope), pair_of(cots, 0), NT)
-            + dot3(split(back * act), pair_of(cots, 1), NT)
-        )
-        sent[1, number] = dot3(pair_of(acts, 2, where), pair_of(wide, 2), NT) + dot3(
-            split(act * up_pre), pair_of(cots, 2), NT
-        )
-        for each in range(last - first):
-
-            @pl.when(number == each)
-            def _():
-                for side, (source, out) in enumerate(outgoing(each)):
-                    pltpu.make_async_copy(source, out, out_sems.at[each, side]).start()
-
-    for each in range(last - first):
-        for side, (source, out) in enumerate(outgoing(each)):
-            pltpu.make_async_copy(source, out, out_sems.at[each, side]).wait()
-
-
-def call(kernel, inputs, in_specs, outs, out_specs, scratch, flops=0):
+def call(kernel, inputs, in_specs, outs, out_specs, scratch, flops=0, grant=26):
     moved = sum(math.prod(value.shape) * value.dtype.itemsize for value in list(inputs) + list(outs))
     return pl.pallas_call(
         kernel,
@@ -488,7 +496,7 @@
         out_specs=out_specs,
         scratch_shapes=scratch,
         cost_estimate=pl.CostEstimate(flops=flops, bytes_accessed=moved, transcendentals=0),
-        compiler_params=pltpu.CompilerParams(vmem_limit_bytes=26 << 20),
+        compiler_params=pltpu.CompilerParams(vmem_limit_bytes=grant << 20),
     )(*inputs)
 
 
@@ -524,9 +532,13 @@
         [shape((3, rows, cols), F32)] * (ROUNDS + 2),
         [HBM] * (ROUNDS + 2),
         [dma((ROUNDS + 2, 3))],
-    )
+        grant=60,
+    )
+    packed = list(packed)
+    packed[0], value_first = lax.optimization_barrier((packed[0], value_rows[0, 0]))
     slots = [lax.ppermute(packed[turn], PLACE, pairs[turn]) for turn in range(ROUNDS)]
-    other = lax.ppermute(packed[ROUNDS + 1], "head", SWAP)
+    slots[0], other = lax.optimization_barrier((slots[0], packed[ROUNDS + 1]))
+    other = lax.ppermute(other, "head", SWAP)
     (together,) = call(
         collect_kernel,
         slots + [packed[ROUNDS], other],
@@ -555,22 +567,29 @@
             outs,
             [HBM] * CELL,
             scratch,
+            grant=60 if scale is not None else 26,
         )
         near = [lax.ppermute(packed[turn], PLACE, pairs[turn]) for turn in range(ROUNDS)]
-        got = lax.ppermute(packed[ROUNDS], "head", SWAP)
-        return near, [packed[ROUNDS], got]
+        near[0], local = lax.optimization_barrier((near[0], packed[ROUNDS]))
+        return near, [local, lax.ppermute(local, "head", SWAP)]
 
     def spread(near, local):
         return near + [lax.ppermute(piece, "head", SWAP) for piece in near] + local
 
-    def hand_back(near, far, first):
+    def combine(near, far):
         across = lax.ppermute(far, "head", SWAP)
         length = near[0].shape[0]
-        back = []
-        for number, part in enumerate(near):
-            total = part + across[number * length : (number + 1) * length]
-            back.append(lax.ppermute(total, PLACE, flipped(pairs[first + number])))
-        return back, far[len(near) * length :] + across[len(near) * length :]
+        found = [
+            part + across[number * length : (number + 1) * length]
+            for number, part in enumerate(near)
+        ]
+        return found, far[len(near) * length :] + across[len(near) * length :]
+
+    def hand_back(totals, first):
+        return [
+            lax.ppermute(total, PLACE, flipped(pairs[first + number]))
+            for number, total in enumerate(totals)
+        ]
 
     def settle(back, local):
         def choose(turn):
@@ -585,8 +604,9 @@
             found.append(jnp.where(at_home, here, remote))
         return found
 
-    inner_near, inner_local = gather(key_rows[0, 0], value_rows[0, 0], -step[:, None])
-    read_near, read_local = gather(query_rows[0, 0], read_cotangent[0, 0], None)
+    inner_near, inner_local = gather(key_rows[0, 0], value_first, -step[:, None])
+    inner_near[0], queries = lax.optimization_barrier((inner_near[0], query_rows[0, 0]))
+    read_near, read_local = gather(queries, read_cotangent[0, 0], None)
     inner_rows = spread(inner_near, inner_local)
 
     size = 2 * half
@@ -598,14 +618,13 @@
     turned = pltpu.VMEM((2, 2, depth, count), BF16)
     acts = pltpu.VMEM((2, 3, count, cols), BF16)
     split_square = pltpu.VMEM((2, 3, width, cols), BF16)
-    weights, gates, ups, backs, steps = call(
+    weights, gates, ups, backs, key_turned, steps = call(
         functools.partial(inner_kernel, cells, reps),
         parts + inner_rows,
         [HBM] * (len(parts) + 8),
-        [square, tall, tall, tall, square],
-        [VMEM] * 5,
-        buffers
-        + [split_square, turned, acts, dma((CELL, 4)), dma((cells * reps * CELL,))],
+        [square, tall, tall, tall, shape((2, 2, depth, count), BF16), square],
+        [VMEM] * 6,
+        buffers + [split_square, acts, dma((CELL, 4)), dma((cells * reps * CELL,))],
         6 * product,
     )
     if cells > 1:
@@ -630,40 +649,65 @@
     totals = read[0]
     if cells > 1:
         totals = lax.psum(totals, "tok", axis_index_groups=cell_groups)
-    cots, acts_cot, *given = call(
+    cots, direct = call(
+        functools.partial(renew_back_kernel, cells),
+        [weights, steps, totals],
+        [VMEM] * 3,
+        [shape((2, 3, width, cols), BF16), square],
+        [VMEM] * 2,
+        [],
+    )
+    middle = 2
+
+    def token_grads(first, last, cots):
+        rounds = min(last, ROUNDS) - first
+        span = slice(first, first + rounds)
+        inputs = inner_rows[:ROUNDS][span] + inner_rows[ROUNDS : 2 * ROUNDS][span]
+        if last > ROUNDS:
+            inputs = inputs + inner_rows[2 * ROUNDS :]
+        blocks = last - first
+        acts, *outs = call(
+            functools.partial(token_grad_kernel, first, last),
+            inputs + [weights, cots, gates, ups, backs],
+            [HBM] * len(inputs) + [VMEM] * 5,
+            [shape((2, 3, blocks * size, cols), BF16)]
+            + [shape((size, depth), F32)] * rounds
+            + [shape((size * (2 * blocks - rounds), depth), F32)],
+            [VMEM] + [HBM] * (rounds + 1),
+            [pltpu.VMEM((blocks, size, depth), F32)] * 2
+            + [
+                split_square,
+                pltpu.VMEM((2, blocks, size, depth), F32),
+                dma((blocks, 4)),
+                dma((blocks, 4)),
+            ],
+            9 * product * blocks // CELL,
+        )
+        return acts, outs[:rounds], outs[rounds]
+
+    acts_first, near_first, far_first = token_grads(0, middle, cots)
+    query_totals, query_local = combine(read[1:4], read[4])
+    cots, *query_totals = lax.optimization_barrier((cots, *query_totals))
+    query_back = hand_back(query_totals, 0)
+    acts_last, near_last, far_last = token_grads(middle, CELL, cots)
+    acts_last, *near_first = lax.optimization_barrier((acts_last, *near_first))
+    totals_first, _ = combine(near_first, far_first)
+    acts_last, *totals_first = lax.optimization_barrier((acts_last, *totals_first))
+    back = hand_back(totals_first, 0)
+    given = call(
         functools.partial(weight_grad_kernel, cells, reps),
-        inner_rows + [weights, steps, totals, gates, ups, backs],
-        [HBM] * 8 + [VMEM] * 6,
-        [shape((2, 3, width, cols), BF16), shape((2, 3, count, cols), BF16)]
-        + [shape((cells, CELL, 3, rows, cols), F32)] * reps,
-        [VMEM] * 2 + [HBM] * reps,
-        buffers
-        + [
-            turned,
-            pltpu.VMEM((3, width, cols), F32),
-            dma((CELL, 4)),
-            dma((cells * reps * CELL,)),
-        ],
-        6 * product,
-    )
-    query_back, query_local = hand_back(read[1:4], read[4], 0)
-    middle = 2
-    piece = shape((size, depth), F32)
-    back = []
-    for first, last in ((0, middle), (middle, CELL)):
-        rounds = min(last, ROUNDS) - first
-        over = size * (2 * (last - first) - rounds)
-        out = call(
-            functools.partial(token_grad_kernel, first, last),
-            [weights, cots, acts_cot, gates, ups, backs],
-            [VMEM] * 6,
-            [piece] * rounds + [shape((over, depth), F32)],
-            [HBM] * (rounds + 1),
-            [split_square, pltpu.VMEM((2, last - first, size, depth), F32), dma((last - first, 4))],
-            6 * product * (last - first) // CELL,
-        )
-        returned, local = hand_back(out[:rounds], out[rounds], first)
-        back += returned
+        [key_turned, direct, acts_first, acts_last],
+        [VMEM] * 4,
+        [shape((cells, CELL, 3, rows, cols), F32)] * reps,
+        [HBM] * reps,
+        [pltpu.VMEM((3, width, cols), F32), dma((cells * reps * CELL,))],
+        3 * product,
+    )
+    given = list(given)
+    far_last, given[0], *query_back = lax.optimization_barrier((far_last, given[0], *query_back))
+    totals_last, local = combine(near_last, far_last)
+    given[0], *totals_last = lax.optimization_barrier((given[0], *totals_last))
+    back += hand_back(totals_last, middle)
     (query_grad,) = settle(query_back, query_local)
     key_grad, target_grad = settle(back, local)
 

time: 174 us -> 234 us (1.34); the launches traced: 171 us -> 233 us
  Pallas kernels: 38.9 us -> 113 us
  waiting for transfers between devices: 82.5 us -> 68.4 us
  starting transfers between devices: 28.7 us -> 36.5 us
  local copies, waits for them, and re-layouts: 8.41 us -> 2.68 us
    pallas_call x10 -> x11, Pallas kernels: 38.9 us -> 113 us  [call(): pl.pallas_call(kernel, out_shape=outs, in_specs=in_specs, out_specs=out_s...]
    ppermute x12, waiting for transfers between devices: 23.8 us -> 14.6 us  [the longest x6 12.5 us: hand_back(): lax.ppermute(total, PLACE, flipped(pairs[first + number]))]
    ppermute x6, waiting for transfers between devices: 32.3 us -> 23.5 us  [gather(): lax.ppermute(packed[turn], PLACE, pairs[turn])]
    ppermute x3, waiting for transfers between devices: 2.4 us -> 7.57 us  [per_device(): lax.ppermute(packed[turn], PLACE, pairs[turn])]
    unnamed x28 -> x30, local copies, waits for them, and re-layouts: 6.64 us -> 1.67 us
    ppermute x12, starting transfers between devices: 9.41 us -> 14 us  [the longest x6 10.9 us: hand_back(): lax.ppermute(total, PLACE, flipped(pairs[first + number]))]
    ppermute x6, starting transfers between devices: 8.75 us -> 5.6 us  [gather(): lax.ppermute(packed[turn], PLACE, pairs[turn])]
    ppermute x6, starting transfers between devices: 2.14 us -> 4.69 us  [spread(): return near + [lax.ppermute(piece, 'head', SWAP) for piece in near] + local]
  transfers between devices with their start and end apart: 33 -> 33, of which waited for: 18 -> 19; matrix products, arithmetic and copies ran while one was open for 7% -> 4% of each run, Pallas kernels for 10% -> 12%
where the time goes in v4:
time: 234 us; the launch traced here: 233 us
  Pallas kernels  113 us (48%)
  waiting for transfers between devices  68.4 us (29%)
  starting transfers between devices  36.5 us (16%)
  other arithmetic  11.7 us (5%)
  local copies, waits for them, and re-layouts  2.68 us (1%)
    pallas_call x11, Pallas kernels, call(): pl.pallas_call(kernel, out_shape=outs, in_specs=in_specs, out_specs=out_s...  113 us
    ppermute x6, waiting for transfers between devices, gather(): lax.ppermute(packed[turn], PLACE, pairs[turn])  23.5 us
    ppermute x6, waiting for transfers between devices, hand_back(): lax.ppermute(total, PLACE, flipped(pairs[first + number]))  12.5 us
    ppermute x1, waiting for transfers between devices, per_device(): total = total + lax.ppermute(given[shift][0], 'rep', shifted(shift, 1))  12.5 us
    ppermute x6, starting transfers between devices, hand_back(): lax.ppermute(total, PLACE, flipped(pairs[first + number]))  10.9 us
    ppermute x3, waiting for transfers between devices, per_device(): lax.ppermute(packed[turn], PLACE, pairs[turn])  7.57 us
    ppermute x3, waiting for transfers between devices, per_device(): lax.ppermute(total[turn], PLACE, flipped(pairs[turn]))  6.86 us
    ppermute x3, starting transfers between devices, per_device(): lax.ppermute(packed[turn], PLACE, pairs[turn])  5.75 us
  transfers between devices with their start and end apart: 33, of which 19 were waited for; matrix products, arithmetic and copies ran while one was open for 4% of the time, Pallas kernels for 12%

profile of v4, /device:TPU:22, one launch (start us, length us, event | category | flops | bytes accessed | tf_op | source)
XLA Modules:
  0.0 233.4 jit_solution(11500912583973696608)
XLA Ops:
  0.6 31.0 %shard_map.135 = (f32[3,64,256]{2,1,0:T(8,128)}, f32[3,64,256]{2,1,0:T(8,128)}, f32[3,64,256]{2,1,0:T(8,128)}, f32[3,64,256]{2,1,0:T(8,128)}, f32[3,64,256]{2,1,0:T(8,128)}) custom-call(f32[64,512]{1,0:T(8,128)} %bitcast.36, f32[64,512]{1,0:T(8,128)} %bitcast.37, f32[64,512]{1,0:T(8,128)} %bitcast.38), custom_call_target="tpu_custom_call" | custom-call | bytes 1376256 | tf_op jit(solution)/shard_map/pallas_call | solution.py:492
  31.7 0.9 copy.20
  32.7 0.7 fusion.4.refs_2_
  33.4 41.8 %shard_map.136 = (f32[256,512]{1,0:T(8,128)}, f32[256,512]{1,0:T(8,128)}, f32[256,512]{1,0:T(8,128)}, f32[512,512]{1,0:T(8,128)}) custom-call(f32[256,512]{1,0:T(8,128)} %bitcast.35, f32[256,512]{1,0:T(8,128)} %bitcast.34, f32[256,1]{1,0:T(8,128)} %fusion.4.refs_2_), custom_call_target="tpu_custom_call" | custom-call | bytes 3671040 | tf_op jit(solution)/shard_map/pallas_call | solution.py:492
  75.4 4.3 %collective-permute-start.5 = (f32[3,64,256]{2,1,0:T(8,128)S(1)}, f32[3,64,256]{2,1,0:T(8,128)S(1)}, u32[]{:S(2)}, u32[]{:S(2)}) collective-permute-start(f32[3,64,256]{2,1,0:T(8,128)S(1)} %copy-done.13), channel_id=1, source_target_pairs={{8,4},{12,5},{1,8},{5,9},{0,0},{4,1},{9,12},{13,13},{10,6},{14,7},... | collective-permute-start | bytes 589832 | tf_op jit(solution)/shard_map/ppermute | solution.py:539
  79.7 1.4 collective-permute-start.6
  81.1 2.6 %collective-permute-start.9 = (f32[256,512]{1,0:T(8,128)}, f32[256,512]{1,0:T(8,128)S(1)}, u32[]{:S(2)}, u32[]{:S(2)}) collective-permute-start(f32[256,512]{1,0:T(8,128)} %get-tuple-element.94), channel_id=1, source_target_pairs={{8,4},{12,5},{1,8},{5,9},{0,0},{4,1},{9,12},{13,13},{10,6},{14,7},... | collective-permute-start | bytes 1572872 | tf_op jit(solution)/shard_map/ppermute | solution.py:572
  83.7 1.9 collective-permute-done.refs_2_.refs_0_
  85.6 1.0 collective-permute-start.10
  86.6 3.2 %collective-permute-done.4.first = f32[3,64,256]{2,1,0:T(8,128)S(1)} collective-permute-done((f32[3,64,256]{2,1,0:T(8,128)S(1)}, f32[3,64,256]{2,1,0:T(8,128)S(1)}, u32[]{:S(2)}, u32[]{:S(2)}) %collective-permute-start.4) | collective-permute-done | bytes 196640 | tf_op jit(solution)/shard_map/ppermute | solution.py:539
  89.8 4.2 %collective-permute-start.11 = (f32[256,512]{1,0:T(8,128)S(1)}, f32[256,512]{1,0:T(8,128)S(1)}, u32[]{:S(2)}, u32[]{:S(2)}) collective-permute-start(f32[256,512]{1,0:T(8,128)S(1)} %collective-permute-done.refs_2_.refs_0_), channel_id=1, source_target_pairs={{0,1},{1,0},{2,3},{3,2},{4,5},{5,4},{6,7},{7,6},{8,9},{9,8},{10,11... | collective-permute-start | bytes 1572872 | tf_op jit(solution)/shard_map/ppermute | solution.py:577
  94.0 4.4 %collective-permute-done.5.second = f32[3,64,256]{2,1,0:T(8,128)S(1)} collective-permute-done((f32[3,64,256]{2,1,0:T(8,128)S(1)}, f32[3,64,256]{2,1,0:T(8,128)S(1)}, u32[]{:S(2)}, u32[]{:S(2)}) %collective-permute-start.5) | collective-permute-done | bytes 196640 | tf_op jit(solution)/shard_map/ppermute | solution.py:539
  98.4 0.5 collective-permute-start.7
  98.9 2.1 collective-permute-done.7.got
  100.9 1.0 shard_map.138.refs_0_
  102.0 0.6 collective-permute-start.8
  102.6 0.3 shard_map.137
  102.9 6.7 %collective-permute-done.9.refs_3_.refs_1_ = f32[256,512]{1,0:T(8,128)S(1)} collective-permute-done((f32[256,512]{1,0:T(8,128)}, f32[256,512]{1,0:T(8,128)S(1)}, u32[]{:S(2)}, u32[]{:S(2)}) %collective-permute-start.9) | collective-permute-done | bytes 524320 | tf_op jit(solution)/shard_map/ppermute | solution.py:572
  109.6 1.4 collective-permute-done.10.refs_4_.refs_0_
  111.0 0.5 collective-permute-done.12.refs_6_.refs_3_
  111.5 1.9 collective-permute-start.2
  113.4 9.2 %collective-permute-done.1.refs_0_ = f32[256,512]{1,0:T(8,128)S(1)} collective-permute-done((f32[256,512]{1,0:T(8,128)S(1)}, f32[256,512]{1,0:T(8,128)S(1)}, u32[]{:S(2)}, u32[]{:S(2)}) %collective-permute-start.1) | collective-permute-done | bytes 524320 | tf_op jit(solution)/shard_map/ppermute | solution.py:572
  122.6 1.9 collective-permute-start.18
  124.4 7.8 %shard_map.139 = (f32[3,512,256]{2,1,0:T(8,128)S(1)}, f32[1024,256]{1,0:T(8,128)S(1)}, f32[1024,256]{1,0:T(8,128)S(1)}, f32[1024,256]{1,0:T(8,128)S(1)}, bf16[2,...) custom-call(f32[4,3,64,256]{3,2,1,0:T(8,128)S(1)} %shard_map.138.refs_0_, ...), custom_call_target="tpu_custom_call" | custom-call | flops 4831838208 | bytes 17301504 | tf_op jit(solution)/shard_map/pallas_call | solution.py:492
  132.3 0.6 shard_map.140
  132.9 1.9 collective-permute-done.2.refs_1_
  134.8 2.4 %collective-permute-done.3.refs_2_ = f32[256,512]{1,0:T(8,128)S(1)} collective-permute-done((f32[256,512]{1,0:T(8,128)S(1)}, f32[256,512]{1,0:T(8,128)S(1)}, u32[]{:S(2)}, u32[]{:S(2)}) %collective-permute-start.3) | collective-permute-done | bytes 524320 | tf_op jit(solution)/shard_map/ppermute | solution.py:572
  137.2 0.5 collective-permute-start.16
  137.7 1.4 collective-permute-done.15.refs_3_
  139.1 0.7 collective-permute-done.16.refs_4_
  139.9 0.7 collective-permute-done.17.refs_5_
  140.6 11.8 %shard_map.141 = (f32[3,512,256]{2,1,0:T(8,128)S(1)}, f32[128,512]{1,0:T(8,128)S(1)}, f32[128,512]{1,0:T(8,128)S(1)}, f32[128,512]{1,0:T(8,128)S(1)}, f32[640,512]{1,0:T(8,128)S(1)}) custom-call(f32[256,512]{1,0:T(8,128)S(1)} %collective-permute-done.1.refs_0_, f32[256,512]{1,0:T(8,128)S(1)} %collective-permute-done.2.refs_1_, ...), custom_call_target="tpu_custom_call" | custom-call | flops 6442450944 | bytes 10485760 | tf_op jit(solution)/shard_map/pallas_call | solution.py:492
  152.5 0.2 collective-permute-start.19
  152.7 1.2 shard_map.142
  153.9 6.8 %shard_map.144 = (bf16[2,3,512,256]{3,2,1,0:T(8,128)(2,1)S(1)}, f32[256,512]{1,0:T(8,128)S(1)}, f32[256,512]{1,0:T(8,128)S(1)}, f32[512,512]{1,0:T(8,128)S(1)}) custom-call(f32[256,512]{1,0:T(8,128)S(1)} %collective-permute-done.refs_2_.refs_0_, f32[256,512]{1,0:T(8,128)S(1)} %collective-permute-done.9.refs_3_.refs_1_, ...), custom_call_target="tpu_custom_call" | custom-call | flops 3623878656 | bytes 12058624 | tf_op jit(solution)/shard_map/pallas_call | solution.py:492
  160.6 0.4 collective-permute-start.20
  161.2 6.8 %shard_map.143 = (bf16[2,3,512,256]{3,2,1,0:T(8,128)(2,1)S(1)}, f32[256,512]{1,0:T(8,128)S(1)}, f32[768,512]{1,0:T(8,128)S(1)}) custom-call(f32[256,512]{1,0:T(8,128)S(1)} %collective-permute-done.10.refs_4_.refs_0_, f32[256,512]{1,0:T(8,128)S(1)} %collective-permute-done.13.refs_7_.refs_1_, f32[512,512]{1,0:T(8,128)S(1)} %copy-done.4, ...), custom_call_target="tpu_custom_call" | custom-call | flops 3623878656 | bytes 13107200 | tf_op jit(solution)/shard_map/pallas_call | solution.py:492
  168.0 0.4 collective-permute-start.21
  168.4 5.0 %collective-permute-start.22 = (f32[128,512]{1,0:T(8,128)S(1)}, f32[128,512]{1,0:T(8,128)S(1)}, u32[]{:S(2)}, u32[]{:S(2)}) collective-permute-start(f32[128,512]{1,0:T(8,128)S(1)} %get-tuple-element.130), channel_id=1, source_target_pairs={{4,8},{5,12},{8,1},{9,5},{0,0},{1,4},{12,9},{13,13},{6,10},{7,14},... | collective-permute-start | bytes 786440 | tf_op jit(solution)/shard_map/ppermute | solution.py:590
  173.4 0.3 collective-permute-start.23
  173.7 1.0 slice_add_fusion.2
  174.7 3.9 %shard_map.145 = (f32[1,4,3,64,256]{4,3,2,1,0:T(8,128)S(1)}, f32[1,4,3,64,256]{4,3,2,1,0:T(8,128)}) custom-call(bf16[2,2,512,1024]{3,2,1,0:T(8,128)(2,1)S(1)} %get-tuple-element.117.turned, f32[3,512,256]{2,1,0:T(8,128)S(1)} %get-tuple-element.118.direct, bf16[2,3,512,256]{3,2,1,0:T(8,128)(2,1)S(1)} %get-tuple-element.119.refs_0_, ...), custom_call_target="tpu_custom_call" | custom-call | flops 2415919104 | bytes 10485760 | tf_op jit(solution)/shard_map/pallas_call | solution.py:492
  178.6 1.1 collective-permute-done.22
  179.7 2.9 %collective-permute-done.23 = f32[128,512]{1,0:T(8,128)S(1)} collective-permute-done((f32[128,512]{1,0:T(8,128)S(1)}, f32[128,512]{1,0:T(8,128)S(1)}, u32[]{:S(2)}, u32[]{:S(2)}) %collective-permute-start.23) | collective-permute-done | bytes 262176 | tf_op jit(solution)/shard_map/ppermute | solution.py:590
  182.7 0.6 copy-done.9
  183.3 0.5 collective-permute-start.28
  183.9 0.9 collective-permute-start.25
  184.7 3.4 %collective-permute-start.26 = (f32[256,512]{1,0:T(8,128)S(1)}, f32[256,512]{1,0:T(8,128)S(1)}, u32[]{:S(2)}, u32[]{:S(2)}) collective-permute-start(f32[256,512]{1,0:T(8,128)S(1)} %get-tuple-element.137), channel_id=1, source_target_pairs={{4,8},{5,12},{8,1},{9,5},{0,0},{1,4},{12,9},{13,13},{6,10},{7,14},... | collective-permute-start | bytes 1572872 | tf_op jit(solution)/shard_map/ppermute | solution.py:590
  188.1 1.2 select_select_fusion.3
  189.3 1.1 slice_add_fusion.1
  190.4 12.5 %collective-permute-done.28 = f32[4,3,64,256]{3,2,1,0:T(8,128)} collective-permute-done((f32[4,3,64,256]{3,2,1,0:T(8,128)}, f32[4,3,64,256]{3,2,1,0:T(8,128)}, u32[]{:S(2)}, u32[]{:S(2)}) %collective-permute-start.28) | collective-permute-done | bytes 786464 | tf_op jit(solution)/shard_map/ppermute | solution.py:721
  202.9 1.2 bitcast_add_fusion
  204.3 1.7 collective-permute-start.30
  206.0 2.1 fusion.2
  208.2 3.4 %collective-permute-start.31 = (f32[3,64,256]{2,1,0:T(8,128)S(1)}, f32[3,64,256]{2,1,0:T(8,128)S(1)}, u32[]{:S(2)}, u32[]{:S(2)}) collective-permute-start(f32[3,64,256]{2,1,0:T(8,128)S(1)} %get-tuple-element.157), channel_id=1, source_target_pairs={{4,8},{5,12},{8,1},{9,5},{0,0},{1,4},{12,9},{13,13},{6,10},{7,14},... | collective-permute-start | bytes 589832 | tf_op jit(solution)/shard_map/ppermute | solution.py:723
  211.7 1.1 collective-permute-start.27
  212.8 1.4 slice_add_fusion
  214.2 2.9 %collective-permute-done.31 = f32[3,64,256]{2,1,0:T(8,128)S(1)} collective-permute-done((f32[3,64,256]{2,1,0:T(8,128)S(1)}, f32[3,64,256]{2,1,0:T(8,128)S(1)}, u32[]{:S(2)}, u32[]{:S(2)}) %collective-permute-start.31) | collective-permute-done | bytes 196640 | tf_op jit(solution)/shard_map/ppermute | solution.py:723
  217.1 4.0 %collective-permute-done.32 = f32[3,64,256]{2,1,0:T(8,128)S(1)} collective-permute-done((f32[3,64,256]{2,1,0:T(8,128)S(1)}, f32[3,64,256]{2,1,0:T(8,128)S(1)}, u32[]{:S(2)}, u32[]{:S(2)}) %collective-permute-start.32) | collective-permute-done | bytes 196640 | tf_op jit(solution)/shard_map/ppermute | solution.py:723
  221.1 0.8 pad_maximum_fusion
  221.9 8.6 %collective-permute-done.27 = f32[256,512]{1,0:T(8,128)S(1)} collective-permute-done((f32[256,512]{1,0:T(8,128)S(1)}, f32[256,512]{1,0:T(8,128)S(1)}, u32[]{:S(2)}, u32[]{:S(2)}) %collective-permute-start.27) | collective-permute-done | bytes 524320 | tf_op jit(solution)/shard_map/ppermute | solution.py:590
  230.7 1.0 copy-done.5
  231.7 1.2 multiply_reduce_fusion
  232.8 0.6 divide_multiply_fusion
  (61 shorter events, 1.1 us)
Async XLA Ops:
  31.7 43.6 %copy-start.14 = (f32[3,64,256]{2,1,0:T(8,128)S(1)}, f32[3,64,256]{2,1,0:T(8,128)}, u32[]{:S(2)}) copy-start(f32[3,64,256]{2,1,0:T(8,128)} %get-tuple-element.86) | copy-start | bytes 589828
  31.7 43.7 %copy-start.13 = (f32[3,64,256]{2,1,0:T(8,128)S(1)}, f32[3,64,256]{2,1,0:T(8,128)}, u32[]{:S(2)}) copy-start(f32[3,64,256]{2,1,0:T(8,128)} %get-tuple-element.89) | copy-start | bytes 589828
  31.7 47.9 %copy-start.12 = (f32[3,64,256]{2,1,0:T(8,128)S(1)}, f32[3,64,256]{2,1,0:T(8,128)}, u32[]{:S(2)}) copy-start(f32[3,64,256]{2,1,0:T(8,128)} %get-tuple-element.90) | copy-start | bytes 589828
  31.7 66.6 %copy-start.11 = (f32[3,64,256]{2,1,0:T(8,128)S(1)}, f32[3,64,256]{2,1,0:T(8,128)}, u32[]{:S(2)}) copy-start(f32[3,64,256]{2,1,0:T(8,128)} %get-tuple-element.92) | copy-start | bytes 589828
  31.7 69.2 %copy-start.3 = (f32[3,64,256]{2,1,0:T(8,128)S(1)}, f32[3,64,256]{2,1,0:T(8,128)}, u32[]{:S(2)}) copy-start(f32[3,64,256]{2,1,0:T(8,128)} %get-tuple-element.91.own) | copy-start | bytes 589828
  32.6 70.0 %copy-start = (f32[1,1,256,512]{3,2,1,0:T(8,128)S(1)}, f32[1,1,256,512]{3,2,1,0:T(8,128)}, u32[]{:S(2)}) copy-start(f32[1,1,256,512]{3,2,1,0:T(8,128)} %param.8) | copy-start | bytes 1572868
  32.6 69.9 %copy-start.1 = (f32[1,1,256,512]{3,2,1,0:T(8,128)S(1)}, f32[1,1,256,512]{3,2,1,0:T(8,128)}, u32[]{:S(2)}) copy-start(f32[1,1,256,512]{3,2,1,0:T(8,128)} %param.12) | copy-start | bytes 1572868
  75.2 49.2 %copy-start.4 = (f32[512,512]{1,0:T(8,128)S(1)}, f32[512,512]{1,0:T(8,128)}, u32[]{:S(2)}) copy-start(f32[512,512]{1,0:T(8,128)} %get-tuple-element.96.refs_8_.refs_2_) | copy-start | bytes 3145732
  75.2 10.4 %collective-permute-start = (f32[256,512]{1,0:T(8,128)}, f32[256,512]{1,0:T(8,128)S(1)}, u32[]{:S(2)}, u32[]{:S(2)}) collective-permute-start(f32[256,512]{1,0:T(8,128)} %get-tuple-element.77), channel_id=1, source_target_pairs={{0,4},{8,5},{13,8},{1,9},{4,0},{5,1},{9,12},{12,13},{2,6},{10,7},{... | collective-permute-start | bytes 1572872 | tf_op jit(solution)/shard_map/ppermute | solution.py:572
  75.3 14.5 %collective-permute-start.4 = (f32[3,64,256]{2,1,0:T(8,128)S(1)}, f32[3,64,256]{2,1,0:T(8,128)S(1)}, u32[]{:S(2)}, u32[]{:S(2)}) collective-permute-start(f32[3,64,256]{2,1,0:T(8,128)S(1)} %copy-done.14), channel_id=1, source_target_pairs={{0,4},{8,5},{13,8},{1,9},{4,0},{5,1},{9,12},{12,13},{2,6},{10,7},{... | collective-permute-start | bytes 589832 | tf_op jit(solution)/shard_map/ppermute | solution.py:539
  75.4 23.0 %collective-permute-start.5 = (f32[3,64,256]{2,1,0:T(8,128)S(1)}, f32[3,64,256]{2,1,0:T(8,128)S(1)}, u32[]{:S(2)}, u32[]{:S(2)}) collective-permute-start(f32[3,64,256]{2,1,0:T(8,128)S(1)} %copy-done.13), channel_id=1, source_target_pairs={{8,4},{12,5},{1,8},{5,9},{0,0},{4,1},{9,12},{13,13},{10,6},{14,7},... | collective-permute-start | bytes 589832 | tf_op jit(solution)/shard_map/ppermute | solution.py:539
  79.7 18.7 %collective-permute-start.6 = (f32[3,64,256]{2,1,0:T(8,128)S(1)}, f32[3,64,256]{2,1,0:T(8,128)S(1)}, u32[]{:S(2)}, u32[]{:S(2)}) collective-permute-start(f32[3,64,256]{2,1,0:T(8,128)S(1)} %copy-done.12), channel_id=1, source_target_pairs={{12,4},{0,5},{5,8},{13,9},{1,0},{4,1},{8,12},{9,13},{14,6},{2,7},{... | collective-permute-start | bytes 589832 | tf_op jit(solution)/shard_map/ppermute | solution.py:539
  81.1 28.5 %collective-permute-start.9 = (f32[256,512]{1,0:T(8,128)}, f32[256,512]{1,0:T(8,128)S(1)}, u32[]{:S(2)}, u32[]{:S(2)}) collective-permute-start(f32[256,512]{1,0:T(8,128)} %get-tuple-element.94), channel_id=1, source_target_pairs={{8,4},{12,5},{1,8},{5,9},{0,0},{4,1},{9,12},{13,13},{10,6},{14,7},... | collective-permute-start | bytes 1572872 | tf_op jit(solution)/shard_map/ppermute | solution.py:572
  85.6 25.4 %collective-permute-start.10 = (f32[256,512]{1,0:T(8,128)}, f32[256,512]{1,0:T(8,128)S(1)}, u32[]{:S(2)}, u32[]{:S(2)}) collective-permute-start(f32[256,512]{1,0:T(8,128)} %get-tuple-element.95), channel_id=1, source_target_pairs={{12,4},{0,5},{5,8},{13,9},{1,0},{4,1},{8,12},{9,13},{14,6},{2,7},{... | collective-permute-start | bytes 1572872 | tf_op jit(solution)/shard_map/ppermute | solution.py:572
  89.8 21.2 %collective-permute-start.11 = (f32[256,512]{1,0:T(8,128)S(1)}, f32[256,512]{1,0:T(8,128)S(1)}, u32[]{:S(2)}, u32[]{:S(2)}) collective-permute-start(f32[256,512]{1,0:T(8,128)S(1)} %collective-permute-done.refs_2_.refs_0_), channel_id=1, source_target_pairs={{0,1},{1,0},{2,3},{3,2},{4,5},{5,4},{6,7},{7,6},{8,9},{9,8},{10,11... | collective-permute-start | bytes 1572872 | tf_op jit(solution)/shard_map/ppermute | solution.py:577
  98.4 26.1 %collective-permute-start.14 = (f32[512,512]{1,0:T(8,128)}, f32[512,512]{1,0:T(8,128)S(1)}, u32[]{:S(2)}, u32[]{:S(2)}) collective-permute-start(f32[512,512]{1,0:T(8,128)} %get-tuple-element.96.refs_8_.refs_2_), channel_id=1, source_target_pairs={{0,1},{1,0},{2,3},{3,2},{4,5},{5,4},{6,7},{7,6},{8,9},{9,8},{10,11... | collective-permute-start | bytes 3145736 | tf_op jit(solution)/shard_map/ppermute | solution.py:574
  98.4 2.6 %collective-permute-start.7 = (f32[3,64,256]{2,1,0:T(8,128)S(1)}, f32[3,64,256]{2,1,0:T(8,128)S(1)}, u32[]{:S(2)}, u32[]{:S(2)}) collective-permute-start(f32[3,64,256]{2,1,0:T(8,128)S(1)} %copy-done.11), channel_id=1, source_target_pairs={{0,1},{1,0},{2,3},{3,2},{4,5},{5,4},{6,7},{7,6},{8,9},{9,8},{10,11... | collective-permute-start | bytes 589832 | tf_op jit(solution)/shard_map/ppermute | solution.py:541
  102.0 22.5 %collective-permute-start.8 = (f32[4,3,64,256]{3,2,1,0:T(8,128)S(1)}, f32[4,3,64,256]{3,2,1,0:T(8,128)S(1)}, u32[]{:S(2)}, u32[]{:S(2)}) collective-permute-start(f32[4,3,64,256]{3,2,1,0:T(8,128)S(1)} %shard_map.138.refs_0_), channel_id=1, source_target_pairs={{0,2},{2,0},{1,3},{3,1},{4,6},{6,4},{5,7},{7,5},{8,10},{10,8},{9,1... | collective-permute-start | bytes 2359304 | tf_op jit(solution)/shard_map/ppermute | solution.py:552
  109.6 1.9 collective-permute-start.12
  111.0 11.6 %collective-permute-start.1 = (f32[256,512]{1,0:T(8,128)S(1)}, f32[256,512]{1,0:T(8,128)S(1)}, u32[]{:S(2)}, u32[]{:S(2)}) collective-permute-start(f32[256,512]{1,0:T(8,128)S(1)} %get-tuple-element.81), channel_id=1, source_target_pairs={{0,4},{8,5},{13,8},{1,9},{4,0},{5,1},{9,12},{12,13},{2,6},{10,7},{... | collective-permute-start | bytes 1572872 | tf_op jit(solution)/shard_map/ppermute | solution.py:572
  111.0 11.6 %collective-permute-start.13 = (f32[256,512]{1,0:T(8,128)S(1)}, f32[256,512]{1,0:T(8,128)S(1)}, u32[]{:S(2)}, u32[]{:S(2)}) collective-permute-start(f32[256,512]{1,0:T(8,128)S(1)} %collective-permute-done.10.refs_4_.refs_0_), channel_id=1, source_target_pairs={{0,1},{1,0},{2,3},{3,2},{4,5},{5,4},{6,7},{7,6},{8,9},{9,8},{10,11... | collective-permute-start | bytes 1572872 | tf_op jit(solution)/shard_map/ppermute | solution.py:577
  111.5 23.3 %collective-permute-start.2 = (f32[256,512]{1,0:T(8,128)S(1)}, f32[256,512]{1,0:T(8,128)S(1)}, u32[]{:S(2)}, u32[]{:S(2)}) collective-permute-start(f32[256,512]{1,0:T(8,128)S(1)} %get-tuple-element.84), channel_id=1, source_target_pairs={{8,4},{12,5},{1,8},{5,9},{0,0},{4,1},{9,12},{13,13},{10,6},{14,7},... | collective-permute-start | bytes 1572872 | tf_op jit(solution)/shard_map/ppermute | solution.py:572
  122.6 14.6 %collective-permute-start.3 = (f32[256,512]{1,0:T(8,128)S(1)}, f32[256,512]{1,0:T(8,128)S(1)}, u32[]{:S(2)}, u32[]{:S(2)}) collective-permute-start(f32[256,512]{1,0:T(8,128)S(1)} %get-tuple-element.85), channel_id=1, source_target_pairs={{12,4},{0,5},{5,8},{13,9},{1,0},{4,1},{8,12},{9,13},{14,6},{2,7},{... | collective-permute-start | bytes 1572872 | tf_op jit(solution)/shard_map/ppermute | solution.py:572
  122.6 18.0 %collective-permute-start.18 = (f32[512,512]{1,0:T(8,128)S(1)}, f32[512,512]{1,0:T(8,128)S(1)}, u32[]{:S(2)}, u32[]{:S(2)}) collective-permute-start(f32[512,512]{1,0:T(8,128)S(1)} %get-tuple-element.103.refs_6_), channel_id=1, source_target_pairs={{0,1},{1,0},{2,3},{3,2},{4,5},{5,4},{6,7},{7,6},{8,9},{9,8},{10,11... | collective-permute-start | bytes 3145736 | tf_op jit(solution)/shard_map/ppermute | solution.py:574
  137.2 1.9 collective-permute-start.15
  137.2 2.7 %collective-permute-start.16 = (f32[256,512]{1,0:T(8,128)S(1)}, f32[256,512]{1,0:T(8,128)S(1)}, u32[]{:S(2)}, u32[]{:S(2)}) collective-permute-start(f32[256,512]{1,0:T(8,128)S(1)} %collective-permute-done.2.refs_1_), channel_id=1, source_target_pairs={{0,1},{1,0},{2,3},{3,2},{4,5},{5,4},{6,7},{7,6},{8,9},{9,8},{10,11... | collective-permute-start | bytes 1572872 | tf_op jit(solution)/shard_map/ppermute | solution.py:577
  137.7 2.9 %collective-permute-start.17 = (f32[256,512]{1,0:T(8,128)S(1)}, f32[256,512]{1,0:T(8,128)S(1)}, u32[]{:S(2)}, u32[]{:S(2)}) collective-permute-start(f32[256,512]{1,0:T(8,128)S(1)} %collective-permute-done.3.refs_2_), channel_id=1, source_target_pairs={{0,1},{1,0},{2,3},{3,2},{4,5},{5,4},{6,7},{7,6},{8,9},{9,8},{10,11... | collective-permute-start | bytes 1572872 | tf_op jit(solution)/shard_map/ppermute | solution.py:577
  152.5 1.4 copy-start.2
  152.5 8.6 %collective-permute-start.19 = (f32[640,512]{1,0:T(8,128)S(1)}, f32[640,512]{1,0:T(8,128)S(1)}, u32[]{:S(2)}, u32[]{:S(2)}) collective-permute-start(f32[640,512]{1,0:T(8,128)S(1)} %get-tuple-element.106), channel_id=1, source_target_pairs={{0,1},{1,0},{2,3},{3,2},{4,5},{5,4},{6,7},{7,6},{8,9},{9,8},{10,11... | collective-permute-start | bytes 3932168 | tf_op jit(solution)/shard_map/ppermute | solution.py:580
  160.6 13.0 %collective-permute-start.20 = (f32[512,512]{1,0:T(8,128)S(1)}, f32[512,512]{1,0:T(8,128)S(1)}, u32[]{:S(2)}, u32[]{:S(2)}) collective-permute-start(f32[512,512]{1,0:T(8,128)S(1)} %get-tuple-element.125), channel_id=1, source_target_pairs={{0,1},{1,0},{2,3},{3,2},{4,5},{5,4},{6,7},{7,6},{8,9},{9,8},{10,11... | collective-permute-start | bytes 3145736 | tf_op jit(solution)/shard_map/ppermute | solution.py:580
  161.1 6.9 %copy-start.6 = (f32[640,512]{1,0:T(8,128)}, f32[640,512]{1,0:T(8,128)S(1)}, u32[]{:S(2)}) copy-start(f32[640,512]{1,0:T(8,128)S(1)} %collective-permute-done.19) | copy-start | bytes 3932164
  168.0 10.6 %collective-permute-start.21 = (f32[128,512]{1,0:T(8,128)S(1)}, f32[128,512]{1,0:T(8,128)S(1)}, u32[]{:S(2)}, u32[]{:S(2)}) collective-permute-start(f32[128,512]{1,0:T(8,128)S(1)} %get-tuple-element.129), channel_id=1, source_target_pairs={{4,0},{5,8},{8,13},{9,1},{0,4},{1,5},{12,9},{13,12},{6,2},{7,10},{... | collective-permute-start | bytes 786440 | tf_op jit(solution)/shard_map/ppermute | solution.py:590
  168.4 11.3 %collective-permute-start.22 = (f32[128,512]{1,0:T(8,128)S(1)}, f32[128,512]{1,0:T(8,128)S(1)}, u32[]{:S(2)}, u32[]{:S(2)}) collective-permute-start(f32[128,512]{1,0:T(8,128)S(1)} %get-tuple-element.130), channel_id=1, source_target_pairs={{4,8},{5,12},{8,1},{9,5},{0,0},{1,4},{12,9},{13,13},{6,10},{7,14},... | collective-permute-start | bytes 786440 | tf_op jit(solution)/shard_map/ppermute | solution.py:590
  173.4 9.2 %collective-permute-start.23 = (f32[128,512]{1,0:T(8,128)S(1)}, f32[128,512]{1,0:T(8,128)S(1)}, u32[]{:S(2)}, u32[]{:S(2)}) collective-permute-start(f32[128,512]{1,0:T(8,128)S(1)} %get-tuple-element.131), channel_id=1, source_target_pairs={{4,12},{5,0},{8,5},{9,13},{0,1},{1,4},{12,8},{13,9},{6,14},{7,2},{... | collective-permute-start | bytes 786440 | tf_op jit(solution)/shard_map/ppermute | solution.py:590
  174.7 9.2 %copy-start.10 = (f32[1,1,256]{2,1,0:T(1,128)S(1)}, f32[1,1,256]{2,1,0:T(1,128)}, u32[]{:S(2)}) copy-start(f32[1,1,256]{2,1,0:T(1,128)} %param.11) | copy-start | bytes 3076
  178.6 4.0 %copy-start.7 = (f32[128,512]{1,0:T(8,128)}, f32[128,512]{1,0:T(8,128)S(1)}, u32[]{:S(2)}) copy-start(f32[128,512]{1,0:T(8,128)S(1)} %collective-permute-done.21) | copy-start | bytes 786436
  179.7 2.9 %copy-start.8 = (f32[128,512]{1,0:T(8,128)}, f32[128,512]{1,0:T(8,128)S(1)}, u32[]{:S(2)}) copy-start(f32[128,512]{1,0:T(8,128)S(1)} %collective-permute-done.22) | copy-start | bytes 786436
  182.6 0.7 copy-start.9
  182.6 6.7 %collective-permute-start.24 = (f32[768,512]{1,0:T(8,128)S(1)}, f32[768,512]{1,0:T(8,128)}, u32[]{:S(2)}, u32[]{:S(2)}) collective-permute-start(f32[768,512]{1,0:T(8,128)S(1)} %get-tuple-element.135), channel_id=1, source_target_pairs={{0,1},{1,0},{2,3},{3,2},{4,5},{5,4},{6,7},{7,6},{8,9},{9,8},{10,11... | collective-permute-start | bytes 4718600 | tf_op jit(solution)/shard_map/ppermute | solution.py:580
  183.3 19.6 %collective-permute-start.28 = (f32[4,3,64,256]{3,2,1,0:T(8,128)}, f32[4,3,64,256]{3,2,1,0:T(8,128)}, u32[]{:S(2)}, u32[]{:S(2)}) collective-permute-start(f32[4,3,64,256]{3,2,1,0:T(8,128)} %bitcast.14), channel_id=1, source_target_pairs={{0,2},{2,0},{1,3},{3,1},{4,6},{6,4},{5,7},{7,5},{8,10},{10,8},{9,1... | collective-permute-start | bytes 2359304 | tf_op jit(solution)/shard_map/ppermute | solution.py:721
  183.9 38.0 %collective-permute-start.25 = (f32[256,512]{1,0:T(8,128)}, f32[256,512]{1,0:T(8,128)S(1)}, u32[]{:S(2)}, u32[]{:S(2)}) collective-permute-start(f32[256,512]{1,0:T(8,128)} %get-tuple-element.136), channel_id=1, source_target_pairs={{4,0},{5,8},{8,13},{9,1},{0,4},{1,5},{12,9},{13,12},{6,2},{7,10},{... | collective-permute-start | bytes 1572872 | tf_op jit(solution)/shard_map/ppermute | solution.py:590
  184.7 37.2 %collective-permute-start.26 = (f32[256,512]{1,0:T(8,128)S(1)}, f32[256,512]{1,0:T(8,128)S(1)}, u32[]{:S(2)}, u32[]{:S(2)}) collective-permute-start(f32[256,512]{1,0:T(8,128)S(1)} %get-tuple-element.137), channel_id=1, source_target_pairs={{4,8},{5,12},{8,1},{9,5},{0,0},{1,4},{12,9},{13,13},{6,10},{7,14},... | collective-permute-start | bytes 1572872 | tf_op jit(solution)/shard_map/ppermute | solution.py:590
  204.2 7.3 %collective-permute-start.29 = (f32[3,64,256]{2,1,0:T(8,128)S(1)}, f32[3,64,256]{2,1,0:T(8,128)S(1)}, u32[]{:S(2)}, u32[]{:S(2)}) collective-permute-start(f32[3,64,256]{2,1,0:T(8,128)S(1)} %get-tuple-element.155), channel_id=1, source_target_pairs={{0,1},{1,0},{2,3},{3,2},{4,5},{5,4},{6,7},{7,6},{8,9},{9,8},{10,11... | collective-permute-start | bytes 589832 | tf_op jit(solution)/shard_map/ppermute | solution.py:726
  204.3 7.4 %collective-permute-start.30 = (f32[3,64,256]{2,1,0:T(8,128)S(1)}, f32[3,64,256]{2,1,0:T(8,128)S(1)}, u32[]{:S(2)}, u32[]{:S(2)}) collective-permute-start(f32[3,64,256]{2,1,0:T(8,128)S(1)} %get-tuple-element.158), channel_id=1, source_target_pairs={{4,0},{5,8},{8,13},{9,1},{0,4},{1,5},{12,9},{13,12},{6,2},{7,10},{... | collective-permute-start | bytes 589832 | tf_op jit(solution)/shard_map/ppermute | solution.py:723
  208.2 8.9 %collective-permute-start.31 = (f32[3,64,256]{2,1,0:T(8,128)S(1)}, f32[3,64,256]{2,1,0:T(8,128)S(1)}, u32[]{:S(2)}, u32[]{:S(2)}) collective-permute-start(f32[3,64,256]{2,1,0:T(8,128)S(1)} %get-tuple-element.157), channel_id=1, source_target_pairs={{4,8},{5,12},{8,1},{9,5},{0,0},{1,4},{12,9},{13,13},{6,10},{7,14},... | collective-permute-start | bytes 589832 | tf_op jit(solution)/shard_map/ppermute | solution.py:723
  211.6 9.5 %collective-permute-start.32 = (f32[3,64,256]{2,1,0:T(8,128)S(1)}, f32[3,64,256]{2,1,0:T(8,128)S(1)}, u32[]{:S(2)}, u32[]{:S(2)}) collective-permute-start(f32[3,64,256]{2,1,0:T(8,128)S(1)} %get-tuple-element.156), channel_id=1, source_target_pairs={{4,12},{5,0},{8,5},{9,13},{0,1},{1,4},{12,8},{13,9},{6,14},{7,2},{... | collective-permute-start | bytes 589832 | tf_op jit(solution)/shard_map/ppermute | solution.py:723
  211.7 18.7 %collective-permute-start.27 = (f32[256,512]{1,0:T(8,128)S(1)}, f32[256,512]{1,0:T(8,128)S(1)}, u32[]{:S(2)}, u32[]{:S(2)}) collective-permute-start(f32[256,512]{1,0:T(8,128)S(1)} %slice_add_fusion.1), channel_id=1, source_target_pairs={{4,12},{5,0},{8,5},{9,13},{0,1},{1,4},{12,8},{13,9},{6,14},{7,2},{... | collective-permute-start | bytes 1572872 | tf_op jit(solution)/shard_map/ppermute | solution.py:590
  230.6 1.0 copy-start.5

commit v5 on v4

--- a/solution.py
+++ b/solution.py
@@ -137,13 +137,9 @@
 
 def pack_rows_kernel(scaled, half, *refs):
     if scaled:
-        first, second, scale, *rest = refs
-        *outs, held, sems, load_sem = rest
-        load = pltpu.make_async_copy(second, held, load_sem)
-        load.start()
+        first, second, scale, *outs, held, sems = refs
     else:
-        first, second, *rest = refs
-        *outs, sems = rest
+        first, second, *outs, sems = refs
     place, core = position()
     _, turn1 = halves_sent(place, core)
 
@@ -169,8 +165,7 @@
     for copy in early:
         copy.start()
     if scaled:
-        load.wait()
-        held[...] = held[...] * scale[...]
+        held[...] = second[...] * scale[...]
         late = copies_of(1, held)
     else:
         late = copies_of(1, second)
@@ -487,7 +482,7 @@
     run_copies(copies)
 
 
-def call(kernel, inputs, in_specs, outs, out_specs, scratch, flops=0, grant=26):
+def call(kernel, inputs, in_specs, outs, out_specs, scratch, flops=0):
     moved = sum(math.prod(value.shape) * value.dtype.itemsize for value in list(inputs) + list(outs))
     return pl.pallas_call(
         kernel,
@@ -496,7 +491,7 @@
         out_specs=out_specs,
         scratch_shapes=scratch,
         cost_estimate=pl.CostEstimate(flops=flops, bytes_accessed=moved, transcendentals=0),
-        compiler_params=pltpu.CompilerParams(vmem_limit_bytes=grant << 20),
+        compiler_params=pltpu.CompilerParams(vmem_limit_bytes=26 << 20),
     )(*inputs)
 
 
@@ -528,11 +523,10 @@
     packed = call(
         pack_weights_kernel,
         (fast_gate[0], fast_up[0], fast_down[0]),
-        [HBM] * 3,
+        [VMEM] * 3,
         [shape((3, rows, cols), F32)] * (ROUNDS + 2),
         [HBM] * (ROUNDS + 2),
         [dma((ROUNDS + 2, 3))],
-        grant=60,
     )
     packed = list(packed)
     packed[0], value_first = lax.optimization_barrier((packed[0], value_rows[0, 0]))
@@ -556,10 +550,10 @@
     def gather(first, second, scale):
         outs = [shape((2 * half, depth), F32)] * ROUNDS + [shape((4 * half, depth), F32)]
         scratch = [dma((CELL, 2))]
-        inputs, specs = [first, second], [HBM, HBM]
+        inputs, specs = [first, second], [VMEM, VMEM]
         if scale is not None:
             inputs, specs = inputs + [scale], specs + [VMEM]
-            scratch = [pltpu.VMEM((2 * half, depth), F32)] + scratch + [dma]
+            scratch = [pltpu.VMEM((2 * half, depth), F32)] + scratch
         packed = call(
             functools.partial(pack_rows_kernel, scale is not None, half),
             inputs,
@@ -567,14 +561,13 @@
             outs,
             [HBM] * CELL,
             scratch,
-            grant=60 if scale is not None else 26,
         )
         near = [lax.ppermute(packed[turn], PLACE, pairs[turn]) for turn in range(ROUNDS)]
-        near[0], local = lax.optimization_barrier((near[0], packed[ROUNDS]))
-        return near, [local, lax.ppermute(local, "head", SWAP)]
+        return near, packed[ROUNDS]
 
     def spread(near, local):
-        return near + [lax.ppermute(piece, "head", SWAP) for piece in near] + local
+        far = [lax.ppermute(piece, "head", SWAP) for piece in near]
+        return near + far + [local, lax.ppermute(local, "head", SWAP)]
 
     def combine(near, far):
         across = lax.ppermute(far, "head", SWAP)
@@ -605,7 +598,9 @@
         return found
 
     inner_near, inner_local = gather(key_rows[0, 0], value_first, -step[:, None])
-    inner_near[0], queries = lax.optimization_barrier((inner_near[0], query_rows[0, 0]))
+    inner_near[0], inner_local, queries = lax.optimization_barrier(
+        (inner_near[0], inner_local, query_rows[0, 0])
+    )
     read_near, read_local = gather(queries, read_cotangent[0, 0], None)
     inner_rows = spread(inner_near, inner_local)
 
@@ -633,7 +628,7 @@
     high, low = call(
         renew_kernel, (weights, steps), [VMEM] * 2, [narrow, narrow], [VMEM] * 2, []
     )
-    *read_near, high = lax.optimization_barrier((*read_near, high))
+    *read_near, read_local, high = lax.optimization_barrier((*read_near, read_local, high))
     read_rows = spread(list(read_near), read_local)
     piece = shape((half, depth), F32)
     read = call(
@@ -707,9 +702,8 @@
     far_last, given[0], *query_back = lax.optimization_barrier((far_last, given[0], *query_back))
     totals_last, local = combine(near_last, far_last)
     given[0], *totals_last = lax.optimization_barrier((given[0], *totals_last))
-    back += hand_back(totals_last, middle)
     (query_grad,) = settle(query_back, query_local)
-    key_grad, target_grad = settle(back, local)
+    given[0], query_grad = lax.optimization_barrier((given[0], query_grad))
 
     if cells > 1:
         given = [
@@ -719,6 +713,9 @@
     total = given[0][0]
     for shift in range(1, reps):
         total = total + lax.ppermute(given[shift][0], "rep", shifted(shift, 1))
+    total, *back = lax.optimization_barrier((total, *back))
+    back += hand_back(totals_last, middle)
+    key_grad, target_grad = settle(back, local)
     returned = [
         lax.ppermute(total[turn], PLACE, flipped(pairs[turn])) for turn in range(ROUNDS)
     ]

time: 234 us -> 171 us (0.73)
  Pallas kernels: 113 us -> 40.3 us
  local copies, waits for them, and re-layouts: 2.68 us -> 9.18 us
  waiting for transfers between devices: 68.4 us -> 73.9 us
  starting transfers between devices: 36.5 us -> 34.1 us
    pallas_call x11, Pallas kernels: 113 us -> 40.3 us  [call(): pl.pallas_call(kernel, out_shape=outs, in_specs=in_specs, out_specs=out_s...]
    ppermute x6, waiting for transfers between devices: 23.5 us -> 5.56 us  [gather(): lax.ppermute(packed[turn], PLACE, pairs[turn])]
    ppermute x3, waiting for transfers between devices: 7.57 us -> 20.5 us  [per_device(): lax.ppermute(packed[turn], PLACE, pairs[turn])]
    ppermute x1, waiting for transfers between devices: 0.01 us -> 10.8 us  [per_device(): parts.append(lax.ppermute(together, 'rep', shifted(shift, 1)))]
    unnamed x30, local copies, waits for them, and re-layouts: 1.67 us -> 8.25 us
    ppermute x6, starting transfers between devices: 10.9 us -> 7.69 us  [hand_back(): lax.ppermute(total, PLACE, flipped(pairs[first + number]))]
  transfers between devices with their start and end apart: 33 -> 33, of which waited for: 19 -> 18; matrix products, arithmetic and copies ran while one was open for 4% -> 5% of each run, Pallas kernels for 12% -> 16%
where the time goes in v5:
time: 171 us; the launch traced here: 170 us
  waiting for transfers between devices  73.9 us (43%)
  Pallas kernels  40.3 us (24%)
  starting transfers between devices  34.1 us (20%)
  other arithmetic  11.1 us (6%)
  local copies, waits for them, and re-layouts  9.18 us (5%)
    pallas_call x11, Pallas kernels, call(): pl.pallas_call(kernel, out_shape=outs, in_specs=in_specs, out_specs=out_s...  40.3 us
    ppermute x3, waiting for transfers between devices, per_device(): lax.ppermute(packed[turn], PLACE, pairs[turn])  20.5 us
    ppermute x6, waiting for transfers between devices, hand_back(): lax.ppermute(total, PLACE, flipped(pairs[first + number]))  12.7 us
    ppermute x1, waiting for transfers between devices, per_device(): total = total + lax.ppermute(given[shift][0], 'rep', shifted(shift, 1))  11.2 us
    ppermute x1, waiting for transfers between devices, per_device(): parts.append(lax.ppermute(together, 'rep', shifted(shift, 1)))  10.8 us
    unnamed x30, local copies, waits for them, and re-layouts  8.25 us
    ppermute x6, starting transfers between devices, hand_back(): lax.ppermute(total, PLACE, flipped(pairs[first + number]))  7.69 us
    ppermute x3, waiting for transfers between devices, per_device(): lax.ppermute(total[turn], PLACE, flipped(pairs[turn]))  7.42 us
  transfers between devices with their start and end apart: 33, of which 18 were waited for; matrix products, arithmetic and copies ran while one was open for 5% of the time, Pallas kernels for 16%

profile of v5, /device:TPU:22, one launch (start us, length us, event | category | flops | bytes accessed | tf_op | source)
XLA Modules:
  0.0 169.6 jit_solution(17161935059268547410)
XLA Ops:
  0.6 0.9 copy-done.6
  1.5 0.9 copy-done.7
  2.4 0.9 copy-done.8
  3.7 0.8 copy.20
  4.6 1.0 copy-done
  5.6 1.0 copy-done.2
  7.2 4.3 %collective-permute-start.5 = (f32[3,64,256]{2,1,0:T(8,128)S(1)}, f32[3,64,256]{2,1,0:T(8,128)S(1)}, u32[]{:S(2)}, u32[]{:S(2)}) collective-permute-start(f32[3,64,256]{2,1,0:T(8,128)S(1)} %get-tuple-element.87), channel_id=1, source_target_pairs={{8,4},{12,5},{1,8},{5,9},{0,0},{4,1},{9,12},{13,13},{10,6},{14,7},... | collective-permute-start | bytes 589832 | tf_op jit(solution)/shard_map/ppermute | solution.py:533
  11.5 1.4 collective-permute-start
  12.9 2.6 %collective-permute-start.9 = (f32[256,512]{1,0:T(8,128)S(1)}, f32[256,512]{1,0:T(8,128)S(1)}, u32[]{:S(2)}, u32[]{:S(2)}) collective-permute-start(f32[256,512]{1,0:T(8,128)S(1)} %get-tuple-element.92), channel_id=1, source_target_pairs={{8,4},{12,5},{1,8},{5,9},{0,0},{4,1},{9,12},{13,13},{10,6},{14,7},... | collective-permute-start | bytes 1572872 | tf_op jit(solution)/shard_map/ppermute | solution.py:565
  15.5 1.5 collective-permute-done.2.refs_2_.refs_0_
  17.0 4.4 %collective-permute-start.3 = (f32[512,512]{1,0:T(8,128)S(1)}, f32[512,512]{1,0:T(8,128)S(1)}, u32[]{:S(2)}, u32[]{:S(2)}) collective-permute-start(f32[512,512]{1,0:T(8,128)S(1)} %get-tuple-element.83.refs_8_.refs_2_), channel_id=1, source_target_pairs={{0,1},{1,0},{2,3},{3,2},{4,5},{5,4},{6,7},{7,6},{8,9},{9,8},{10,11... | collective-permute-start | bytes 3145736 | tf_op jit(solution)/shard_map/ppermute | solution.py:570
  21.4 0.9 collective-permute-start.6
  22.3 7.7 %collective-permute-done.5.second = f32[3,64,256]{2,1,0:T(8,128)S(1)} collective-permute-done((f32[3,64,256]{2,1,0:T(8,128)S(1)}, f32[3,64,256]{2,1,0:T(8,128)S(1)}, u32[]{:S(2)}, u32[]{:S(2)}) %collective-permute-start.5) | collective-permute-done | bytes 196640 | tf_op jit(solution)/shard_map/ppermute | solution.py:533
  30.0 12.7 %collective-permute-done.6.third = f32[3,64,256]{2,1,0:T(8,128)S(1)} collective-permute-done((f32[3,64,256]{2,1,0:T(8,128)S(1)}, f32[3,64,256]{2,1,0:T(8,128)S(1)}, u32[]{:S(2)}, u32[]{:S(2)}) %collective-permute-start.6) | collective-permute-done | bytes 196640 | tf_op jit(solution)/shard_map/ppermute | solution.py:533
  42.7 1.0 shard_map.137.refs_0_
  43.8 0.6 collective-permute-start.8
  44.4 0.5 collective-permute-start.1
  45.3 1.0 collective-permute-done.10.refs_5_.refs_2_
  46.3 0.7 collective-permute-done.1.refs_7_.refs_1_
  47.1 1.9 %collective-permute-start.13 = (f32[256,512]{1,0:T(8,128)S(1)}, f32[256,512]{1,0:T(8,128)S(1)}, u32[]{:S(2)}, u32[]{:S(2)}) collective-permute-start(f32[256,512]{1,0:T(8,128)S(1)} %get-tuple-element.97), channel_id=1, source_target_pairs={{8,4},{12,5},{1,8},{5,9},{0,0},{4,1},{9,12},{13,13},{10,6},{14,7},... | collective-permute-start | bytes 1572872 | tf_op jit(solution)/shard_map/ppermute | solution.py:565
  49.0 1.0 collective-permute-start.14
  50.0 10.8 %collective-permute-done.8.refs_1_ = f32[4,3,64,256]{3,2,1,0:T(8,128)S(1)} collective-permute-done((f32[4,3,64,256]{3,2,1,0:T(8,128)S(1)}, f32[4,3,64,256]{3,2,1,0:T(8,128)S(1)}, u32[]{:S(2)}, u32[]{:S(2)}) %collective-permute-start.8) | collective-permute-done | bytes 786464 | tf_op jit(solution)/shard_map/ppermute | solution.py:546
  60.8 7.8 %shard_map.138 = (f32[3,512,256]{2,1,0:T(8,128)S(1)}, f32[1024,256]{1,0:T(8,128)S(1)}, f32[1024,256]{1,0:T(8,128)S(1)}, f32[1024,256]{1,0:T(8,128)S(1)}, bf16[2,...) custom-call(f32[4,3,64,256]{3,2,1,0:T(8,128)S(1)} %shard_map.137.refs_0_, ...), custom_call_target="tpu_custom_call" | custom-call | flops 4831838208 | bytes 17301504 | tf_op jit(solution)/shard_map/pallas_call | solution.py:487
  68.6 0.6 shard_map.140
  69.2 2.4 %collective-permute-done.13.refs_1_ = f32[256,512]{1,0:T(8,128)S(1)} collective-permute-done((f32[256,512]{1,0:T(8,128)S(1)}, f32[256,512]{1,0:T(8,128)S(1)}, u32[]{:S(2)}, u32[]{:S(2)}) %collective-permute-start.13) | collective-permute-done | bytes 524320 | tf_op jit(solution)/shard_map/ppermute | solution.py:565
  71.6 1.7 collective-permute-done.14.refs_2_
  73.3 0.5 collective-permute-start.15
  73.8 0.5 collective-permute-start.17
  74.3 2.4 %collective-permute-done.15.refs_3_ = f32[256,512]{1,0:T(8,128)S(1)} collective-permute-done((f32[256,512]{1,0:T(8,128)S(1)}, f32[256,512]{1,0:T(8,128)S(1)}, u32[]{:S(2)}, u32[]{:S(2)}) %collective-permute-start.15) | collective-permute-done | bytes 524320 | tf_op jit(solution)/shard_map/ppermute | solution.py:569
  76.7 0.7 collective-permute-done.16.refs_4_
  77.4 0.7 collective-permute-done.17.refs_5_
  78.2 11.8 %shard_map.141 = (f32[3,512,256]{2,1,0:T(8,128)S(1)}, f32[128,512]{1,0:T(8,128)S(1)}, f32[128,512]{1,0:T(8,128)S(1)}, f32[128,512]{1,0:T(8,128)S(1)}, f32[640,512]{1,0:T(8,128)S(1)}) custom-call(f32[256,512]{1,0:T(8,128)S(1)} %collective-permute-done.12.refs_0_, f32[256,512]{1,0:T(8,128)S(1)} %collective-permute-done.13.refs_1_, ...), custom_call_target="tpu_custom_call" | custom-call | flops 6442450944 | bytes 10485760 | tf_op jit(solution)/shard_map/pallas_call | solution.py:487
  90.2 1.2 shard_map.142
  91.4 6.8 %shard_map.144 = (bf16[2,3,512,256]{3,2,1,0:T(8,128)(2,1)S(1)}, f32[256,512]{1,0:T(8,128)S(1)}, f32[256,512]{1,0:T(8,128)S(1)}, f32[512,512]{1,0:T(8,128)S(1)}) custom-call(f32[256,512]{1,0:T(8,128)S(1)} %collective-permute-done.2.refs_2_.refs_0_, f32[256,512]{1,0:T(8,128)S(1)} %collective-permute-done.9.refs_3_.refs_1_, ...), custom_call_target="tpu_custom_call" | custom-call | flops 3623878656 | bytes 12058624 | tf_op jit(solution)/shard_map/pallas_call | solution.py:487
  98.2 0.4 collective-permute-start.20
  98.8 0.9 copy-done.10
  99.7 6.7 %shard_map.143 = (bf16[2,3,512,256]{3,2,1,0:T(8,128)(2,1)S(1)}, f32[256,512]{1,0:T(8,128)S(1)}, f32[768,512]{1,0:T(8,128)S(1)}) custom-call(f32[256,512]{1,0:T(8,128)S(1)} %collective-permute-done.refs_4_.refs_0_, f32[256,512]{1,0:T(8,128)S(1)} %collective-permute-done.1.refs_7_.refs_1_, f32[512,512]{1,0:T(8,128)S(1)} %get-tuple-element.83.refs_8_.refs_2_, ...), custom_call_target="tpu_custom_call" | custom-call | flops 3623878656 | bytes 13107200 | tf_op jit(solution)/shard_map/pallas_call | solution.py:487
  106.5 2.8 %collective-permute-start.22 = (f32[128,512]{1,0:T(8,128)S(1)}, f32[128,512]{1,0:T(8,128)S(1)}, u32[]{:S(2)}, u32[]{:S(2)}) collective-permute-start(f32[128,512]{1,0:T(8,128)S(1)} %get-tuple-element.131), channel_id=1, source_target_pairs={{4,8},{5,12},{8,1},{9,5},{0,0},{1,4},{12,9},{13,13},{6,10},{7,14},... | collective-permute-start | bytes 786440 | tf_op jit(solution)/shard_map/ppermute | solution.py:583
  109.3 2.3 %collective-permute-start.23 = (f32[128,512]{1,0:T(8,128)S(1)}, f32[128,512]{1,0:T(8,128)S(1)}, u32[]{:S(2)}, u32[]{:S(2)}) collective-permute-start(f32[128,512]{1,0:T(8,128)S(1)} %get-tuple-element.132), channel_id=1, source_target_pairs={{4,12},{5,0},{8,5},{9,13},{0,1},{1,4},{12,8},{13,9},{6,14},{7,2},{... | collective-permute-start | bytes 786440 | tf_op jit(solution)/shard_map/ppermute | solution.py:583
  111.6 1.0 slice_add_fusion.3
  112.6 3.4 %shard_map.145 = (f32[1,4,3,64,256]{4,3,2,1,0:T(8,128)S(1)}, f32[1,4,3,64,256]{4,3,2,1,0:T(8,128)S(1)}) custom-call(bf16[2,2,512,1024]{3,2,1,0:T(8,128)(2,1)S(1)} %get-tuple-element.118.turned, f32[3,512,256]{2,1,0:T(8,128)S(1)} %get-tuple-element.119.direct, bf16[2,3,512,256]{3,2,1,0:T(8,128)(2,1)S(1)} %get-tuple-element.120.refs_0_, ...), custom_call_target="tpu_custom_call" | custom-call | flops 2415919104 | bytes 10485760 | tf_op jit(solution)/shard_map/pallas_call | solution.py:487
  116.0 0.9 copy-done.9
  116.9 0.7 collective-permute-done.22
  117.6 3.4 %collective-permute-done.23 = f32[128,512]{1,0:T(8,128)S(1)} collective-permute-done((f32[128,512]{1,0:T(8,128)S(1)}, f32[128,512]{1,0:T(8,128)S(1)}, u32[]{:S(2)}, u32[]{:S(2)}) %collective-permute-start.23) | collective-permute-done | bytes 262176 | tf_op jit(solution)/shard_map/ppermute | solution.py:583
  121.1 0.6 copy-done.13
  121.8 1.6 collective-permute-start.25
  123.7 2.1 %collective-permute-start.27 = (f32[256,512]{1,0:T(8,128)S(1)}, f32[256,512]{1,0:T(8,128)S(1)}, u32[]{:S(2)}, u32[]{:S(2)}) collective-permute-start(f32[256,512]{1,0:T(8,128)S(1)} %get-tuple-element.144), channel_id=1, source_target_pairs={{4,8},{5,12},{8,1},{9,5},{0,0},{1,4},{12,9},{13,13},{6,10},{7,14},... | collective-permute-start | bytes 1572872 | tf_op jit(solution)/shard_map/ppermute | solution.py:583
  125.8 1.2 select_select_fusion.3
  127.0 2.1 %fusion.1 = f32[256,512]{1,0:T(8,128)} fusion(f32[640,512]{1,0:T(8,128)} %copy-done.10, f32[128,512]{1,0:T(8,128)S(1)} %get-tuple-element.166, f32[128,512]{1,0:T(8,128)S(1)} %get-tuple-element.165, f32[640,512]{1,0:T(8,128)} %copy-done.5, pred[]{:T(512)S(6)} %eq.12), kind=kLoop, calls=%fused_computation.6 | loop fusion | flops 393216 | bytes 2097153 | tf_op jit(solution)/shard_map/jit(_where)/select_n | solution.py:597
  129.1 1.1 slice_add_fusion.2
  130.2 11.2 %collective-permute-done.25 = f32[4,3,64,256]{3,2,1,0:T(8,128)} collective-permute-done((f32[4,3,64,256]{3,2,1,0:T(8,128)}, f32[4,3,64,256]{3,2,1,0:T(8,128)}, u32[]{:S(2)}, u32[]{:S(2)}) %collective-permute-start.25) | collective-permute-done | bytes 786464 | tf_op jit(solution)/shard_map/ppermute | solution.py:715
  141.5 1.2 bitcast_add_fusion
  142.9 2.2 %collective-permute-start.30 = (f32[3,64,256]{2,1,0:T(8,128)S(1)}, f32[3,64,256]{2,1,0:T(8,128)S(1)}, u32[]{:S(2)}, u32[]{:S(2)}) collective-permute-start(f32[3,64,256]{2,1,0:T(8,128)S(1)} %get-tuple-element.164), channel_id=1, source_target_pairs={{4,0},{5,8},{8,13},{9,1},{0,4},{1,5},{12,9},{13,12},{6,2},{7,10},{... | collective-permute-start | bytes 589832 | tf_op jit(solution)/shard_map/ppermute | solution.py:720
  145.1 1.9 %collective-permute-start.31 = (f32[3,64,256]{2,1,0:T(8,128)S(1)}, f32[3,64,256]{2,1,0:T(8,128)S(1)}, u32[]{:S(2)}, u32[]{:S(2)}) collective-permute-start(f32[3,64,256]{2,1,0:T(8,128)S(1)} %get-tuple-element.163), channel_id=1, source_target_pairs={{4,8},{5,12},{8,1},{9,5},{0,0},{1,4},{12,9},{13,13},{6,10},{7,14},... | collective-permute-start | bytes 589832 | tf_op jit(solution)/shard_map/ppermute | solution.py:720
  147.0 1.2 collective-permute-start.32
  148.3 1.4 slice_add_fusion
  149.7 1.3 collective-permute-done.30
  151.1 2.6 %collective-permute-done.31 = f32[3,64,256]{2,1,0:T(8,128)S(1)} collective-permute-done((f32[3,64,256]{2,1,0:T(8,128)S(1)}, f32[3,64,256]{2,1,0:T(8,128)S(1)}, u32[]{:S(2)}, u32[]{:S(2)}) %collective-permute-start.31) | collective-permute-done | bytes 196640 | tf_op jit(solution)/shard_map/ppermute | solution.py:720
  153.6 3.5 %collective-permute-done.32 = f32[3,64,256]{2,1,0:T(8,128)S(1)} collective-permute-done((f32[3,64,256]{2,1,0:T(8,128)S(1)}, f32[3,64,256]{2,1,0:T(8,128)S(1)}, u32[]{:S(2)}, u32[]{:S(2)}) %collective-permute-start.32) | collective-permute-done | bytes 196640 | tf_op jit(solution)/shard_map/ppermute | solution.py:720
  157.2 0.8 pad_maximum_fusion
  158.0 8.6 %collective-permute-done.28 = f32[256,512]{1,0:T(8,128)S(1)} collective-permute-done((f32[256,512]{1,0:T(8,128)S(1)}, f32[256,512]{1,0:T(8,128)S(1)}, u32[]{:S(2)}, u32[]{:S(2)}) %collective-permute-start.28) | collective-permute-done | bytes 524320 | tf_op jit(solution)/shard_map/ppermute | solution.py:583
  166.9 1.0 copy-done.1
  167.8 1.2 multiply_reduce_fusion
  169.0 0.6 divide_multiply_fusion
  (61 shorter events, 2.7 us)
Async XLA Ops:
  0.6 0.9 copy-start.6
  1.5 0.9 copy-start.7
  2.4 0.9 copy-start.8
  4.6 1.0 copy-start
  5.6 1.0 copy-start.2
  6.7 38.3 %copy-start.3 = (f32[1,1,256,512]{3,2,1,0:T(8,128)S(1)}, f32[1,1,256,512]{3,2,1,0:T(8,128)}, u32[]{:S(2)}) copy-start(f32[1,1,256,512]{3,2,1,0:T(8,128)} %param.8) | copy-start | bytes 1572868
  6.7 38.3 %copy-start.4 = (f32[1,1,256,512]{3,2,1,0:T(8,128)S(1)}, f32[1,1,256,512]{3,2,1,0:T(8,128)}, u32[]{:S(2)}) copy-start(f32[1,1,256,512]{3,2,1,0:T(8,128)} %param.12) | copy-start | bytes 1572868
  7.1 10.0 %collective-permute-start.2 = (f32[256,512]{1,0:T(8,128)S(1)}, f32[256,512]{1,0:T(8,128)S(1)}, u32[]{:S(2)}, u32[]{:S(2)}) collective-permute-start(f32[256,512]{1,0:T(8,128)S(1)} %get-tuple-element.81), channel_id=1, source_target_pairs={{0,4},{8,5},{13,8},{1,9},{4,0},{5,1},{9,12},{12,13},{2,6},{10,7},{... | collective-permute-start | bytes 1572872 | tf_op jit(solution)/shard_map/ppermute | solution.py:565
  7.1 14.3 %collective-permute-start.4 = (f32[3,64,256]{2,1,0:T(8,128)S(1)}, f32[3,64,256]{2,1,0:T(8,128)S(1)}, u32[]{:S(2)}, u32[]{:S(2)}) collective-permute-start(f32[3,64,256]{2,1,0:T(8,128)S(1)} %get-tuple-element.84), channel_id=1, source_target_pairs={{0,4},{8,5},{13,8},{1,9},{4,0},{5,1},{9,12},{12,13},{2,6},{10,7},{... | collective-permute-start | bytes 589832 | tf_op jit(solution)/shard_map/ppermute | solution.py:533
  7.2 22.8 %collective-permute-start.5 = (f32[3,64,256]{2,1,0:T(8,128)S(1)}, f32[3,64,256]{2,1,0:T(8,128)S(1)}, u32[]{:S(2)}, u32[]{:S(2)}) collective-permute-start(f32[3,64,256]{2,1,0:T(8,128)S(1)} %get-tuple-element.87), channel_id=1, source_target_pairs={{8,4},{12,5},{1,8},{5,9},{0,0},{4,1},{9,12},{13,13},{10,6},{14,7},... | collective-permute-start | bytes 589832 | tf_op jit(solution)/shard_map/ppermute | solution.py:533
  11.5 32.9 %collective-permute-start = (f32[256,512]{1,0:T(8,128)S(1)}, f32[256,512]{1,0:T(8,128)S(1)}, u32[]{:S(2)}, u32[]{:S(2)}) collective-permute-start(f32[256,512]{1,0:T(8,128)S(1)} %get-tuple-element.80), channel_id=1, source_target_pairs={{12,4},{0,5},{5,8},{13,9},{1,0},{4,1},{8,12},{9,13},{14,6},{2,7},{... | collective-permute-start | bytes 1572872 | tf_op jit(solution)/shard_map/ppermute | solution.py:565
  12.9 32.0 %collective-permute-start.9 = (f32[256,512]{1,0:T(8,128)S(1)}, f32[256,512]{1,0:T(8,128)S(1)}, u32[]{:S(2)}, u32[]{:S(2)}) collective-permute-start(f32[256,512]{1,0:T(8,128)S(1)} %get-tuple-element.92), channel_id=1, source_target_pairs={{8,4},{12,5},{1,8},{5,9},{0,0},{4,1},{9,12},{13,13},{10,6},{14,7},... | collective-permute-start | bytes 1572872 | tf_op jit(solution)/shard_map/ppermute | solution.py:565
  17.0 43.8 %collective-permute-start.3 = (f32[512,512]{1,0:T(8,128)S(1)}, f32[512,512]{1,0:T(8,128)S(1)}, u32[]{:S(2)}, u32[]{:S(2)}) collective-permute-start(f32[512,512]{1,0:T(8,128)S(1)} %get-tuple-element.83.refs_8_.refs_2_), channel_id=1, source_target_pairs={{0,1},{1,0},{2,3},{3,2},{4,5},{5,4},{6,7},{7,6},{8,9},{9,8},{10,11... | collective-permute-start | bytes 3145736 | tf_op jit(solution)/shard_map/ppermute | solution.py:570
  21.4 21.4 %collective-permute-start.6 = (f32[3,64,256]{2,1,0:T(8,128)S(1)}, f32[3,64,256]{2,1,0:T(8,128)S(1)}, u32[]{:S(2)}, u32[]{:S(2)}) collective-permute-start(f32[3,64,256]{2,1,0:T(8,128)S(1)} %get-tuple-element.88), channel_id=1, source_target_pairs={{12,4},{0,5},{5,8},{13,9},{1,0},{4,1},{8,12},{9,13},{14,6},{2,7},{... | collective-permute-start | bytes 589832 | tf_op jit(solution)/shard_map/ppermute | solution.py:533
  30.0 12.8 %collective-permute-start.7 = (f32[3,64,256]{2,1,0:T(8,128)S(1)}, f32[3,64,256]{2,1,0:T(8,128)S(1)}, u32[]{:S(2)}, u32[]{:S(2)}) collective-permute-start(f32[3,64,256]{2,1,0:T(8,128)S(1)} %get-tuple-element.90), channel_id=1, source_target_pairs={{0,1},{1,0},{2,3},{3,2},{4,5},{5,4},{6,7},{7,6},{8,9},{9,8},{10,11... | collective-permute-start | bytes 589832 | tf_op jit(solution)/shard_map/ppermute | solution.py:535
  43.8 17.0 %collective-permute-start.8 = (f32[4,3,64,256]{3,2,1,0:T(8,128)S(1)}, f32[4,3,64,256]{3,2,1,0:T(8,128)S(1)}, u32[]{:S(2)}, u32[]{:S(2)}) collective-permute-start(f32[4,3,64,256]{3,2,1,0:T(8,128)S(1)} %shard_map.137.refs_0_), channel_id=1, source_target_pairs={{0,2},{2,0},{1,3},{3,1},{4,6},{6,4},{5,7},{7,5},{8,10},{10,8},{9,1... | collective-permute-start | bytes 2359304 | tf_op jit(solution)/shard_map/ppermute | solution.py:546
  44.4 1.9 %collective-permute-start.10 = (f32[256,512]{1,0:T(8,128)S(1)}, f32[256,512]{1,0:T(8,128)S(1)}, u32[]{:S(2)}, u32[]{:S(2)}) collective-permute-start(f32[256,512]{1,0:T(8,128)S(1)} %collective-permute-done.2.refs_2_.refs_0_), channel_id=1, source_target_pairs={{0,1},{1,0},{2,3},{3,2},{4,5},{5,4},{6,7},{7,6},{8,9},{9,8},{10,11... | collective-permute-start | bytes 1572872 | tf_op jit(solution)/shard_map/ppermute | solution.py:569
  44.4 2.7 %collective-permute-start.1 = (f32[256,512]{1,0:T(8,128)S(1)}, f32[256,512]{1,0:T(8,128)S(1)}, u32[]{:S(2)}, u32[]{:S(2)}) collective-permute-start(f32[256,512]{1,0:T(8,128)S(1)} %collective-permute-done.refs_4_.refs_0_), channel_id=1, source_target_pairs={{0,1},{1,0},{2,3},{3,2},{4,5},{5,4},{6,7},{7,6},{8,9},{9,8},{10,11... | collective-permute-start | bytes 1572872 | tf_op jit(solution)/shard_map/ppermute | solution.py:569
  44.9 4.1 %collective-permute-start.11 = (f32[256,512]{1,0:T(8,128)S(1)}, f32[256,512]{1,0:T(8,128)S(1)}, u32[]{:S(2)}, u32[]{:S(2)}) collective-permute-start(f32[256,512]{1,0:T(8,128)S(1)} %collective-permute-done.9.refs_3_.refs_1_), channel_id=1, source_target_pairs={{0,1},{1,0},{2,3},{3,2},{4,5},{5,4},{6,7},{7,6},{8,9},{9,8},{10,11... | collective-permute-start | bytes 1572872 | tf_op jit(solution)/shard_map/ppermute | solution.py:569
  46.3 22.9 %collective-permute-start.12 = (f32[256,512]{1,0:T(8,128)S(1)}, f32[256,512]{1,0:T(8,128)S(1)}, u32[]{:S(2)}, u32[]{:S(2)}) collective-permute-start(f32[256,512]{1,0:T(8,128)S(1)} %get-tuple-element.96), channel_id=1, source_target_pairs={{0,4},{8,5},{13,8},{1,9},{4,0},{5,1},{9,12},{12,13},{2,6},{10,7},{... | collective-permute-start | bytes 1572872 | tf_op jit(solution)/shard_map/ppermute | solution.py:565
  47.1 24.6 %collective-permute-start.13 = (f32[256,512]{1,0:T(8,128)S(1)}, f32[256,512]{1,0:T(8,128)S(1)}, u32[]{:S(2)}, u32[]{:S(2)}) collective-permute-start(f32[256,512]{1,0:T(8,128)S(1)} %get-tuple-element.97), channel_id=1, source_target_pairs={{8,4},{12,5},{1,8},{5,9},{0,0},{4,1},{9,12},{13,13},{10,6},{14,7},... | collective-permute-start | bytes 1572872 | tf_op jit(solution)/shard_map/ppermute | solution.py:565
  49.0 24.3 %collective-permute-start.14 = (f32[256,512]{1,0:T(8,128)S(1)}, f32[256,512]{1,0:T(8,128)S(1)}, u32[]{:S(2)}, u32[]{:S(2)}) collective-permute-start(f32[256,512]{1,0:T(8,128)S(1)} %get-tuple-element.98), channel_id=1, source_target_pairs={{12,4},{0,5},{5,8},{13,9},{1,0},{4,1},{8,12},{9,13},{14,6},{2,7},{... | collective-permute-start | bytes 1572872 | tf_op jit(solution)/shard_map/ppermute | solution.py:565
  73.3 4.9 %collective-permute-start.18 = (f32[512,512]{1,0:T(8,128)S(1)}, f32[512,512]{1,0:T(8,128)S(1)}, u32[]{:S(2)}, u32[]{:S(2)}) collective-permute-start(f32[512,512]{1,0:T(8,128)S(1)} %get-tuple-element.104.refs_6_), channel_id=1, source_target_pairs={{0,1},{1,0},{2,3},{3,2},{4,5},{5,4},{6,7},{7,6},{8,9},{9,8},{10,11... | collective-permute-start | bytes 3145736 | tf_op jit(solution)/shard_map/ppermute | solution.py:570
  73.3 3.4 %collective-permute-start.15 = (f32[256,512]{1,0:T(8,128)S(1)}, f32[256,512]{1,0:T(8,128)S(1)}, u32[]{:S(2)}, u32[]{:S(2)}) collective-permute-start(f32[256,512]{1,0:T(8,128)S(1)} %collective-permute-done.12.refs_0_), channel_id=1, source_target_pairs={{0,1},{1,0},{2,3},{3,2},{4,5},{5,4},{6,7},{7,6},{8,9},{9,8},{10,11... | collective-permute-start | bytes 1572872 | tf_op jit(solution)/shard_map/ppermute | solution.py:569
  73.8 3.6 %collective-permute-start.16 = (f32[256,512]{1,0:T(8,128)S(1)}, f32[256,512]{1,0:T(8,128)S(1)}, u32[]{:S(2)}, u32[]{:S(2)}) collective-permute-start(f32[256,512]{1,0:T(8,128)S(1)} %collective-permute-done.13.refs_1_), channel_id=1, source_target_pairs={{0,1},{1,0},{2,3},{3,2},{4,5},{5,4},{6,7},{7,6},{8,9},{9,8},{10,11... | collective-permute-start | bytes 1572872 | tf_op jit(solution)/shard_map/ppermute | solution.py:569
  73.8 4.4 %collective-permute-start.17 = (f32[256,512]{1,0:T(8,128)S(1)}, f32[256,512]{1,0:T(8,128)S(1)}, u32[]{:S(2)}, u32[]{:S(2)}) collective-permute-start(f32[256,512]{1,0:T(8,128)S(1)} %collective-permute-done.14.refs_2_), channel_id=1, source_target_pairs={{0,1},{1,0},{2,3},{3,2},{4,5},{5,4},{6,7},{7,6},{8,9},{9,8},{10,11... | collective-permute-start | bytes 1572872 | tf_op jit(solution)/shard_map/ppermute | solution.py:569
  90.0 1.4 copy-start.5
  90.0 8.6 %collective-permute-start.19 = (f32[640,512]{1,0:T(8,128)S(1)}, f32[640,512]{1,0:T(8,128)S(1)}, u32[]{:S(2)}, u32[]{:S(2)}) collective-permute-start(f32[640,512]{1,0:T(8,128)S(1)} %get-tuple-element.110), channel_id=1, source_target_pairs={{0,1},{1,0},{2,3},{3,2},{4,5},{5,4},{6,7},{7,6},{8,9},{9,8},{10,11... | collective-permute-start | bytes 3932168 | tf_op jit(solution)/shard_map/ppermute | solution.py:573
  98.2 13.5 %collective-permute-start.20 = (f32[512,512]{1,0:T(8,128)S(1)}, f32[512,512]{1,0:T(8,128)S(1)}, u32[]{:S(2)}, u32[]{:S(2)}) collective-permute-start(f32[512,512]{1,0:T(8,128)S(1)} %get-tuple-element.126), channel_id=1, source_target_pairs={{0,1},{1,0},{2,3},{3,2},{4,5},{5,4},{6,7},{7,6},{8,9},{9,8},{10,11... | collective-permute-start | bytes 3145736 | tf_op jit(solution)/shard_map/ppermute | solution.py:573
  98.6 1.1 copy-start.10
  106.4 10.5 %collective-permute-start.21 = (f32[128,512]{1,0:T(8,128)S(1)}, f32[128,512]{1,0:T(8,128)S(1)}, u32[]{:S(2)}, u32[]{:S(2)}) collective-permute-start(f32[128,512]{1,0:T(8,128)S(1)} %get-tuple-element.130), channel_id=1, source_target_pairs={{4,0},{5,8},{8,13},{9,1},{0,4},{1,5},{12,9},{13,12},{6,2},{7,10},{... | collective-permute-start | bytes 786440 | tf_op jit(solution)/shard_map/ppermute | solution.py:583
  106.5 11.1 %collective-permute-start.22 = (f32[128,512]{1,0:T(8,128)S(1)}, f32[128,512]{1,0:T(8,128)S(1)}, u32[]{:S(2)}, u32[]{:S(2)}) collective-permute-start(f32[128,512]{1,0:T(8,128)S(1)} %get-tuple-element.131), channel_id=1, source_target_pairs={{4,8},{5,12},{8,1},{9,5},{0,0},{1,4},{12,9},{13,13},{6,10},{7,14},... | collective-permute-start | bytes 786440 | tf_op jit(solution)/shard_map/ppermute | solution.py:583
  109.3 11.8 %collective-permute-start.23 = (f32[128,512]{1,0:T(8,128)S(1)}, f32[128,512]{1,0:T(8,128)S(1)}, u32[]{:S(2)}, u32[]{:S(2)}) collective-permute-start(f32[128,512]{1,0:T(8,128)S(1)} %get-tuple-element.132), channel_id=1, source_target_pairs={{4,12},{5,0},{8,5},{9,13},{0,1},{1,4},{12,8},{13,9},{6,14},{7,2},{... | collective-permute-start | bytes 786440 | tf_op jit(solution)/shard_map/ppermute | solution.py:583
  112.6 9.1 %copy-start.14 = (f32[1,1,256]{2,1,0:T(1,128)S(1)}, f32[1,1,256]{2,1,0:T(1,128)}, u32[]{:S(2)}) copy-start(f32[1,1,256]{2,1,0:T(1,128)} %param.11) | copy-start | bytes 3076
  116.0 0.9 copy-start.9
  116.9 4.1 %copy-start.11 = (f32[128,512]{1,0:T(8,128)}, f32[128,512]{1,0:T(8,128)S(1)}, u32[]{:S(2)}) copy-start(f32[128,512]{1,0:T(8,128)S(1)} %collective-permute-done.21) | copy-start | bytes 786436
  117.6 3.4 %copy-start.12 = (f32[128,512]{1,0:T(8,128)}, f32[128,512]{1,0:T(8,128)S(1)}, u32[]{:S(2)}) copy-start(f32[128,512]{1,0:T(8,128)S(1)} %collective-permute-done.22) | copy-start | bytes 786436
  121.0 0.7 copy-start.13
  121.0 8.1 %collective-permute-start.24 = (f32[768,512]{1,0:T(8,128)S(1)}, f32[768,512]{1,0:T(8,128)}, u32[]{:S(2)}, u32[]{:S(2)}) collective-permute-start(f32[768,512]{1,0:T(8,128)S(1)} %get-tuple-element.135), channel_id=1, source_target_pairs={{0,1},{1,0},{2,3},{3,2},{4,5},{5,4},{6,7},{7,6},{8,9},{9,8},{10,11... | collective-permute-start | bytes 4718600 | tf_op jit(solution)/shard_map/ppermute | solution.py:573
  121.8 19.7 %collective-permute-start.25 = (f32[4,3,64,256]{3,2,1,0:T(8,128)}, f32[4,3,64,256]{3,2,1,0:T(8,128)}, u32[]{:S(2)}, u32[]{:S(2)}) collective-permute-start(f32[4,3,64,256]{3,2,1,0:T(8,128)} %bitcast.38), channel_id=1, source_target_pairs={{0,2},{2,0},{1,3},{3,1},{4,6},{6,4},{5,7},{7,5},{8,10},{10,8},{9,1... | collective-permute-start | bytes 2359304 | tf_op jit(solution)/shard_map/ppermute | solution.py:715
  123.3 19.4 %collective-permute-start.26 = (f32[256,512]{1,0:T(8,128)}, f32[256,512]{1,0:T(8,128)S(1)}, u32[]{:S(2)}, u32[]{:S(2)}) collective-permute-start(f32[256,512]{1,0:T(8,128)} %get-tuple-element.143), channel_id=1, source_target_pairs={{4,0},{5,8},{8,13},{9,1},{0,4},{1,5},{12,9},{13,12},{6,2},{7,10},{... | collective-permute-start | bytes 1572872 | tf_op jit(solution)/shard_map/ppermute | solution.py:583
  123.7 19.1 %collective-permute-start.27 = (f32[256,512]{1,0:T(8,128)S(1)}, f32[256,512]{1,0:T(8,128)S(1)}, u32[]{:S(2)}, u32[]{:S(2)}) collective-permute-start(f32[256,512]{1,0:T(8,128)S(1)} %get-tuple-element.144), channel_id=1, source_target_pairs={{4,8},{5,12},{8,1},{9,5},{0,0},{1,4},{12,9},{13,13},{6,10},{7,14},... | collective-permute-start | bytes 1572872 | tf_op jit(solution)/shard_map/ppermute | solution.py:583
  142.8 6.9 %collective-permute-start.29 = (f32[3,64,256]{2,1,0:T(8,128)S(1)}, f32[3,64,256]{2,1,0:T(8,128)S(1)}, u32[]{:S(2)}, u32[]{:S(2)}) collective-permute-start(f32[3,64,256]{2,1,0:T(8,128)S(1)} %get-tuple-element.161), channel_id=1, source_target_pairs={{0,1},{1,0},{2,3},{3,2},{4,5},{5,4},{6,7},{7,6},{8,9},{9,8},{10,11... | collective-permute-start | bytes 589832 | tf_op jit(solution)/shard_map/ppermute | solution.py:723
  142.9 8.2 %collective-permute-start.30 = (f32[3,64,256]{2,1,0:T(8,128)S(1)}, f32[3,64,256]{2,1,0:T(8,128)S(1)}, u32[]{:S(2)}, u32[]{:S(2)}) collective-permute-start(f32[3,64,256]{2,1,0:T(8,128)S(1)} %get-tuple-element.164), channel_id=1, source_target_pairs={{4,0},{5,8},{8,13},{9,1},{0,4},{1,5},{12,9},{13,12},{6,2},{7,10},{... | collective-permute-start | bytes 589832 | tf_op jit(solution)/shard_map/ppermute | solution.py:720
  145.1 8.5 %collective-permute-start.31 = (f32[3,64,256]{2,1,0:T(8,128)S(1)}, f32[3,64,256]{2,1,0:T(8,128)S(1)}, u32[]{:S(2)}, u32[]{:S(2)}) collective-permute-start(f32[3,64,256]{2,1,0:T(8,128)S(1)} %get-tuple-element.163), channel_id=1, source_target_pairs={{4,8},{5,12},{8,1},{9,5},{0,0},{1,4},{12,9},{13,13},{6,10},{7,14},... | collective-permute-start | bytes 589832 | tf_op jit(solution)/shard_map/ppermute | solution.py:720
  147.0 10.1 %collective-permute-start.32 = (f32[3,64,256]{2,1,0:T(8,128)S(1)}, f32[3,64,256]{2,1,0:T(8,128)S(1)}, u32[]{:S(2)}, u32[]{:S(2)}) collective-permute-start(f32[3,64,256]{2,1,0:T(8,128)S(1)} %get-tuple-element.162), channel_id=1, source_target_pairs={{4,12},{5,0},{8,5},{9,13},{0,1},{1,4},{12,8},{13,9},{6,14},{7,2},{... | collective-permute-start | bytes 589832 | tf_op jit(solution)/shard_map/ppermute | solution.py:720
  148.2 18.4 %collective-permute-start.28 = (f32[256,512]{1,0:T(8,128)S(1)}, f32[256,512]{1,0:T(8,128)S(1)}, u32[]{:S(2)}, u32[]{:S(2)}) collective-permute-start(f32[256,512]{1,0:T(8,128)S(1)} %slice_add_fusion.2), channel_id=1, source_target_pairs={{4,12},{5,0},{8,5},{9,13},{0,1},{1,4},{12,8},{13,9},{6,14},{7,2},{... | collective-permute-start | bytes 1572872 | tf_op jit(solution)/shard_map/ppermute | solution.py:583
  166.8 1.0 copy-start.1

commit v6 on v5

--- a/solution.py
+++ b/solution.py
@@ -91,53 +91,20 @@
         copy.wait()
 
 
-def pack_weights_kernel(gate, up, down, *rest):
-    outs, sems = rest[:-1], rest[-1]
-    place, core = position()
-    _, turn1 = halves_sent(place, core)
-    cols = outs[0].shape[2]
-    copies = []
-    for piece, out in enumerate(outs):
-        if piece < ROUNDS:
-            part = jnp.where(turn1 == piece, 1, 0)
-        else:
-            part = core if piece == ROUNDS else 1 - core
-        begin = pl.multiple_of(part * cols, cols)
-        for which, ref in enumerate((gate, up, down)):
-            copies.append(
-                pltpu.make_async_copy(
-                    ref.at[:, pl.ds(begin, cols)], out.at[which], sems.at[piece, which]
-                )
-            )
-    run_copies(copies)
-
-
-def collect_kernel(first, second, third, own, got, out, sems):
-    place, core = position()
-    mine = core == place - home_of(0)
-    copies = [
-        pltpu.make_async_copy(piece, out.at[slot], sems.at[slot])
-        for slot, piece in enumerate((first, second, third))
-    ]
-    for copy in copies:
-        copy.start()
-
-    @pl.when(mine)
-    def _():
-        pltpu.make_async_copy(own, out.at[ROUNDS], sems.at[ROUNDS]).start()
-
-    @pl.when(jnp.logical_not(mine))
-    def _():
-        pltpu.make_async_copy(got, out.at[ROUNDS], sems.at[ROUNDS]).start()
-
-    for copy in copies:
-        copy.wait()
-    pltpu.make_async_copy(own, out.at[ROUNDS], sems.at[ROUNDS]).wait()
-
-
-def pack_rows_kernel(scaled, half, *refs):
-    if scaled:
-        first, second, scale, *outs, held, sems = refs
+def weight_rows(rows):
+    return rows * 3 // 2 if rows % 16 == 0 else rows * 2
+
+
+def weight_blocks(rows, cols):
+    blocks = [(0, 0, rows, 0, 0), (1, 0, rows, 0, cols)]
+    if rows % 16 == 0:
+        return blocks + [(2, 0, rows // 2, rows, 0), (2, rows // 2, rows // 2, rows, cols)]
+    return blocks + [(2, 0, rows, rows, 0)]
+
+
+def pack_kernel(half, with_weights, *refs):
+    if with_weights:
+        first, second, scale, gate, up, down, *outs, held, sems, weight_sems = refs
     else:
         first, second, *outs, sems = refs
     place, core = position()
@@ -161,17 +128,34 @@
         )
         return copies
 
-    early = copies_of(0, first)
-    for copy in early:
+    copies = copies_of(0, first)
+    if with_weights:
+        rows, width = gate.shape
+        cols = width // 2
+        for piece, out in enumerate(outs):
+            if piece < ROUNDS:
+                part, top = jnp.where(turn1 == piece, 1, 0), 2 * half
+            elif piece == ROUNDS:
+                part, top = 1 - core, 4 * half
+            else:
+                part, top = core, 0
+            begin = pl.multiple_of(part * cols, cols)
+            for number, (which, start, size, row, col) in enumerate(weight_blocks(rows, cols)):
+                copies.append(
+                    pltpu.make_async_copy(
+                        (gate, up, down)[which].at[pl.ds(start, size), pl.ds(begin, cols)],
+                        out.at[pl.ds(top + row, size), pl.ds(col, cols)],
+                        weight_sems.at[piece, number],
+                    )
+                )
+    for copy in copies:
         copy.start()
-    if scaled:
+    if with_weights:
         held[...] = second[...] * scale[...]
-        late = copies_of(1, held)
-    else:
-        late = copies_of(1, second)
+    late = copies_of(1, held if with_weights else second)
     for copy in late:
         copy.start()
-    for copy in early + late:
+    for copy in copies + late:
         copy.wait()
 
 
@@ -254,16 +238,18 @@
     near, far, (own, got), refs = refs[:3], refs[3:6], refs[6:8], refs[8:]
     weights, gates, ups, backs, turned, steps, *scratch = refs
     keys, targets, wide, acts, row_sems, weight_sems = scratch
-    rows = parts[0].shape[-2]
-    starts = row_starts(cells, reps, rows)
+    rows, cols = weights.shape[1] // (cells * reps * CELL), weights.shape[2]
     copies = []
-    for number, ((cell, shift, slot), begin) in enumerate(starts.items()):
+    for (cell, shift, slot), begin in row_starts(cells, reps, rows).items():
         source = parts[shift].at[slot] if cells == 1 else parts[0].at[cell, shift, slot]
-        copies.append(
-            pltpu.make_async_copy(
-                source, weights.at[:, pl.ds(begin, rows)], weight_sems.at[number]
+        for which, start, size, row, col in weight_blocks(rows, cols):
+            copies.append(
+                pltpu.make_async_copy(
+                    source.at[pl.ds(row, size), pl.ds(col, cols)],
+                    weights.at[which, pl.ds(pl.multiple_of(begin + start, size), size)],
+                    weight_sems.at[len(copies)],
+                )
             )
-        )
     for copy in copies:
         copy.start()
     fetch_rows(near, far, own, got, (keys, targets), row_sems)
@@ -373,15 +359,49 @@
         store_split(cots, (which,), -moved_cot)
 
 
-def token_grad_kernel(first, last, *refs):
+def write_grads(cells, reps, turned, direct, parts, pieces, grads, grad_sems):
+    for which in range(3):
+        total = direct[which]
+        begin = 0
+        for acts in parts:
+            span = pl.ds(begin, acts.shape[2])
+            begin += acts.shape[2]
+            left = turned[0, which // 2, :, span], turned[1, which // 2, :, span]
+            total = total + dot3(left, pair_of(acts, which), NN)
+        grads[which] = total
+    rows = pieces[0].shape[-2]
+    copies = []
+    place, core = position()
+    rep = lax.axis_index("rep")
+    for cell in range(cells):
+        for shift in range(reps):
+            owner_rep = lax.rem(rep + shift, reps)
+            for slot in range(CELL):
+                spot = spot_of(place, core, slot)
+                begin = pl.multiple_of(((cell * CELL + spot) * reps + owner_rep) * rows, rows)
+                copies.append(
+                    pltpu.make_async_copy(
+                        grads.at[:, pl.ds(begin, rows)],
+                        pieces[shift].at[cell, slot],
+                        grad_sems.at[len(copies)],
+                    )
+                )
+    run_copies(copies)
+
+
+def token_grad_kernel(cells, reps, first, last, *refs):
     rounds = min(last, ROUNDS) - first
     near, far, refs = refs[:rounds], refs[rounds : 2 * rounds], refs[2 * rounds :]
-    own, got = None, None
-    if last > ROUNDS:
-        (own, got), refs = refs[:2], refs[2:]
+    own, got, final = None, None, last > ROUNDS
+    if final:
+        (own, got, turned, direct, before), refs = refs[:5], refs[5:]
     (weights, cots, gates, ups, backs), refs = refs[:5], refs[5:]
-    acts, near_out, far_out, scratch = refs[0], refs[1 : 1 + rounds], refs[1 + rounds], refs[2 + rounds :]
-    keys, targets, wide, sent, row_sems, out_sems = scratch
+    near_out, far_out, refs = refs[:rounds], refs[rounds], refs[rounds + 1 :]
+    if final:
+        pieces, (acts, grads, grad_sems), refs = refs[:reps], refs[reps : reps + 3], refs[reps + 3 :]
+    else:
+        acts, refs = refs[0], refs[1:]
+    keys, targets, wide, sent, row_sems, out_sems = refs
     fetch_rows(near, far, own, got, (keys, targets), row_sems)
     size = sent.shape[2]
     half = size // 2
@@ -446,40 +466,11 @@
                 for side, (source, out) in enumerate(outgoing(each)):
                     pltpu.make_async_copy(source, out, out_sems.at[each, side]).start()
 
+    if final:
+        write_grads(cells, reps, turned, direct, (before, acts), pieces, grads, grad_sems)
     for each in range(last - first):
         for side, (source, out) in enumerate(outgoing(each)):
             pltpu.make_async_copy(source, out, out_sems.at[each, side]).wait()
-
-
-def weight_grad_kernel(cells, reps, turned, direct, *refs):
-    parts, pieces, (grads, grad_sems) = refs[: -reps - 2], refs[-reps - 2 : -2], refs[-2:]
-    for which in range(3):
-        total = direct[which]
-        begin = 0
-        for acts in parts:
-            span = pl.ds(begin, acts.shape[2])
-            begin += acts.shape[2]
-            left = turned[0, which // 2, :, span], turned[1, which // 2, :, span]
-            total = total + dot3(left, pair_of(acts, which), NN)
-        grads[which] = total
-    rows = pieces[0].shape[-2]
-    copies = []
-    place, core = position()
-    rep = lax.axis_index("rep")
-    for cell in range(cells):
-        for shift in range(reps):
-            owner_rep = lax.rem(rep + shift, reps)
-            for slot in range(CELL):
-                spot = spot_of(place, core, slot)
-                begin = pl.multiple_of(((cell * CELL + spot) * reps + owner_rep) * rows, rows)
-                copies.append(
-                    pltpu.make_async_copy(
-                        grads.at[:, pl.ds(begin, rows)],
-                        pieces[shift].at[cell, slot],
-                        grad_sems.at[len(copies)],
-                    )
-                )
-    run_copies(copies)
 
 
 def call(kernel, inputs, in_specs, outs, out_specs, scratch, flops=0):
@@ -520,50 +511,27 @@
 
     step = jax.nn.softplus(step_logits[0, 0]) * factor
 
-    packed = call(
-        pack_weights_kernel,
-        (fast_gate[0], fast_up[0], fast_down[0]),
-        [VMEM] * 3,
-        [shape((3, rows, cols), F32)] * (ROUNDS + 2),
-        [HBM] * (ROUNDS + 2),
-        [dma((ROUNDS + 2, 3))],
-    )
-    packed = list(packed)
-    packed[0], value_first = lax.optimization_barrier((packed[0], value_rows[0, 0]))
-    slots = [lax.ppermute(packed[turn], PLACE, pairs[turn]) for turn in range(ROUNDS)]
-    slots[0], other = lax.optimization_barrier((slots[0], packed[ROUNDS + 1]))
-    other = lax.ppermute(other, "head", SWAP)
-    (together,) = call(
-        collect_kernel,
-        slots + [packed[ROUNDS], other],
-        [HBM] * 5,
-        [shape((CELL, 3, rows, cols), F32)],
-        [HBM],
-        [dma((CELL,))],
-    )
-    parts = [together]
-    for shift in range(1, reps):
-        parts.append(lax.ppermute(together, "rep", shifted(shift, 1)))
-    if cells > 1:
-        parts = [lax.all_gather(jnp.stack(parts), "tok", axis_index_groups=cell_groups)]
-
-    def gather(first, second, scale):
-        outs = [shape((2 * half, depth), F32)] * ROUNDS + [shape((4 * half, depth), F32)]
+    weight_count = weight_rows(rows)
+
+    def gather(first, second, *rest):
+        extra = weight_count if rest else 0
+        outs = [shape((2 * half + extra, depth), F32)] * ROUNDS
+        outs.append(shape((4 * half + extra, depth), F32))
         scratch = [dma((CELL, 2))]
-        inputs, specs = [first, second], [VMEM, VMEM]
-        if scale is not None:
-            inputs, specs = inputs + [scale], specs + [VMEM]
-            scratch = [pltpu.VMEM((2 * half, depth), F32)] + scratch
+        if rest:
+            outs.append(shape((extra, depth), F32))
+            scratch = [pltpu.VMEM((2 * half, depth), F32)] + scratch + [dma((CELL + 1, 4))]
+        inputs = [first, second, *rest]
         packed = call(
-            functools.partial(pack_rows_kernel, scale is not None, half),
+            functools.partial(pack_kernel, half, bool(rest)),
             inputs,
-            specs,
+            [VMEM] * len(inputs),
             outs,
-            [HBM] * CELL,
+            [HBM] * len(outs),
             scratch,
         )
         near = [lax.ppermute(packed[turn], PLACE, pairs[turn]) for turn in range(ROUNDS)]
-        return near, packed[ROUNDS]
+        return near, *packed[ROUNDS:]
 
     def spread(near, local):
         far = [lax.ppermute(piece, "head", SWAP) for piece in near]
@@ -597,12 +565,26 @@
             found.append(jnp.where(at_home, here, remote))
         return found
 
-    inner_near, inner_local = gather(key_rows[0, 0], value_first, -step[:, None])
-    inner_near[0], inner_local, queries = lax.optimization_barrier(
-        (inner_near[0], inner_local, query_rows[0, 0])
+    inner_near, inner_local, kept = gather(
+        key_rows[0, 0],
+        value_rows[0, 0],
+        -step[:, None],
+        fast_gate[0],
+        fast_up[0],
+        fast_down[0],
     )
-    read_near, read_local = gather(queries, read_cotangent[0, 0], None)
+    inner_near = list(lax.optimization_barrier(tuple(inner_near)))
     inner_rows = spread(inner_near, inner_local)
+    inner_rows[-1], queries = lax.optimization_barrier((inner_rows[-1], query_rows[0, 0]))
+    read_near, read_local = gather(queries, read_cotangent[0, 0])
+    slots = [piece[2 * half :] for piece in inner_near]
+    slots.append(jnp.where(core == place - home_of(0), kept, inner_rows[-1][4 * half :]))
+    together = jnp.stack(slots)
+    parts = [together]
+    for shift in range(1, reps):
+        parts.append(lax.ppermute(together, "rep", shifted(shift, 1)))
+    if cells > 1:
+        parts = [lax.all_gather(jnp.stack(parts), "tok", axis_index_groups=cell_groups)]
 
     size = 2 * half
     count = CELL * size
@@ -619,7 +601,7 @@
         [HBM] * (len(parts) + 8),
         [square, tall, tall, tall, shape((2, 2, depth, count), BF16), square],
         [VMEM] * 6,
-        buffers + [split_square, acts, dma((CELL, 4)), dma((cells * reps * CELL,))],
+        buffers + [split_square, acts, dma((CELL, 4)), dma((cells * reps * CELL * 4,))],
         6 * product,
     )
     if cells > 1:
@@ -654,56 +636,61 @@
     )
     middle = 2
 
-    def token_grads(first, last, cots):
+    def token_grads(first, last, cots, *more):
         rounds = min(last, ROUNDS) - first
         span = slice(first, first + rounds)
         inputs = inner_rows[:ROUNDS][span] + inner_rows[ROUNDS : 2 * ROUNDS][span]
-        if last > ROUNDS:
+        if more:
             inputs = inputs + inner_rows[2 * ROUNDS :]
         blocks = last - first
-        acts, *outs = call(
-            functools.partial(token_grad_kernel, first, last),
-            inputs + [weights, cots, gates, ups, backs],
-            [HBM] * len(inputs) + [VMEM] * 5,
-            [shape((2, 3, blocks * size, cols), BF16)]
-            + [shape((size, depth), F32)] * rounds
-            + [shape((size * (2 * blocks - rounds), depth), F32)],
-            [VMEM] + [HBM] * (rounds + 1),
-            [pltpu.VMEM((blocks, size, depth), F32)] * 2
+        specs = [HBM] * len(inputs) + [VMEM] * (len(more) + 5)
+        outs = [shape((size, depth), F32)] * rounds
+        outs.append(shape((size * (2 * blocks - rounds), depth), F32))
+        acts = (2, 3, blocks * size, cols)
+        if more:
+            outs += [shape((cells, CELL, 3, rows, cols), F32)] * reps
+            scratch = [
+                pltpu.VMEM(acts, BF16),
+                pltpu.VMEM((3, width, cols), F32),
+                dma((cells * reps * CELL,)),
+            ]
+            out_specs = [HBM] * len(outs)
+        else:
+            out_specs = [HBM] * len(outs) + [VMEM]
+            outs.append(shape(acts, BF16))
+            scratch = []
+        outs = call(
+            functools.partial(token_grad_kernel, cells, reps, first, last),
+            inputs + [*more, weights, cots, gates, ups, backs],
+            specs,
+            outs,
+            out_specs,
+            scratch
+            + [pltpu.VMEM((blocks, size, depth), F32)] * 2
             + [
                 split_square,
                 pltpu.VMEM((2, blocks, size, depth), F32),
                 dma((blocks, 4)),
                 dma((blocks, 4)),
             ],
-            9 * product * blocks // CELL,
+            9 * product * blocks // CELL + (3 * product if more else 0),
         )
-        return acts, outs[:rounds], outs[rounds]
-
-    acts_first, near_first, far_first = token_grads(0, middle, cots)
+        return outs[:rounds], outs[rounds], list(outs[rounds + 1 :])
+
+    near_first, far_first, (acts_first,) = token_grads(0, middle, cots)
     query_totals, query_local = combine(read[1:4], read[4])
     cots, *query_totals = lax.optimization_barrier((cots, *query_totals))
     query_back = hand_back(query_totals, 0)
-    acts_last, near_last, far_last = token_grads(middle, CELL, cots)
-    acts_last, *near_first = lax.optimization_barrier((acts_last, *near_first))
+    near_last, far_last, given = token_grads(middle, CELL, cots, key_turned, direct, acts_first)
+    far_last, *rest = lax.optimization_barrier((far_last, *near_first, *query_back))
+    near_first, query_back = rest[:-ROUNDS], rest[-ROUNDS:]
     totals_first, _ = combine(near_first, far_first)
-    acts_last, *totals_first = lax.optimization_barrier((acts_last, *totals_first))
     back = hand_back(totals_first, 0)
-    given = call(
-        functools.partial(weight_grad_kernel, cells, reps),
-        [key_turned, direct, acts_first, acts_last],
-        [VMEM] * 4,
-        [shape((cells, CELL, 3, rows, cols), F32)] * reps,
-        [HBM] * reps,
-        [pltpu.VMEM((3, width, cols), F32), dma((cells * reps * CELL,))],
-        3 * product,
-    )
-    given = list(given)
-    far_last, given[0], *query_back = lax.optimization_barrier((far_last, given[0], *query_back))
     totals_last, local = combine(near_last, far_last)
-    given[0], *totals_last = lax.optimization_barrier((given[0], *totals_last))
+    back += hand_back(totals_last, middle)
+    given[0], *back = lax.optimization_barrier((given[0], *back))
     (query_grad,) = settle(query_back, query_local)
-    given[0], query_grad = lax.optimization_barrier((given[0], query_grad))
+    key_grad, target_grad = settle(back, local)
 
     if cells > 1:
         given = [
@@ -713,9 +700,6 @@
     total = given[0][0]
     for shift in range(1, reps):
         total = total + lax.ppermute(given[shift][0], "rep", shifted(shift, 1))
-    total, *back = lax.optimization_barrier((total, *back))
-    back += hand_back(totals_last, middle)
-    key_grad, target_grad = settle(back, local)
     returned = [
         lax.ppermute(total[turn], PLACE, flipped(pairs[turn])) for turn in range(ROUNDS)
     ]

time: 171 us -> 162 us (0.947)
  starting transfers between devices: 34.1 us -> 27.1 us
  waiting for transfers between devices: 73.9 us -> 71.6 us
    ppermute x6, waiting for transfers between devices: 5.56 us -> 32.1 us  [gather(): lax.ppermute(packed[turn], PLACE, pairs[turn])]
    ppermute x4 -> x0, waiting for transfers between devices: 20.5 us -> none  [the longest x3 20.5 us: per_device(): lax.ppermute(packed[turn], PLACE, pairs[turn])]
    ppermute x1, waiting for transfers between devices: 11.2 us -> 0.01 us  [per_device(): total = total + lax.ppermute(given[shift][0], 'rep', shifted(shift, 1))]
    ppermute x4 -> x0, starting transfers between devices: 5.23 us -> none  [the longest x3 5.23 us: per_device(): lax.ppermute(packed[turn], PLACE, pairs[turn])]
    ppermute x1, waiting for transfers between devices: 10.8 us -> 15.5 us  [per_device(): parts.append(lax.ppermute(together, 'rep', shifted(shift, 1)))]
    ppermute x2, starting transfers between devices: 4.37 us -> 0.07 us  [spread(): return near + far + [local, lax.ppermute(local, 'head', SWAP)]]
    ppermute x3, waiting for transfers between devices: 7.42 us -> 3.92 us  [per_device(): lax.ppermute(total[turn], PLACE, flipped(pairs[turn]))]
    ppermute x6, waiting for transfers between devices: 12.7 us -> 16.1 us  [hand_back(): lax.ppermute(total, PLACE, flipped(pairs[first + number]))]
  transfers between devices with their start and end apart: 33 -> 29, of which waited for: 18 -> 13; matrix products, arithmetic and copies ran while one was open for 5% -> 6% of each run, Pallas kernels for 16% -> 17%
where the time goes in v6:
time: 162 us; the launch traced here: 160 us
  waiting for transfers between devices  71.6 us (44%)
  Pallas kernels  41 us (25%)
  starting transfers between devices  27.1 us (17%)
  other arithmetic  10.5 us (6%)
  local copies, waits for them, and re-layouts  8.53 us (5%)
    pallas_call x8, Pallas kernels, call(): pl.pallas_call(kernel, out_shape=outs, in_specs=in_specs, out_specs=out_s...  41 us
    ppermute x6, waiting for transfers between devices, gather(): lax.ppermute(packed[turn], PLACE, pairs[turn])  32.1 us
    ppermute x6, waiting for transfers between devices, hand_back(): lax.ppermute(total, PLACE, flipped(pairs[first + number]))  16.1 us
    ppermute x1, waiting for transfers between devices, per_device(): parts.append(lax.ppermute(together, 'rep', shifted(shift, 1)))  15.5 us
    ppermute x6, starting transfers between devices, hand_back(): lax.ppermute(total, PLACE, flipped(pairs[first + number]))  10.2 us
    unnamed x42, local copies, waits for them, and re-layouts  7.55 us
    ppermute x6, starting transfers between devices, gather(): lax.ppermute(packed[turn], PLACE, pairs[turn])  7.14 us
    ppermute x3, starting transfers between devices, per_device(): lax.ppermute(total[turn], PLACE, flipped(pairs[turn]))  5.26 us
  transfers between devices with their start and end apart: 29, of which 13 were waited for; matrix products, arithmetic and copies ran while one was open for 6% of the time, Pallas kernels for 17%

profile of v6, /device:TPU:22, one launch (start us, length us, event | category | flops | bytes accessed | tf_op | source)
XLA Modules:
  0.0 159.8 jit_solution(12309455892926077234)
XLA Ops:
  0.6 0.8 copy.20
  1.4 0.1 fusion.4.refs_2_
  1.5 1.0 copy-done
  2.6 1.0 copy-done.2
  3.6 0.9 copy-done.7
  4.5 0.9 copy-done.8
  5.4 0.9 copy-done.9
  6.3 1.8 %shard_map.135 = (f32[352,512]{1,0:T(8,128)}, f32[352,512]{1,0:T(8,128)}, f32[352,512]{1,0:T(8,128)S(1)}, f32[608,512]{1,0:T(8,128)}, f32[96,512]{1,0:T(8,128)S(1)}) custom-call(f32[256,512]{1,0:T(8,128)S(1)} %bitcast.41, f32[256,512]{1,0:T(8,128)S(1)} %bitcast.40, f32[256,1]{1,0:T(8,128)S(1)} %fusion.4.refs_2_, f32[64,512]{1,0:T(8,128)S(1)} %bitcast.44, ...), custom_call_target="tpu_custom_call" | custom-call | bytes 5047296 | tf_op jit(solution)/shard_map/pallas_call | solution.py:478
  8.2 0.1 collective-permute-start
  8.2 0.6 collective-permute-start.4
  8.8 2.3 %collective-permute-start.5 = (f32[352,512]{1,0:T(8,128)}, f32[352,512]{1,0:T(8,128)S(1)}, u32[]{:S(2)}, u32[]{:S(2)}) collective-permute-start(f32[352,512]{1,0:T(8,128)} %get-tuple-element.70), channel_id=1, source_target_pairs={{8,4},{12,5},{1,8},{5,9},{0,0},{4,1},{9,12},{13,13},{10,6},{14,7},... | collective-permute-start | bytes 2162696 | tf_op jit(solution)/shard_map/ppermute | solution.py:533
  11.1 1.3 collective-permute-start.6
  12.4 11.9 %collective-permute-done.4.refs_2_.refs_0_ = f32[352,512]{1,0:T(8,128)S(1)} collective-permute-done((f32[352,512]{1,0:T(8,128)}, f32[352,512]{1,0:T(8,128)S(1)}, u32[]{:S(2)}, u32[]{:S(2)}) %collective-permute-start.4) | collective-permute-done | bytes 720928 | tf_op jit(solution)/shard_map/ppermute | solution.py:533
  24.3 18.6 %collective-permute-done.5.refs_3_.refs_1_ = f32[352,512]{1,0:T(8,128)S(1)} collective-permute-done((f32[352,512]{1,0:T(8,128)}, f32[352,512]{1,0:T(8,128)S(1)}, u32[]{:S(2)}, u32[]{:S(2)}) %collective-permute-start.5) | collective-permute-done | bytes 720928 | tf_op jit(solution)/shard_map/ppermute | solution.py:533
  43.0 1.5 collective-permute-done.6.refs_4_.refs_0_
  44.4 0.5 collective-permute-start.8
  45.0 1.0 select_bitcast_fusion
  46.1 0.6 collective-permute-start.7
  46.7 0.3 shard_map.136
  47.1 1.9 %collective-permute-start.2 = (f32[256,512]{1,0:T(8,128)S(1)}, f32[256,512]{1,0:T(8,128)S(1)}, u32[]{:S(2)}, u32[]{:S(2)}) collective-permute-start(f32[256,512]{1,0:T(8,128)S(1)} %get-tuple-element.66), channel_id=1, source_target_pairs={{8,4},{12,5},{1,8},{5,9},{0,0},{4,1},{9,12},{13,13},{10,6},{14,7},... | collective-permute-start | bytes 1572872 | tf_op jit(solution)/shard_map/ppermute | solution.py:533
  49.1 1.0 collective-permute-start.3
  50.1 15.5 %collective-permute-done.7.refs_1_ = f32[4,96,512]{2,1,0:T(8,128)S(1)} collective-permute-done((f32[4,96,512]{2,1,0:T(8,128)S(1)}, f32[4,96,512]{2,1,0:T(8,128)S(1)}, u32[]{:S(2)}, u32[]{:S(2)}) %collective-permute-start.7) | collective-permute-done | bytes 786464 | tf_op jit(solution)/shard_map/ppermute | solution.py:585
  65.6 7.7 %shard_map.137 = (f32[3,512,256]{2,1,0:T(8,128)S(1)}, f32[1024,256]{1,0:T(8,128)S(1)}, f32[1024,256]{1,0:T(8,128)S(1)}, f32[1024,256]{1,0:T(8,128)S(1)}, bf16[2,...) custom-call(f32[4,96,512]{2,1,0:T(8,128)S(1)} %pad_maximum_fusion.refs_0_, ...), custom_call_target="tpu_custom_call" | custom-call | flops 4831838208 | bytes 18874368 | tf_op jit(solution)/shard_map/pallas_call | solution.py:478
  73.3 0.6 shard_map.138
  74.0 0.1 collective-permute-done.3.refs_2_
  74.1 0.5 collective-permute-start.11
  74.6 0.5 collective-permute-start.13
  75.1 2.4 %collective-permute-done.11.refs_3_ = f32[256,512]{1,0:T(8,128)S(1)} collective-permute-done((f32[256,512]{1,0:T(8,128)S(1)}, f32[256,512]{1,0:T(8,128)S(1)}, u32[]{:S(2)}, u32[]{:S(2)}) %collective-permute-start.11) | collective-permute-done | bytes 524320 | tf_op jit(solution)/shard_map/ppermute | solution.py:537
  77.5 0.7 collective-permute-done.12.refs_4_
  78.2 0.7 collective-permute-done.13.refs_5_
  79.0 11.8 %shard_map.139 = (f32[3,512,256]{2,1,0:T(8,128)S(1)}, f32[128,512]{1,0:T(8,128)S(1)}, f32[128,512]{1,0:T(8,128)S(1)}, f32[128,512]{1,0:T(8,128)S(1)}, f32[640,512]{1,0:T(8,128)S(1)}) custom-call(f32[256,512]{1,0:T(8,128)S(1)} %collective-permute-done.1.refs_0_, f32[256,512]{1,0:T(8,128)S(1)} %collective-permute-done.2.refs_1_, ...), custom_call_target="tpu_custom_call" | custom-call | flops 6442450944 | bytes 10485760 | tf_op jit(solution)/shard_map/pallas_call | solution.py:478
  90.8 0.2 collective-permute-start.15
  91.0 1.2 shard_map.140
  92.2 7.5 %shard_map.141 = (f32[256,512]{1,0:T(8,128)S(1)}, f32[256,512]{1,0:T(8,128)S(1)}, f32[512,512]{1,0:T(8,128)}, bf16[2,3,512,256]{3,2,1,0:T(8,128)(2,1)S(1)}) custom-call(f32[352,512]{1,0:T(8,128)S(1)} %collective-permute-done.4.refs_2_.refs_0_, f32[352,512]{1,0:T(8,128)S(1)} %collective-permute-done.5.refs_3_.refs_1_, ...), custom_call_target="tpu_custom_call" | custom-call | flops 3623878656 | bytes 12845056 | tf_op jit(solution)/shard_map/pallas_call | solution.py:478
  99.7 0.4 collective-permute-start.20
  100.2 0.1 slice_add_fusion.5
  100.4 2.8 %collective-permute-start.17 = (f32[128,512]{1,0:T(8,128)S(1)}, f32[128,512]{1,0:T(8,128)S(1)}, u32[]{:S(2)}, u32[]{:S(2)}) collective-permute-start(f32[128,512]{1,0:T(8,128)S(1)} %get-tuple-element.103), channel_id=1, source_target_pairs={{4,8},{5,12},{8,1},{9,5},{0,0},{1,4},{12,9},{13,13},{6,10},{7,14},... | collective-permute-start | bytes 786440 | tf_op jit(solution)/shard_map/ppermute | solution.py:551
  103.1 2.4 %collective-permute-start.18 = (f32[128,512]{1,0:T(8,128)S(1)}, f32[128,512]{1,0:T(8,128)S(1)}, u32[]{:S(2)}, u32[]{:S(2)}) collective-permute-start(f32[128,512]{1,0:T(8,128)S(1)} %get-tuple-element.104), channel_id=1, source_target_pairs={{4,12},{5,0},{8,5},{9,13},{0,1},{1,4},{12,8},{13,9},{6,14},{7,2},{... | collective-permute-start | bytes 786440 | tf_op jit(solution)/shard_map/ppermute | solution.py:551
  105.5 10.1 %shard_map.142 = (f32[256,512]{1,0:T(8,128)S(1)}, f32[768,512]{1,0:T(8,128)S(1)}, f32[1,4,3,64,256]{4,3,2,1,0:T(8,128)S(1)}, f32[1,4,3,64,256]{4,3,2,1,0:T(8,128)S(1)}) custom-call(f32[352,512]{1,0:T(8,128)S(1)} %copy-done.11, f32[352,512]{1,0:T(8,128)S(1)} %collective-permute-done.10.refs_7_.refs_1_, f32[608,512]{1,0:T(8,128)} %get-tuple-element.63.refs_8_.refs_2_, ...), custom_call_target="tpu_custom_call" | custom-call | flops 6039797760 | bytes 21233664 | tf_op jit(solution)/shard_map/pallas_call | solution.py:478
  115.6 0.9 copy-done.12
  116.6 0.7 copy-done.14
  117.2 0.1 copy-done.16
  117.3 0.1 copy-done.18
  117.5 1.6 collective-permute-start.24
  119.0 1.6 slice_add_fusion.2
  120.7 3.3 %collective-permute-start.22 = (f32[256,512]{1,0:T(8,128)S(1)}, f32[256,512]{1,0:T(8,128)S(1)}, u32[]{:S(2)}, u32[]{:S(2)}) collective-permute-start(f32[256,512]{1,0:T(8,128)S(1)} %get-tuple-element.129), channel_id=1, source_target_pairs={{4,8},{5,12},{8,1},{9,5},{0,0},{1,4},{12,9},{13,13},{6,10},{7,14},... | collective-permute-start | bytes 1572872 | tf_op jit(solution)/shard_map/ppermute | solution.py:551
  124.1 1.1 slice_add_fusion.1
  125.3 1.6 %collective-permute-start.23 = (f32[256,512]{1,0:T(8,128)S(1)}, f32[256,512]{1,0:T(8,128)S(1)}, u32[]{:S(2)}, u32[]{:S(2)}) collective-permute-start(f32[256,512]{1,0:T(8,128)S(1)} %slice_add_fusion.1), channel_id=1, source_target_pairs={{4,12},{5,0},{8,5},{9,13},{0,1},{1,4},{12,8},{13,9},{6,14},{7,2},{... | collective-permute-start | bytes 1572872 | tf_op jit(solution)/shard_map/ppermute | solution.py:551
  126.9 2.1 %fusion.2 = f32[1,1,256,512]{3,2,1,0:T(8,128)} fusion(f32[640,512]{1,0:T(8,128)} %copy-done.13, f32[128,512]{1,0:T(8,128)S(1)} %get-tuple-element.136, f32[128,512]{1,0:T(8,128)S(1)} %get-tuple-element.135, f32[640,512]{1,0:T(8,128)} %copy-done.6, pred[]{:T(512)S(6)} %eq.14), kind=kLoop, calls=%fused_computation.11 | loop fusion | flops 393216 | bytes 2097153 | tf_op jit(solution)/shard_map/broadcast_in_dim | solution.py:720
  129.1 1.4 slice_add_fusion
  130.5 1.9 %collective-permute-done.21 = f32[256,512]{1,0:T(8,128)S(1)} collective-permute-done((f32[256,512]{1,0:T(8,128)S(1)}, f32[256,512]{1,0:T(8,128)S(1)}, u32[]{:S(2)}, u32[]{:S(2)}) %collective-permute-start.21) | collective-permute-done | bytes 524320 | tf_op jit(solution)/shard_map/ppermute | solution.py:551
  132.3 5.1 %collective-permute-done.22 = f32[256,512]{1,0:T(8,128)S(1)} collective-permute-done((f32[256,512]{1,0:T(8,128)S(1)}, f32[256,512]{1,0:T(8,128)S(1)}, u32[]{:S(2)}, u32[]{:S(2)}) %collective-permute-start.22) | collective-permute-done | bytes 524320 | tf_op jit(solution)/shard_map/ppermute | solution.py:551
  137.4 9.1 %collective-permute-done.23 = f32[256,512]{1,0:T(8,128)S(1)} collective-permute-done((f32[256,512]{1,0:T(8,128)S(1)}, f32[256,512]{1,0:T(8,128)S(1)}, u32[]{:S(2)}, u32[]{:S(2)}) %collective-permute-start.23) | collective-permute-done | bytes 524320 | tf_op jit(solution)/shard_map/ppermute | solution.py:551
  146.5 0.1 bitcast_add_fusion
  146.8 1.2 collective-permute-start.26
  147.9 1.9 %collective-permute-start.27 = (f32[3,64,256]{2,1,0:T(8,128)S(1)}, f32[3,64,256]{2,1,0:T(8,128)S(1)}, u32[]{:S(2)}, u32[]{:S(2)}) collective-permute-start(f32[3,64,256]{2,1,0:T(8,128)S(1)} %get-tuple-element.133), channel_id=1, source_target_pairs={{4,8},{5,12},{8,1},{9,5},{0,0},{1,4},{12,9},{13,13},{6,10},{7,14},... | collective-permute-start | bytes 589832 | tf_op jit(solution)/shard_map/ppermute | solution.py:704
  149.9 2.2 %collective-permute-start.28 = (f32[3,64,256]{2,1,0:T(8,128)S(1)}, f32[3,64,256]{2,1,0:T(8,128)S(1)}, u32[]{:S(2)}, u32[]{:S(2)}) collective-permute-start(f32[3,64,256]{2,1,0:T(8,128)S(1)} %get-tuple-element.132), channel_id=1, source_target_pairs={{4,12},{5,0},{8,5},{9,13},{0,1},{1,4},{12,8},{13,9},{6,14},{7,2},{... | collective-permute-start | bytes 589832 | tf_op jit(solution)/shard_map/ppermute | solution.py:704
  152.1 0.2 select_select_fusion.1
  152.3 0.9 copy-done.1
  153.3 1.2 multiply_reduce_fusion
  154.5 0.6 divide_multiply_fusion
  155.1 2.4 %collective-permute-done.27 = f32[3,64,256]{2,1,0:T(8,128)S(1)} collective-permute-done((f32[3,64,256]{2,1,0:T(8,128)S(1)}, f32[3,64,256]{2,1,0:T(8,128)S(1)}, u32[]{:S(2)}, u32[]{:S(2)}) %collective-permute-start.27) | collective-permute-done | bytes 196640 | tf_op jit(solution)/shard_map/ppermute | solution.py:704
  157.4 1.5 collective-permute-done.28
  159.1 0.8 pad_maximum_fusion.1
  (67 shorter events, 0.8 us)
Async XLA Ops:
  1.5 1.0 copy-start
  2.6 1.0 copy-start.2
  3.6 0.9 copy-start.7
  4.5 0.9 copy-start.8
  5.4 0.9 copy-start.9
  8.2 36.8 %collective-permute-start = (f32[608,512]{1,0:T(8,128)}, f32[608,512]{1,0:T(8,128)}, u32[]{:S(2)}, u32[]{:S(2)}) collective-permute-start(f32[608,512]{1,0:T(8,128)} %get-tuple-element.63.refs_8_.refs_2_), channel_id=1, source_target_pairs={{0,1},{1,0},{2,3},{3,2},{4,5},{5,4},{6,7},{7,6},{8,9},{9,8},{10,11... | collective-permute-start | bytes 3735560 | tf_op jit(solution)/shard_map/ppermute | solution.py:538
  8.2 16.1 %collective-permute-start.4 = (f32[352,512]{1,0:T(8,128)}, f32[352,512]{1,0:T(8,128)S(1)}, u32[]{:S(2)}, u32[]{:S(2)}) collective-permute-start(f32[352,512]{1,0:T(8,128)} %get-tuple-element.69), channel_id=1, source_target_pairs={{0,4},{8,5},{13,8},{1,9},{4,0},{5,1},{9,12},{12,13},{2,6},{10,7},{... | collective-permute-start | bytes 2162696 | tf_op jit(solution)/shard_map/ppermute | solution.py:533
  8.8 34.2 %collective-permute-start.5 = (f32[352,512]{1,0:T(8,128)}, f32[352,512]{1,0:T(8,128)S(1)}, u32[]{:S(2)}, u32[]{:S(2)}) collective-permute-start(f32[352,512]{1,0:T(8,128)} %get-tuple-element.70), channel_id=1, source_target_pairs={{8,4},{12,5},{1,8},{5,9},{0,0},{4,1},{9,12},{13,13},{10,6},{14,7},... | collective-permute-start | bytes 2162696 | tf_op jit(solution)/shard_map/ppermute | solution.py:533
  11.1 33.3 %collective-permute-start.6 = (f32[352,512]{1,0:T(8,128)S(1)}, f32[352,512]{1,0:T(8,128)S(1)}, u32[]{:S(2)}, u32[]{:S(2)}) collective-permute-start(f32[352,512]{1,0:T(8,128)S(1)} %get-tuple-element.71), channel_id=1, source_target_pairs={{12,4},{0,5},{5,8},{13,9},{1,0},{4,1},{8,12},{9,13},{14,6},{2,7},{... | collective-permute-start | bytes 2162696 | tf_op jit(solution)/shard_map/ppermute | solution.py:533
  44.4 21.2 %copy-start.10 = (f32[352,512]{1,0:T(8,128)}, f32[352,512]{1,0:T(8,128)S(1)}, u32[]{:S(2)}) copy-start(f32[352,512]{1,0:T(8,128)S(1)} %collective-permute-done.6.refs_4_.refs_0_) | copy-start | bytes 2162692
  44.4 2.7 %collective-permute-start.10 = (f32[352,512]{1,0:T(8,128)S(1)}, f32[352,512]{1,0:T(8,128)S(1)}, u32[]{:S(2)}, u32[]{:S(2)}) collective-permute-start(f32[352,512]{1,0:T(8,128)S(1)} %collective-permute-done.6.refs_4_.refs_0_), channel_id=1, source_target_pairs={{0,1},{1,0},{2,3},{3,2},{4,5},{5,4},{6,7},{7,6},{8,9},{9,8},{10,11... | collective-permute-start | bytes 2162696 | tf_op jit(solution)/shard_map/ppermute | solution.py:537
  44.4 4.6 %collective-permute-start.8 = (f32[352,512]{1,0:T(8,128)S(1)}, f32[352,512]{1,0:T(8,128)S(1)}, u32[]{:S(2)}, u32[]{:S(2)}) collective-permute-start(f32[352,512]{1,0:T(8,128)S(1)} %collective-permute-done.4.refs_2_.refs_0_), channel_id=1, source_target_pairs={{0,1},{1,0},{2,3},{3,2},{4,5},{5,4},{6,7},{7,6},{8,9},{9,8},{10,11... | collective-permute-start | bytes 2162696 | tf_op jit(solution)/shard_map/ppermute | solution.py:537
  44.9 1.8 %copy-start.3 = (f32[1,1,256,512]{3,2,1,0:T(8,128)S(1)}, f32[1,1,256,512]{3,2,1,0:T(8,128)}, u32[]{:S(2)}) copy-start(f32[1,1,256,512]{3,2,1,0:T(8,128)} %param.8) | copy-start | bytes 1572868
  45.0 1.8 %copy-start.4 = (f32[1,1,256,512]{3,2,1,0:T(8,128)S(1)}, f32[1,1,256,512]{3,2,1,0:T(8,128)}, u32[]{:S(2)}) copy-start(f32[1,1,256,512]{3,2,1,0:T(8,128)} %param.12) | copy-start | bytes 1572868
  46.1 19.5 %collective-permute-start.7 = (f32[4,96,512]{2,1,0:T(8,128)S(1)}, f32[4,96,512]{2,1,0:T(8,128)S(1)}, u32[]{:S(2)}, u32[]{:S(2)}) collective-permute-start(f32[4,96,512]{2,1,0:T(8,128)S(1)} %pad_maximum_fusion.refs_0_), channel_id=1, source_target_pairs={{0,2},{2,0},{1,3},{3,1},{4,6},{6,4},{5,7},{7,5},{8,10},{10,8},{9,1... | collective-permute-start | bytes 2359304 | tf_op jit(solution)/shard_map/ppermute | solution.py:585
  46.7 3.4 %collective-permute-start.9 = (f32[352,512]{1,0:T(8,128)S(1)}, f32[352,512]{1,0:T(8,128)S(1)}, u32[]{:S(2)}, u32[]{:S(2)}) collective-permute-start(f32[352,512]{1,0:T(8,128)S(1)} %collective-permute-done.5.refs_3_.refs_1_), channel_id=1, source_target_pairs={{0,1},{1,0},{2,3},{3,2},{4,5},{5,4},{6,7},{7,6},{8,9},{9,8},{10,11... | collective-permute-start | bytes 2162696 | tf_op jit(solution)/shard_map/ppermute | solution.py:537
  47.0 26.9 %collective-permute-start.1 = (f32[256,512]{1,0:T(8,128)S(1)}, f32[256,512]{1,0:T(8,128)S(1)}, u32[]{:S(2)}, u32[]{:S(2)}) collective-permute-start(f32[256,512]{1,0:T(8,128)S(1)} %get-tuple-element.65), channel_id=1, source_target_pairs={{0,4},{8,5},{13,8},{1,9},{4,0},{5,1},{9,12},{12,13},{2,6},{10,7},{... | collective-permute-start | bytes 1572872 | tf_op jit(solution)/shard_map/ppermute | solution.py:533
  47.1 26.8 %collective-permute-start.2 = (f32[256,512]{1,0:T(8,128)S(1)}, f32[256,512]{1,0:T(8,128)S(1)}, u32[]{:S(2)}, u32[]{:S(2)}) collective-permute-start(f32[256,512]{1,0:T(8,128)S(1)} %get-tuple-element.66), channel_id=1, source_target_pairs={{8,4},{12,5},{1,8},{5,9},{0,0},{4,1},{9,12},{13,13},{10,6},{14,7},... | collective-permute-start | bytes 1572872 | tf_op jit(solution)/shard_map/ppermute | solution.py:533
  49.1 25.0 %collective-permute-start.3 = (f32[256,512]{1,0:T(8,128)S(1)}, f32[256,512]{1,0:T(8,128)S(1)}, u32[]{:S(2)}, u32[]{:S(2)}) collective-permute-start(f32[256,512]{1,0:T(8,128)S(1)} %get-tuple-element.67), channel_id=1, source_target_pairs={{12,4},{0,5},{5,8},{13,9},{1,0},{4,1},{8,12},{9,13},{14,6},{2,7},{... | collective-permute-start | bytes 1572872 | tf_op jit(solution)/shard_map/ppermute | solution.py:533
  74.1 4.9 %collective-permute-start.14 = (f32[512,512]{1,0:T(8,128)S(1)}, f32[512,512]{1,0:T(8,128)S(1)}, u32[]{:S(2)}, u32[]{:S(2)}) collective-permute-start(f32[512,512]{1,0:T(8,128)S(1)} %get-tuple-element.83.refs_6_), channel_id=1, source_target_pairs={{0,1},{1,0},{2,3},{3,2},{4,5},{5,4},{6,7},{7,6},{8,9},{9,8},{10,11... | collective-permute-start | bytes 3145736 | tf_op jit(solution)/shard_map/ppermute | solution.py:538
  74.1 3.4 %collective-permute-start.11 = (f32[256,512]{1,0:T(8,128)S(1)}, f32[256,512]{1,0:T(8,128)S(1)}, u32[]{:S(2)}, u32[]{:S(2)}) collective-permute-start(f32[256,512]{1,0:T(8,128)S(1)} %collective-permute-done.1.refs_0_), channel_id=1, source_target_pairs={{0,1},{1,0},{2,3},{3,2},{4,5},{5,4},{6,7},{7,6},{8,9},{9,8},{10,11... | collective-permute-start | bytes 1572872 | tf_op jit(solution)/shard_map/ppermute | solution.py:537
  74.6 3.6 %collective-permute-start.12 = (f32[256,512]{1,0:T(8,128)S(1)}, f32[256,512]{1,0:T(8,128)S(1)}, u32[]{:S(2)}, u32[]{:S(2)}) collective-permute-start(f32[256,512]{1,0:T(8,128)S(1)} %collective-permute-done.2.refs_1_), channel_id=1, source_target_pairs={{0,1},{1,0},{2,3},{3,2},{4,5},{5,4},{6,7},{7,6},{8,9},{9,8},{10,11... | collective-permute-start | bytes 1572872 | tf_op jit(solution)/shard_map/ppermute | solution.py:537
  74.6 4.4 %collective-permute-start.13 = (f32[256,512]{1,0:T(8,128)S(1)}, f32[256,512]{1,0:T(8,128)S(1)}, u32[]{:S(2)}, u32[]{:S(2)}) collective-permute-start(f32[256,512]{1,0:T(8,128)S(1)} %collective-permute-done.3.refs_2_), channel_id=1, source_target_pairs={{0,1},{1,0},{2,3},{3,2},{4,5},{5,4},{6,7},{7,6},{8,9},{9,8},{10,11... | collective-permute-start | bytes 1572872 | tf_op jit(solution)/shard_map/ppermute | solution.py:537
  90.8 1.4 copy-start.6
  90.8 9.3 %collective-permute-start.15 = (f32[640,512]{1,0:T(8,128)S(1)}, f32[640,512]{1,0:T(8,128)S(1)}, u32[]{:S(2)}, u32[]{:S(2)}) collective-permute-start(f32[640,512]{1,0:T(8,128)S(1)} %get-tuple-element.86), channel_id=1, source_target_pairs={{0,1},{1,0},{2,3},{3,2},{4,5},{5,4},{6,7},{7,6},{8,9},{9,8},{10,11... | collective-permute-start | bytes 3932168 | tf_op jit(solution)/shard_map/ppermute | solution.py:541
  99.7 5.8 %copy-start.5 = (f32[256,512]{1,0:T(8,128)}, f32[256,512]{1,0:T(8,128)S(1)}, u32[]{:S(2)}) copy-start(f32[256,512]{1,0:T(8,128)S(1)} %get-tuple-element.112) | copy-start | bytes 1572868
  99.7 5.8 %copy-start.11 = (f32[352,512]{1,0:T(8,128)S(1)}, f32[352,512]{1,0:T(8,128)}, u32[]{:S(2)}) copy-start(f32[352,512]{1,0:T(8,128)} %copy-done.10) | copy-start | bytes 2162692
  99.7 19.3 %collective-permute-start.20 = (f32[512,512]{1,0:T(8,128)}, f32[512,512]{1,0:T(8,128)}, u32[]{:S(2)}, u32[]{:S(2)}) collective-permute-start(f32[512,512]{1,0:T(8,128)} %get-tuple-element.111), channel_id=1, source_target_pairs={{0,1},{1,0},{2,3},{3,2},{4,5},{5,4},{6,7},{7,6},{8,9},{9,8},{10,11... | collective-permute-start | bytes 3145736 | tf_op jit(solution)/shard_map/ppermute | solution.py:541
  100.1 5.3 %copy-start.13 = (f32[640,512]{1,0:T(8,128)}, f32[640,512]{1,0:T(8,128)S(1)}, u32[]{:S(2)}) copy-start(f32[640,512]{1,0:T(8,128)S(1)} %collective-permute-done.15) | copy-start | bytes 3932164
  100.3 16.2 %collective-permute-start.16 = (f32[128,512]{1,0:T(8,128)S(1)}, f32[128,512]{1,0:T(8,128)S(1)}, u32[]{:S(2)}, u32[]{:S(2)}) collective-permute-start(f32[128,512]{1,0:T(8,128)S(1)} %get-tuple-element.102), channel_id=1, source_target_pairs={{4,0},{5,8},{8,13},{9,1},{0,4},{1,5},{12,9},{13,12},{6,2},{7,10},{... | collective-permute-start | bytes 786440 | tf_op jit(solution)/shard_map/ppermute | solution.py:551
  100.4 16.1 %collective-permute-start.17 = (f32[128,512]{1,0:T(8,128)S(1)}, f32[128,512]{1,0:T(8,128)S(1)}, u32[]{:S(2)}, u32[]{:S(2)}) collective-permute-start(f32[128,512]{1,0:T(8,128)S(1)} %get-tuple-element.103), channel_id=1, source_target_pairs={{4,8},{5,12},{8,1},{9,5},{0,0},{1,4},{12,9},{13,13},{6,10},{7,14},... | collective-permute-start | bytes 786440 | tf_op jit(solution)/shard_map/ppermute | solution.py:551
  103.1 13.4 %collective-permute-start.18 = (f32[128,512]{1,0:T(8,128)S(1)}, f32[128,512]{1,0:T(8,128)S(1)}, u32[]{:S(2)}, u32[]{:S(2)}) collective-permute-start(f32[128,512]{1,0:T(8,128)S(1)} %get-tuple-element.104), channel_id=1, source_target_pairs={{4,12},{5,0},{8,5},{9,13},{0,1},{1,4},{12,8},{13,9},{6,14},{7,2},{... | collective-permute-start | bytes 786440 | tf_op jit(solution)/shard_map/ppermute | solution.py:551
  105.5 11.9 %copy-start.20 = (f32[1,1,256]{2,1,0:T(1,128)S(1)}, f32[1,1,256]{2,1,0:T(1,128)}, u32[]{:S(2)}) copy-start(f32[1,1,256]{2,1,0:T(1,128)} %param.11) | copy-start | bytes 3076
  115.6 0.9 copy-start.12
  116.5 0.7 copy-start.14
  116.5 0.8 copy-start.16
  116.5 0.9 copy-start.18
  117.4 6.7 %collective-permute-start.19 = (f32[768,512]{1,0:T(8,128)S(1)}, f32[768,512]{1,0:T(8,128)}, u32[]{:S(2)}, u32[]{:S(2)}) collective-permute-start(f32[768,512]{1,0:T(8,128)S(1)} %get-tuple-element.108), channel_id=1, source_target_pairs={{0,1},{1,0},{2,3},{3,2},{4,5},{5,4},{6,7},{7,6},{8,9},{9,8},{10,11... | collective-permute-start | bytes 4718600 | tf_op jit(solution)/shard_map/ppermute | solution.py:541
  117.4 6.6 %copy-start.15 = (f32[128,512]{1,0:T(8,128)S(1)}, f32[128,512]{1,0:T(8,128)}, u32[]{:S(2)}) copy-start(f32[128,512]{1,0:T(8,128)} %copy-done.14) | copy-start | bytes 786436
  117.5 6.6 %copy-start.17 = (f32[128,512]{1,0:T(8,128)S(1)}, f32[128,512]{1,0:T(8,128)}, u32[]{:S(2)}) copy-start(f32[128,512]{1,0:T(8,128)} %copy-done.16) | copy-start | bytes 786436
  117.5 6.6 %copy-start.19 = (f32[128,512]{1,0:T(8,128)S(1)}, f32[128,512]{1,0:T(8,128)}, u32[]{:S(2)}) copy-start(f32[128,512]{1,0:T(8,128)} %copy-done.18) | copy-start | bytes 786436
  117.5 29.1 %collective-permute-start.24 = (f32[4,3,64,256]{3,2,1,0:T(8,128)}, f32[4,3,64,256]{3,2,1,0:T(8,128)S(1)}, u32[]{:S(2)}, u32[]{:S(2)}) collective-permute-start(f32[4,3,64,256]{3,2,1,0:T(8,128)} %bitcast.47), channel_id=1, source_target_pairs={{0,2},{2,0},{1,3},{3,1},{4,6},{6,4},{5,7},{7,5},{8,10},{10,8},{9,1... | collective-permute-start | bytes 2359304 | tf_op jit(solution)/shard_map/ppermute | solution.py:702
  120.6 11.7 %collective-permute-start.21 = (f32[256,512]{1,0:T(8,128)S(1)}, f32[256,512]{1,0:T(8,128)S(1)}, u32[]{:S(2)}, u32[]{:S(2)}) collective-permute-start(f32[256,512]{1,0:T(8,128)S(1)} %get-tuple-element.130), channel_id=1, source_target_pairs={{4,0},{5,8},{8,13},{9,1},{0,4},{1,5},{12,9},{13,12},{6,2},{7,10},{... | collective-permute-start | bytes 1572872 | tf_op jit(solution)/shard_map/ppermute | solution.py:551
  120.7 16.8 %collective-permute-start.22 = (f32[256,512]{1,0:T(8,128)S(1)}, f32[256,512]{1,0:T(8,128)S(1)}, u32[]{:S(2)}, u32[]{:S(2)}) collective-permute-start(f32[256,512]{1,0:T(8,128)S(1)} %get-tuple-element.129), channel_id=1, source_target_pairs={{4,8},{5,12},{8,1},{9,5},{0,0},{1,4},{12,9},{13,13},{6,10},{7,14},... | collective-permute-start | bytes 1572872 | tf_op jit(solution)/shard_map/ppermute | solution.py:551
  125.3 21.3 %collective-permute-start.23 = (f32[256,512]{1,0:T(8,128)S(1)}, f32[256,512]{1,0:T(8,128)S(1)}, u32[]{:S(2)}, u32[]{:S(2)}) collective-permute-start(f32[256,512]{1,0:T(8,128)S(1)} %slice_add_fusion.1), channel_id=1, source_target_pairs={{4,12},{5,0},{8,5},{9,13},{0,1},{1,4},{12,8},{13,9},{6,14},{7,2},{... | collective-permute-start | bytes 1572872 | tf_op jit(solution)/shard_map/ppermute | solution.py:551
  146.7 8.4 %collective-permute-start.25 = (f32[3,64,256]{2,1,0:T(8,128)S(1)}, f32[3,64,256]{2,1,0:T(8,128)S(1)}, u32[]{:S(2)}, u32[]{:S(2)}) collective-permute-start(f32[3,64,256]{2,1,0:T(8,128)S(1)} %get-tuple-element.131), channel_id=1, source_target_pairs={{0,1},{1,0},{2,3},{3,2},{4,5},{5,4},{6,7},{7,6},{8,9},{9,8},{10,11... | collective-permute-start | bytes 589832 | tf_op jit(solution)/shard_map/ppermute | solution.py:707
  146.8 8.3 %collective-permute-start.26 = (f32[3,64,256]{2,1,0:T(8,128)S(1)}, f32[3,64,256]{2,1,0:T(8,128)S(1)}, u32[]{:S(2)}, u32[]{:S(2)}) collective-permute-start(f32[3,64,256]{2,1,0:T(8,128)S(1)} %get-tuple-element.134), channel_id=1, source_target_pairs={{4,0},{5,8},{8,13},{9,1},{0,4},{1,5},{12,9},{13,12},{6,2},{7,10},{... | collective-permute-start | bytes 589832 | tf_op jit(solution)/shard_map/ppermute | solution.py:704
  147.9 9.5 %collective-permute-start.27 = (f32[3,64,256]{2,1,0:T(8,128)S(1)}, f32[3,64,256]{2,1,0:T(8,128)S(1)}, u32[]{:S(2)}, u32[]{:S(2)}) collective-permute-start(f32[3,64,256]{2,1,0:T(8,128)S(1)} %get-tuple-element.133), channel_id=1, source_target_pairs={{4,8},{5,12},{8,1},{9,5},{0,0},{1,4},{12,9},{13,13},{6,10},{7,14},... | collective-permute-start | bytes 589832 | tf_op jit(solution)/shard_map/ppermute | solution.py:704
  149.9 9.1 %collective-permute-start.28 = (f32[3,64,256]{2,1,0:T(8,128)S(1)}, f32[3,64,256]{2,1,0:T(8,128)S(1)}, u32[]{:S(2)}, u32[]{:S(2)}) collective-permute-start(f32[3,64,256]{2,1,0:T(8,128)S(1)} %get-tuple-element.132), channel_id=1, source_target_pairs={{4,12},{5,0},{8,5},{9,13},{0,1},{1,4},{12,8},{13,9},{6,14},{7,2},{... | collective-permute-start | bytes 589832 | tf_op jit(solution)/shard_map/ppermute | solution.py:704
  152.2 1.0 copy-start.1

commit v7 on v6

--- a/solution.py
+++ b/solution.py
@@ -17,6 +17,7 @@
 BF16 = jnp.bfloat16
 NN = ((1,), (0,))
 NT = ((1,), (1,))
+GROUP = 2
 HBM = pl.BlockSpec(memory_space=pltpu.MemorySpace.HBM)
 VMEM = pl.BlockSpec(memory_space=pltpu.VMEM)
 
@@ -104,7 +105,16 @@
 
 def pack_kernel(half, with_weights, *refs):
     if with_weights:
-        first, second, scale, gate, up, down, *outs, held, sems, weight_sems = refs
+        *sources, scale = refs[:6]
+        first, second, gate, up, down = refs[-9:-4]
+        outs, (load_sems, held, sems, weight_sems) = refs[6:-9], refs[-4:]
+        loads = [
+            pltpu.make_async_copy(source, there, load_sems.at[number])
+            for number, (source, there) in enumerate(zip(sources, (first, second, gate, up, down)))
+        ]
+        for load in loads:
+            load.start()
+        loads[0].wait()
     else:
         first, second, *outs, sems = refs
     place, core = position()
@@ -129,7 +139,17 @@
         return copies
 
     copies = copies_of(0, first)
+    for copy in copies:
+        copy.start()
     if with_weights:
+        loads[1].wait()
+        held[...] = second[...] * scale[...]
+    late = copies_of(1, held if with_weights else second)
+    for copy in late:
+        copy.start()
+    if with_weights:
+        for load in loads[2:]:
+            load.wait()
         rows, width = gate.shape
         cols = width // 2
         for piece, out in enumerate(outs):
@@ -148,13 +168,7 @@
                         weight_sems.at[piece, number],
                     )
                 )
-    for copy in copies:
-        copy.start()
-    if with_weights:
-        held[...] = second[...] * scale[...]
-    late = copies_of(1, held if with_weights else second)
-    for copy in late:
-        copy.start()
+                copies[-1].start()
     for copy in copies + late:
         copy.wait()
 
@@ -195,11 +209,18 @@
         local(got)
 
 
-def wait_rows(buffers, block, sems):
-    half = buffers[0].shape[1] // 2
-    for part in range(4):
-        view = buffers[part // 2].at[block, pl.ds((part % 2) * half, half)]
-        pltpu.make_async_copy(view, view, sems.at[block, part]).wait()
+def take_rows(buffers, group, sems):
+    size, depth = buffers[0].shape[1:]
+    half = size // 2
+    for each in range(GROUP):
+        block = group * GROUP + each
+        for part in range(4):
+            view = buffers[part // 2].at[block, pl.ds((part % 2) * half, half)]
+            pltpu.make_async_copy(view, view, sems.at[block, part]).wait()
+    first, second = (
+        buffer[pl.ds(group * GROUP, GROUP)].reshape(GROUP * size, depth) for buffer in buffers
+    )
+    return split(first), split(second)
 
 
 def row_starts(cells, reps, rows):
@@ -257,13 +278,12 @@
         copy.wait()
     for which in range(3):
         store_split(wide, (which,), weights[which])
-    size = keys.shape[1]
-
-    @pl.loop(0, CELL)
-    def _(block):
-        wait_rows((keys, targets), block, row_sems)
-        where = pl.ds(pl.multiple_of(block * size, size), size)
-        key, target = split(keys[block]), split(targets[block])
+    size = keys.shape[1] * GROUP
+
+    @pl.loop(0, CELL // GROUP)
+    def _(group):
+        key, target = take_rows((keys, targets), group, row_sems)
+        where = pl.ds(pl.multiple_of(group * size, size), size)
         gate_pre = dot3(key, pair_of(wide, 0), NN)
         up_pre = dot3(key, pair_of(wide, 1), NN)
         back = dot3(target, pair_of(wide, 2), NN)
@@ -310,11 +330,10 @@
             ]
         return [(sent.at[block], far_out.at[pl.ds(ROUNDS * half, size)])]
 
-    @pl.loop(0, CELL)
-    def _(block):
-        wait_rows((queries, cots), block, row_sems)
-        where = pl.ds(pl.multiple_of(block * size, size), size)
-        query, cot = split(queries[block]), split(cots[block])
+    @pl.loop(0, CELL // GROUP)
+    def _(group):
+        query, cot = take_rows((queries, cots), group, row_sems)
+        where = pl.ds(pl.multiple_of(group * GROUP * size, GROUP * size), GROUP * size)
         gate_pre = dot3(query, weight(0), NN)
         up_pre = dot3(query, weight(1), NN)
         back = dot3(cot, weight(2), NN)
@@ -327,10 +346,11 @@
             turned[part, 0, :, where] = query[part].T
             turned[part, 1, :, where] = cot[part].T
         store_split(acts, (2, where), act * up_pre)
-        sent[block] = dot3(gate_back, weight(0), NT) + dot3(up_back, weight(1), NT)
+        result = dot3(gate_back, weight(0), NT) + dot3(up_back, weight(1), NT)
+        sent[pl.ds(group * GROUP, GROUP)] = result.reshape(GROUP, size, result.shape[1])
         for number in range(CELL):
 
-            @pl.when(block == number)
+            @pl.when(group == number // GROUP)
             def _():
                 for side, (source, out) in enumerate(outgoing(number)):
                     pltpu.make_async_copy(source, out, out_sems.at[number, side]).start()
@@ -427,12 +447,13 @@
             for which in range(2)
         ]
 
-    @pl.loop(0, last - first)
-    def _(number):
-        wait_rows((keys, targets), number, row_sems)
-        where = pl.ds(pl.multiple_of((first + number) * size, size), size)
-        here = pl.ds(pl.multiple_of(number * size, size), size)
-        key, target = split(keys[number]), split(targets[number])
+    @pl.loop(0, (last - first) // GROUP)
+    def _(group):
+        key, target = take_rows((keys, targets), group, row_sems)
+        many = GROUP * size
+        where = pl.ds(pl.multiple_of(first * size + group * many, many), many)
+        here = pl.ds(pl.multiple_of(group * many, many), many)
+        there = pl.ds(group * GROUP, GROUP)
         gate_back_cot = dot3(key, pair_of(cots, 0), NN)
         up_back_cot = dot3(key, pair_of(cots, 1), NN)
         hidden_cot = dot3(target, pair_of(cots, 2), NN)
@@ -450,18 +471,20 @@
             acts[part, 0, here] = gate_cot[part]
             acts[part, 1, here] = up_cot[part]
             acts[part, 2, here] = back_cot[part]
-        sent[0, number] = (
+        key_part = (
             dot3(gate_cot, pair_of(wide, 0), NT)
             + dot3(up_cot, pair_of(wide, 1), NT)
             + dot3(split(back * up_pre * slope), pair_of(cots, 0), NT)
             + dot3(split(back * act), pair_of(cots, 1), NT)
         )
-        sent[1, number] = dot3(back_cot, pair_of(wide, 2), NT) + dot3(
+        target_part = dot3(back_cot, pair_of(wide, 2), NT) + dot3(
             split(act * up_pre), pair_of(cots, 2), NT
         )
+        sent[0, there] = key_part.reshape(GROUP, size, key_part.shape[1])
+        sent[1, there] = target_part.reshape(GROUP, size, target_part.shape[1])
         for each in range(last - first):
 
-            @pl.when(number == each)
+            @pl.when(group == each // GROUP)
             def _():
                 for side, (source, out) in enumerate(outgoing(each)):
                     pltpu.make_async_copy(source, out, out_sems.at[each, side]).start()
@@ -473,7 +496,7 @@
             pltpu.make_async_copy(source, out, out_sems.at[each, side]).wait()
 
 
-def call(kernel, inputs, in_specs, outs, out_specs, scratch, flops=0):
+def call(kernel, inputs, in_specs, outs, out_specs, scratch, flops=0, grant=26):
     moved = sum(math.prod(value.shape) * value.dtype.itemsize for value in list(inputs) + list(outs))
     return pl.pallas_call(
         kernel,
@@ -482,7 +505,7 @@
         out_specs=out_specs,
         scratch_shapes=scratch,
         cost_estimate=pl.CostEstimate(flops=flops, bytes_accessed=moved, transcendentals=0),
-        compiler_params=pltpu.CompilerParams(vmem_limit_bytes=26 << 20),
+        compiler_params=pltpu.CompilerParams(vmem_limit_bytes=grant << 20),
     )(*inputs)
 
 
@@ -520,15 +543,23 @@
         scratch = [dma((CELL, 2))]
         if rest:
             outs.append(shape((extra, depth), F32))
-            scratch = [pltpu.VMEM((2 * half, depth), F32)] + scratch + [dma((CELL + 1, 4))]
+            weights_held = [pltpu.VMEM((rows, width), F32)] * 3
+            scratch = (
+                [pltpu.VMEM((2 * half, depth), F32)] * 2
+                + weights_held
+                + [dma((5,)), pltpu.VMEM((2 * half, depth), F32)]
+                + scratch
+                + [dma((CELL + 1, 4))]
+            )
         inputs = [first, second, *rest]
         packed = call(
             functools.partial(pack_kernel, half, bool(rest)),
             inputs,
-            [VMEM] * len(inputs),
+            [HBM] * 5 + [VMEM] if rest else [VMEM] * 2,
             outs,
             [HBM] * len(outs),
             scratch,
+            grant=60 if rest else 26,
         )
         near = [lax.ppermute(packed[turn], PLACE, pairs[turn]) for turn in range(ROUNDS)]
         return near, *packed[ROUNDS:]
@@ -568,10 +599,10 @@
     inner_near, inner_local, kept = gather(
         key_rows[0, 0],
         value_rows[0, 0],
-        -step[:, None],
         fast_gate[0],
         fast_up[0],
         fast_down[0],
+        -step[:, None],
     )
     inner_near = list(lax.optimization_barrier(tuple(inner_near)))
     inner_rows = spread(inner_near, inner_local)

time: 162 us -> 159 us (0.981)
  local copies, waits for them, and re-layouts: 8.53 us -> 3.74 us
    unnamed x42 -> x38, local copies, waits for them, and re-layouts: 7.55 us -> 2.75 us
  transfers between devices with their start and end apart: 29 -> 29, of which waited for: 13 -> 13; matrix products, arithmetic and copies ran while one was open for 6% -> 5% of each run, Pallas kernels for 17% -> 17%
where the time goes in v7:
time: 159 us; the launch traced here: 157 us
  waiting for transfers between devices  71 us (45%)
  Pallas kernels  42.2 us (27%)
  starting transfers between devices  28.3 us (18%)
  other arithmetic  10.2 us (6%)
  local copies, waits for them, and re-layouts  3.74 us (2%)
    pallas_call x8, Pallas kernels, call(): pl.pallas_call(kernel, out_shape=outs, in_specs=in_specs, out_specs=out_s...  42.2 us
    ppermute x6, waiting for transfers between devices, gather(): lax.ppermute(packed[turn], PLACE, pairs[turn])  32.1 us
    ppermute x6, waiting for transfers between devices, hand_back(): lax.ppermute(total, PLACE, flipped(pairs[first + number]))  16.1 us
    ppermute x1, waiting for transfers between devices, per_device(): parts.append(lax.ppermute(together, 'rep', shifted(shift, 1)))  14.9 us
    ppermute x6, starting transfers between devices, hand_back(): lax.ppermute(total, PLACE, flipped(pairs[first + number]))  10.2 us
    ppermute x6, starting transfers between devices, gather(): lax.ppermute(packed[turn], PLACE, pairs[turn])  7.46 us
    ppermute x3, starting transfers between devices, per_device(): lax.ppermute(total[turn], PLACE, flipped(pairs[turn]))  5.26 us
    ppermute x3, waiting for transfers between devices, per_device(): lax.ppermute(total[turn], PLACE, flipped(pairs[turn]))  3.98 us
  transfers between devices with their start and end apart: 29, of which 13 were waited for; matrix products, arithmetic and copies ran while one was open for 5% of the time, Pallas kernels for 17%

profile of v7, /device:TPU:22, one launch (start us, length us, event | category | flops | bytes accessed | tf_op | source)
XLA Modules:
  0.0 156.5 jit_solution(16010575605977838297)
XLA Ops:
  0.6 0.8 copy.20
  1.4 0.7 fusion.4.refs_5_
  2.2 4.0 %shard_map.135 = (f32[352,512]{1,0:T(8,128)}, f32[352,512]{1,0:T(8,128)}, f32[352,512]{1,0:T(8,128)}, f32[608,512]{1,0:T(8,128)}, f32[96,512]{1,0:T(8,128)}) custom-call(f32[256,512]{1,0:T(8,128)} %bitcast.44, f32[256,512]{1,0:T(8,128)} %bitcast.43, f32[64,512]{1,0:T(8,128)} %bitcast.45, f32[64,512]{1,0:T(8,128)} %bitcast.46, f32[64,512]{1,0:T(8,128)} %bitcast.47, ...), custom_call_target="tpu_custom_call" | custom-call | bytes 5047296 | tf_op jit(solution)/shard_map/pallas_call | solution.py:501
  6.2 0.1 collective-permute-start
  6.3 0.6 collective-permute-start.4
  6.9 2.3 %collective-permute-start.5 = (f32[352,512]{1,0:T(8,128)}, f32[352,512]{1,0:T(8,128)S(1)}, u32[]{:S(2)}, u32[]{:S(2)}) collective-permute-start(f32[352,512]{1,0:T(8,128)} %get-tuple-element.70), channel_id=1, source_target_pairs={{8,4},{12,5},{1,8},{5,9},{0,0},{4,1},{9,12},{13,13},{10,6},{14,7},... | collective-permute-start | bytes 2162696 | tf_op jit(solution)/shard_map/ppermute | solution.py:564
  9.2 1.3 collective-permute-start.6
  10.4 11.9 %collective-permute-done.4.refs_2_.refs_0_ = f32[352,512]{1,0:T(8,128)S(1)} collective-permute-done((f32[352,512]{1,0:T(8,128)}, f32[352,512]{1,0:T(8,128)S(1)}, u32[]{:S(2)}, u32[]{:S(2)}) %collective-permute-start.4) | collective-permute-done | bytes 720928 | tf_op jit(solution)/shard_map/ppermute | solution.py:564
  22.4 18.6 %collective-permute-done.5.refs_3_.refs_1_ = f32[352,512]{1,0:T(8,128)S(1)} collective-permute-done((f32[352,512]{1,0:T(8,128)}, f32[352,512]{1,0:T(8,128)S(1)}, u32[]{:S(2)}, u32[]{:S(2)}) %collective-permute-start.5) | collective-permute-done | bytes 720928 | tf_op jit(solution)/shard_map/ppermute | solution.py:564
  41.0 1.5 collective-permute-done.6.refs_4_.refs_0_
  42.5 0.5 collective-permute-start.8
  43.2 0.6 collective-permute-start.7
  43.8 1.1 collective-permute-start.9
  44.9 0.3 shard_map.136
  45.2 1.9 %collective-permute-start.2 = (f32[256,512]{1,0:T(8,128)S(1)}, f32[256,512]{1,0:T(8,128)S(1)}, u32[]{:S(2)}, u32[]{:S(2)}) collective-permute-start(f32[256,512]{1,0:T(8,128)S(1)} %get-tuple-element.66), channel_id=1, source_target_pairs={{8,4},{12,5},{1,8},{5,9},{0,0},{4,1},{9,12},{13,13},{10,6},{14,7},... | collective-permute-start | bytes 1572872 | tf_op jit(solution)/shard_map/ppermute | solution.py:564
  47.2 1.3 collective-permute-start.3
  48.5 14.9 %collective-permute-done.7.refs_1_ = f32[4,96,512]{2,1,0:T(8,128)S(1)} collective-permute-done((f32[4,96,512]{2,1,0:T(8,128)S(1)}, f32[4,96,512]{2,1,0:T(8,128)S(1)}, u32[]{:S(2)}, u32[]{:S(2)}) %collective-permute-start.7) | collective-permute-done | bytes 786464 | tf_op jit(solution)/shard_map/ppermute | solution.py:616
  63.4 7.5 %shard_map.137 = (f32[3,512,256]{2,1,0:T(8,128)S(1)}, f32[1024,256]{1,0:T(8,128)S(1)}, f32[1024,256]{1,0:T(8,128)S(1)}, f32[1024,256]{1,0:T(8,128)S(1)}, bf16[2,...) custom-call(f32[4,96,512]{2,1,0:T(8,128)S(1)} %pad_maximum_fusion.refs_0_, ...), custom_call_target="tpu_custom_call" | custom-call | flops 4831838208 | bytes 18874368 | tf_op jit(solution)/shard_map/pallas_call | solution.py:501
  70.9 0.6 shard_map.138
  71.6 0.1 collective-permute-done.3.refs_2_
  71.7 0.4 collective-permute-start.14
  72.1 0.1 collective-permute-start.11
  72.2 0.4 collective-permute-start.12
  72.6 0.1 collective-permute-start.13
  72.7 2.4 %collective-permute-done.11.refs_3_ = f32[256,512]{1,0:T(8,128)S(1)} collective-permute-done((f32[256,512]{1,0:T(8,128)S(1)}, f32[256,512]{1,0:T(8,128)S(1)}, u32[]{:S(2)}, u32[]{:S(2)}) %collective-permute-start.11) | collective-permute-done | bytes 524320 | tf_op jit(solution)/shard_map/ppermute | solution.py:568
  75.1 0.7 collective-permute-done.12.refs_4_
  75.9 0.7 collective-permute-done.13.refs_5_
  76.6 11.3 %shard_map.139 = (f32[3,512,256]{2,1,0:T(8,128)S(1)}, f32[128,512]{1,0:T(8,128)S(1)}, f32[128,512]{1,0:T(8,128)S(1)}, f32[128,512]{1,0:T(8,128)S(1)}, f32[640,512]{1,0:T(8,128)S(1)}) custom-call(f32[256,512]{1,0:T(8,128)S(1)} %collective-permute-done.1.refs_0_, f32[256,512]{1,0:T(8,128)S(1)} %collective-permute-done.2.refs_1_, ...), custom_call_target="tpu_custom_call" | custom-call | flops 6442450944 | bytes 10485760 | tf_op jit(solution)/shard_map/pallas_call | solution.py:501
  87.9 0.4 collective-permute-start.15
  88.4 1.2 shard_map.140
  89.5 7.2 %shard_map.141 = (f32[256,512]{1,0:T(8,128)S(1)}, f32[256,512]{1,0:T(8,128)S(1)}, f32[512,512]{1,0:T(8,128)}, bf16[2,3,512,256]{3,2,1,0:T(8,128)(2,1)S(1)}) custom-call(f32[352,512]{1,0:T(8,128)S(1)} %collective-permute-done.4.refs_2_.refs_0_, f32[352,512]{1,0:T(8,128)S(1)} %collective-permute-done.5.refs_3_.refs_1_, ...), custom_call_target="tpu_custom_call" | custom-call | flops 3623878656 | bytes 12845056 | tf_op jit(solution)/shard_map/pallas_call | solution.py:501
  96.8 0.2 collective-permute-start.20
  97.0 0.1 slice_add_fusion.5
  97.2 3.2 %collective-permute-start.17 = (f32[128,512]{1,0:T(8,128)S(1)}, f32[128,512]{1,0:T(8,128)S(1)}, u32[]{:S(2)}, u32[]{:S(2)}) collective-permute-start(f32[128,512]{1,0:T(8,128)S(1)} %get-tuple-element.103), channel_id=1, source_target_pairs={{4,8},{5,12},{8,1},{9,5},{0,0},{1,4},{12,9},{13,13},{6,10},{7,14},... | collective-permute-start | bytes 786440 | tf_op jit(solution)/shard_map/ppermute | solution.py:582
  100.5 1.9 %collective-permute-start.18 = (f32[128,512]{1,0:T(8,128)S(1)}, f32[128,512]{1,0:T(8,128)S(1)}, u32[]{:S(2)}, u32[]{:S(2)}) collective-permute-start(f32[128,512]{1,0:T(8,128)S(1)} %get-tuple-element.104), channel_id=1, source_target_pairs={{4,12},{5,0},{8,5},{9,13},{0,1},{1,4},{12,8},{13,9},{6,14},{7,2},{... | collective-permute-start | bytes 786440 | tf_op jit(solution)/shard_map/ppermute | solution.py:582
  102.4 10.1 %shard_map.142 = (f32[256,512]{1,0:T(8,128)S(1)}, f32[768,512]{1,0:T(8,128)S(1)}, f32[1,4,3,64,256]{4,3,2,1,0:T(8,128)S(1)}, f32[1,4,3,64,256]{4,3,2,1,0:T(8,128)S(1)}) custom-call(f32[352,512]{1,0:T(8,128)S(1)} %copy-done.5, f32[352,512]{1,0:T(8,128)S(1)} %collective-permute-done.10.refs_7_.refs_1_, f32[608,512]{1,0:T(8,128)S(1)} %copy-done.8, ...), custom_call_target="tpu_custom_call" | custom-call | flops 6039797760 | bytes 21233664 | tf_op jit(solution)/shard_map/pallas_call | solution.py:501
  112.6 0.9 copy-done.9
  113.5 0.7 copy-done.12
  114.1 0.1 copy-done.14
  114.2 0.1 copy-done.16
  114.4 1.3 collective-permute-start.24
  115.7 1.6 slice_add_fusion.2
  117.3 0.3 collective-permute-start.21
  117.6 3.2 %collective-permute-start.22 = (f32[256,512]{1,0:T(8,128)S(1)}, f32[256,512]{1,0:T(8,128)S(1)}, u32[]{:S(2)}, u32[]{:S(2)}) collective-permute-start(f32[256,512]{1,0:T(8,128)S(1)} %get-tuple-element.129), channel_id=1, source_target_pairs={{4,8},{5,12},{8,1},{9,5},{0,0},{1,4},{12,9},{13,13},{6,10},{7,14},... | collective-permute-start | bytes 1572872 | tf_op jit(solution)/shard_map/ppermute | solution.py:582
  120.9 1.1 slice_add_fusion.1
  122.1 1.5 collective-permute-start.23
  123.6 2.1 %fusion.2 = f32[1,1,256,512]{3,2,1,0:T(8,128)} fusion(f32[640,512]{1,0:T(8,128)} %copy-done.11, f32[128,512]{1,0:T(8,128)S(1)} %get-tuple-element.136, f32[128,512]{1,0:T(8,128)S(1)} %get-tuple-element.135, f32[640,512]{1,0:T(8,128)} %copy-done.3, pred[]{:T(512)S(6)} %eq.14), kind=kLoop, calls=%fused_computation.11 | loop fusion | flops 393216 | bytes 2097153 | tf_op jit(solution)/shard_map/broadcast_in_dim | solution.py:751
  125.7 1.4 slice_add_fusion
  127.1 1.6 %collective-permute-done.21 = f32[256,512]{1,0:T(8,128)S(1)} collective-permute-done((f32[256,512]{1,0:T(8,128)S(1)}, f32[256,512]{1,0:T(8,128)S(1)}, u32[]{:S(2)}, u32[]{:S(2)}) %collective-permute-start.21) | collective-permute-done | bytes 524320 | tf_op jit(solution)/shard_map/ppermute | solution.py:582
  128.8 5.5 %collective-permute-done.22 = f32[256,512]{1,0:T(8,128)S(1)} collective-permute-done((f32[256,512]{1,0:T(8,128)S(1)}, f32[256,512]{1,0:T(8,128)S(1)}, u32[]{:S(2)}, u32[]{:S(2)}) %collective-permute-start.22) | collective-permute-done | bytes 524320 | tf_op jit(solution)/shard_map/ppermute | solution.py:582
  134.3 8.9 %collective-permute-done.23 = f32[256,512]{1,0:T(8,128)S(1)} collective-permute-done((f32[256,512]{1,0:T(8,128)S(1)}, f32[256,512]{1,0:T(8,128)S(1)}, u32[]{:S(2)}, u32[]{:S(2)}) %collective-permute-start.23) | collective-permute-done | bytes 524320 | tf_op jit(solution)/shard_map/ppermute | solution.py:582
  143.2 0.1 bitcast_add_fusion
  143.4 0.1 collective-permute-start.25
  143.5 1.2 collective-permute-start.26
  144.6 2.0 %collective-permute-start.27 = (f32[3,64,256]{2,1,0:T(8,128)S(1)}, f32[3,64,256]{2,1,0:T(8,128)S(1)}, u32[]{:S(2)}, u32[]{:S(2)}) collective-permute-start(f32[3,64,256]{2,1,0:T(8,128)S(1)} %get-tuple-element.133), channel_id=1, source_target_pairs={{4,8},{5,12},{8,1},{9,5},{0,0},{1,4},{12,9},{13,13},{6,10},{7,14},... | collective-permute-start | bytes 589832 | tf_op jit(solution)/shard_map/ppermute | solution.py:735
  146.6 2.1 %collective-permute-start.28 = (f32[3,64,256]{2,1,0:T(8,128)S(1)}, f32[3,64,256]{2,1,0:T(8,128)S(1)}, u32[]{:S(2)}, u32[]{:S(2)}) collective-permute-start(f32[3,64,256]{2,1,0:T(8,128)S(1)} %get-tuple-element.132), channel_id=1, source_target_pairs={{4,12},{5,0},{8,5},{9,13},{0,1},{1,4},{12,8},{13,9},{6,14},{7,2},{... | collective-permute-start | bytes 589832 | tf_op jit(solution)/shard_map/ppermute | solution.py:735
  148.7 0.2 select_select_fusion.1
  149.0 0.9 copy-done.10
  149.9 1.2 multiply_reduce_fusion
  151.1 0.6 divide_multiply_fusion
  151.7 2.4 %collective-permute-done.27 = f32[3,64,256]{2,1,0:T(8,128)S(1)} collective-permute-done((f32[3,64,256]{2,1,0:T(8,128)S(1)}, f32[3,64,256]{2,1,0:T(8,128)S(1)}, u32[]{:S(2)}, u32[]{:S(2)}) %collective-permute-start.27) | collective-permute-done | bytes 196640 | tf_op jit(solution)/shard_map/ppermute | solution.py:735
  154.1 1.6 collective-permute-done.28
  155.7 0.1 select_select_fusion.4
  155.8 0.8 pad_maximum_fusion.1
  (63 shorter events, 0.6 us)
Async XLA Ops:
  6.2 36.8 %collective-permute-start = (f32[608,512]{1,0:T(8,128)}, f32[608,512]{1,0:T(8,128)S(1)}, u32[]{:S(2)}, u32[]{:S(2)}) collective-permute-start(f32[608,512]{1,0:T(8,128)} %get-tuple-element.63.refs_8_.refs_2_), channel_id=1, source_target_pairs={{0,1},{1,0},{2,3},{3,2},{4,5},{5,4},{6,7},{7,6},{8,9},{9,8},{10,11... | collective-permute-start | bytes 3735560 | tf_op jit(solution)/shard_map/ppermute | solution.py:569
  6.3 16.1 %collective-permute-start.4 = (f32[352,512]{1,0:T(8,128)}, f32[352,512]{1,0:T(8,128)S(1)}, u32[]{:S(2)}, u32[]{:S(2)}) collective-permute-start(f32[352,512]{1,0:T(8,128)} %get-tuple-element.69), channel_id=1, source_target_pairs={{0,4},{8,5},{13,8},{1,9},{4,0},{5,1},{9,12},{12,13},{2,6},{10,7},{... | collective-permute-start | bytes 2162696 | tf_op jit(solution)/shard_map/ppermute | solution.py:564
  6.9 34.2 %collective-permute-start.5 = (f32[352,512]{1,0:T(8,128)}, f32[352,512]{1,0:T(8,128)S(1)}, u32[]{:S(2)}, u32[]{:S(2)}) collective-permute-start(f32[352,512]{1,0:T(8,128)} %get-tuple-element.70), channel_id=1, source_target_pairs={{8,4},{12,5},{1,8},{5,9},{0,0},{4,1},{9,12},{13,13},{10,6},{14,7},... | collective-permute-start | bytes 2162696 | tf_op jit(solution)/shard_map/ppermute | solution.py:564
  9.2 33.3 %collective-permute-start.6 = (f32[352,512]{1,0:T(8,128)}, f32[352,512]{1,0:T(8,128)S(1)}, u32[]{:S(2)}, u32[]{:S(2)}) collective-permute-start(f32[352,512]{1,0:T(8,128)} %get-tuple-element.71), channel_id=1, source_target_pairs={{12,4},{0,5},{5,8},{13,9},{1,0},{4,1},{8,12},{9,13},{14,6},{2,7},{... | collective-permute-start | bytes 2162696 | tf_op jit(solution)/shard_map/ppermute | solution.py:564
  42.5 20.9 %copy-start.4 = (f32[352,512]{1,0:T(8,128)}, f32[352,512]{1,0:T(8,128)S(1)}, u32[]{:S(2)}) copy-start(f32[352,512]{1,0:T(8,128)S(1)} %collective-permute-done.6.refs_4_.refs_0_) | copy-start | bytes 2162692
  42.5 2.8 %collective-permute-start.10 = (f32[352,512]{1,0:T(8,128)S(1)}, f32[352,512]{1,0:T(8,128)S(1)}, u32[]{:S(2)}, u32[]{:S(2)}) collective-permute-start(f32[352,512]{1,0:T(8,128)S(1)} %collective-permute-done.6.refs_4_.refs_0_), channel_id=1, source_target_pairs={{0,1},{1,0},{2,3},{3,2},{4,5},{5,4},{6,7},{7,6},{8,9},{9,8},{10,11... | collective-permute-start | bytes 2162696 | tf_op jit(solution)/shard_map/ppermute | solution.py:568
  42.5 4.7 %collective-permute-start.8 = (f32[352,512]{1,0:T(8,128)S(1)}, f32[352,512]{1,0:T(8,128)S(1)}, u32[]{:S(2)}, u32[]{:S(2)}) collective-permute-start(f32[352,512]{1,0:T(8,128)S(1)} %collective-permute-done.4.refs_2_.refs_0_), channel_id=1, source_target_pairs={{0,1},{1,0},{2,3},{3,2},{4,5},{5,4},{6,7},{7,6},{8,9},{9,8},{10,11... | collective-permute-start | bytes 2162696 | tf_op jit(solution)/shard_map/ppermute | solution.py:568
  43.0 1.9 %copy-start = (f32[1,1,256,512]{3,2,1,0:T(8,128)S(1)}, f32[1,1,256,512]{3,2,1,0:T(8,128)}, u32[]{:S(2)}) copy-start(f32[1,1,256,512]{3,2,1,0:T(8,128)} %param.8) | copy-start | bytes 1572868
  43.0 1.9 %copy-start.1 = (f32[1,1,256,512]{3,2,1,0:T(8,128)S(1)}, f32[1,1,256,512]{3,2,1,0:T(8,128)}, u32[]{:S(2)}) copy-start(f32[1,1,256,512]{3,2,1,0:T(8,128)} %param.12) | copy-start | bytes 1572868
  43.1 20.3 %copy-start.6 = (f32[608,512]{1,0:T(8,128)}, f32[608,512]{1,0:T(8,128)S(1)}, u32[]{:S(2)}) copy-start(f32[608,512]{1,0:T(8,128)S(1)} %collective-permute-done.refs_9_.refs_3_) | copy-start | bytes 3735556
  43.1 20.3 %copy-start.8 = (f32[608,512]{1,0:T(8,128)S(1)}, f32[608,512]{1,0:T(8,128)}, u32[]{:S(2)}) copy-start(f32[608,512]{1,0:T(8,128)} %get-tuple-element.63.refs_8_.refs_2_) | copy-start | bytes 3735556
  43.2 20.2 %collective-permute-start.7 = (f32[4,96,512]{2,1,0:T(8,128)S(1)}, f32[4,96,512]{2,1,0:T(8,128)S(1)}, u32[]{:S(2)}, u32[]{:S(2)}) collective-permute-start(f32[4,96,512]{2,1,0:T(8,128)S(1)} %pad_maximum_fusion.refs_0_), channel_id=1, source_target_pairs={{0,2},{2,0},{1,3},{3,1},{4,6},{6,4},{5,7},{7,5},{8,10},{10,8},{9,1... | collective-permute-start | bytes 2359304 | tf_op jit(solution)/shard_map/ppermute | solution.py:616
  43.8 4.7 %collective-permute-start.9 = (f32[352,512]{1,0:T(8,128)S(1)}, f32[352,512]{1,0:T(8,128)S(1)}, u32[]{:S(2)}, u32[]{:S(2)}) collective-permute-start(f32[352,512]{1,0:T(8,128)S(1)} %collective-permute-done.5.refs_3_.refs_1_), channel_id=1, source_target_pairs={{0,1},{1,0},{2,3},{3,2},{4,5},{5,4},{6,7},{7,6},{8,9},{9,8},{10,11... | collective-permute-start | bytes 2162696 | tf_op jit(solution)/shard_map/ppermute | solution.py:568
  45.2 26.4 %collective-permute-start.1 = (f32[256,512]{1,0:T(8,128)S(1)}, f32[256,512]{1,0:T(8,128)S(1)}, u32[]{:S(2)}, u32[]{:S(2)}) collective-permute-start(f32[256,512]{1,0:T(8,128)S(1)} %get-tuple-element.65), channel_id=1, source_target_pairs={{0,4},{8,5},{13,8},{1,9},{4,0},{5,1},{9,12},{12,13},{2,6},{10,7},{... | collective-permute-start | bytes 1572872 | tf_op jit(solution)/shard_map/ppermute | solution.py:564
  45.2 26.4 %collective-permute-start.2 = (f32[256,512]{1,0:T(8,128)S(1)}, f32[256,512]{1,0:T(8,128)S(1)}, u32[]{:S(2)}, u32[]{:S(2)}) collective-permute-start(f32[256,512]{1,0:T(8,128)S(1)} %get-tuple-element.66), channel_id=1, source_target_pairs={{8,4},{12,5},{1,8},{5,9},{0,0},{4,1},{9,12},{13,13},{10,6},{14,7},... | collective-permute-start | bytes 1572872 | tf_op jit(solution)/shard_map/ppermute | solution.py:564
  47.2 24.5 %collective-permute-start.3 = (f32[256,512]{1,0:T(8,128)S(1)}, f32[256,512]{1,0:T(8,128)S(1)}, u32[]{:S(2)}, u32[]{:S(2)}) collective-permute-start(f32[256,512]{1,0:T(8,128)S(1)} %get-tuple-element.67), channel_id=1, source_target_pairs={{12,4},{0,5},{5,8},{13,9},{1,0},{4,1},{8,12},{9,13},{14,6},{2,7},{... | collective-permute-start | bytes 1572872 | tf_op jit(solution)/shard_map/ppermute | solution.py:564
  71.7 4.9 %collective-permute-start.14 = (f32[512,512]{1,0:T(8,128)S(1)}, f32[512,512]{1,0:T(8,128)S(1)}, u32[]{:S(2)}, u32[]{:S(2)}) collective-permute-start(f32[512,512]{1,0:T(8,128)S(1)} %get-tuple-element.83.refs_6_), channel_id=1, source_target_pairs={{0,1},{1,0},{2,3},{3,2},{4,5},{5,4},{6,7},{7,6},{8,9},{9,8},{10,11... | collective-permute-start | bytes 3145736 | tf_op jit(solution)/shard_map/ppermute | solution.py:569
  72.1 3.0 %collective-permute-start.11 = (f32[256,512]{1,0:T(8,128)S(1)}, f32[256,512]{1,0:T(8,128)S(1)}, u32[]{:S(2)}, u32[]{:S(2)}) collective-permute-start(f32[256,512]{1,0:T(8,128)S(1)} %collective-permute-done.1.refs_0_), channel_id=1, source_target_pairs={{0,1},{1,0},{2,3},{3,2},{4,5},{5,4},{6,7},{7,6},{8,9},{9,8},{10,11... | collective-permute-start | bytes 1572872 | tf_op jit(solution)/shard_map/ppermute | solution.py:568
  72.2 3.6 %collective-permute-start.12 = (f32[256,512]{1,0:T(8,128)S(1)}, f32[256,512]{1,0:T(8,128)S(1)}, u32[]{:S(2)}, u32[]{:S(2)}) collective-permute-start(f32[256,512]{1,0:T(8,128)S(1)} %collective-permute-done.2.refs_1_), channel_id=1, source_target_pairs={{0,1},{1,0},{2,3},{3,2},{4,5},{5,4},{6,7},{7,6},{8,9},{9,8},{10,11... | collective-permute-start | bytes 1572872 | tf_op jit(solution)/shard_map/ppermute | solution.py:568
  72.6 4.0 %collective-permute-start.13 = (f32[256,512]{1,0:T(8,128)S(1)}, f32[256,512]{1,0:T(8,128)S(1)}, u32[]{:S(2)}, u32[]{:S(2)}) collective-permute-start(f32[256,512]{1,0:T(8,128)S(1)} %collective-permute-done.3.refs_2_), channel_id=1, source_target_pairs={{0,1},{1,0},{2,3},{3,2},{4,5},{5,4},{6,7},{7,6},{8,9},{9,8},{10,11... | collective-permute-start | bytes 1572872 | tf_op jit(solution)/shard_map/ppermute | solution.py:568
  87.9 1.6 %copy-start.3 = (f32[640,512]{1,0:T(8,128)}, f32[640,512]{1,0:T(8,128)S(1)}, u32[]{:S(2)}) copy-start(f32[640,512]{1,0:T(8,128)S(1)} %get-tuple-element.86) | copy-start | bytes 3932164
  87.9 9.1 %collective-permute-start.15 = (f32[640,512]{1,0:T(8,128)S(1)}, f32[640,512]{1,0:T(8,128)S(1)}, u32[]{:S(2)}, u32[]{:S(2)}) collective-permute-start(f32[640,512]{1,0:T(8,128)S(1)} %get-tuple-element.86), channel_id=1, source_target_pairs={{0,1},{1,0},{2,3},{3,2},{4,5},{5,4},{6,7},{7,6},{8,9},{9,8},{10,11... | collective-permute-start | bytes 3932168 | tf_op jit(solution)/shard_map/ppermute | solution.py:572
  96.8 5.6 %copy-start.2 = (f32[256,512]{1,0:T(8,128)}, f32[256,512]{1,0:T(8,128)S(1)}, u32[]{:S(2)}) copy-start(f32[256,512]{1,0:T(8,128)S(1)} %get-tuple-element.112) | copy-start | bytes 1572868
  96.8 5.6 %copy-start.5 = (f32[352,512]{1,0:T(8,128)S(1)}, f32[352,512]{1,0:T(8,128)}, u32[]{:S(2)}) copy-start(f32[352,512]{1,0:T(8,128)} %copy-done.4) | copy-start | bytes 2162692
  96.8 5.6 %copy-start.7 = (f32[608,512]{1,0:T(8,128)S(1)}, f32[608,512]{1,0:T(8,128)}, u32[]{:S(2)}) copy-start(f32[608,512]{1,0:T(8,128)} %copy-done.6) | copy-start | bytes 3735556
  96.8 18.9 %collective-permute-start.20 = (f32[512,512]{1,0:T(8,128)}, f32[512,512]{1,0:T(8,128)}, u32[]{:S(2)}, u32[]{:S(2)}) collective-permute-start(f32[512,512]{1,0:T(8,128)} %get-tuple-element.111), channel_id=1, source_target_pairs={{0,1},{1,0},{2,3},{3,2},{4,5},{5,4},{6,7},{7,6},{8,9},{9,8},{10,11... | collective-permute-start | bytes 3145736 | tf_op jit(solution)/shard_map/ppermute | solution.py:572
  97.0 15.5 %copy-start.11 = (f32[640,512]{1,0:T(8,128)}, f32[640,512]{1,0:T(8,128)S(1)}, u32[]{:S(2)}) copy-start(f32[640,512]{1,0:T(8,128)S(1)} %collective-permute-done.15) | copy-start | bytes 3932164
  97.2 16.3 %collective-permute-start.16 = (f32[128,512]{1,0:T(8,128)S(1)}, f32[128,512]{1,0:T(8,128)S(1)}, u32[]{:S(2)}, u32[]{:S(2)}) collective-permute-start(f32[128,512]{1,0:T(8,128)S(1)} %get-tuple-element.102), channel_id=1, source_target_pairs={{4,0},{5,8},{8,13},{9,1},{0,4},{1,5},{12,9},{13,12},{6,2},{7,10},{... | collective-permute-start | bytes 786440 | tf_op jit(solution)/shard_map/ppermute | solution.py:582
  97.2 16.2 %collective-permute-start.17 = (f32[128,512]{1,0:T(8,128)S(1)}, f32[128,512]{1,0:T(8,128)S(1)}, u32[]{:S(2)}, u32[]{:S(2)}) collective-permute-start(f32[128,512]{1,0:T(8,128)S(1)} %get-tuple-element.103), channel_id=1, source_target_pairs={{4,8},{5,12},{8,1},{9,5},{0,0},{1,4},{12,9},{13,13},{6,10},{7,14},... | collective-permute-start | bytes 786440 | tf_op jit(solution)/shard_map/ppermute | solution.py:582
  100.5 13.0 %collective-permute-start.18 = (f32[128,512]{1,0:T(8,128)S(1)}, f32[128,512]{1,0:T(8,128)S(1)}, u32[]{:S(2)}, u32[]{:S(2)}) collective-permute-start(f32[128,512]{1,0:T(8,128)S(1)} %get-tuple-element.104), channel_id=1, source_target_pairs={{4,12},{5,0},{8,5},{9,13},{0,1},{1,4},{12,8},{13,9},{6,14},{7,2},{... | collective-permute-start | bytes 786440 | tf_op jit(solution)/shard_map/ppermute | solution.py:582
  102.4 12.0 %copy-start.18 = (f32[1,1,256]{2,1,0:T(1,128)S(1)}, f32[1,1,256]{2,1,0:T(1,128)}, u32[]{:S(2)}) copy-start(f32[1,1,256]{2,1,0:T(1,128)} %param.11) | copy-start | bytes 3076
  112.5 0.9 copy-start.9
  113.4 0.7 copy-start.12
  113.4 0.8 copy-start.14
  113.5 0.9 copy-start.16
  114.3 6.6 %collective-permute-start.19 = (f32[768,512]{1,0:T(8,128)S(1)}, f32[768,512]{1,0:T(8,128)}, u32[]{:S(2)}, u32[]{:S(2)}) collective-permute-start(f32[768,512]{1,0:T(8,128)S(1)} %get-tuple-element.108), channel_id=1, source_target_pairs={{0,1},{1,0},{2,3},{3,2},{4,5},{5,4},{6,7},{7,6},{8,9},{9,8},{10,11... | collective-permute-start | bytes 4718600 | tf_op jit(solution)/shard_map/ppermute | solution.py:572
  114.3 6.5 %copy-start.13 = (f32[128,512]{1,0:T(8,128)S(1)}, f32[128,512]{1,0:T(8,128)}, u32[]{:S(2)}) copy-start(f32[128,512]{1,0:T(8,128)} %copy-done.12) | copy-start | bytes 786436
  114.4 6.5 %copy-start.15 = (f32[128,512]{1,0:T(8,128)S(1)}, f32[128,512]{1,0:T(8,128)}, u32[]{:S(2)}) copy-start(f32[128,512]{1,0:T(8,128)} %copy-done.14) | copy-start | bytes 786436
  114.4 6.5 %copy-start.17 = (f32[128,512]{1,0:T(8,128)S(1)}, f32[128,512]{1,0:T(8,128)}, u32[]{:S(2)}) copy-start(f32[128,512]{1,0:T(8,128)} %copy-done.16) | copy-start | bytes 786436
  114.4 28.8 %collective-permute-start.24 = (f32[4,3,64,256]{3,2,1,0:T(8,128)}, f32[4,3,64,256]{3,2,1,0:T(8,128)S(1)}, u32[]{:S(2)}, u32[]{:S(2)}) collective-permute-start(f32[4,3,64,256]{3,2,1,0:T(8,128)} %bitcast.42), channel_id=1, source_target_pairs={{0,2},{2,0},{1,3},{3,1},{4,6},{6,4},{5,7},{7,5},{8,10},{10,8},{9,1... | collective-permute-start | bytes 2359304 | tf_op jit(solution)/shard_map/ppermute | solution.py:733
  117.3 11.5 %collective-permute-start.21 = (f32[256,512]{1,0:T(8,128)S(1)}, f32[256,512]{1,0:T(8,128)S(1)}, u32[]{:S(2)}, u32[]{:S(2)}) collective-permute-start(f32[256,512]{1,0:T(8,128)S(1)} %get-tuple-element.130), channel_id=1, source_target_pairs={{4,0},{5,8},{8,13},{9,1},{0,4},{1,5},{12,9},{13,12},{6,2},{7,10},{... | collective-permute-start | bytes 1572872 | tf_op jit(solution)/shard_map/ppermute | solution.py:582
  117.6 16.7 %collective-permute-start.22 = (f32[256,512]{1,0:T(8,128)S(1)}, f32[256,512]{1,0:T(8,128)S(1)}, u32[]{:S(2)}, u32[]{:S(2)}) collective-permute-start(f32[256,512]{1,0:T(8,128)S(1)} %get-tuple-element.129), channel_id=1, source_target_pairs={{4,8},{5,12},{8,1},{9,5},{0,0},{1,4},{12,9},{13,13},{6,10},{7,14},... | collective-permute-start | bytes 1572872 | tf_op jit(solution)/shard_map/ppermute | solution.py:582
  122.1 21.1 %collective-permute-start.23 = (f32[256,512]{1,0:T(8,128)S(1)}, f32[256,512]{1,0:T(8,128)S(1)}, u32[]{:S(2)}, u32[]{:S(2)}) collective-permute-start(f32[256,512]{1,0:T(8,128)S(1)} %slice_add_fusion.1), channel_id=1, source_target_pairs={{4,12},{5,0},{8,5},{9,13},{0,1},{1,4},{12,8},{13,9},{6,14},{7,2},{... | collective-permute-start | bytes 1572872 | tf_op jit(solution)/shard_map/ppermute | solution.py:582
  143.4 8.3 %collective-permute-start.25 = (f32[3,64,256]{2,1,0:T(8,128)S(1)}, f32[3,64,256]{2,1,0:T(8,128)S(1)}, u32[]{:S(2)}, u32[]{:S(2)}) collective-permute-start(f32[3,64,256]{2,1,0:T(8,128)S(1)} %get-tuple-element.131), channel_id=1, source_target_pairs={{0,1},{1,0},{2,3},{3,2},{4,5},{5,4},{6,7},{7,6},{8,9},{9,8},{10,11... | collective-permute-start | bytes 589832 | tf_op jit(solution)/shard_map/ppermute | solution.py:738
  143.5 8.2 %collective-permute-start.26 = (f32[3,64,256]{2,1,0:T(8,128)S(1)}, f32[3,64,256]{2,1,0:T(8,128)S(1)}, u32[]{:S(2)}, u32[]{:S(2)}) collective-permute-start(f32[3,64,256]{2,1,0:T(8,128)S(1)} %get-tuple-element.134), channel_id=1, source_target_pairs={{4,0},{5,8},{8,13},{9,1},{0,4},{1,5},{12,9},{13,12},{6,2},{7,10},{... | collective-permute-start | bytes 589832 | tf_op jit(solution)/shard_map/ppermute | solution.py:735
  144.6 9.5 %collective-permute-start.27 = (f32[3,64,256]{2,1,0:T(8,128)S(1)}, f32[3,64,256]{2,1,0:T(8,128)S(1)}, u32[]{:S(2)}, u32[]{:S(2)}) collective-permute-start(f32[3,64,256]{2,1,0:T(8,128)S(1)} %get-tuple-element.133), channel_id=1, source_target_pairs={{4,8},{5,12},{8,1},{9,5},{0,0},{1,4},{12,9},{13,13},{6,10},{7,14},... | collective-permute-start | bytes 589832 | tf_op jit(solution)/shard_map/ppermute | solution.py:735
  146.6 9.0 %collective-permute-start.28 = (f32[3,64,256]{2,1,0:T(8,128)S(1)}, f32[3,64,256]{2,1,0:T(8,128)S(1)}, u32[]{:S(2)}, u32[]{:S(2)}) collective-permute-start(f32[3,64,256]{2,1,0:T(8,128)S(1)} %get-tuple-element.132), channel_id=1, source_target_pairs={{4,12},{5,0},{8,5},{9,13},{0,1},{1,4},{12,8},{13,9},{6,14},{7,2},{... | collective-permute-start | bytes 589832 | tf_op jit(solution)/shard_map/ppermute | solution.py:735
  148.9 1.0 copy-start.10

commit v8 on v7

--- a/solution.py
+++ b/solution.py
@@ -17,7 +17,6 @@
 BF16 = jnp.bfloat16
 NN = ((1,), (0,))
 NT = ((1,), (1,))
-GROUP = 2
 HBM = pl.BlockSpec(memory_space=pltpu.MemorySpace.HBM)
 VMEM = pl.BlockSpec(memory_space=pltpu.VMEM)
 
@@ -173,32 +172,25 @@
         copy.wait()
 
 
-def fetch_rows(near, far, own, got, buffers, sems):
-    half = buffers[0].shape[1] // 2
+def fetch_rows(rounds, own, got, side, buffers, sems):
+    half = buffers[0].shape[0] // CELL
     place, core = position()
     mine = core == place - home_of(0)
-    last = len(near)
-    for block in range(last):
-        for which in range(2):
-            rows = pl.ds(which * half, half)
-            for side, group in enumerate((near, far)):
-                pltpu.make_async_copy(
-                    group[block].at[rows],
-                    buffers[which].at[block, pl.ds(side * half, half)],
-                    sems.at[block, which * 2 + side],
-                ).start()
+    for which in range(2):
+        for turn, piece in enumerate(rounds):
+            pltpu.make_async_copy(
+                piece.at[pl.ds(which * half, half)],
+                buffers[which].at[pl.ds(turn * half, half)],
+                sems.at[which, turn],
+            ).start()
 
     def local(source):
         for which in range(2):
-            for side in range(2):
-                pltpu.make_async_copy(
-                    source.at[pl.ds((which * 2 + side) * half, half)],
-                    buffers[which].at[last, pl.ds(side * half, half)],
-                    sems.at[last, which * 2 + side],
-                ).start()
-
-    if own is None:
-        return
+            pltpu.make_async_copy(
+                source.at[pl.ds((which * 2 + side) * half, half)],
+                buffers[which].at[pl.ds(ROUNDS * half, half)],
+                sems.at[which, ROUNDS],
+            ).start()
 
     @pl.when(mine)
     def _():
@@ -209,18 +201,13 @@
         local(got)
 
 
-def take_rows(buffers, group, sems):
-    size, depth = buffers[0].shape[1:]
-    half = size // 2
-    for each in range(GROUP):
-        block = group * GROUP + each
-        for part in range(4):
-            view = buffers[part // 2].at[block, pl.ds((part % 2) * half, half)]
-            pltpu.make_async_copy(view, view, sems.at[block, part]).wait()
-    first, second = (
-        buffer[pl.ds(group * GROUP, GROUP)].reshape(GROUP * size, depth) for buffer in buffers
-    )
-    return split(first), split(second)
+def take_rows(buffers, sems):
+    half = buffers[0].shape[0] // CELL
+    for which in range(2):
+        for chunk in range(CELL):
+            view = buffers[which].at[pl.ds(chunk * half, half)]
+            pltpu.make_async_copy(view, view, sems.at[which, chunk]).wait()
+    return split(buffers[0][...]), split(buffers[1][...])
 
 
 def row_starts(cells, reps, rows):
@@ -273,17 +260,19 @@
             )
     for copy in copies:
         copy.start()
-    fetch_rows(near, far, own, got, (keys, targets), row_sems)
+    for side, rounds in enumerate((near, far)):
+        buffers = keys.at[side], targets.at[side]
+        fetch_rows(rounds, own, got, side, buffers, row_sems.at[side])
     for copy in copies:
         copy.wait()
     for which in range(3):
         store_split(wide, (which,), weights[which])
-    size = keys.shape[1] * GROUP
-
-    @pl.loop(0, CELL // GROUP)
-    def _(group):
-        key, target = take_rows((keys, targets), group, row_sems)
-        where = pl.ds(pl.multiple_of(group * size, size), size)
+    size = keys.shape[1]
+
+    @pl.loop(0, 2)
+    def _(side):
+        key, target = take_rows((keys.at[side], targets.at[side]), row_sems.at[side])
+        where = pl.ds(pl.multiple_of(side * size, size), size)
         gate_pre = dot3(key, pair_of(wide, 0), NN)
         up_pre = dot3(key, pair_of(wide, 1), NN)
         back = dot3(target, pair_of(wide, 2), NN)
@@ -311,55 +300,54 @@
         high[which], low[which] = split(moved * (jnp.sqrt(old) / jnp.sqrt(new)))
 
 
-def read_kernel(*refs):
-    near, far, (own, got, high, low), refs = refs[:3], refs[3:6], refs[6:10], refs[10:]
-    totals, near_out, far_out, scratch = refs[0], refs[1:4], refs[4], refs[5:]
-    queries, cots, turned, acts, sent, row_sems, out_sems = scratch
-    fetch_rows(near, far, own, got, (queries, cots), row_sems)
-    size = queries.shape[1]
-    half = size // 2
+def read_kernel(side, *refs):
+    rounds, (own, got, high, low), refs = refs[:3], refs[3:7], refs[7:]
+    before, refs = (refs[:2], refs[2:]) if side else ((), refs)
+    main, refs = (refs[0], refs[1:]) if side else (None, refs)
+    round_out, rest_out = (refs[:3], refs[3]) if side == 0 else (None, refs[0])
+    refs = refs[4:] if side == 0 else refs[1:]
+    turned, acts, queries, cots, sent, row_sems, out_sems = refs
+    half = queries.shape[0] // CELL
+    fetch_rows(rounds, own, got, side, (queries, cots), row_sems)
 
     def weight(which):
         return high[which], low[which]
 
-    def outgoing(block):
-        if block < ROUNDS:
-            return [
-                (sent.at[block, pl.ds(0, half)], near_out[block]),
-                (sent.at[block, pl.ds(half, half)], far_out.at[pl.ds(block * half, half)]),
-            ]
-        return [(sent.at[block], far_out.at[pl.ds(ROUNDS * half, size)])]
-
-    @pl.loop(0, CELL // GROUP)
-    def _(group):
-        query, cot = take_rows((queries, cots), group, row_sems)
-        where = pl.ds(pl.multiple_of(group * GROUP * size, GROUP * size), GROUP * size)
-        gate_pre = dot3(query, weight(0), NN)
-        up_pre = dot3(query, weight(1), NN)
-        back = dot3(cot, weight(2), NN)
-        _, act, slope = silu_parts(gate_pre)
-        gate_back = split(back * up_pre * slope)
-        up_back = split(back * act)
-        for part in range(2):
-            acts[part, 0, where] = gate_back[part]
-            acts[part, 1, where] = up_back[part]
-            turned[part, 0, :, where] = query[part].T
-            turned[part, 1, :, where] = cot[part].T
-        store_split(acts, (2, where), act * up_pre)
-        result = dot3(gate_back, weight(0), NT) + dot3(up_back, weight(1), NT)
-        sent[pl.ds(group * GROUP, GROUP)] = result.reshape(GROUP, size, result.shape[1])
-        for number in range(CELL):
-
-            @pl.when(group == number // GROUP)
-            def _():
-                for side, (source, out) in enumerate(outgoing(number)):
-                    pltpu.make_async_copy(source, out, out_sems.at[number, side]).start()
-
-    for which in range(3):
-        totals[which] = dot3(pair_of(turned, which // 2), pair_of(acts, which), NN)
-    for block in range(CELL):
-        for side, (source, out) in enumerate(outgoing(block)):
-            pltpu.make_async_copy(source, out, out_sems.at[block, side]).wait()
+    query, cot = take_rows((queries, cots), row_sems)
+    gate_pre = dot3(query, weight(0), NN)
+    up_pre = dot3(query, weight(1), NN)
+    back = dot3(cot, weight(2), NN)
+    _, act, slope = silu_parts(gate_pre)
+    gate_back = split(back * up_pre * slope)
+    up_back = split(back * act)
+    sent[...] = dot3(gate_back, weight(0), NT) + dot3(up_back, weight(1), NT)
+    if side == 0:
+        copies = [
+            pltpu.make_async_copy(sent.at[pl.ds(turn * half, half)], out, out_sems.at[turn])
+            for turn, out in enumerate(round_out)
+        ]
+        copies.append(
+            pltpu.make_async_copy(
+                sent.at[pl.ds(ROUNDS * half, half)], rest_out, out_sems.at[ROUNDS]
+            )
+        )
+    else:
+        copies = [pltpu.make_async_copy(sent, rest_out, out_sems.at[0])]
+    for copy in copies:
+        copy.start()
+    for part in range(2):
+        acts[part, 0] = gate_back[part]
+        acts[part, 1] = up_back[part]
+        turned[part, 0] = query[part].T
+        turned[part, 1] = cot[part].T
+    store_split(acts, (2,), act * up_pre)
+    if side:
+        for which in range(3):
+            main[which] = dot3(
+                pair_of(before[0], which // 2), pair_of(before[1], which), NN
+            ) + dot3(pair_of(turned, which // 2), pair_of(acts, which), NN)
+    for copy in copies:
+        copy.wait()
 
 
 def renew_back_kernel(cells, weights, steps, totals, cots, direct):
@@ -379,16 +367,38 @@
         store_split(cots, (which,), -moved_cot)
 
 
-def write_grads(cells, reps, turned, direct, parts, pieces, grads, grad_sems):
+def weight_grad_kernel(cells, reps, *refs):
+    near, far, (own, got, turned, direct), refs = refs[:3], refs[3:6], refs[6:10], refs[10:]
+    (cots, gates, ups, backs), refs = refs[:4], refs[4:]
+    acts, pieces, refs = refs[0], refs[1 : 1 + reps], refs[1 + reps :]
+    keys, targets, grads, row_sems, grad_sems = refs
+    for side, rounds in enumerate((near, far)):
+        buffers = keys.at[side], targets.at[side]
+        fetch_rows(rounds, own, got, side, buffers, row_sems.at[side])
+    size = keys.shape[1]
+
+    @pl.loop(0, 2)
+    def _(side):
+        key, target = take_rows((keys.at[side], targets.at[side]), row_sems.at[side])
+        where = pl.ds(pl.multiple_of(side * size, size), size)
+        gate_back_cot = dot3(key, pair_of(cots, 0), NN)
+        up_back_cot = dot3(key, pair_of(cots, 1), NN)
+        hidden_cot = dot3(target, pair_of(cots, 2), NN)
+        gate_pre, up_pre, back = gates[where], ups[where], backs[where]
+        sigma, act, slope = silu_parts(gate_pre)
+        bend = sigma * (1.0 - sigma) * (2.0 + gate_pre * (1.0 - 2.0 * sigma))
+        mixed = gate_back_cot * slope
+        store_split(
+            acts,
+            (0, where),
+            gate_back_cot * back * up_pre * bend
+            + (up_back_cot * back + hidden_cot * up_pre) * slope,
+        )
+        store_split(acts, (1, where), mixed * back + hidden_cot * act)
+        store_split(acts, (2, where), mixed * up_pre + up_back_cot * act)
+
     for which in range(3):
-        total = direct[which]
-        begin = 0
-        for acts in parts:
-            span = pl.ds(begin, acts.shape[2])
-            begin += acts.shape[2]
-            left = turned[0, which // 2, :, span], turned[1, which // 2, :, span]
-            total = total + dot3(left, pair_of(acts, which), NN)
-        grads[which] = total
+        grads[which] = direct[which] + dot3(pair_of(turned, which // 2), pair_of(acts, which), NN)
     rows = pieces[0].shape[-2]
     copies = []
     place, core = position()
@@ -409,91 +419,47 @@
     run_copies(copies)
 
 
-def token_grad_kernel(cells, reps, first, last, *refs):
-    rounds = min(last, ROUNDS) - first
-    near, far, refs = refs[:rounds], refs[rounds : 2 * rounds], refs[2 * rounds :]
-    own, got, final = None, None, last > ROUNDS
-    if final:
-        (own, got, turned, direct, before), refs = refs[:5], refs[5:]
-    (weights, cots, gates, ups, backs), refs = refs[:5], refs[5:]
-    near_out, far_out, refs = refs[:rounds], refs[rounds], refs[rounds + 1 :]
-    if final:
-        pieces, (acts, grads, grad_sems), refs = refs[:reps], refs[reps : reps + 3], refs[reps + 3 :]
-    else:
-        acts, refs = refs[0], refs[1:]
-    keys, targets, wide, sent, row_sems, out_sems = refs
-    fetch_rows(near, far, own, got, (keys, targets), row_sems)
-    size = sent.shape[2]
-    half = size // 2
+def token_grad_kernel(side, *refs):
+    (weights, cots, acts, gates, ups, backs), refs = refs[:6], refs[6:]
+    outs, (wide, sent, out_sems) = refs[:-3], refs[-3:]
+    size = sent.shape[1]
+    half = size // CELL
     for which in range(3):
         store_split(wide, (which,), weights[which])
-
-    def outgoing(number):
-        if number < rounds:
-            near = [
-                (sent.at[which, number, pl.ds(0, half)], near_out[number].at[pl.ds(which * half, half)])
-                for which in range(2)
-            ]
-            far = [
-                (
-                    sent.at[which, number, pl.ds(half, half)],
-                    far_out.at[pl.ds(number * size + which * half, half)],
+    where = pl.ds(side * size, size)
+    gate_pre, up_pre, back = gates[where], ups[where], backs[where]
+    _, act, slope = silu_parts(gate_pre)
+    sent[1] = dot3(pair_of(acts, 2, where), pair_of(wide, 2), NT) + dot3(
+        split(act * up_pre), pair_of(cots, 2), NT
+    )
+
+    def copies_of(which):
+        copies = []
+        for chunk in range(CELL):
+            out = outs[chunk] if side == 0 else outs[0].at[pl.ds(chunk * 2 * half, 2 * half)]
+            copies.append(
+                pltpu.make_async_copy(
+                    sent.at[which, pl.ds(chunk * half, half)],
+                    out.at[pl.ds(which * half, half)],
+                    out_sems.at[which, chunk],
                 )
-                for which in range(2)
-            ]
-            return near + far
-        return [
-            (sent.at[which, number], far_out.at[pl.ds((rounds + which) * size, size)])
-            for which in range(2)
-        ]
-
-    @pl.loop(0, (last - first) // GROUP)
-    def _(group):
-        key, target = take_rows((keys, targets), group, row_sems)
-        many = GROUP * size
-        where = pl.ds(pl.multiple_of(first * size + group * many, many), many)
-        here = pl.ds(pl.multiple_of(group * many, many), many)
-        there = pl.ds(group * GROUP, GROUP)
-        gate_back_cot = dot3(key, pair_of(cots, 0), NN)
-        up_back_cot = dot3(key, pair_of(cots, 1), NN)
-        hidden_cot = dot3(target, pair_of(cots, 2), NN)
-        gate_pre, up_pre, back = gates[where], ups[where], backs[where]
-        sigma, act, slope = silu_parts(gate_pre)
-        bend = sigma * (1.0 - sigma) * (2.0 + gate_pre * (1.0 - 2.0 * sigma))
-        mixed = gate_back_cot * slope
-        gate_cot = split(
-            gate_back_cot * back * up_pre * bend
-            + (up_back_cot * back + hidden_cot * up_pre) * slope
-        )
-        up_cot = split(mixed * back + hidden_cot * act)
-        back_cot = split(mixed * up_pre + up_back_cot * act)
-        for part in range(2):
-            acts[part, 0, here] = gate_cot[part]
-            acts[part, 1, here] = up_cot[part]
-            acts[part, 2, here] = back_cot[part]
-        key_part = (
-            dot3(gate_cot, pair_of(wide, 0), NT)
-            + dot3(up_cot, pair_of(wide, 1), NT)
-            + dot3(split(back * up_pre * slope), pair_of(cots, 0), NT)
-            + dot3(split(back * act), pair_of(cots, 1), NT)
-        )
-        target_part = dot3(back_cot, pair_of(wide, 2), NT) + dot3(
-            split(act * up_pre), pair_of(cots, 2), NT
-        )
-        sent[0, there] = key_part.reshape(GROUP, size, key_part.shape[1])
-        sent[1, there] = target_part.reshape(GROUP, size, target_part.shape[1])
-        for each in range(last - first):
-
-            @pl.when(group == each // GROUP)
-            def _():
-                for side, (source, out) in enumerate(outgoing(each)):
-                    pltpu.make_async_copy(source, out, out_sems.at[each, side]).start()
-
-    if final:
-        write_grads(cells, reps, turned, direct, (before, acts), pieces, grads, grad_sems)
-    for each in range(last - first):
-        for side, (source, out) in enumerate(outgoing(each)):
-            pltpu.make_async_copy(source, out, out_sems.at[each, side]).wait()
+            )
+        return copies
+
+    late = copies_of(1)
+    for copy in late:
+        copy.start()
+    sent[0] = (
+        dot3(pair_of(acts, 0, where), pair_of(wide, 0), NT)
+        + dot3(pair_of(acts, 1, where), pair_of(wide, 1), NT)
+        + dot3(split(back * up_pre * slope), pair_of(cots, 0), NT)
+        + dot3(split(back * act), pair_of(cots, 1), NT)
+    )
+    early = copies_of(0)
+    for copy in early:
+        copy.start()
+    for copy in late + early:
+        copy.wait()
 
 
 def call(kernel, inputs, in_specs, outs, out_specs, scratch, flops=0, grant=26):
@@ -568,33 +534,24 @@
         far = [lax.ppermute(piece, "head", SWAP) for piece in near]
         return near + far + [local, lax.ppermute(local, "head", SWAP)]
 
-    def combine(near, far):
-        across = lax.ppermute(far, "head", SWAP)
+    def hand_back(near, far):
         length = near[0].shape[0]
-        found = [
-            part + across[number * length : (number + 1) * length]
-            for number, part in enumerate(near)
+        totals = [
+            part + far[turn * length : (turn + 1) * length]
+            for turn, part in enumerate(near[:ROUNDS])
         ]
-        return found, far[len(near) * length :] + across[len(near) * length :]
-
-    def hand_back(totals, first):
-        return [
-            lax.ppermute(total, PLACE, flipped(pairs[first + number]))
-            for number, total in enumerate(totals)
-        ]
-
-    def settle(back, local):
+        return [lax.ppermute(totals[turn], PLACE, flipped(pairs[turn])) for turn in range(ROUNDS)]
+
+    def settle(back, first, second):
         def choose(turn):
             return jnp.where(turn == 0, back[0], jnp.where(turn == 1, back[1], back[2]))
 
-        low, high = choose(turn0), choose(turn1)
-        found = []
-        for which in range(low.shape[0] // half):
-            span = slice(which * half, (which + 1) * half)
-            remote = jnp.concatenate((low[span], high[span]))
-            here = local[which * 2 * half : (which + 1) * 2 * half]
-            found.append(jnp.where(at_home, here, remote))
-        return found
+        low = jnp.where(at_home, first, choose(turn0))
+        high = jnp.where(at_home, second, choose(turn1))
+        return [
+            jnp.concatenate((low[at : at + half], high[at : at + half]))
+            for at in range(0, low.shape[0], half)
+        ]
 
     inner_near, inner_local, kept = gather(
         key_rows[0, 0],
@@ -617,14 +574,13 @@
     if cells > 1:
         parts = [lax.all_gather(jnp.stack(parts), "tok", axis_index_groups=cell_groups)]
 
-    size = 2 * half
-    count = CELL * size
+    size = CELL * half
+    count = 2 * size
     square = shape((3, width, cols), F32)
     tall = shape((count, cols), F32)
     product = 6 * count * width * cols
-    buffers = [pltpu.VMEM((CELL, size, depth), F32)] * 2
-    turned = pltpu.VMEM((2, 2, depth, count), BF16)
-    acts = pltpu.VMEM((2, 3, count, cols), BF16)
+    buffers = [pltpu.VMEM((size, depth), F32)] * 2
+    both = [pltpu.VMEM((2, size, depth), F32)] * 2
     split_square = pltpu.VMEM((2, 3, width, cols), BF16)
     weights, gates, ups, backs, key_turned, steps = call(
         functools.partial(inner_kernel, cells, reps),
@@ -632,7 +588,13 @@
         [HBM] * (len(parts) + 8),
         [square, tall, tall, tall, shape((2, 2, depth, count), BF16), square],
         [VMEM] * 6,
-        buffers + [split_square, acts, dma((CELL, 4)), dma((cells * reps * CELL * 4,))],
+        both
+        + [
+            split_square,
+            pltpu.VMEM((2, 3, count, cols), BF16),
+            dma((2, 2, CELL)),
+            dma((cells * reps * CELL * 4,)),
+        ],
         6 * product,
     )
     if cells > 1:
@@ -644,17 +606,29 @@
     *read_near, read_local, high = lax.optimization_barrier((*read_near, read_local, high))
     read_rows = spread(list(read_near), read_local)
     piece = shape((half, depth), F32)
-    read = call(
-        read_kernel,
-        read_rows + [high, low],
-        [HBM] * 8 + [VMEM] * 2,
-        [square] + [piece] * ROUNDS + [shape((ROUNDS * half + size, depth), F32)],
-        [VMEM] + [HBM] * (ROUNDS + 1),
-        buffers
-        + [turned, acts, pltpu.VMEM((CELL, size, depth), F32), dma((CELL, 4)), dma((CELL, 2))],
-        8 * product,
-    )
-    totals = read[0]
+    turned = shape((2, 2, depth, size), BF16)
+    acts = shape((2, 3, size, cols), BF16)
+    read_scratch = buffers + [pltpu.VMEM((size, depth), F32), dma((2, CELL)), dma((CELL,))]
+    *query_near, query_first, turned_first, acts_first = call(
+        functools.partial(read_kernel, 0),
+        read_rows[:ROUNDS] + read_rows[2 * ROUNDS :] + [high, low],
+        [HBM] * (ROUNDS + 2) + [VMEM] * 2,
+        [piece] * CELL + [turned, acts],
+        [HBM] * CELL + [VMEM] * 2,
+        read_scratch,
+        5 * product // 2,
+        18,
+    )
+    totals, query_far = call(
+        functools.partial(read_kernel, 1),
+        read_rows[ROUNDS:] + [high, low, turned_first, acts_first],
+        [HBM] * (ROUNDS + 2) + [VMEM] * 4,
+        [square, shape((size, depth), F32)],
+        [VMEM, HBM],
+        [pltpu.VMEM(turned.shape, BF16), pltpu.VMEM(acts.shape, BF16)] + read_scratch,
+        11 * product // 2,
+        18,
+    )
     if cells > 1:
         totals = lax.psum(totals, "tok", axis_index_groups=cell_groups)
     cots, direct = call(
@@ -665,63 +639,58 @@
         [VMEM] * 2,
         [],
     )
-    middle = 2
-
-    def token_grads(first, last, cots, *more):
-        rounds = min(last, ROUNDS) - first
-        span = slice(first, first + rounds)
-        inputs = inner_rows[:ROUNDS][span] + inner_rows[ROUNDS : 2 * ROUNDS][span]
-        if more:
-            inputs = inputs + inner_rows[2 * ROUNDS :]
-        blocks = last - first
-        specs = [HBM] * len(inputs) + [VMEM] * (len(more) + 5)
-        outs = [shape((size, depth), F32)] * rounds
-        outs.append(shape((size * (2 * blocks - rounds), depth), F32))
-        acts = (2, 3, blocks * size, cols)
-        if more:
-            outs += [shape((cells, CELL, 3, rows, cols), F32)] * reps
-            scratch = [
-                pltpu.VMEM(acts, BF16),
-                pltpu.VMEM((3, width, cols), F32),
-                dma((cells * reps * CELL,)),
-            ]
-            out_specs = [HBM] * len(outs)
-        else:
-            out_specs = [HBM] * len(outs) + [VMEM]
-            outs.append(shape(acts, BF16))
-            scratch = []
-        outs = call(
-            functools.partial(token_grad_kernel, cells, reps, first, last),
-            inputs + [*more, weights, cots, gates, ups, backs],
-            specs,
+    acts_cot, *given = call(
+        functools.partial(weight_grad_kernel, cells, reps),
+        inner_rows + [key_turned, direct, cots, gates, ups, backs],
+        [HBM] * 8 + [VMEM] * 6,
+        [shape((2, 3, count, cols), BF16)] + [shape((cells, CELL, 3, rows, cols), F32)] * reps,
+        [VMEM] + [HBM] * reps,
+        both
+        + [pltpu.VMEM((3, width, cols), F32), dma((2, 2, CELL)), dma((cells * reps * CELL,))],
+        6 * product,
+        18,
+    )
+
+    def token_grads(side, acts):
+        piece = shape((2 * half, depth), F32)
+        outs = [shape((2 * size, depth), F32)] if side else [piece] * CELL
+        return call(
+            functools.partial(token_grad_kernel, side),
+            [weights, cots, acts, gates, ups, backs],
+            [VMEM] * 6,
             outs,
-            out_specs,
-            scratch
-            + [pltpu.VMEM((blocks, size, depth), F32)] * 2
-            + [
-                split_square,
-                pltpu.VMEM((2, blocks, size, depth), F32),
-                dma((blocks, 4)),
-                dma((blocks, 4)),
-            ],
-            9 * product * blocks // CELL + (3 * product if more else 0),
+            [HBM] * len(outs),
+            [split_square, pltpu.VMEM((2, size, depth), F32), dma((2, CELL))],
+            3 * product,
+            14,
         )
-        return outs[:rounds], outs[rounds], list(outs[rounds + 1 :])
-
-    near_first, far_first, (acts_first,) = token_grads(0, middle, cots)
-    query_totals, query_local = combine(read[1:4], read[4])
-    cots, *query_totals = lax.optimization_barrier((cots, *query_totals))
-    query_back = hand_back(query_totals, 0)
-    near_last, far_last, given = token_grads(middle, CELL, cots, key_turned, direct, acts_first)
-    far_last, *rest = lax.optimization_barrier((far_last, *near_first, *query_back))
-    near_first, query_back = rest[:-ROUNDS], rest[-ROUNDS:]
-    totals_first, _ = combine(near_first, far_first)
-    back = hand_back(totals_first, 0)
-    totals_last, local = combine(near_last, far_last)
-    back += hand_back(totals_last, middle)
+
+    def across(value):
+        return lax.ppermute(value, "head", SWAP)
+
+    query_got = across(query_far)
+    query_low = query_first + across(query_first)
+    query_high = (query_far + query_got)[ROUNDS * half :]
+    query_got, acts_cot = lax.optimization_barrier((query_got, acts_cot))
+    totals_query = [
+        part + query_got[turn * half : (turn + 1) * half] for turn, part in enumerate(query_near)
+    ]
+    acts_cot, *totals_query = lax.optimization_barrier((acts_cot, *totals_query))
+    query_back = [
+        lax.ppermute(totals_query[turn], PLACE, flipped(pairs[turn])) for turn in range(ROUNDS)
+    ]
+    (token_far,) = token_grads(1, acts_cot)
+    acts_cot, token_far = lax.optimization_barrier((acts_cot, token_far))
+    token_got = across(token_far)
+    token_near = list(token_grads(0, acts_cot))
+    token_near[0], *query_back = lax.optimization_barrier((token_near[0], *query_back))
+    back = hand_back(token_near, token_got)
+    token_low = token_near[ROUNDS] + across(token_near[ROUNDS])
+    token_high = (token_far + token_got)[ROUNDS * 2 * half :]
+    given = list(given)
     given[0], *back = lax.optimization_barrier((given[0], *back))
-    (query_grad,) = settle(query_back, query_local)
-    key_grad, target_grad = settle(back, local)
+    (query_grad,) = settle(query_back, query_low, query_high)
+    key_grad, target_grad = settle(back, token_low, token_high)
 
     if cells > 1:
         given = [

time: 159 us -> 163 us (1.025)
  local copies, waits for them, and re-layouts: 3.74 us -> 9.2 us
  other arithmetic: 10.2 us -> 12.1 us
  starting transfers between devices: 28.3 us -> 26.5 us
    unnamed x38 -> x50, local copies, waits for them, and re-layouts: 2.75 us -> 8.12 us
    ppermute x6, waiting for transfers between devices: 3.9 us -> 0.02 us  [spread(): far = [lax.ppermute(piece, 'head', SWAP) for piece in near]]
    select_n x2, other arithmetic: 0.23 us -> 3.18 us  [settle(): low = jnp.where(at_home, first, choose(turn0))]
    ppermute x9 -> x10, waiting for transfers between devices: 16.1 us -> 18.5 us  [the longest x3 18.4 us: hand_back(): lax.ppermute(totals[turn], PLACE, flipped(pairs[turn]))]
    ppermute x3, waiting for transfers between devices: 3.98 us -> 1.67 us  [per_device(): lax.ppermute(total[turn], PLACE, flipped(pairs[turn]))]
    ppermute x2, waiting for transfers between devices: 0.01 us -> 1.64 us  [spread(): return near + far + [local, lax.ppermute(local, 'head', SWAP)]]
    add x4 -> x2, other arithmetic: 4.26 us -> 2.76 us  [the longest x1 1.71 us: hand_back(): part + far[turn * length:(turn + 1) * length]]
    pallas_call x8 -> x10, Pallas kernels: 42.2 us -> 41.7 us  [call(): pl.pallas_call(kernel, out_shape=outs, in_specs=in_specs, out_specs=out_s...]
  transfers between devices with their start and end apart: 29 -> 30, of which waited for: 13 -> 11; matrix products, arithmetic and copies ran while one was open for 5% -> 6% of each run, Pallas kernels for 17% -> 17%
where the time goes in v8:
time: 163 us; the launch traced here: 160 us
  waiting for transfers between devices  69.4 us (43%)
  Pallas kernels  41.7 us (26%)
  starting transfers between devices  26.5 us (16%)
  other arithmetic  12.1 us (7%)
  local copies, waits for them, and re-layouts  9.2 us (6%)
    pallas_call x10, Pallas kernels, call(): pl.pallas_call(kernel, out_shape=outs, in_specs=in_specs, out_specs=out_s...  41.7 us
    ppermute x6, waiting for transfers between devices, gather(): lax.ppermute(packed[turn], PLACE, pairs[turn])  32 us
    ppermute x3, waiting for transfers between devices, hand_back(): lax.ppermute(totals[turn], PLACE, flipped(pairs[turn]))  18.4 us
    ppermute x1, waiting for transfers between devices, per_device(): parts.append(lax.ppermute(together, 'rep', shifted(shift, 1)))  15.5 us
    unnamed x50, local copies, waits for them, and re-layouts  8.12 us
    ppermute x6, starting transfers between devices, gather(): lax.ppermute(packed[turn], PLACE, pairs[turn])  7.23 us
    ppermute x3, starting transfers between devices, per_device(): lax.ppermute(totals_query[turn], PLACE, flipped(pairs[turn]))  5.48 us
    ppermute x3, starting transfers between devices, per_device(): lax.ppermute(total[turn], PLACE, flipped(pairs[turn]))  5.26 us
  transfers between devices with their start and end apart: 30, of which 11 were waited for; matrix products, arithmetic and copies ran while one was open for 6% of the time, Pallas kernels for 17%

profile of v8, /device:TPU:22, one launch (start us, length us, event | category | flops | bytes accessed | tf_op | source)
XLA Modules:
  0.0 160.1 jit_solution(17727004439928794227)
XLA Ops:
  0.6 0.8 copy.20
  1.4 0.7 fusion.4.refs_5_
  2.2 4.1 %shard_map.135 = (f32[352,512]{1,0:T(8,128)}, f32[352,512]{1,0:T(8,128)}, f32[352,512]{1,0:T(8,128)}, f32[608,512]{1,0:T(8,128)}, f32[96,512]{1,0:T(8,128)}) custom-call(f32[256,512]{1,0:T(8,128)} %bitcast.46, f32[256,512]{1,0:T(8,128)} %bitcast.45, f32[64,512]{1,0:T(8,128)} %bitcast.47, f32[64,512]{1,0:T(8,128)} %bitcast.48, f32[64,512]{1,0:T(8,128)} %bitcast.49, ...), custom_call_target="tpu_custom_call" | custom-call | bytes 5047296 | tf_op jit(solution)/shard_map/pallas_call | solution.py:467
  6.3 0.6 collective-permute-start.4
  6.9 2.3 %collective-permute-start.5 = (f32[352,512]{1,0:T(8,128)}, f32[352,512]{1,0:T(8,128)S(1)}, u32[]{:S(2)}, u32[]{:S(2)}) collective-permute-start(f32[352,512]{1,0:T(8,128)} %get-tuple-element.74), channel_id=1, source_target_pairs={{8,4},{12,5},{1,8},{5,9},{0,0},{4,1},{9,12},{13,13},{10,6},{14,7},... | collective-permute-start | bytes 2162696 | tf_op jit(solution)/shard_map/ppermute | solution.py:530
  9.2 1.3 collective-permute-start.6
  10.5 11.9 %collective-permute-done.4.refs_2_.refs_0_ = f32[352,512]{1,0:T(8,128)S(1)} collective-permute-done((f32[352,512]{1,0:T(8,128)}, f32[352,512]{1,0:T(8,128)S(1)}, u32[]{:S(2)}, u32[]{:S(2)}) %collective-permute-start.4) | collective-permute-done | bytes 720928 | tf_op jit(solution)/shard_map/ppermute | solution.py:530
  22.4 18.6 %collective-permute-done.5.refs_3_.refs_1_ = f32[352,512]{1,0:T(8,128)S(1)} collective-permute-done((f32[352,512]{1,0:T(8,128)}, f32[352,512]{1,0:T(8,128)S(1)}, u32[]{:S(2)}, u32[]{:S(2)}) %collective-permute-start.5) | collective-permute-done | bytes 720928 | tf_op jit(solution)/shard_map/ppermute | solution.py:530
  41.1 1.5 collective-permute-done.6.refs_4_.refs_2_
  42.5 0.5 collective-permute-start.8
  43.1 1.1 select_bitcast_fusion
  44.3 0.6 collective-permute-start.7
  44.9 0.3 shard_map.136
  45.3 1.9 %collective-permute-start.2 = (f32[256,512]{1,0:T(8,128)S(1)}, f32[256,512]{1,0:T(8,128)S(1)}, u32[]{:S(2)}, u32[]{:S(2)}) collective-permute-start(f32[256,512]{1,0:T(8,128)S(1)} %get-tuple-element.70), channel_id=1, source_target_pairs={{8,4},{12,5},{1,8},{5,9},{0,0},{4,1},{9,12},{13,13},{10,6},{14,7},... | collective-permute-start | bytes 1572872 | tf_op jit(solution)/shard_map/ppermute | solution.py:530
  47.3 1.1 collective-permute-start.3
  48.4 15.5 %collective-permute-done.7.refs_1_ = f32[4,96,512]{2,1,0:T(8,128)S(1)} collective-permute-done((f32[4,96,512]{2,1,0:T(8,128)S(1)}, f32[4,96,512]{2,1,0:T(8,128)S(1)}, u32[]{:S(2)}, u32[]{:S(2)}) %collective-permute-start.7) | collective-permute-done | bytes 786464 | tf_op jit(solution)/shard_map/ppermute | solution.py:573
  63.9 1.1 copy-done.18
  65.0 8.0 %shard_map.137 = (f32[3,512,256]{2,1,0:T(8,128)S(1)}, f32[1024,256]{1,0:T(8,128)S(1)}, f32[1024,256]{1,0:T(8,128)S(1)}, f32[1024,256]{1,0:T(8,128)S(1)}, bf16[2,...) custom-call(f32[4,96,512]{2,1,0:T(8,128)S(1)} %pad_maximum_fusion.refs_0_, ...), custom_call_target="tpu_custom_call" | custom-call | flops 4831838208 | bytes 18874368 | tf_op jit(solution)/shard_map/pallas_call | solution.py:467
  73.1 0.6 shard_map.138
  73.8 0.5 collective-permute-start.13
  74.4 0.4 collective-permute-start.15
  74.8 1.6 %collective-permute-done.11.refs_4_ = f32[512,512]{1,0:T(8,128)S(1)} collective-permute-done((f32[512,512]{1,0:T(8,128)S(1)}, f32[512,512]{1,0:T(8,128)S(1)}, u32[]{:S(2)}, u32[]{:S(2)}) %collective-permute-start.11) | collective-permute-done | bytes 1048608 | tf_op jit(solution)/shard_map/ppermute | solution.py:535
  76.4 5.0 %shard_map.139 = (f32[128,512]{1,0:T(8,128)S(1)}, f32[128,512]{1,0:T(8,128)S(1)}, f32[128,512]{1,0:T(8,128)S(1)}, f32[128,512]{1,0:T(8,128)S(1)}, bf16[2,2,512,5...) custom-call(f32[256,512]{1,0:T(8,128)S(1)} %collective-permute-done.1.refs_0_, ...), custom_call_target="tpu_custom_call" | custom-call | flops 2013265920 | bytes 9961472 | tf_op jit(solution)/shard_map/pallas_call | solution.py:467
  81.5 7.1 %shard_map.140 = (f32[3,512,256]{2,1,0:T(8,128)S(1)}, f32[512,512]{1,0:T(8,128)S(1)}) custom-call(f32[256,512]{1,0:T(8,128)S(1)} %collective-permute-done.13.refs_0_, f32[256,512]{1,0:T(8,128)S(1)} %collective-permute-done.14.refs_1_, f32[256,512]{1,0:T(8,128)S(1)} %collective-permute-done.15.refs_2_, f32[512,512]{1,0:T(8,128)S(1)} %get-tuple-element.87.refs_3_, ...), custom_call_target="tpu_custom_call" | custom-call | flops 4429185024 | bytes 11534336 | tf_op jit(solution)/shard_map/pallas_call | solution.py:467
  88.6 0.2 collective-permute-start.16
  88.8 1.1 shard_map.141
  90.0 0.1 copy-done.14
  90.1 0.2 copy-done.16
  90.3 0.2 copy-done.19
  90.5 8.4 %shard_map.142 = (bf16[2,3,1024,256]{3,2,1,0:T(8,128)(2,1)S(1)}, f32[1,4,3,64,256]{4,3,2,1,0:T(8,128)S(1)}, f32[1,4,3,64,256]{4,3,2,1,0:T(8,128)S(1)}) custom-call(f32[352,512]{1,0:T(8,128)S(1)} %copy-done.14, f32[352,512]{1,0:T(8,128)S(1)} %copy-done.16, f32[352,512]{1,0:T(8,128)S(1)} %copy-done.19, f32[352,512]{1,0:T(8,128)S(1)} %collective-permute-done.8.refs_5_.refs_3_, ...), custom_call_target="tpu_custom_call" | custom-call | flops 4831838208 | bytes 22020096 | tf_op jit(solution)/shard_map/pallas_call | solution.py:467
  98.9 1.0 slice_add_fusion.5
  100.0 3.7 %shard_map.143 = f32[1024,512]{1,0:T(8,128)} custom-call(f32[3,512,256]{2,1,0:T(8,128)S(1)} %get-tuple-element.81.weights.refs_0_, bf16[2,3,512,256]{3,2,1,0:T(8,128)(2,1)S(1)} %get-tuple-element.94.refs_10_.refs_1_, bf16[2,3,1024,256]{3,2,1,0:T(8,128)(2,1)S(1)} %get-tuple-element.108.refs_2_, f32[1024,256]{1,0:T(8,128)S(1)} %get-tuple-element.98.refs_11_.refs_3_, ...), custom_call_target="tpu_custom_call" | custom-call | flops 2415919104 | bytes 11534336 | tf_op jit(solution)/shard_map/pallas_call | solution.py:467
  103.9 2.1 %collective-permute-start.18 = (f32[128,512]{1,0:T(8,128)}, f32[128,512]{1,0:T(8,128)}, u32[]{:S(2)}, u32[]{:S(2)}) collective-permute-start(f32[128,512]{1,0:T(8,128)} %get-tuple-element.111), channel_id=1, source_target_pairs={{4,8},{5,12},{8,1},{9,5},{0,0},{1,4},{12,9},{13,13},{6,10},{7,14},... | collective-permute-start | bytes 786440 | tf_op jit(solution)/shard_map/ppermute | solution.py:680
  106.0 3.4 %collective-permute-start.19 = (f32[128,512]{1,0:T(8,128)}, f32[128,512]{1,0:T(8,128)}, u32[]{:S(2)}, u32[]{:S(2)}) collective-permute-start(f32[128,512]{1,0:T(8,128)} %get-tuple-element.112), channel_id=1, source_target_pairs={{4,12},{5,0},{8,5},{9,13},{0,1},{1,4},{12,8},{13,9},{6,14},{7,2},{... | collective-permute-start | bytes 786440 | tf_op jit(solution)/shard_map/ppermute | solution.py:680
  109.4 0.5 collective-permute-start.25
  109.9 1.9 %copy-done.1 = bf16[2,3,1024,256]{3,2,1,0:T(8,128)(2,1)S(1)} copy-done((bf16[2,3,1024,256]{3,2,1,0:T(8,128)(2,1)S(1)}, bf16[2,3,1024,256]{3,2,1,0:T(8,128)(2,1)}, u32[]{:S(2)}) %copy-start.1) | copy-done | bytes 3145752
  111.8 1.2 copy-done.3
  113.0 1.2 copy-done.5
  114.2 1.2 copy-done.7
  115.5 3.4 %shard_map.144 = (f32[256,512]{1,0:T(8,128)S(1)}, f32[256,512]{1,0:T(8,128)S(1)}, f32[256,512]{1,0:T(8,128)S(1)}, f32[256,512]{1,0:T(8,128)S(1)}) custom-call(f32[3,512,256]{2,1,0:T(8,128)S(1)} %get-tuple-element.81.weights.refs_0_, bf16[2,3,512,256]{3,2,1,0:T(8,128)(2,1)S(1)} %get-tuple-element.94.refs_10_.refs_1_, bf16[2,3,1024,256]{3,2,1,0:T(8,128)(2,1)S(1)} %copy-done.1, ...), custom_call_target="tpu_custom_call" | custom-call | flops 2415919104 | bytes 11534336 | tf_op jit(solution)/shard_map/pallas_call | solution.py:467
  119.0 0.1 collective-permute-done.19
  119.1 1.7 %slice_add_fusion.1 = (f32[256,512]{1,0:T(8,128)S(1)}, f32[256,512]{1,0:T(8,128)S(1)}, f32[256,512]{1,0:T(8,128)S(1)}) fusion(f32[256,512]{1,0:T(8,128)S(1)} %get-tuple-element.121, f32[1024,512]{1,0:T(8,128)} %collective-permute-done.21, f32[256,512]{1,0:T(8,128)S(1)} %get-tuple-element.120, f32[256,512]{1,0:T(8,128)S(1)} %get-tuple-element.118), kind=kLoop, calls=%fused_computation.4 | loop fusion | flops 393216 | bytes 4718592 | tf_op jit(solution)/shard_map/add | solution.py:540
  120.9 3.4 %collective-permute-start.23 = (f32[256,512]{1,0:T(8,128)S(1)}, f32[256,512]{1,0:T(8,128)S(1)}, u32[]{:S(2)}, u32[]{:S(2)}) collective-permute-start(f32[256,512]{1,0:T(8,128)S(1)} %get-tuple-element.128), channel_id=1, source_target_pairs={{4,8},{5,12},{8,1},{9,5},{0,0},{1,4},{12,9},{13,13},{6,10},{7,14},... | collective-permute-start | bytes 1572872 | tf_op jit(solution)/shard_map/ppermute | solution.py:543
  124.2 1.8 %collective-permute-start.24 = (f32[256,512]{1,0:T(8,128)S(1)}, f32[256,512]{1,0:T(8,128)S(1)}, u32[]{:S(2)}, u32[]{:S(2)}) collective-permute-start(f32[256,512]{1,0:T(8,128)S(1)} %get-tuple-element.127), channel_id=1, source_target_pairs={{4,12},{5,0},{8,5},{9,13},{0,1},{1,4},{12,8},{13,9},{6,14},{7,2},{... | collective-permute-start | bytes 1572872 | tf_op jit(solution)/shard_map/ppermute | solution.py:543
  126.1 1.5 select_select_fusion.1
  127.7 0.8 maximum_bitcast_fusion
  128.5 4.0 %collective-permute-done.22 = f32[256,512]{1,0:T(8,128)S(1)} collective-permute-done((f32[256,512]{1,0:T(8,128)S(1)}, f32[256,512]{1,0:T(8,128)S(1)}, u32[]{:S(2)}, u32[]{:S(2)}) %collective-permute-start.22) | collective-permute-done | bytes 524320 | tf_op jit(solution)/shard_map/ppermute | solution.py:543
  132.5 5.1 %collective-permute-done.23 = f32[256,512]{1,0:T(8,128)S(1)} collective-permute-done((f32[256,512]{1,0:T(8,128)S(1)}, f32[256,512]{1,0:T(8,128)S(1)}, u32[]{:S(2)}, u32[]{:S(2)}) %collective-permute-start.23) | collective-permute-done | bytes 524320 | tf_op jit(solution)/shard_map/ppermute | solution.py:543
  137.6 9.3 %collective-permute-done.24 = f32[256,512]{1,0:T(8,128)S(1)} collective-permute-done((f32[256,512]{1,0:T(8,128)S(1)}, f32[256,512]{1,0:T(8,128)S(1)}, u32[]{:S(2)}, u32[]{:S(2)}) %collective-permute-start.24) | collective-permute-done | bytes 524320 | tf_op jit(solution)/shard_map/ppermute | solution.py:543
  146.9 0.1 bitcast_add_fusion
  147.1 1.0 collective-permute-start.27
  148.1 1.9 %collective-permute-start.28 = (f32[3,64,256]{2,1,0:T(8,128)S(1)}, f32[3,64,256]{2,1,0:T(8,128)S(1)}, u32[]{:S(2)}, u32[]{:S(2)}) collective-permute-start(f32[3,64,256]{2,1,0:T(8,128)S(1)} %get-tuple-element.139), channel_id=1, source_target_pairs={{4,8},{5,12},{8,1},{9,5},{0,0},{1,4},{12,9},{13,13},{6,10},{7,14},... | collective-permute-start | bytes 589832 | tf_op jit(solution)/shard_map/ppermute | solution.py:704
  150.1 2.4 %collective-permute-start.29 = (f32[3,64,256]{2,1,0:T(8,128)S(1)}, f32[3,64,256]{2,1,0:T(8,128)S(1)}, u32[]{:S(2)}, u32[]{:S(2)}) collective-permute-start(f32[3,64,256]{2,1,0:T(8,128)S(1)} %get-tuple-element.138), channel_id=1, source_target_pairs={{4,12},{5,0},{8,5},{9,13},{0,1},{1,4},{12,8},{13,9},{6,14},{7,2},{... | collective-permute-start | bytes 589832 | tf_op jit(solution)/shard_map/ppermute | solution.py:704
  152.4 1.6 %select_select_fusion = (f32[256,512]{1,0:T(8,128)S(1)}, f32[256,512]{1,0:T(8,128)S(1)}) fusion(f32[256,512]{1,0:T(8,128)S(1)} %collective-permute-done.22, f32[256,512]{1,0:T(8,128)S(1)} %collective-permute-done.23, f32[256,512]{1,0:T(8,128)S(1)} %collective-permute-done.24, f32[256,512]{1,0:T(8,128)S(1)} %get-tuple-element.116, ...), kind=kLoop, calls=%fused_computation.12 | loop fusion | flops 1048576 | bytes 4718597 | tf_op jit(solution)/shard_map/jit(_where)/select_n | solution.py:549
  154.1 0.1 fusion.9
  154.2 0.1 fusion.10
  154.3 0.8 copy-done.22
  155.1 0.1 fusion.1
  155.3 0.8 maximum_bitcast_fusion.1
  156.1 0.9 maximum_multiply_fusion
  157.0 0.6 divide_multiply_fusion
  157.6 0.2 collective-permute-done.28
  157.8 1.4 collective-permute-done.29
  159.3 0.8 pad_maximum_fusion.1
  (79 shorter events, 1.1 us)
Async XLA Ops:
  6.3 36.8 %collective-permute-start = (f32[608,512]{1,0:T(8,128)}, f32[608,512]{1,0:T(8,128)}, u32[]{:S(2)}, u32[]{:S(2)}) collective-permute-start(f32[608,512]{1,0:T(8,128)} %get-tuple-element.67.refs_8_.refs_6_), channel_id=1, source_target_pairs={{0,1},{1,0},{2,3},{3,2},{4,5},{5,4},{6,7},{7,6},{8,9},{9,8},{10,11... | collective-permute-start | bytes 3735560 | tf_op jit(solution)/shard_map/ppermute | solution.py:535
  6.3 16.1 %collective-permute-start.4 = (f32[352,512]{1,0:T(8,128)}, f32[352,512]{1,0:T(8,128)S(1)}, u32[]{:S(2)}, u32[]{:S(2)}) collective-permute-start(f32[352,512]{1,0:T(8,128)} %get-tuple-element.73), channel_id=1, source_target_pairs={{0,4},{8,5},{13,8},{1,9},{4,0},{5,1},{9,12},{12,13},{2,6},{10,7},{... | collective-permute-start | bytes 2162696 | tf_op jit(solution)/shard_map/ppermute | solution.py:530
  6.9 34.2 %collective-permute-start.5 = (f32[352,512]{1,0:T(8,128)}, f32[352,512]{1,0:T(8,128)S(1)}, u32[]{:S(2)}, u32[]{:S(2)}) collective-permute-start(f32[352,512]{1,0:T(8,128)} %get-tuple-element.74), channel_id=1, source_target_pairs={{8,4},{12,5},{1,8},{5,9},{0,0},{4,1},{9,12},{13,13},{10,6},{14,7},... | collective-permute-start | bytes 2162696 | tf_op jit(solution)/shard_map/ppermute | solution.py:530
  9.2 33.3 %collective-permute-start.6 = (f32[352,512]{1,0:T(8,128)}, f32[352,512]{1,0:T(8,128)S(1)}, u32[]{:S(2)}, u32[]{:S(2)}) collective-permute-start(f32[352,512]{1,0:T(8,128)} %get-tuple-element.75), channel_id=1, source_target_pairs={{12,4},{0,5},{5,8},{13,9},{1,0},{4,1},{8,12},{9,13},{14,6},{2,7},{... | collective-permute-start | bytes 2162696 | tf_op jit(solution)/shard_map/ppermute | solution.py:530
  22.4 41.5 %copy-start.13 = (f32[352,512]{1,0:T(8,128)}, f32[352,512]{1,0:T(8,128)S(1)}, u32[]{:S(2)}) copy-start(f32[352,512]{1,0:T(8,128)S(1)} %collective-permute-done.4.refs_2_.refs_0_) | copy-start | bytes 2162692
  41.1 22.9 %copy-start.15 = (f32[352,512]{1,0:T(8,128)}, f32[352,512]{1,0:T(8,128)S(1)}, u32[]{:S(2)}) copy-start(f32[352,512]{1,0:T(8,128)S(1)} %collective-permute-done.5.refs_3_.refs_1_) | copy-start | bytes 2162692
  42.5 1.8 %copy-start.17 = (f32[352,512]{1,0:T(8,128)}, f32[352,512]{1,0:T(8,128)S(1)}, u32[]{:S(2)}) copy-start(f32[352,512]{1,0:T(8,128)S(1)} %collective-permute-done.6.refs_4_.refs_2_) | copy-start | bytes 2162692
  42.5 2.8 %collective-permute-start.10 = (f32[352,512]{1,0:T(8,128)S(1)}, f32[352,512]{1,0:T(8,128)S(1)}, u32[]{:S(2)}, u32[]{:S(2)}) collective-permute-start(f32[352,512]{1,0:T(8,128)S(1)} %collective-permute-done.6.refs_4_.refs_2_), channel_id=1, source_target_pairs={{0,1},{1,0},{2,3},{3,2},{4,5},{5,4},{6,7},{7,6},{8,9},{9,8},{10,11... | collective-permute-start | bytes 2162696 | tf_op jit(solution)/shard_map/ppermute | solution.py:534
  42.5 4.7 %collective-permute-start.8 = (f32[352,512]{1,0:T(8,128)S(1)}, f32[352,512]{1,0:T(8,128)S(1)}, u32[]{:S(2)}, u32[]{:S(2)}) collective-permute-start(f32[352,512]{1,0:T(8,128)S(1)} %collective-permute-done.4.refs_2_.refs_0_), channel_id=1, source_target_pairs={{0,1},{1,0},{2,3},{3,2},{4,5},{5,4},{6,7},{7,6},{8,9},{9,8},{10,11... | collective-permute-start | bytes 2162696 | tf_op jit(solution)/shard_map/ppermute | solution.py:534
  43.1 1.9 %copy-start.10 = (f32[1,1,256,512]{3,2,1,0:T(8,128)S(1)}, f32[1,1,256,512]{3,2,1,0:T(8,128)}, u32[]{:S(2)}) copy-start(f32[1,1,256,512]{3,2,1,0:T(8,128)} %param.8) | copy-start | bytes 1572868
  43.1 1.9 %copy-start.11 = (f32[1,1,256,512]{3,2,1,0:T(8,128)S(1)}, f32[1,1,256,512]{3,2,1,0:T(8,128)}, u32[]{:S(2)}) copy-start(f32[1,1,256,512]{3,2,1,0:T(8,128)} %param.12) | copy-start | bytes 1572868
  43.1 20.8 %copy-start.20 = (f32[608,512]{1,0:T(8,128)S(1)}, f32[608,512]{1,0:T(8,128)}, u32[]{:S(2)}) copy-start(f32[608,512]{1,0:T(8,128)} %get-tuple-element.67.refs_8_.refs_6_) | copy-start | bytes 3735556
  44.3 19.6 %collective-permute-start.7 = (f32[4,96,512]{2,1,0:T(8,128)S(1)}, f32[4,96,512]{2,1,0:T(8,128)S(1)}, u32[]{:S(2)}, u32[]{:S(2)}) collective-permute-start(f32[4,96,512]{2,1,0:T(8,128)S(1)} %pad_maximum_fusion.refs_0_), channel_id=1, source_target_pairs={{0,2},{2,0},{1,3},{3,1},{4,6},{6,4},{5,7},{7,5},{8,10},{10,8},{9,1... | collective-permute-start | bytes 2359304 | tf_op jit(solution)/shard_map/ppermute | solution.py:573
  44.9 3.5 %collective-permute-start.9 = (f32[352,512]{1,0:T(8,128)S(1)}, f32[352,512]{1,0:T(8,128)S(1)}, u32[]{:S(2)}, u32[]{:S(2)}) collective-permute-start(f32[352,512]{1,0:T(8,128)S(1)} %collective-permute-done.5.refs_3_.refs_1_), channel_id=1, source_target_pairs={{0,1},{1,0},{2,3},{3,2},{4,5},{5,4},{6,7},{7,6},{8,9},{9,8},{10,11... | collective-permute-start | bytes 2162696 | tf_op jit(solution)/shard_map/ppermute | solution.py:534
  45.2 28.4 %collective-permute-start.1 = (f32[256,512]{1,0:T(8,128)S(1)}, f32[256,512]{1,0:T(8,128)S(1)}, u32[]{:S(2)}, u32[]{:S(2)}) collective-permute-start(f32[256,512]{1,0:T(8,128)S(1)} %get-tuple-element.69), channel_id=1, source_target_pairs={{0,4},{8,5},{13,8},{1,9},{4,0},{5,1},{9,12},{12,13},{2,6},{10,7},{... | collective-permute-start | bytes 1572872 | tf_op jit(solution)/shard_map/ppermute | solution.py:530
  45.3 28.4 %collective-permute-start.2 = (f32[256,512]{1,0:T(8,128)S(1)}, f32[256,512]{1,0:T(8,128)S(1)}, u32[]{:S(2)}, u32[]{:S(2)}) collective-permute-start(f32[256,512]{1,0:T(8,128)S(1)} %get-tuple-element.70), channel_id=1, source_target_pairs={{8,4},{12,5},{1,8},{5,9},{0,0},{4,1},{9,12},{13,13},{10,6},{14,7},... | collective-permute-start | bytes 1572872 | tf_op jit(solution)/shard_map/ppermute | solution.py:530
  47.3 26.4 %collective-permute-start.3 = (f32[256,512]{1,0:T(8,128)S(1)}, f32[256,512]{1,0:T(8,128)S(1)}, u32[]{:S(2)}, u32[]{:S(2)}) collective-permute-start(f32[256,512]{1,0:T(8,128)S(1)} %get-tuple-element.71), channel_id=1, source_target_pairs={{12,4},{0,5},{5,8},{13,9},{1,0},{4,1},{8,12},{9,13},{14,6},{2,7},{... | collective-permute-start | bytes 1572872 | tf_op jit(solution)/shard_map/ppermute | solution.py:530
  63.9 1.1 copy-start.18
  73.0 27.0 %copy-start.2 = (f32[1024,256]{1,0:T(8,128)}, f32[1024,256]{1,0:T(8,128)S(1)}, u32[]{:S(2)}) copy-start(f32[1024,256]{1,0:T(8,128)S(1)} %get-tuple-element.98.refs_11_.refs_3_) | copy-start | bytes 3145732
  73.0 27.0 %copy-start.4 = (f32[1024,256]{1,0:T(8,128)}, f32[1024,256]{1,0:T(8,128)S(1)}, u32[]{:S(2)}) copy-start(f32[1024,256]{1,0:T(8,128)S(1)} %get-tuple-element.99.refs_12_.refs_4_) | copy-start | bytes 3145732
  73.0 27.0 %copy-start.6 = (f32[1024,256]{1,0:T(8,128)}, f32[1024,256]{1,0:T(8,128)S(1)}, u32[]{:S(2)}) copy-start(f32[1024,256]{1,0:T(8,128)S(1)} %get-tuple-element.100.refs_13_.refs_5_) | copy-start | bytes 3145732
  73.7 2.7 %collective-permute-start.11 = (f32[512,512]{1,0:T(8,128)S(1)}, f32[512,512]{1,0:T(8,128)S(1)}, u32[]{:S(2)}, u32[]{:S(2)}) collective-permute-start(f32[512,512]{1,0:T(8,128)S(1)} %get-tuple-element.87.refs_3_), channel_id=1, source_target_pairs={{0,1},{1,0},{2,3},{3,2},{4,5},{5,4},{6,7},{7,6},{8,9},{9,8},{10,11... | collective-permute-start | bytes 3145736 | tf_op jit(solution)/shard_map/ppermute | solution.py:535
  73.8 7.7 %collective-permute-start.13 = (f32[256,512]{1,0:T(8,128)S(1)}, f32[256,512]{1,0:T(8,128)S(1)}, u32[]{:S(2)}, u32[]{:S(2)}) collective-permute-start(f32[256,512]{1,0:T(8,128)S(1)} %collective-permute-done.1.refs_0_), channel_id=1, source_target_pairs={{0,1},{1,0},{2,3},{3,2},{4,5},{5,4},{6,7},{7,6},{8,9},{9,8},{10,11... | collective-permute-start | bytes 1572872 | tf_op jit(solution)/shard_map/ppermute | solution.py:534
  74.3 7.2 %collective-permute-start.14 = (f32[256,512]{1,0:T(8,128)S(1)}, f32[256,512]{1,0:T(8,128)S(1)}, u32[]{:S(2)}, u32[]{:S(2)}) collective-permute-start(f32[256,512]{1,0:T(8,128)S(1)} %collective-permute-done.2.refs_1_), channel_id=1, source_target_pairs={{0,1},{1,0},{2,3},{3,2},{4,5},{5,4},{6,7},{7,6},{8,9},{9,8},{10,11... | collective-permute-start | bytes 1572872 | tf_op jit(solution)/shard_map/ppermute | solution.py:534
  74.4 7.1 %collective-permute-start.15 = (f32[256,512]{1,0:T(8,128)S(1)}, f32[256,512]{1,0:T(8,128)S(1)}, u32[]{:S(2)}, u32[]{:S(2)}) collective-permute-start(f32[256,512]{1,0:T(8,128)S(1)} %collective-permute-done.3.refs_2_), channel_id=1, source_target_pairs={{0,1},{1,0},{2,3},{3,2},{4,5},{5,4},{6,7},{7,6},{8,9},{9,8},{10,11... | collective-permute-start | bytes 1572872 | tf_op jit(solution)/shard_map/ppermute | solution.py:534
  88.6 1.4 copy-start.12
  88.6 10.3 %collective-permute-start.16 = (f32[512,512]{1,0:T(8,128)S(1)}, f32[512,512]{1,0:T(8,128)S(1)}, u32[]{:S(2)}, u32[]{:S(2)}) collective-permute-start(f32[512,512]{1,0:T(8,128)S(1)} %get-tuple-element.95), channel_id=1, source_target_pairs={{0,1},{1,0},{2,3},{3,2},{4,5},{5,4},{6,7},{7,6},{8,9},{9,8},{10,11... | collective-permute-start | bytes 3145736 | tf_op jit(solution)/shard_map/ppermute | solution.py:669
  88.8 1.3 copy-start.14
  88.8 1.5 copy-start.16
  88.8 1.7 %copy-start.19 = (f32[352,512]{1,0:T(8,128)S(1)}, f32[352,512]{1,0:T(8,128)}, u32[]{:S(2)}) copy-start(f32[352,512]{1,0:T(8,128)} %copy-done.17) | copy-start | bytes 2162692
  98.9 4.9 %copy-start = (bf16[2,3,1024,256]{3,2,1,0:T(8,128)(2,1)}, bf16[2,3,1024,256]{3,2,1,0:T(8,128)(2,1)S(1)}, u32[]{:S(2)}) copy-start(bf16[2,3,1024,256]{3,2,1,0:T(8,128)(2,1)S(1)} %get-tuple-element.108.refs_2_) | copy-start | bytes 9437188
  98.9 4.9 %copy-start.8 = (f32[1,4,3,64,256]{4,3,2,1,0:T(8,128)}, f32[1,4,3,64,256]{4,3,2,1,0:T(8,128)S(1)}, u32[]{:S(2)}) copy-start(f32[1,4,3,64,256]{4,3,2,1,0:T(8,128)S(1)} %get-tuple-element.125) | copy-start | bytes 2359300
  98.9 4.9 %copy-start.21 = (f32[1,4,3,64,256]{4,3,2,1,0:T(8,128)}, f32[1,4,3,64,256]{4,3,2,1,0:T(8,128)S(1)}, u32[]{:S(2)}) copy-start(f32[1,4,3,64,256]{4,3,2,1,0:T(8,128)S(1)} %get-tuple-element.126) | copy-start | bytes 2359300
  98.9 4.8 %copy-start.23 = (f32[512,512]{1,0:T(8,128)}, f32[512,512]{1,0:T(8,128)S(1)}, u32[]{:S(2)}) copy-start(f32[512,512]{1,0:T(8,128)S(1)} %collective-permute-done.16) | copy-start | bytes 3145732
  103.8 15.3 %collective-permute-start.21 = (f32[1024,512]{1,0:T(8,128)}, f32[1024,512]{1,0:T(8,128)}, u32[]{:S(2)}, u32[]{:S(2)}) collective-permute-start(f32[1024,512]{1,0:T(8,128)} %shard_map.143), channel_id=1, source_target_pairs={{0,1},{1,0},{2,3},{3,2},{4,5},{5,4},{6,7},{7,6},{8,9},{9,8},{10,11... | collective-permute-start | bytes 6291464 | tf_op jit(solution)/shard_map/ppermute | solution.py:669
  103.9 15.0 %collective-permute-start.17 = (f32[128,512]{1,0:T(8,128)}, f32[128,512]{1,0:T(8,128)}, u32[]{:S(2)}, u32[]{:S(2)}) collective-permute-start(f32[128,512]{1,0:T(8,128)} %get-tuple-element.110), channel_id=1, source_target_pairs={{4,0},{5,8},{8,13},{9,1},{0,4},{1,5},{12,9},{13,12},{6,2},{7,10},{... | collective-permute-start | bytes 786440 | tf_op jit(solution)/shard_map/ppermute | solution.py:680
  103.9 15.0 %collective-permute-start.18 = (f32[128,512]{1,0:T(8,128)}, f32[128,512]{1,0:T(8,128)}, u32[]{:S(2)}, u32[]{:S(2)}) collective-permute-start(f32[128,512]{1,0:T(8,128)} %get-tuple-element.111), channel_id=1, source_target_pairs={{4,8},{5,12},{8,1},{9,5},{0,0},{1,4},{12,9},{13,13},{6,10},{7,14},... | collective-permute-start | bytes 786440 | tf_op jit(solution)/shard_map/ppermute | solution.py:680
  106.0 13.1 %collective-permute-start.19 = (f32[128,512]{1,0:T(8,128)}, f32[128,512]{1,0:T(8,128)}, u32[]{:S(2)}, u32[]{:S(2)}) collective-permute-start(f32[128,512]{1,0:T(8,128)} %get-tuple-element.112), channel_id=1, source_target_pairs={{4,12},{5,0},{8,5},{9,13},{0,1},{1,4},{12,8},{13,9},{6,14},{7,2},{... | collective-permute-start | bytes 786440 | tf_op jit(solution)/shard_map/ppermute | solution.py:680
  109.4 37.5 %collective-permute-start.25 = (f32[4,3,64,256]{3,2,1,0:T(8,128)}, f32[4,3,64,256]{3,2,1,0:T(8,128)S(1)}, u32[]{:S(2)}, u32[]{:S(2)}) collective-permute-start(f32[4,3,64,256]{3,2,1,0:T(8,128)} %bitcast.44), channel_id=1, source_target_pairs={{0,2},{2,0},{1,3},{3,1},{4,6},{6,4},{5,7},{7,5},{8,10},{10,8},{9,1... | collective-permute-start | bytes 2359304 | tf_op jit(solution)/shard_map/ppermute | solution.py:702
  109.9 1.9 %copy-start.1 = (bf16[2,3,1024,256]{3,2,1,0:T(8,128)(2,1)S(1)}, bf16[2,3,1024,256]{3,2,1,0:T(8,128)(2,1)}, u32[]{:S(2)}) copy-start(bf16[2,3,1024,256]{3,2,1,0:T(8,128)(2,1)} %copy-done) | copy-start | bytes 9437188
  111.8 1.2 copy-start.3
  113.0 1.2 copy-start.5
  114.2 1.2 copy-start.7
  118.9 7.2 %collective-permute-start.12 = (f32[128,512]{1,0:T(8,128)S(1)}, f32[128,512]{1,0:T(8,128)S(1)}, u32[]{:S(2)}, u32[]{:S(2)}) collective-permute-start(f32[128,512]{1,0:T(8,128)S(1)} %get-tuple-element.90), channel_id=1, source_target_pairs={{0,1},{1,0},{2,3},{3,2},{4,5},{5,4},{6,7},{7,6},{8,9},{9,8},{10,11... | collective-permute-start | bytes 786440 | tf_op jit(solution)/shard_map/ppermute | solution.py:669
  119.1 6.9 %copy-start.24 = (f32[1,1,256]{2,1,0:T(1,128)S(1)}, f32[1,1,256]{2,1,0:T(1,128)}, u32[]{:S(2)}) copy-start(f32[1,1,256]{2,1,0:T(1,128)} %param.11) | copy-start | bytes 3076
  120.8 11.7 %collective-permute-start.22 = (f32[256,512]{1,0:T(8,128)S(1)}, f32[256,512]{1,0:T(8,128)S(1)}, u32[]{:S(2)}, u32[]{:S(2)}) collective-permute-start(f32[256,512]{1,0:T(8,128)S(1)} %get-tuple-element.129), channel_id=1, source_target_pairs={{4,0},{5,8},{8,13},{9,1},{0,4},{1,5},{12,9},{13,12},{6,2},{7,10},{... | collective-permute-start | bytes 1572872 | tf_op jit(solution)/shard_map/ppermute | solution.py:543
  120.9 16.8 %collective-permute-start.23 = (f32[256,512]{1,0:T(8,128)S(1)}, f32[256,512]{1,0:T(8,128)S(1)}, u32[]{:S(2)}, u32[]{:S(2)}) collective-permute-start(f32[256,512]{1,0:T(8,128)S(1)} %get-tuple-element.128), channel_id=1, source_target_pairs={{4,8},{5,12},{8,1},{9,5},{0,0},{1,4},{12,9},{13,13},{6,10},{7,14},... | collective-permute-start | bytes 1572872 | tf_op jit(solution)/shard_map/ppermute | solution.py:543
  124.2 22.7 %collective-permute-start.24 = (f32[256,512]{1,0:T(8,128)S(1)}, f32[256,512]{1,0:T(8,128)S(1)}, u32[]{:S(2)}, u32[]{:S(2)}) collective-permute-start(f32[256,512]{1,0:T(8,128)S(1)} %get-tuple-element.127), channel_id=1, source_target_pairs={{4,12},{5,0},{8,5},{9,13},{0,1},{1,4},{12,8},{13,9},{6,14},{7,2},{... | collective-permute-start | bytes 1572872 | tf_op jit(solution)/shard_map/ppermute | solution.py:543
  126.0 20.8 %copy-start.9 = (f32[1,4,3,64,256]{4,3,2,1,0:T(8,128)S(1)}, f32[1,4,3,64,256]{4,3,2,1,0:T(8,128)}, u32[]{:S(2)}) copy-start(f32[1,4,3,64,256]{4,3,2,1,0:T(8,128)} %copy-done.8) | copy-start | bytes 2359300
  126.1 26.4 %collective-permute-start.20 = (f32[256,512]{1,0:T(8,128)S(1)}, f32[256,512]{1,0:T(8,128)S(1)}, u32[]{:S(2)}, u32[]{:S(2)}) collective-permute-start(f32[256,512]{1,0:T(8,128)S(1)} %get-tuple-element.116), channel_id=1, source_target_pairs={{0,1},{1,0},{2,3},{3,2},{4,5},{5,4},{6,7},{7,6},{8,9},{9,8},{10,11... | collective-permute-start | bytes 1572872 | tf_op jit(solution)/shard_map/ppermute | solution.py:669
  147.1 10.5 %collective-permute-start.26 = (f32[3,64,256]{2,1,0:T(8,128)S(1)}, f32[3,64,256]{2,1,0:T(8,128)S(1)}, u32[]{:S(2)}, u32[]{:S(2)}) collective-permute-start(f32[3,64,256]{2,1,0:T(8,128)S(1)} %get-tuple-element.137), channel_id=1, source_target_pairs={{0,1},{1,0},{2,3},{3,2},{4,5},{5,4},{6,7},{7,6},{8,9},{9,8},{10,11... | collective-permute-start | bytes 589832 | tf_op jit(solution)/shard_map/ppermute | solution.py:707
  147.1 10.4 %collective-permute-start.27 = (f32[3,64,256]{2,1,0:T(8,128)S(1)}, f32[3,64,256]{2,1,0:T(8,128)S(1)}, u32[]{:S(2)}, u32[]{:S(2)}) collective-permute-start(f32[3,64,256]{2,1,0:T(8,128)S(1)} %get-tuple-element.140), channel_id=1, source_target_pairs={{4,0},{5,8},{8,13},{9,1},{0,4},{1,5},{12,9},{13,12},{6,2},{7,10},{... | collective-permute-start | bytes 589832 | tf_op jit(solution)/shard_map/ppermute | solution.py:704
  148.1 9.7 %collective-permute-start.28 = (f32[3,64,256]{2,1,0:T(8,128)S(1)}, f32[3,64,256]{2,1,0:T(8,128)S(1)}, u32[]{:S(2)}, u32[]{:S(2)}) collective-permute-start(f32[3,64,256]{2,1,0:T(8,128)S(1)} %get-tuple-element.139), channel_id=1, source_target_pairs={{4,8},{5,12},{8,1},{9,5},{0,0},{1,4},{12,9},{13,13},{6,10},{7,14},... | collective-permute-start | bytes 589832 | tf_op jit(solution)/shard_map/ppermute | solution.py:704
  150.1 9.2 %collective-permute-start.29 = (f32[3,64,256]{2,1,0:T(8,128)S(1)}, f32[3,64,256]{2,1,0:T(8,128)S(1)}, u32[]{:S(2)}, u32[]{:S(2)}) collective-permute-start(f32[3,64,256]{2,1,0:T(8,128)S(1)} %get-tuple-element.138), channel_id=1, source_target_pairs={{4,12},{5,0},{8,5},{9,13},{0,1},{1,4},{12,8},{13,9},{6,14},{7,2},{... | collective-permute-start | bytes 589832 | tf_op jit(solution)/shard_map/ppermute | solution.py:704
  154.1 1.0 copy-start.22

commit v9 on v7

--- a/solution.py
+++ b/solution.py
@@ -223,6 +223,44 @@
     return split(first), split(second)
 
 
+def fetch_half(rounds, own, got, side, buffers, sems):
+    half = buffers[0].shape[0] // CELL
+    place, core = position()
+    mine = core == place - home_of(0)
+    for which in range(2):
+        for turn, piece in enumerate(rounds):
+            pltpu.make_async_copy(
+                piece.at[pl.ds(which * half, half)],
+                buffers[which].at[pl.ds(turn * half, half)],
+                sems.at[which, turn],
+            ).start()
+
+    def local(source):
+        for which in range(2):
+            pltpu.make_async_copy(
+                source.at[pl.ds((which * 2 + side) * half, half)],
+                buffers[which].at[pl.ds(ROUNDS * half, half)],
+                sems.at[which, ROUNDS],
+            ).start()
+
+    @pl.when(mine)
+    def _():
+        local(own)
+
+    @pl.when(jnp.logical_not(mine))
+    def _():
+        local(got)
+
+
+def take_half(buffers, sems):
+    half = buffers[0].shape[0] // CELL
+    for which in range(2):
+        for chunk in range(CELL):
+            view = buffers[which].at[pl.ds(chunk * half, half)]
+            pltpu.make_async_copy(view, view, sems.at[which, chunk]).wait()
+    return split(buffers[0][...]), split(buffers[1][...])
+
+
 def row_starts(cells, reps, rows):
     place, core = position()
     rep = lax.axis_index("rep")
@@ -311,55 +349,54 @@
         high[which], low[which] = split(moved * (jnp.sqrt(old) / jnp.sqrt(new)))
 
 
-def read_kernel(*refs):
-    near, far, (own, got, high, low), refs = refs[:3], refs[3:6], refs[6:10], refs[10:]
-    totals, near_out, far_out, scratch = refs[0], refs[1:4], refs[4], refs[5:]
-    queries, cots, turned, acts, sent, row_sems, out_sems = scratch
-    fetch_rows(near, far, own, got, (queries, cots), row_sems)
-    size = queries.shape[1]
-    half = size // 2
+def read_kernel(side, *refs):
+    rounds, (own, got, high, low), refs = refs[:3], refs[3:7], refs[7:]
+    before, refs = (refs[:2], refs[2:]) if side else ((), refs)
+    main, refs = (refs[0], refs[1:]) if side else (None, refs)
+    round_out, rest_out = (refs[:3], refs[3]) if side == 0 else (None, refs[0])
+    refs = refs[4:] if side == 0 else refs[1:]
+    turned, acts, queries, cots, sent, row_sems, out_sems = refs
+    half = queries.shape[0] // CELL
+    fetch_half(rounds, own, got, side, (queries, cots), row_sems)
 
     def weight(which):
         return high[which], low[which]
 
-    def outgoing(block):
-        if block < ROUNDS:
-            return [
-                (sent.at[block, pl.ds(0, half)], near_out[block]),
-                (sent.at[block, pl.ds(half, half)], far_out.at[pl.ds(block * half, half)]),
-            ]
-        return [(sent.at[block], far_out.at[pl.ds(ROUNDS * half, size)])]
-
-    @pl.loop(0, CELL // GROUP)
-    def _(group):
-        query, cot = take_rows((queries, cots), group, row_sems)
-        where = pl.ds(pl.multiple_of(group * GROUP * size, GROUP * size), GROUP * size)
-        gate_pre = dot3(query, weight(0), NN)
-        up_pre = dot3(query, weight(1), NN)
-        back = dot3(cot, weight(2), NN)
-        _, act, slope = silu_parts(gate_pre)
-        gate_back = split(back * up_pre * slope)
-        up_back = split(back * act)
-        for part in range(2):
-            acts[part, 0, where] = gate_back[part]
-            acts[part, 1, where] = up_back[part]
-            turned[part, 0, :, where] = query[part].T
-            turned[part, 1, :, where] = cot[part].T
-        store_split(acts, (2, where), act * up_pre)
-        result = dot3(gate_back, weight(0), NT) + dot3(up_back, weight(1), NT)
-        sent[pl.ds(group * GROUP, GROUP)] = result.reshape(GROUP, size, result.shape[1])
-        for number in range(CELL):
-
-            @pl.when(group == number // GROUP)
-            def _():
-                for side, (source, out) in enumerate(outgoing(number)):
-                    pltpu.make_async_copy(source, out, out_sems.at[number, side]).start()
-
-    for which in range(3):
-        totals[which] = dot3(pair_of(turned, which // 2), pair_of(acts, which), NN)
-    for block in range(CELL):
-        for side, (source, out) in enumerate(outgoing(block)):
-            pltpu.make_async_copy(source, out, out_sems.at[block, side]).wait()
+    query, cot = take_half((queries, cots), row_sems)
+    gate_pre = dot3(query, weight(0), NN)
+    up_pre = dot3(query, weight(1), NN)
+    back = dot3(cot, weight(2), NN)
+    _, act, slope = silu_parts(gate_pre)
+    gate_back = split(back * up_pre * slope)
+    up_back = split(back * act)
+    sent[...] = dot3(gate_back, weight(0), NT) + dot3(up_back, weight(1), NT)
+    if side == 0:
+        copies = [
+            pltpu.make_async_copy(sent.at[pl.ds(turn * half, half)], out, out_sems.at[turn])
+            for turn, out in enumerate(round_out)
+        ]
+        copies.append(
+            pltpu.make_async_copy(
+                sent.at[pl.ds(ROUNDS * half, half)], rest_out, out_sems.at[ROUNDS]
+            )
+        )
+    else:
+        copies = [pltpu.make_async_copy(sent, rest_out, out_sems.at[0])]
+    for copy in copies:
+        copy.start()
+    for part in range(2):
+        acts[part, 0] = gate_back[part]
+        acts[part, 1] = up_back[part]
+        turned[part, 0] = query[part].T
+        turned[part, 1] = cot[part].T
+    store_split(acts, (2,), act * up_pre)
+    if side:
+        for which in range(3):
+            main[which] = dot3(
+                pair_of(before[0], which // 2), pair_of(before[1], which), NN
+            ) + dot3(pair_of(turned, which // 2), pair_of(acts, which), NN)
+    for copy in copies:
+        copy.wait()
 
 
 def renew_back_kernel(cells, weights, steps, totals, cots, direct):
@@ -568,8 +605,9 @@
         far = [lax.ppermute(piece, "head", SWAP) for piece in near]
         return near + far + [local, lax.ppermute(local, "head", SWAP)]
 
-    def combine(near, far):
-        across = lax.ppermute(far, "head", SWAP)
+    def combine(near, far, across=None):
+        if across is None:
+            across = lax.ppermute(far, "head", SWAP)
         length = near[0].shape[0]
         found = [
             part + across[number * length : (number + 1) * length]
@@ -643,18 +681,31 @@
     )
     *read_near, read_local, high = lax.optimization_barrier((*read_near, read_local, high))
     read_rows = spread(list(read_near), read_local)
+    span = CELL * half
     piece = shape((half, depth), F32)
-    read = call(
-        read_kernel,
-        read_rows + [high, low],
-        [HBM] * 8 + [VMEM] * 2,
-        [square] + [piece] * ROUNDS + [shape((ROUNDS * half + size, depth), F32)],
-        [VMEM] + [HBM] * (ROUNDS + 1),
-        buffers
-        + [turned, acts, pltpu.VMEM((CELL, size, depth), F32), dma((CELL, 4)), dma((CELL, 2))],
-        8 * product,
-    )
-    totals = read[0]
+    turned_shape = shape((2, 2, depth, span), BF16)
+    acts_shape = shape((2, 3, span, cols), BF16)
+    read_scratch = [pltpu.VMEM((span, depth), F32)] * 3 + [dma((2, CELL)), dma((CELL,))]
+    *query_near, query_first, turned_first, read_acts = call(
+        functools.partial(read_kernel, 0),
+        read_rows[:ROUNDS] + read_rows[2 * ROUNDS :] + [high, low],
+        [HBM] * (ROUNDS + 2) + [VMEM] * 2,
+        [piece] * CELL + [turned_shape, acts_shape],
+        [HBM] * CELL + [VMEM] * 2,
+        read_scratch,
+        5 * product // 2,
+        18,
+    )
+    totals, query_far = call(
+        functools.partial(read_kernel, 1),
+        read_rows[ROUNDS:] + [high, low, turned_first, read_acts],
+        [HBM] * (ROUNDS + 2) + [VMEM] * 4,
+        [square, shape((span, depth), F32)],
+        [VMEM, HBM],
+        [pltpu.VMEM(turned_shape.shape, BF16), pltpu.VMEM(acts_shape.shape, BF16)] + read_scratch,
+        11 * product // 2,
+        18,
+    )
     if cells > 1:
         totals = lax.psum(totals, "tok", axis_index_groups=cell_groups)
     cots, direct = call(
@@ -709,16 +760,29 @@
         return outs[:rounds], outs[rounds], list(outs[rounds + 1 :])
 
     near_first, far_first, (acts_first,) = token_grads(0, middle, cots)
-    query_totals, query_local = combine(read[1:4], read[4])
+    query_got = lax.ppermute(query_far, "head", SWAP)
+    query_totals = [
+        part + query_got[turn * half : (turn + 1) * half] for turn, part in enumerate(query_near)
+    ]
     cots, *query_totals = lax.optimization_barrier((cots, *query_totals))
     query_back = hand_back(query_totals, 0)
     near_last, far_last, given = token_grads(middle, CELL, cots, key_turned, direct, acts_first)
-    far_last, *rest = lax.optimization_barrier((far_last, *near_first, *query_back))
+    got_first = lax.ppermute(far_first, "head", SWAP)
+    far_last, got_first, *rest = lax.optimization_barrier(
+        (far_last, got_first, *near_first, *query_back)
+    )
     near_first, query_back = rest[:-ROUNDS], rest[-ROUNDS:]
-    totals_first, _ = combine(near_first, far_first)
+    totals_first, _ = combine(near_first, far_first, got_first)
     back = hand_back(totals_first, 0)
     totals_last, local = combine(near_last, far_last)
     back += hand_back(totals_last, middle)
+    query_first, *totals_last = lax.optimization_barrier((query_first, *totals_last))
+    query_local = jnp.concatenate(
+        (
+            query_first + lax.ppermute(query_first, "head", SWAP),
+            (query_far + query_got)[ROUNDS * half :],
+        )
+    )
     given[0], *back = lax.optimization_barrier((given[0], *back))
     (query_grad,) = settle(query_back, query_local)
     key_grad, target_grad = settle(back, local)

time: 159 us -> 158 us (level)
    ppermute x6, waiting for transfers between devices: 3.9 us -> 0.02 us  [spread(): far = [lax.ppermute(piece, 'head', SWAP) for piece in near]]
    broadcast_in_dim x1 -> x0, other arithmetic: 2.14 us -> none  [per_device(): query_grad[None, None]]
    ppermute x2, waiting for transfers between devices: 0.01 us -> 1.64 us  [spread(): return near + far + [local, lax.ppermute(local, 'head', SWAP)]]
    unnamed x38 -> x42, local copies, waits for them, and re-layouts: 2.75 us -> 3.76 us
    pallas_call x8 -> x9, Pallas kernels: 42.2 us -> 42.2 us  [call(): pl.pallas_call(kernel, out_shape=outs, in_specs=in_specs, out_specs=out_s...]
  transfers between devices with their start and end apart: 29 -> 30, of which waited for: 13 -> 12; matrix products, arithmetic and copies ran while one was open for 5% -> 5% of each run, Pallas kernels for 17% -> 20%
where the time goes in v9:
time: 158 us; the launch traced here: 156 us
  waiting for transfers between devices  69.9 us (44%)
  Pallas kernels  42.2 us (27%)
  starting transfers between devices  28.2 us (18%)
  other arithmetic  9.74 us (6%)
  local copies, waits for them, and re-layouts  4.74 us (3%)
    pallas_call x9, Pallas kernels, call(): pl.pallas_call(kernel, out_shape=outs, in_specs=in_specs, out_specs=out_s...  42.2 us
    ppermute x6, waiting for transfers between devices, gather(): lax.ppermute(packed[turn], PLACE, pairs[turn])  32.1 us
    ppermute x6, waiting for transfers between devices, hand_back(): lax.ppermute(total, PLACE, flipped(pairs[first + number]))  17.2 us
    ppermute x1, waiting for transfers between devices, per_device(): parts.append(lax.ppermute(together, 'rep', shifted(shift, 1)))  14.9 us
    ppermute x6, starting transfers between devices, hand_back(): lax.ppermute(total, PLACE, flipped(pairs[first + number]))  10.2 us
    ppermute x6, starting transfers between devices, gather(): lax.ppermute(packed[turn], PLACE, pairs[turn])  7.46 us
    ppermute x3, starting transfers between devices, per_device(): lax.ppermute(total[turn], PLACE, flipped(pairs[turn]))  5.26 us
    ppermute x3, waiting for transfers between devices, per_device(): lax.ppermute(total[turn], PLACE, flipped(pairs[turn]))  3.96 us
  transfers between devices with their start and end apart: 30, of which 12 were waited for; matrix products, arithmetic and copies ran while one was open for 5% of the time, Pallas kernels for 20%

profile of v9, /device:TPU:22, one launch (start us, length us, event | category | flops | bytes accessed | tf_op | source)
XLA Modules:
  0.0 155.8 jit_solution(7994578737515886050)
XLA Ops:
  0.6 0.8 copy.20
  1.4 0.7 fusion.3.refs_5_
  2.2 4.0 %shard_map.135 = (f32[352,512]{1,0:T(8,128)}, f32[352,512]{1,0:T(8,128)}, f32[352,512]{1,0:T(8,128)}, f32[608,512]{1,0:T(8,128)}, f32[96,512]{1,0:T(8,128)}) custom-call(f32[256,512]{1,0:T(8,128)} %bitcast.50, f32[256,512]{1,0:T(8,128)} %bitcast.49, f32[64,512]{1,0:T(8,128)} %bitcast.51, f32[64,512]{1,0:T(8,128)} %bitcast.52, f32[64,512]{1,0:T(8,128)} %bitcast.53, ...), custom_call_target="tpu_custom_call" | custom-call | bytes 5047296 | tf_op jit(solution)/shard_map/pallas_call | solution.py:538
  6.2 0.1 collective-permute-start
  6.3 0.6 collective-permute-start.4
  6.9 2.3 %collective-permute-start.5 = (f32[352,512]{1,0:T(8,128)}, f32[352,512]{1,0:T(8,128)S(1)}, u32[]{:S(2)}, u32[]{:S(2)}) collective-permute-start(f32[352,512]{1,0:T(8,128)} %get-tuple-element.75), channel_id=1, source_target_pairs={{8,4},{12,5},{1,8},{5,9},{0,0},{4,1},{9,12},{13,13},{10,6},{14,7},... | collective-permute-start | bytes 2162696 | tf_op jit(solution)/shard_map/ppermute | solution.py:601
  9.2 1.3 collective-permute-start.6
  10.5 11.9 %collective-permute-done.4.refs_2_.refs_0_ = f32[352,512]{1,0:T(8,128)S(1)} collective-permute-done((f32[352,512]{1,0:T(8,128)}, f32[352,512]{1,0:T(8,128)S(1)}, u32[]{:S(2)}, u32[]{:S(2)}) %collective-permute-start.4) | collective-permute-done | bytes 720928 | tf_op jit(solution)/shard_map/ppermute | solution.py:601
  22.4 18.6 %collective-permute-done.5.refs_3_.refs_1_ = f32[352,512]{1,0:T(8,128)S(1)} collective-permute-done((f32[352,512]{1,0:T(8,128)}, f32[352,512]{1,0:T(8,128)S(1)}, u32[]{:S(2)}, u32[]{:S(2)}) %collective-permute-start.5) | collective-permute-done | bytes 720928 | tf_op jit(solution)/shard_map/ppermute | solution.py:601
  41.0 1.5 collective-permute-done.6.refs_4_.refs_0_
  42.5 0.5 collective-permute-start.8
  43.2 0.6 collective-permute-start.7
  43.8 1.1 collective-permute-start.9
  44.9 0.3 shard_map.136
  45.3 1.9 %collective-permute-start.2 = (f32[256,512]{1,0:T(8,128)S(1)}, f32[256,512]{1,0:T(8,128)S(1)}, u32[]{:S(2)}, u32[]{:S(2)}) collective-permute-start(f32[256,512]{1,0:T(8,128)S(1)} %get-tuple-element.71), channel_id=1, source_target_pairs={{8,4},{12,5},{1,8},{5,9},{0,0},{4,1},{9,12},{13,13},{10,6},{14,7},... | collective-permute-start | bytes 1572872 | tf_op jit(solution)/shard_map/ppermute | solution.py:601
  47.2 1.3 collective-permute-start.3
  48.5 14.9 %collective-permute-done.7.refs_1_ = f32[4,96,512]{2,1,0:T(8,128)S(1)} collective-permute-done((f32[4,96,512]{2,1,0:T(8,128)S(1)}, f32[4,96,512]{2,1,0:T(8,128)S(1)}, u32[]{:S(2)}, u32[]{:S(2)}) %collective-permute-start.7) | collective-permute-done | bytes 786464 | tf_op jit(solution)/shard_map/ppermute | solution.py:654
  63.4 7.5 %shard_map.137 = (f32[3,512,256]{2,1,0:T(8,128)S(1)}, f32[1024,256]{1,0:T(8,128)S(1)}, f32[1024,256]{1,0:T(8,128)S(1)}, f32[1024,256]{1,0:T(8,128)S(1)}, bf16[2,...) custom-call(f32[4,96,512]{2,1,0:T(8,128)S(1)} %pad_maximum_fusion.refs_0_, ...), custom_call_target="tpu_custom_call" | custom-call | flops 4831838208 | bytes 18874368 | tf_op jit(solution)/shard_map/pallas_call | solution.py:538
  71.0 0.6 shard_map.138
  71.6 0.1 collective-permute-done.3.refs_2_
  71.7 0.4 collective-permute-start.11
  72.1 0.1 collective-permute-start.12
  72.2 0.4 collective-permute-start.13
  72.6 0.1 collective-permute-start.14
  72.8 1.6 %collective-permute-done.11.refs_4_ = f32[512,512]{1,0:T(8,128)S(1)} collective-permute-done((f32[512,512]{1,0:T(8,128)S(1)}, f32[512,512]{1,0:T(8,128)S(1)}, u32[]{:S(2)}, u32[]{:S(2)}) %collective-permute-start.11) | collective-permute-done | bytes 1048608 | tf_op jit(solution)/shard_map/ppermute | solution.py:606
  74.4 5.0 %shard_map.139 = (f32[128,512]{1,0:T(8,128)S(1)}, f32[128,512]{1,0:T(8,128)S(1)}, f32[128,512]{1,0:T(8,128)S(1)}, f32[128,512]{1,0:T(8,128)S(1)}, bf16[2,2,512,5...) custom-call(f32[256,512]{1,0:T(8,128)S(1)} %collective-permute-done.1.refs_0_, ...), custom_call_target="tpu_custom_call" | custom-call | flops 2013265920 | bytes 9961472 | tf_op jit(solution)/shard_map/pallas_call | solution.py:538
  79.4 0.7 copy-done.3
  80.1 7.1 %shard_map.140 = (f32[3,512,256]{2,1,0:T(8,128)S(1)}, f32[512,512]{1,0:T(8,128)S(1)}) custom-call(f32[256,512]{1,0:T(8,128)S(1)} %collective-permute-done.12.refs_0_, f32[256,512]{1,0:T(8,128)S(1)} %collective-permute-done.13.refs_1_, f32[256,512]{1,0:T(8,128)S(1)} %collective-permute-done.14.refs_2_, f32[512,512]{1,0:T(8,128)S(1)} %get-tuple-element.88.refs_3_, ...), custom_call_target="tpu_custom_call" | custom-call | flops 4429185024 | bytes 11534336 | tf_op jit(solution)/shard_map/pallas_call | solution.py:538
  87.2 0.4 collective-permute-start.15
  87.6 1.2 shard_map.141
  88.8 6.3 %shard_map.142 = (f32[256,512]{1,0:T(8,128)S(1)}, f32[256,512]{1,0:T(8,128)S(1)}, f32[512,512]{1,0:T(8,128)S(1)}, bf16[2,3,512,256]{3,2,1,0:T(8,128)(2,1)S(1)}) custom-call(f32[352,512]{1,0:T(8,128)S(1)} %collective-permute-done.4.refs_2_.refs_0_, f32[352,512]{1,0:T(8,128)S(1)} %collective-permute-done.5.refs_3_.refs_1_, ...), custom_call_target="tpu_custom_call" | custom-call | flops 3623878656 | bytes 12845056 | tf_op jit(solution)/shard_map/pallas_call | solution.py:538
  95.2 0.2 collective-permute-start.16
  95.4 0.9 slice_add_fusion.5
  96.3 3.2 %collective-permute-start.18 = (f32[128,512]{1,0:T(8,128)S(1)}, f32[128,512]{1,0:T(8,128)S(1)}, u32[]{:S(2)}, u32[]{:S(2)}) collective-permute-start(f32[128,512]{1,0:T(8,128)S(1)} %get-tuple-element.113), channel_id=1, source_target_pairs={{4,8},{5,12},{8,1},{9,5},{0,0},{1,4},{12,9},{13,13},{6,10},{7,14},... | collective-permute-start | bytes 786440 | tf_op jit(solution)/shard_map/ppermute | solution.py:620
  99.5 1.9 %collective-permute-start.19 = (f32[128,512]{1,0:T(8,128)S(1)}, f32[128,512]{1,0:T(8,128)S(1)}, u32[]{:S(2)}, u32[]{:S(2)}) collective-permute-start(f32[128,512]{1,0:T(8,128)S(1)} %get-tuple-element.114), channel_id=1, source_target_pairs={{4,12},{5,0},{8,5},{9,13},{0,1},{1,4},{12,8},{13,9},{6,14},{7,2},{... | collective-permute-start | bytes 786440 | tf_op jit(solution)/shard_map/ppermute | solution.py:620
  101.4 10.1 %shard_map.143 = (f32[256,512]{1,0:T(8,128)S(1)}, f32[768,512]{1,0:T(8,128)S(1)}, f32[1,4,3,64,256]{4,3,2,1,0:T(8,128)S(1)}, f32[1,4,3,64,256]{4,3,2,1,0:T(8,128)S(1)}) custom-call(f32[352,512]{1,0:T(8,128)S(1)} %copy-done.6, f32[352,512]{1,0:T(8,128)S(1)} %collective-permute-done.10.refs_7_.refs_1_, f32[608,512]{1,0:T(8,128)S(1)} %copy-done.9, ...), custom_call_target="tpu_custom_call" | custom-call | flops 6039797760 | bytes 21233664 | tf_op jit(solution)/shard_map/pallas_call | solution.py:538
  111.6 0.9 copy-done.10
  112.5 0.9 copy-done.12
  113.5 0.1 copy-done.14
  113.5 0.1 copy-done.16
  113.6 0.1 copy-done.18
  113.7 1.3 collective-permute-start.25
  115.1 1.6 %slice_add_fusion.2 = (f32[256,512]{1,0:T(8,128)S(1)}, f32[256,512]{1,0:T(8,128)S(1)}) fusion(f32[256,512]{1,0:T(8,128)} %copy-done.2, f32[512,512]{1,0:T(8,128)} %copy-done.12, f32[256,512]{1,0:T(8,128)S(1)} %get-tuple-element.121), kind=kLoop, calls=%fused_computation.12 | loop fusion | flops 262144 | bytes 3145728 | tf_op jit(solution)/shard_map/add | solution.py:613
  116.7 0.3 collective-permute-start.22
  117.0 2.9 %collective-permute-start.23 = (f32[256,512]{1,0:T(8,128)S(1)}, f32[256,512]{1,0:T(8,128)S(1)}, u32[]{:S(2)}, u32[]{:S(2)}) collective-permute-start(f32[256,512]{1,0:T(8,128)S(1)} %get-tuple-element.136), channel_id=1, source_target_pairs={{4,8},{5,12},{8,1},{9,5},{0,0},{1,4},{12,9},{13,13},{6,10},{7,14},... | collective-permute-start | bytes 1572872 | tf_op jit(solution)/shard_map/ppermute | solution.py:620
  120.0 1.1 slice_add_fusion.1
  121.2 1.8 %collective-permute-start.24 = (f32[256,512]{1,0:T(8,128)S(1)}, f32[256,512]{1,0:T(8,128)S(1)}, u32[]{:S(2)}, u32[]{:S(2)}) collective-permute-start(f32[256,512]{1,0:T(8,128)S(1)} %slice_add_fusion.1), channel_id=1, source_target_pairs={{4,12},{5,0},{8,5},{9,13},{0,1},{1,4},{12,8},{13,9},{6,14},{7,2},{... | collective-permute-start | bytes 1572872 | tf_op jit(solution)/shard_map/ppermute | solution.py:620
  123.0 1.5 slice_add_fusion
  124.5 0.9 maximum_select_fusion
  125.4 2.7 %collective-permute-done.22 = f32[256,512]{1,0:T(8,128)S(1)} collective-permute-done((f32[256,512]{1,0:T(8,128)S(1)}, f32[256,512]{1,0:T(8,128)S(1)}, u32[]{:S(2)}, u32[]{:S(2)}) %collective-permute-start.22) | collective-permute-done | bytes 524320 | tf_op jit(solution)/shard_map/ppermute | solution.py:620
  128.2 5.6 %collective-permute-done.23 = f32[256,512]{1,0:T(8,128)S(1)} collective-permute-done((f32[256,512]{1,0:T(8,128)S(1)}, f32[256,512]{1,0:T(8,128)S(1)}, u32[]{:S(2)}, u32[]{:S(2)}) %collective-permute-start.23) | collective-permute-done | bytes 524320 | tf_op jit(solution)/shard_map/ppermute | solution.py:620
  133.7 8.9 %collective-permute-done.24 = f32[256,512]{1,0:T(8,128)S(1)} collective-permute-done((f32[256,512]{1,0:T(8,128)S(1)}, f32[256,512]{1,0:T(8,128)S(1)}, u32[]{:S(2)}, u32[]{:S(2)}) %collective-permute-start.24) | collective-permute-done | bytes 524320 | tf_op jit(solution)/shard_map/ppermute | solution.py:620
  142.6 0.1 bitcast_add_fusion
  142.8 0.1 collective-permute-start.26
  142.8 1.2 collective-permute-start.27
  144.0 1.9 %collective-permute-start.28 = (f32[3,64,256]{2,1,0:T(8,128)S(1)}, f32[3,64,256]{2,1,0:T(8,128)S(1)}, u32[]{:S(2)}, u32[]{:S(2)}) collective-permute-start(f32[3,64,256]{2,1,0:T(8,128)S(1)} %get-tuple-element.144), channel_id=1, source_target_pairs={{4,8},{5,12},{8,1},{9,5},{0,0},{1,4},{12,9},{13,13},{6,10},{7,14},... | collective-permute-start | bytes 589832 | tf_op jit(solution)/shard_map/ppermute | solution.py:799
  145.9 2.2 %collective-permute-start.29 = (f32[3,64,256]{2,1,0:T(8,128)S(1)}, f32[3,64,256]{2,1,0:T(8,128)S(1)}, u32[]{:S(2)}, u32[]{:S(2)}) collective-permute-start(f32[3,64,256]{2,1,0:T(8,128)S(1)} %get-tuple-element.143), channel_id=1, source_target_pairs={{4,12},{5,0},{8,5},{9,13},{0,1},{1,4},{12,8},{13,9},{6,14},{7,2},{... | collective-permute-start | bytes 589832 | tf_op jit(solution)/shard_map/ppermute | solution.py:799
  148.1 0.2 select_select_fusion.1
  148.4 0.9 copy-done.11
  149.3 1.2 multiply_reduce_fusion
  150.5 0.6 divide_multiply_fusion
  151.1 2.4 %collective-permute-done.28 = f32[3,64,256]{2,1,0:T(8,128)S(1)} collective-permute-done((f32[3,64,256]{2,1,0:T(8,128)S(1)}, f32[3,64,256]{2,1,0:T(8,128)S(1)}, u32[]{:S(2)}, u32[]{:S(2)}) %collective-permute-start.28) | collective-permute-done | bytes 196640 | tf_op jit(solution)/shard_map/ppermute | solution.py:799
  153.5 1.5 collective-permute-done.29
  155.1 0.8 pad_maximum_fusion.1
  (71 shorter events, 0.7 us)
Async XLA Ops:
  6.2 36.8 %collective-permute-start = (f32[608,512]{1,0:T(8,128)}, f32[608,512]{1,0:T(8,128)S(1)}, u32[]{:S(2)}, u32[]{:S(2)}) collective-permute-start(f32[608,512]{1,0:T(8,128)} %get-tuple-element.68.refs_8_.refs_2_), channel_id=1, source_target_pairs={{0,1},{1,0},{2,3},{3,2},{4,5},{5,4},{6,7},{7,6},{8,9},{9,8},{10,11... | collective-permute-start | bytes 3735560 | tf_op jit(solution)/shard_map/ppermute | solution.py:606
  6.3 16.1 %collective-permute-start.4 = (f32[352,512]{1,0:T(8,128)}, f32[352,512]{1,0:T(8,128)S(1)}, u32[]{:S(2)}, u32[]{:S(2)}) collective-permute-start(f32[352,512]{1,0:T(8,128)} %get-tuple-element.74), channel_id=1, source_target_pairs={{0,4},{8,5},{13,8},{1,9},{4,0},{5,1},{9,12},{12,13},{2,6},{10,7},{... | collective-permute-start | bytes 2162696 | tf_op jit(solution)/shard_map/ppermute | solution.py:601
  6.9 34.2 %collective-permute-start.5 = (f32[352,512]{1,0:T(8,128)}, f32[352,512]{1,0:T(8,128)S(1)}, u32[]{:S(2)}, u32[]{:S(2)}) collective-permute-start(f32[352,512]{1,0:T(8,128)} %get-tuple-element.75), channel_id=1, source_target_pairs={{8,4},{12,5},{1,8},{5,9},{0,0},{4,1},{9,12},{13,13},{10,6},{14,7},... | collective-permute-start | bytes 2162696 | tf_op jit(solution)/shard_map/ppermute | solution.py:601
  9.2 33.3 %collective-permute-start.6 = (f32[352,512]{1,0:T(8,128)}, f32[352,512]{1,0:T(8,128)S(1)}, u32[]{:S(2)}, u32[]{:S(2)}) collective-permute-start(f32[352,512]{1,0:T(8,128)} %get-tuple-element.76), channel_id=1, source_target_pairs={{12,4},{0,5},{5,8},{13,9},{1,0},{4,1},{8,12},{9,13},{14,6},{2,7},{... | collective-permute-start | bytes 2162696 | tf_op jit(solution)/shard_map/ppermute | solution.py:601
  42.5 20.9 %copy-start.5 = (f32[352,512]{1,0:T(8,128)}, f32[352,512]{1,0:T(8,128)S(1)}, u32[]{:S(2)}) copy-start(f32[352,512]{1,0:T(8,128)S(1)} %collective-permute-done.6.refs_4_.refs_0_) | copy-start | bytes 2162692
  42.5 2.8 %collective-permute-start.10 = (f32[352,512]{1,0:T(8,128)S(1)}, f32[352,512]{1,0:T(8,128)S(1)}, u32[]{:S(2)}, u32[]{:S(2)}) collective-permute-start(f32[352,512]{1,0:T(8,128)S(1)} %collective-permute-done.6.refs_4_.refs_0_), channel_id=1, source_target_pairs={{0,1},{1,0},{2,3},{3,2},{4,5},{5,4},{6,7},{7,6},{8,9},{9,8},{10,11... | collective-permute-start | bytes 2162696 | tf_op jit(solution)/shard_map/ppermute | solution.py:605
  42.5 4.7 %collective-permute-start.8 = (f32[352,512]{1,0:T(8,128)S(1)}, f32[352,512]{1,0:T(8,128)S(1)}, u32[]{:S(2)}, u32[]{:S(2)}) collective-permute-start(f32[352,512]{1,0:T(8,128)S(1)} %collective-permute-done.4.refs_2_.refs_0_), channel_id=1, source_target_pairs={{0,1},{1,0},{2,3},{3,2},{4,5},{5,4},{6,7},{7,6},{8,9},{9,8},{10,11... | collective-permute-start | bytes 2162696 | tf_op jit(solution)/shard_map/ppermute | solution.py:605
  43.0 1.9 %copy-start = (f32[1,1,256,512]{3,2,1,0:T(8,128)S(1)}, f32[1,1,256,512]{3,2,1,0:T(8,128)}, u32[]{:S(2)}) copy-start(f32[1,1,256,512]{3,2,1,0:T(8,128)} %param.8) | copy-start | bytes 1572868
  43.0 1.9 %copy-start.1 = (f32[1,1,256,512]{3,2,1,0:T(8,128)S(1)}, f32[1,1,256,512]{3,2,1,0:T(8,128)}, u32[]{:S(2)}) copy-start(f32[1,1,256,512]{3,2,1,0:T(8,128)} %param.12) | copy-start | bytes 1572868
  43.1 20.3 %copy-start.7 = (f32[608,512]{1,0:T(8,128)}, f32[608,512]{1,0:T(8,128)S(1)}, u32[]{:S(2)}) copy-start(f32[608,512]{1,0:T(8,128)S(1)} %collective-permute-done.refs_9_.refs_3_) | copy-start | bytes 3735556
  43.1 20.3 %copy-start.9 = (f32[608,512]{1,0:T(8,128)S(1)}, f32[608,512]{1,0:T(8,128)}, u32[]{:S(2)}) copy-start(f32[608,512]{1,0:T(8,128)} %get-tuple-element.68.refs_8_.refs_2_) | copy-start | bytes 3735556
  43.2 20.2 %collective-permute-start.7 = (f32[4,96,512]{2,1,0:T(8,128)S(1)}, f32[4,96,512]{2,1,0:T(8,128)S(1)}, u32[]{:S(2)}, u32[]{:S(2)}) collective-permute-start(f32[4,96,512]{2,1,0:T(8,128)S(1)} %pad_maximum_fusion.refs_0_), channel_id=1, source_target_pairs={{0,2},{2,0},{1,3},{3,1},{4,6},{6,4},{5,7},{7,5},{8,10},{10,8},{9,1... | collective-permute-start | bytes 2359304 | tf_op jit(solution)/shard_map/ppermute | solution.py:654
  43.8 4.7 %collective-permute-start.9 = (f32[352,512]{1,0:T(8,128)S(1)}, f32[352,512]{1,0:T(8,128)S(1)}, u32[]{:S(2)}, u32[]{:S(2)}) collective-permute-start(f32[352,512]{1,0:T(8,128)S(1)} %collective-permute-done.5.refs_3_.refs_1_), channel_id=1, source_target_pairs={{0,1},{1,0},{2,3},{3,2},{4,5},{5,4},{6,7},{7,6},{8,9},{9,8},{10,11... | collective-permute-start | bytes 2162696 | tf_op jit(solution)/shard_map/ppermute | solution.py:605
  45.2 26.4 %collective-permute-start.1 = (f32[256,512]{1,0:T(8,128)S(1)}, f32[256,512]{1,0:T(8,128)S(1)}, u32[]{:S(2)}, u32[]{:S(2)}) collective-permute-start(f32[256,512]{1,0:T(8,128)S(1)} %get-tuple-element.70), channel_id=1, source_target_pairs={{0,4},{8,5},{13,8},{1,9},{4,0},{5,1},{9,12},{12,13},{2,6},{10,7},{... | collective-permute-start | bytes 1572872 | tf_op jit(solution)/shard_map/ppermute | solution.py:601
  45.3 26.4 %collective-permute-start.2 = (f32[256,512]{1,0:T(8,128)S(1)}, f32[256,512]{1,0:T(8,128)S(1)}, u32[]{:S(2)}, u32[]{:S(2)}) collective-permute-start(f32[256,512]{1,0:T(8,128)S(1)} %get-tuple-element.71), channel_id=1, source_target_pairs={{8,4},{12,5},{1,8},{5,9},{0,0},{4,1},{9,12},{13,13},{10,6},{14,7},... | collective-permute-start | bytes 1572872 | tf_op jit(solution)/shard_map/ppermute | solution.py:601
  47.2 24.5 %collective-permute-start.3 = (f32[256,512]{1,0:T(8,128)S(1)}, f32[256,512]{1,0:T(8,128)S(1)}, u32[]{:S(2)}, u32[]{:S(2)}) collective-permute-start(f32[256,512]{1,0:T(8,128)S(1)} %get-tuple-element.72), channel_id=1, source_target_pairs={{12,4},{0,5},{5,8},{13,9},{1,0},{4,1},{8,12},{9,13},{14,6},{2,7},{... | collective-permute-start | bytes 1572872 | tf_op jit(solution)/shard_map/ppermute | solution.py:601
  71.7 2.7 %collective-permute-start.11 = (f32[512,512]{1,0:T(8,128)S(1)}, f32[512,512]{1,0:T(8,128)S(1)}, u32[]{:S(2)}, u32[]{:S(2)}) collective-permute-start(f32[512,512]{1,0:T(8,128)S(1)} %get-tuple-element.88.refs_3_), channel_id=1, source_target_pairs={{0,1},{1,0},{2,3},{3,2},{4,5},{5,4},{6,7},{7,6},{8,9},{9,8},{10,11... | collective-permute-start | bytes 3145736 | tf_op jit(solution)/shard_map/ppermute | solution.py:606
  72.1 8.0 %collective-permute-start.12 = (f32[256,512]{1,0:T(8,128)S(1)}, f32[256,512]{1,0:T(8,128)S(1)}, u32[]{:S(2)}, u32[]{:S(2)}) collective-permute-start(f32[256,512]{1,0:T(8,128)S(1)} %collective-permute-done.1.refs_0_), channel_id=1, source_target_pairs={{0,1},{1,0},{2,3},{3,2},{4,5},{5,4},{6,7},{7,6},{8,9},{9,8},{10,11... | collective-permute-start | bytes 1572872 | tf_op jit(solution)/shard_map/ppermute | solution.py:605
  72.2 7.9 %collective-permute-start.13 = (f32[256,512]{1,0:T(8,128)S(1)}, f32[256,512]{1,0:T(8,128)S(1)}, u32[]{:S(2)}, u32[]{:S(2)}) collective-permute-start(f32[256,512]{1,0:T(8,128)S(1)} %collective-permute-done.2.refs_1_), channel_id=1, source_target_pairs={{0,1},{1,0},{2,3},{3,2},{4,5},{5,4},{6,7},{7,6},{8,9},{9,8},{10,11... | collective-permute-start | bytes 1572872 | tf_op jit(solution)/shard_map/ppermute | solution.py:605
  72.6 7.5 %collective-permute-start.14 = (f32[256,512]{1,0:T(8,128)S(1)}, f32[256,512]{1,0:T(8,128)S(1)}, u32[]{:S(2)}, u32[]{:S(2)}) collective-permute-start(f32[256,512]{1,0:T(8,128)S(1)} %collective-permute-done.3.refs_2_), channel_id=1, source_target_pairs={{0,1},{1,0},{2,3},{3,2},{4,5},{5,4},{6,7},{7,6},{8,9},{9,8},{10,11... | collective-permute-start | bytes 1572872 | tf_op jit(solution)/shard_map/ppermute | solution.py:605
  79.4 0.7 copy-start.3
  87.2 8.2 %collective-permute-start.15 = (f32[512,512]{1,0:T(8,128)S(1)}, f32[512,512]{1,0:T(8,128)S(1)}, u32[]{:S(2)}, u32[]{:S(2)}) collective-permute-start(f32[512,512]{1,0:T(8,128)S(1)} %get-tuple-element.103), channel_id=1, source_target_pairs={{0,1},{1,0},{2,3},{3,2},{4,5},{5,4},{6,7},{7,6},{8,9},{9,8},{10,11... | collective-permute-start | bytes 3145736 | tf_op jit(solution)/shard_map/ppermute | solution.py:763
  95.2 1.1 copy-start.2
  95.2 17.3 %collective-permute-start.16 = (f32[512,512]{1,0:T(8,128)S(1)}, f32[512,512]{1,0:T(8,128)S(1)}, u32[]{:S(2)}, u32[]{:S(2)}) collective-permute-start(f32[512,512]{1,0:T(8,128)S(1)} %get-tuple-element.109), channel_id=1, source_target_pairs={{0,1},{1,0},{2,3},{3,2},{4,5},{5,4},{6,7},{7,6},{8,9},{9,8},{10,11... | collective-permute-start | bytes 3145736 | tf_op jit(solution)/shard_map/ppermute | solution.py:770
  95.4 6.1 %copy-start.6 = (f32[352,512]{1,0:T(8,128)S(1)}, f32[352,512]{1,0:T(8,128)}, u32[]{:S(2)}) copy-start(f32[352,512]{1,0:T(8,128)} %copy-done.5) | copy-start | bytes 2162692
  95.4 6.1 %copy-start.8 = (f32[608,512]{1,0:T(8,128)S(1)}, f32[608,512]{1,0:T(8,128)}, u32[]{:S(2)}) copy-start(f32[608,512]{1,0:T(8,128)} %copy-done.7) | copy-start | bytes 3735556
  96.3 16.2 %collective-permute-start.17 = (f32[128,512]{1,0:T(8,128)S(1)}, f32[128,512]{1,0:T(8,128)S(1)}, u32[]{:S(2)}, u32[]{:S(2)}) collective-permute-start(f32[128,512]{1,0:T(8,128)S(1)} %get-tuple-element.112), channel_id=1, source_target_pairs={{4,0},{5,8},{8,13},{9,1},{0,4},{1,5},{12,9},{13,12},{6,2},{7,10},{... | collective-permute-start | bytes 786440 | tf_op jit(solution)/shard_map/ppermute | solution.py:620
  96.3 16.2 %collective-permute-start.18 = (f32[128,512]{1,0:T(8,128)S(1)}, f32[128,512]{1,0:T(8,128)S(1)}, u32[]{:S(2)}, u32[]{:S(2)}) collective-permute-start(f32[128,512]{1,0:T(8,128)S(1)} %get-tuple-element.113), channel_id=1, source_target_pairs={{4,8},{5,12},{8,1},{9,5},{0,0},{1,4},{12,9},{13,13},{6,10},{7,14},... | collective-permute-start | bytes 786440 | tf_op jit(solution)/shard_map/ppermute | solution.py:620
  99.5 13.0 %collective-permute-start.19 = (f32[128,512]{1,0:T(8,128)S(1)}, f32[128,512]{1,0:T(8,128)S(1)}, u32[]{:S(2)}, u32[]{:S(2)}) collective-permute-start(f32[128,512]{1,0:T(8,128)S(1)} %get-tuple-element.114), channel_id=1, source_target_pairs={{4,12},{5,0},{8,5},{9,13},{0,1},{1,4},{12,8},{13,9},{6,14},{7,2},{... | collective-permute-start | bytes 786440 | tf_op jit(solution)/shard_map/ppermute | solution.py:620
  101.4 12.3 %copy-start.20 = (f32[1,1,256]{2,1,0:T(1,128)S(1)}, f32[1,1,256]{2,1,0:T(1,128)}, u32[]{:S(2)}) copy-start(f32[1,1,256]{2,1,0:T(1,128)} %param.11) | copy-start | bytes 3076
  111.6 0.9 copy-start.10
  112.5 1.0 copy-start.12
  112.5 1.1 copy-start.14
  112.5 1.1 copy-start.16
  112.5 1.2 copy-start.18
  113.7 6.3 %collective-permute-start.20 = (f32[768,512]{1,0:T(8,128)S(1)}, f32[768,512]{1,0:T(8,128)}, u32[]{:S(2)}, u32[]{:S(2)}) collective-permute-start(f32[768,512]{1,0:T(8,128)S(1)} %get-tuple-element.115), channel_id=1, source_target_pairs={{0,1},{1,0},{2,3},{3,2},{4,5},{5,4},{6,7},{7,6},{8,9},{9,8},{10,11... | collective-permute-start | bytes 4718600 | tf_op jit(solution)/shard_map/ppermute | solution.py:610
  113.7 6.2 %copy-start.15 = (f32[128,512]{1,0:T(8,128)S(1)}, f32[128,512]{1,0:T(8,128)}, u32[]{:S(2)}) copy-start(f32[128,512]{1,0:T(8,128)} %copy-done.14) | copy-start | bytes 786436
  113.7 6.2 %copy-start.17 = (f32[128,512]{1,0:T(8,128)S(1)}, f32[128,512]{1,0:T(8,128)}, u32[]{:S(2)}) copy-start(f32[128,512]{1,0:T(8,128)} %copy-done.16) | copy-start | bytes 786436
  113.7 6.2 %copy-start.19 = (f32[128,512]{1,0:T(8,128)S(1)}, f32[128,512]{1,0:T(8,128)}, u32[]{:S(2)}) copy-start(f32[128,512]{1,0:T(8,128)} %copy-done.18) | copy-start | bytes 786436
  113.7 28.8 %collective-permute-start.25 = (f32[4,3,64,256]{3,2,1,0:T(8,128)}, f32[4,3,64,256]{3,2,1,0:T(8,128)S(1)}, u32[]{:S(2)}, u32[]{:S(2)}) collective-permute-start(f32[4,3,64,256]{3,2,1,0:T(8,128)} %bitcast.48), channel_id=1, source_target_pairs={{0,2},{2,0},{1,3},{3,1},{4,6},{6,4},{5,7},{7,5},{8,10},{10,8},{9,1... | collective-permute-start | bytes 2359304 | tf_op jit(solution)/shard_map/ppermute | solution.py:797
  116.6 6.3 %copy-start.4 = (f32[128,512]{1,0:T(8,128)S(1)}, f32[128,512]{1,0:T(8,128)}, u32[]{:S(2)}) copy-start(f32[128,512]{1,0:T(8,128)} %copy-done.3) | copy-start | bytes 786436
  116.7 11.5 %collective-permute-start.22 = (f32[256,512]{1,0:T(8,128)S(1)}, f32[256,512]{1,0:T(8,128)S(1)}, u32[]{:S(2)}, u32[]{:S(2)}) collective-permute-start(f32[256,512]{1,0:T(8,128)S(1)} %get-tuple-element.137), channel_id=1, source_target_pairs={{4,0},{5,8},{8,13},{9,1},{0,4},{1,5},{12,9},{13,12},{6,2},{7,10},{... | collective-permute-start | bytes 1572872 | tf_op jit(solution)/shard_map/ppermute | solution.py:620
  117.0 16.7 %collective-permute-start.23 = (f32[256,512]{1,0:T(8,128)S(1)}, f32[256,512]{1,0:T(8,128)S(1)}, u32[]{:S(2)}, u32[]{:S(2)}) collective-permute-start(f32[256,512]{1,0:T(8,128)S(1)} %get-tuple-element.136), channel_id=1, source_target_pairs={{4,8},{5,12},{8,1},{9,5},{0,0},{1,4},{12,9},{13,13},{6,10},{7,14},... | collective-permute-start | bytes 1572872 | tf_op jit(solution)/shard_map/ppermute | solution.py:620
  121.2 21.4 %collective-permute-start.24 = (f32[256,512]{1,0:T(8,128)S(1)}, f32[256,512]{1,0:T(8,128)S(1)}, u32[]{:S(2)}, u32[]{:S(2)}) collective-permute-start(f32[256,512]{1,0:T(8,128)S(1)} %slice_add_fusion.1), channel_id=1, source_target_pairs={{4,12},{5,0},{8,5},{9,13},{0,1},{1,4},{12,8},{13,9},{6,14},{7,2},{... | collective-permute-start | bytes 1572872 | tf_op jit(solution)/shard_map/ppermute | solution.py:620
  123.0 1.6 %copy-start.13 = (f32[1,1,128,512]{3,2,1,0:T(8,128)S(1)}, f32[1,1,128,512]{3,2,1,0:T(8,128)}, u32[]{:S(2)}) copy-start(f32[1,1,128,512]{3,2,1,0:T(8,128)} %get-tuple-element.139) | copy-start | bytes 786436
  123.0 1.5 collective-permute-start.21
  142.8 8.3 %collective-permute-start.26 = (f32[3,64,256]{2,1,0:T(8,128)S(1)}, f32[3,64,256]{2,1,0:T(8,128)S(1)}, u32[]{:S(2)}, u32[]{:S(2)}) collective-permute-start(f32[3,64,256]{2,1,0:T(8,128)S(1)} %get-tuple-element.142), channel_id=1, source_target_pairs={{0,1},{1,0},{2,3},{3,2},{4,5},{5,4},{6,7},{7,6},{8,9},{9,8},{10,11... | collective-permute-start | bytes 589832 | tf_op jit(solution)/shard_map/ppermute | solution.py:802
  142.8 8.2 %collective-permute-start.27 = (f32[3,64,256]{2,1,0:T(8,128)S(1)}, f32[3,64,256]{2,1,0:T(8,128)S(1)}, u32[]{:S(2)}, u32[]{:S(2)}) collective-permute-start(f32[3,64,256]{2,1,0:T(8,128)S(1)} %get-tuple-element.145), channel_id=1, source_target_pairs={{4,0},{5,8},{8,13},{9,1},{0,4},{1,5},{12,9},{13,12},{6,2},{7,10},{... | collective-permute-start | bytes 589832 | tf_op jit(solution)/shard_map/ppermute | solution.py:799
  144.0 9.5 %collective-permute-start.28 = (f32[3,64,256]{2,1,0:T(8,128)S(1)}, f32[3,64,256]{2,1,0:T(8,128)S(1)}, u32[]{:S(2)}, u32[]{:S(2)}) collective-permute-start(f32[3,64,256]{2,1,0:T(8,128)S(1)} %get-tuple-element.144), channel_id=1, source_target_pairs={{4,8},{5,12},{8,1},{9,5},{0,0},{1,4},{12,9},{13,13},{6,10},{7,14},... | collective-permute-start | bytes 589832 | tf_op jit(solution)/shard_map/ppermute | solution.py:799
  145.9 9.1 %collective-permute-start.29 = (f32[3,64,256]{2,1,0:T(8,128)S(1)}, f32[3,64,256]{2,1,0:T(8,128)S(1)}, u32[]{:S(2)}, u32[]{:S(2)}) collective-permute-start(f32[3,64,256]{2,1,0:T(8,128)S(1)} %get-tuple-element.143), channel_id=1, source_target_pairs={{4,12},{5,0},{8,5},{9,13},{0,1},{1,4},{12,8},{13,9},{6,14},{7,2},{... | collective-permute-start | bytes 589832 | tf_op jit(solution)/shard_map/ppermute | solution.py:799
  148.3 1.0 copy-start.11

commit v10 on v9

--- a/solution.py
+++ b/solution.py
@@ -416,7 +416,8 @@
         store_split(cots, (which,), -moved_cot)
 
 
-def write_grads(cells, reps, turned, direct, parts, pieces, grads, grad_sems):
+def weight_grad_kernel(cells, reps, turned, direct, before, after, *refs):
+    parts, pieces, (grads, grad_sems) = (before, after), refs[:reps], refs[reps:]
     for which in range(3):
         total = direct[which]
         begin = 0
@@ -446,18 +447,15 @@
     run_copies(copies)
 
 
-def token_grad_kernel(cells, reps, first, last, *refs):
+def token_grad_kernel(first, last, *refs):
     rounds = min(last, ROUNDS) - first
     near, far, refs = refs[:rounds], refs[rounds : 2 * rounds], refs[2 * rounds :]
     own, got, final = None, None, last > ROUNDS
     if final:
-        (own, got, turned, direct, before), refs = refs[:5], refs[5:]
+        (own, got), refs = refs[:2], refs[2:]
     (weights, cots, gates, ups, backs), refs = refs[:5], refs[5:]
     near_out, far_out, refs = refs[:rounds], refs[rounds], refs[rounds + 1 :]
-    if final:
-        pieces, (acts, grads, grad_sems), refs = refs[:reps], refs[reps : reps + 3], refs[reps + 3 :]
-    else:
-        acts, refs = refs[0], refs[1:]
+    acts, refs = refs[0], refs[1:]
     keys, targets, wide, sent, row_sems, out_sems = refs
     fetch_rows(near, far, own, got, (keys, targets), row_sems)
     size = sent.shape[2]
@@ -526,8 +524,6 @@
                 for side, (source, out) in enumerate(outgoing(each)):
                     pltpu.make_async_copy(source, out, out_sems.at[each, side]).start()
 
-    if final:
-        write_grads(cells, reps, turned, direct, (before, acts), pieces, grads, grad_sems)
     for each in range(last - first):
         for side, (source, out) in enumerate(outgoing(each)):
             pltpu.make_async_copy(source, out, out_sems.at[each, side]).wait()
@@ -718,44 +714,33 @@
     )
     middle = 2
 
-    def token_grads(first, last, cots, *more):
+    def token_grads(first, last, cots):
         rounds = min(last, ROUNDS) - first
         span = slice(first, first + rounds)
         inputs = inner_rows[:ROUNDS][span] + inner_rows[ROUNDS : 2 * ROUNDS][span]
-        if more:
+        if last > ROUNDS:
             inputs = inputs + inner_rows[2 * ROUNDS :]
         blocks = last - first
-        specs = [HBM] * len(inputs) + [VMEM] * (len(more) + 5)
+        specs = [HBM] * len(inputs) + [VMEM] * 5
         outs = [shape((size, depth), F32)] * rounds
         outs.append(shape((size * (2 * blocks - rounds), depth), F32))
         acts = (2, 3, blocks * size, cols)
-        if more:
-            outs += [shape((cells, CELL, 3, rows, cols), F32)] * reps
-            scratch = [
-                pltpu.VMEM(acts, BF16),
-                pltpu.VMEM((3, width, cols), F32),
-                dma((cells * reps * CELL,)),
-            ]
-            out_specs = [HBM] * len(outs)
-        else:
-            out_specs = [HBM] * len(outs) + [VMEM]
-            outs.append(shape(acts, BF16))
-            scratch = []
+        out_specs = [HBM] * len(outs) + [VMEM]
+        outs.append(shape(acts, BF16))
         outs = call(
-            functools.partial(token_grad_kernel, cells, reps, first, last),
-            inputs + [*more, weights, cots, gates, ups, backs],
+            functools.partial(token_grad_kernel, first, last),
+            inputs + [weights, cots, gates, ups, backs],
             specs,
             outs,
             out_specs,
-            scratch
-            + [pltpu.VMEM((blocks, size, depth), F32)] * 2
+            [pltpu.VMEM((blocks, size, depth), F32)] * 2
             + [
                 split_square,
                 pltpu.VMEM((2, blocks, size, depth), F32),
                 dma((blocks, 4)),
                 dma((blocks, 4)),
             ],
-            9 * product * blocks // CELL + (3 * product if more else 0),
+            9 * product * blocks // CELL,
         )
         return outs[:rounds], outs[rounds], list(outs[rounds + 1 :])
 
@@ -766,14 +751,27 @@
     ]
     cots, *query_totals = lax.optimization_barrier((cots, *query_totals))
     query_back = hand_back(query_totals, 0)
-    near_last, far_last, given = token_grads(middle, CELL, cots, key_turned, direct, acts_first)
+    near_last, far_last, (acts_last,) = token_grads(middle, CELL, cots)
     got_first = lax.ppermute(far_first, "head", SWAP)
     far_last, got_first, *rest = lax.optimization_barrier(
         (far_last, got_first, *near_first, *query_back)
     )
     near_first, query_back = rest[:-ROUNDS], rest[-ROUNDS:]
     totals_first, _ = combine(near_first, far_first, got_first)
+    acts_last, *totals_first = lax.optimization_barrier((acts_last, *totals_first))
     back = hand_back(totals_first, 0)
+    given = list(
+        call(
+            functools.partial(weight_grad_kernel, cells, reps),
+            [key_turned, direct, acts_first, acts_last],
+            [VMEM] * 4,
+            [shape((cells, CELL, 3, rows, cols), F32)] * reps,
+            [HBM] * reps,
+            [pltpu.VMEM((3, width, cols), F32), dma((cells * reps * CELL,))],
+            3 * product,
+            16,
+        )
+    )
     totals_last, local = combine(near_last, far_last)
     back += hand_back(totals_last, middle)
     query_first, *totals_last = lax.optimization_barrier((query_first, *totals_last))

time: 158 us -> 162 us (1.025)
  local copies, waits for them, and re-layouts: 4.74 us -> 10.7 us
    unnamed x42 -> x52, local copies, waits for them, and re-layouts: 3.76 us -> 9.73 us
    ppermute x6, waiting for transfers between devices: 17.2 us -> 11.8 us  [hand_back(): lax.ppermute(total, PLACE, flipped(pairs[first + number]))]
    ppermute x1, waiting for transfers between devices: 0.01 us -> 4.07 us  [per_device(): total = total + lax.ppermute(given[shift][0], 'rep', shifted(shift, 1))]
    pallas_call x9 -> x10, Pallas kernels: 42.2 us -> 41.9 us  [call(): pl.pallas_call(kernel, out_shape=outs, in_specs=in_specs, out_specs=out_s...]
  transfers between devices with their start and end apart: 30 -> 30, of which waited for: 12 -> 12; matrix products, arithmetic and copies ran while one was open for 5% -> 5% of each run, Pallas kernels for 20% -> 19%
where the time goes in v10:
time: 162 us; the launch traced here: 159 us
  waiting for transfers between devices  68.4 us (42%)
  Pallas kernels  41.9 us (26%)
  starting transfers between devices  27.4 us (17%)
  local copies, waits for them, and re-layouts  10.7 us (7%)
  other arithmetic  9.72 us (6%)
    pallas_call x10, Pallas kernels, call(): pl.pallas_call(kernel, out_shape=outs, in_specs=in_specs, out_specs=out_s...  41.9 us
    ppermute x6, waiting for transfers between devices, gather(): lax.ppermute(packed[turn], PLACE, pairs[turn])  32 us
    ppermute x1, waiting for transfers between devices, per_device(): parts.append(lax.ppermute(together, 'rep', shifted(shift, 1)))  14.9 us
    ppermute x6, waiting for transfers between devices, hand_back(): lax.ppermute(total, PLACE, flipped(pairs[first + number]))  11.8 us
    ppermute x6, starting transfers between devices, hand_back(): lax.ppermute(total, PLACE, flipped(pairs[first + number]))  10.1 us
    unnamed x52, local copies, waits for them, and re-layouts  9.73 us
    ppermute x6, starting transfers between devices, gather(): lax.ppermute(packed[turn], PLACE, pairs[turn])  7.46 us
    ppermute x3, starting transfers between devices, per_device(): lax.ppermute(total[turn], PLACE, flipped(pairs[turn]))  5.26 us
  transfers between devices with their start and end apart: 30, of which 12 were waited for; matrix products, arithmetic and copies ran while one was open for 5% of the time, Pallas kernels for 19%

profile of v10, /device:TPU:22, one launch (start us, length us, event | category | flops | bytes accessed | tf_op | source)
XLA Modules:
  0.0 159.3 jit_solution(8256670540779777617)
XLA Ops:
  0.6 0.8 copy.20
  1.4 0.7 fusion.3.refs_5_
  2.2 4.0 %shard_map.135 = (f32[352,512]{1,0:T(8,128)}, f32[352,512]{1,0:T(8,128)}, f32[352,512]{1,0:T(8,128)}, f32[608,512]{1,0:T(8,128)}, f32[96,512]{1,0:T(8,128)}) custom-call(f32[256,512]{1,0:T(8,128)} %bitcast.50, f32[256,512]{1,0:T(8,128)} %bitcast.49, f32[64,512]{1,0:T(8,128)} %bitcast.51, f32[64,512]{1,0:T(8,128)} %bitcast.52, f32[64,512]{1,0:T(8,128)} %bitcast.53, ...), custom_call_target="tpu_custom_call" | custom-call | bytes 5047296 | tf_op jit(solution)/shard_map/pallas_call | solution.py:534
  6.3 0.6 collective-permute-start.4
  6.9 2.3 %collective-permute-start.5 = (f32[352,512]{1,0:T(8,128)}, f32[352,512]{1,0:T(8,128)S(1)}, u32[]{:S(2)}, u32[]{:S(2)}) collective-permute-start(f32[352,512]{1,0:T(8,128)} %get-tuple-element.79), channel_id=1, source_target_pairs={{8,4},{12,5},{1,8},{5,9},{0,0},{4,1},{9,12},{13,13},{10,6},{14,7},... | collective-permute-start | bytes 2162696 | tf_op jit(solution)/shard_map/ppermute | solution.py:597
  9.2 1.3 collective-permute-start.6
  10.4 11.9 %collective-permute-done.4.refs_2_.refs_0_ = f32[352,512]{1,0:T(8,128)S(1)} collective-permute-done((f32[352,512]{1,0:T(8,128)}, f32[352,512]{1,0:T(8,128)S(1)}, u32[]{:S(2)}, u32[]{:S(2)}) %collective-permute-start.4) | collective-permute-done | bytes 720928 | tf_op jit(solution)/shard_map/ppermute | solution.py:597
  22.4 18.6 %collective-permute-done.5.refs_3_.refs_1_ = f32[352,512]{1,0:T(8,128)S(1)} collective-permute-done((f32[352,512]{1,0:T(8,128)}, f32[352,512]{1,0:T(8,128)S(1)}, u32[]{:S(2)}, u32[]{:S(2)}) %collective-permute-start.5) | collective-permute-done | bytes 720928 | tf_op jit(solution)/shard_map/ppermute | solution.py:597
  41.0 1.5 collective-permute-done.6.refs_4_.refs_0_
  42.5 0.5 collective-permute-start.8
  43.2 0.6 collective-permute-start.7
  43.8 1.1 collective-permute-start.9
  44.9 0.3 shard_map.136
  45.2 1.9 %collective-permute-start.2 = (f32[256,512]{1,0:T(8,128)S(1)}, f32[256,512]{1,0:T(8,128)S(1)}, u32[]{:S(2)}, u32[]{:S(2)}) collective-permute-start(f32[256,512]{1,0:T(8,128)S(1)} %get-tuple-element.75), channel_id=1, source_target_pairs={{8,4},{12,5},{1,8},{5,9},{0,0},{4,1},{9,12},{13,13},{10,6},{14,7},... | collective-permute-start | bytes 1572872 | tf_op jit(solution)/shard_map/ppermute | solution.py:597
  47.2 1.3 collective-permute-start.3
  48.5 14.9 %collective-permute-done.7.refs_1_ = f32[4,96,512]{2,1,0:T(8,128)S(1)} collective-permute-done((f32[4,96,512]{2,1,0:T(8,128)S(1)}, f32[4,96,512]{2,1,0:T(8,128)S(1)}, u32[]{:S(2)}, u32[]{:S(2)}) %collective-permute-start.7) | collective-permute-done | bytes 786464 | tf_op jit(solution)/shard_map/ppermute | solution.py:650
  63.4 7.5 %shard_map.137 = (f32[3,512,256]{2,1,0:T(8,128)S(1)}, f32[1024,256]{1,0:T(8,128)S(1)}, f32[1024,256]{1,0:T(8,128)S(1)}, f32[1024,256]{1,0:T(8,128)S(1)}, bf16[2,...) custom-call(f32[4,96,512]{2,1,0:T(8,128)S(1)} %pad_maximum_fusion.refs_0_, ...), custom_call_target="tpu_custom_call" | custom-call | flops 4831838208 | bytes 18874368 | tf_op jit(solution)/shard_map/pallas_call | solution.py:534
  71.0 2.0 %copy-done.11 = bf16[2,2,512,1024]{3,2,1,0:T(8,128)(2,1)} copy-done((bf16[2,2,512,1024]{3,2,1,0:T(8,128)(2,1)}, bf16[2,2,512,1024]{3,2,1,0:T(8,128)(2,1)S(1)}, u32[]{:S(2)}) %copy-start.11) | copy-done | bytes 4194328
  72.9 0.6 shard_map.138
  73.6 0.5 collective-permute-start.11
  74.1 0.1 collective-permute-start.12
  74.2 0.4 collective-permute-start.13
  74.6 0.1 collective-permute-start.14
  74.7 1.7 %collective-permute-done.11.refs_4_ = f32[512,512]{1,0:T(8,128)S(1)} collective-permute-done((f32[512,512]{1,0:T(8,128)S(1)}, f32[512,512]{1,0:T(8,128)S(1)}, u32[]{:S(2)}, u32[]{:S(2)}) %collective-permute-start.11) | collective-permute-done | bytes 1048608 | tf_op jit(solution)/shard_map/ppermute | solution.py:602
  76.4 5.0 %shard_map.139 = (f32[128,512]{1,0:T(8,128)S(1)}, f32[128,512]{1,0:T(8,128)S(1)}, f32[128,512]{1,0:T(8,128)S(1)}, f32[128,512]{1,0:T(8,128)S(1)}, bf16[2,2,512,5...) custom-call(f32[256,512]{1,0:T(8,128)S(1)} %collective-permute-done.1.refs_0_, ...), custom_call_target="tpu_custom_call" | custom-call | flops 2013265920 | bytes 9961472 | tf_op jit(solution)/shard_map/pallas_call | solution.py:534
  81.4 7.1 %shard_map.140 = (f32[3,512,256]{2,1,0:T(8,128)S(1)}, f32[512,512]{1,0:T(8,128)S(1)}) custom-call(f32[256,512]{1,0:T(8,128)S(1)} %collective-permute-done.12.refs_0_, f32[256,512]{1,0:T(8,128)S(1)} %collective-permute-done.13.refs_1_, f32[256,512]{1,0:T(8,128)S(1)} %collective-permute-done.14.refs_2_, f32[512,512]{1,0:T(8,128)S(1)} %get-tuple-element.92.refs_3_, ...), custom_call_target="tpu_custom_call" | custom-call | flops 4429185024 | bytes 11534336 | tf_op jit(solution)/shard_map/pallas_call | solution.py:534
  88.5 0.4 collective-permute-start.15
  88.9 1.2 shard_map.141
  90.1 1.2 copy-done.8
  91.3 6.3 %shard_map.143 = (f32[256,512]{1,0:T(8,128)S(1)}, f32[256,512]{1,0:T(8,128)S(1)}, f32[512,512]{1,0:T(8,128)S(1)}, bf16[2,3,512,256]{3,2,1,0:T(8,128)(2,1)S(1)}) custom-call(f32[352,512]{1,0:T(8,128)S(1)} %collective-permute-done.4.refs_2_.refs_0_, f32[352,512]{1,0:T(8,128)S(1)} %copy-done.5, f32[352,512]{1,0:T(8,128)S(1)} %collective-permute-done.8.refs_5_.refs_2_, ...), custom_call_target="tpu_custom_call" | custom-call | flops 3623878656 | bytes 12845056 | tf_op jit(solution)/shard_map/pallas_call | solution.py:534
  97.6 0.2 collective-permute-start.16
  97.9 0.9 slice_add_fusion.5
  98.8 0.1 copy-done.13
  98.9 2.0 %collective-permute-start.18 = (f32[128,512]{1,0:T(8,128)S(1)}, f32[128,512]{1,0:T(8,128)S(1)}, u32[]{:S(2)}, u32[]{:S(2)}) collective-permute-start(f32[128,512]{1,0:T(8,128)S(1)} %get-tuple-element.114), channel_id=1, source_target_pairs={{4,8},{5,12},{8,1},{9,5},{0,0},{1,4},{12,9},{13,13},{6,10},{7,14},... | collective-permute-start | bytes 786440 | tf_op jit(solution)/shard_map/ppermute | solution.py:616
  101.0 3.0 %collective-permute-start.19 = (f32[128,512]{1,0:T(8,128)S(1)}, f32[128,512]{1,0:T(8,128)S(1)}, u32[]{:S(2)}, u32[]{:S(2)}) collective-permute-start(f32[128,512]{1,0:T(8,128)S(1)} %get-tuple-element.115), channel_id=1, source_target_pairs={{4,12},{5,0},{8,5},{9,13},{0,1},{1,4},{12,8},{13,9},{6,14},{7,2},{... | collective-permute-start | bytes 786440 | tf_op jit(solution)/shard_map/ppermute | solution.py:616
  103.9 6.6 %shard_map.142 = (f32[256,512]{1,0:T(8,128)S(1)}, f32[768,512]{1,0:T(8,128)S(1)}, bf16[2,3,512,256]{3,2,1,0:T(8,128)(2,1)S(1)}) custom-call(f32[352,512]{1,0:T(8,128)S(1)} %copy-done.3, f32[352,512]{1,0:T(8,128)S(1)} %collective-permute-done.10.refs_7_.refs_1_, f32[608,512]{1,0:T(8,128)S(1)} %copy-done.10, f32[608,512]{1,0:T(8,128)S(1)} %copy-done.7, ...), custom_call_target="tpu_custom_call" | custom-call | flops 3623878656 | bytes 13893632 | tf_op jit(solution)/shard_map/pallas_call | solution.py:534
  110.5 1.1 copy-done.15
  111.7 1.9 %collective-permute-done.19 = f32[128,512]{1,0:T(8,128)S(1)} collective-permute-done((f32[128,512]{1,0:T(8,128)S(1)}, f32[128,512]{1,0:T(8,128)S(1)}, u32[]{:S(2)}, u32[]{:S(2)}) %collective-permute-start.19) | collective-permute-done | bytes 262176 | tf_op jit(solution)/shard_map/ppermute | solution.py:616
  113.6 0.7 copy-done.23
  114.3 1.6 slice_add_fusion.2
  115.9 1.2 collective-permute-start.22
  117.1 1.9 %collective-permute-start.23 = (f32[256,512]{1,0:T(8,128)S(1)}, f32[256,512]{1,0:T(8,128)S(1)}, u32[]{:S(2)}, u32[]{:S(2)}) collective-permute-start(f32[256,512]{1,0:T(8,128)S(1)} %get-tuple-element.131), channel_id=1, source_target_pairs={{4,8},{5,12},{8,1},{9,5},{0,0},{1,4},{12,9},{13,13},{6,10},{7,14},... | collective-permute-start | bytes 1572872 | tf_op jit(solution)/shard_map/ppermute | solution.py:616
  119.0 2.2 %copy-done.12 = bf16[2,2,512,1024]{3,2,1,0:T(8,128)(2,1)S(1)} copy-done((bf16[2,2,512,1024]{3,2,1,0:T(8,128)(2,1)S(1)}, bf16[2,2,512,1024]{3,2,1,0:T(8,128)(2,1)}, u32[]{:S(2)}) %copy-start.12) | copy-done | bytes 4194328
  121.2 1.4 copy-done.16
  122.6 3.4 %shard_map.144 = (f32[1,4,3,64,256]{4,3,2,1,0:T(8,128)S(1)}, f32[1,4,3,64,256]{4,3,2,1,0:T(8,128)S(1)}) custom-call(bf16[2,2,512,1024]{3,2,1,0:T(8,128)(2,1)S(1)} %copy-done.12, f32[3,512,256]{2,1,0:T(8,128)S(1)} %copy-done.9, bf16[2,3,512,256]{3,2,1,0:T(8,128)(2,1)S(1)} %copy-done.14, bf16[2,3,512,256]{3,2,1,0:T(8,128)(2,1)S(1)} %copy-done.16), custom_call_target="tpu_custom_call" | custom-call | flops 2415919104 | bytes 10485760 | tf_op jit(solution)/shard_map/pallas_call | solution.py:534
  126.0 0.6 collective-permute-start.25
  126.7 1.1 slice_add_fusion.1
  127.8 1.9 %collective-permute-start.24 = (f32[256,512]{1,0:T(8,128)S(1)}, f32[256,512]{1,0:T(8,128)S(1)}, u32[]{:S(2)}, u32[]{:S(2)}) collective-permute-start(f32[256,512]{1,0:T(8,128)S(1)} %slice_add_fusion.1), channel_id=1, source_target_pairs={{4,12},{5,0},{8,5},{9,13},{0,1},{1,4},{12,8},{13,9},{6,14},{7,2},{... | collective-permute-start | bytes 1572872 | tf_op jit(solution)/shard_map/ppermute | solution.py:616
  129.7 1.5 slice_add_fusion
  131.3 0.9 maximum_select_fusion
  132.2 1.6 %collective-permute-done.23 = f32[256,512]{1,0:T(8,128)S(1)} collective-permute-done((f32[256,512]{1,0:T(8,128)S(1)}, f32[256,512]{1,0:T(8,128)S(1)}, u32[]{:S(2)}, u32[]{:S(2)}) %collective-permute-start.23) | collective-permute-done | bytes 524320 | tf_op jit(solution)/shard_map/ppermute | solution.py:616
  133.8 8.3 %collective-permute-done.24 = f32[256,512]{1,0:T(8,128)S(1)} collective-permute-done((f32[256,512]{1,0:T(8,128)S(1)}, f32[256,512]{1,0:T(8,128)S(1)}, u32[]{:S(2)}, u32[]{:S(2)}) %collective-permute-start.24) | collective-permute-done | bytes 524320 | tf_op jit(solution)/shard_map/ppermute | solution.py:616
  142.1 4.1 %collective-permute-done.25 = f32[4,3,64,256]{3,2,1,0:T(8,128)S(1)} collective-permute-done((f32[4,3,64,256]{3,2,1,0:T(8,128)S(1)}, f32[4,3,64,256]{3,2,1,0:T(8,128)S(1)}, u32[]{:S(2)}, u32[]{:S(2)}) %collective-permute-start.25) | collective-permute-done | bytes 786464 | tf_op jit(solution)/shard_map/ppermute | solution.py:795
  146.2 0.1 bitcast_add_fusion
  146.4 0.1 collective-permute-start.26
  146.5 5.0 %collective-permute-start.28 = (f32[3,64,256]{2,1,0:T(8,128)S(1)}, f32[3,64,256]{2,1,0:T(8,128)S(1)}, u32[]{:S(2)}, u32[]{:S(2)}) collective-permute-start(f32[3,64,256]{2,1,0:T(8,128)S(1)} %get-tuple-element.152), channel_id=1, source_target_pairs={{4,8},{5,12},{8,1},{9,5},{0,0},{1,4},{12,9},{13,13},{6,10},{7,14},... | collective-permute-start | bytes 589832 | tf_op jit(solution)/shard_map/ppermute | solution.py:797
  151.5 0.2 collective-permute-start.29
  151.7 0.2 select_select_fusion.1
  152.0 0.9 copy-done.17
  152.9 1.2 multiply_reduce_fusion
  154.1 0.6 divide_multiply_fusion
  154.7 0.6 collective-permute-done.28
  155.3 3.2 %collective-permute-done.29 = f32[3,64,256]{2,1,0:T(8,128)S(1)} collective-permute-done((f32[3,64,256]{2,1,0:T(8,128)S(1)}, f32[3,64,256]{2,1,0:T(8,128)S(1)}, u32[]{:S(2)}, u32[]{:S(2)}) %collective-permute-start.29) | collective-permute-done | bytes 196640 | tf_op jit(solution)/shard_map/ppermute | solution.py:797
  158.6 0.8 pad_maximum_fusion.1
  (82 shorter events, 0.8 us)
Async XLA Ops:
  6.2 36.8 %collective-permute-start = (f32[608,512]{1,0:T(8,128)}, f32[608,512]{1,0:T(8,128)S(1)}, u32[]{:S(2)}, u32[]{:S(2)}) collective-permute-start(f32[608,512]{1,0:T(8,128)} %get-tuple-element.72.refs_8_.refs_2_), channel_id=1, source_target_pairs={{0,1},{1,0},{2,3},{3,2},{4,5},{5,4},{6,7},{7,6},{8,9},{9,8},{10,11... | collective-permute-start | bytes 3735560 | tf_op jit(solution)/shard_map/ppermute | solution.py:602
  6.3 16.1 %collective-permute-start.4 = (f32[352,512]{1,0:T(8,128)}, f32[352,512]{1,0:T(8,128)S(1)}, u32[]{:S(2)}, u32[]{:S(2)}) collective-permute-start(f32[352,512]{1,0:T(8,128)} %get-tuple-element.78), channel_id=1, source_target_pairs={{0,4},{8,5},{13,8},{1,9},{4,0},{5,1},{9,12},{12,13},{2,6},{10,7},{... | collective-permute-start | bytes 2162696 | tf_op jit(solution)/shard_map/ppermute | solution.py:597
  6.9 34.2 %collective-permute-start.5 = (f32[352,512]{1,0:T(8,128)}, f32[352,512]{1,0:T(8,128)S(1)}, u32[]{:S(2)}, u32[]{:S(2)}) collective-permute-start(f32[352,512]{1,0:T(8,128)} %get-tuple-element.79), channel_id=1, source_target_pairs={{8,4},{12,5},{1,8},{5,9},{0,0},{4,1},{9,12},{13,13},{10,6},{14,7},... | collective-permute-start | bytes 2162696 | tf_op jit(solution)/shard_map/ppermute | solution.py:597
  9.2 33.3 %collective-permute-start.6 = (f32[352,512]{1,0:T(8,128)}, f32[352,512]{1,0:T(8,128)S(1)}, u32[]{:S(2)}, u32[]{:S(2)}) collective-permute-start(f32[352,512]{1,0:T(8,128)} %get-tuple-element.80), channel_id=1, source_target_pairs={{12,4},{0,5},{5,8},{13,9},{1,0},{4,1},{8,12},{9,13},{14,6},{2,7},{... | collective-permute-start | bytes 2162696 | tf_op jit(solution)/shard_map/ppermute | solution.py:597
  41.0 22.4 %copy-start.4 = (f32[352,512]{1,0:T(8,128)}, f32[352,512]{1,0:T(8,128)S(1)}, u32[]{:S(2)}) copy-start(f32[352,512]{1,0:T(8,128)S(1)} %collective-permute-done.5.refs_3_.refs_1_) | copy-start | bytes 2162692
  42.5 20.9 %copy-start.2 = (f32[352,512]{1,0:T(8,128)}, f32[352,512]{1,0:T(8,128)S(1)}, u32[]{:S(2)}) copy-start(f32[352,512]{1,0:T(8,128)S(1)} %collective-permute-done.6.refs_4_.refs_0_) | copy-start | bytes 2162692
  42.5 2.8 %collective-permute-start.10 = (f32[352,512]{1,0:T(8,128)S(1)}, f32[352,512]{1,0:T(8,128)S(1)}, u32[]{:S(2)}, u32[]{:S(2)}) collective-permute-start(f32[352,512]{1,0:T(8,128)S(1)} %collective-permute-done.6.refs_4_.refs_0_), channel_id=1, source_target_pairs={{0,1},{1,0},{2,3},{3,2},{4,5},{5,4},{6,7},{7,6},{8,9},{9,8},{10,11... | collective-permute-start | bytes 2162696 | tf_op jit(solution)/shard_map/ppermute | solution.py:601
  42.5 4.7 %collective-permute-start.8 = (f32[352,512]{1,0:T(8,128)S(1)}, f32[352,512]{1,0:T(8,128)S(1)}, u32[]{:S(2)}, u32[]{:S(2)}) collective-permute-start(f32[352,512]{1,0:T(8,128)S(1)} %collective-permute-done.4.refs_2_.refs_0_), channel_id=1, source_target_pairs={{0,1},{1,0},{2,3},{3,2},{4,5},{5,4},{6,7},{7,6},{8,9},{9,8},{10,11... | collective-permute-start | bytes 2162696 | tf_op jit(solution)/shard_map/ppermute | solution.py:601
  43.0 1.9 %copy-start = (f32[1,1,256,512]{3,2,1,0:T(8,128)S(1)}, f32[1,1,256,512]{3,2,1,0:T(8,128)}, u32[]{:S(2)}) copy-start(f32[1,1,256,512]{3,2,1,0:T(8,128)} %param.8) | copy-start | bytes 1572868
  43.0 1.9 %copy-start.1 = (f32[1,1,256,512]{3,2,1,0:T(8,128)S(1)}, f32[1,1,256,512]{3,2,1,0:T(8,128)}, u32[]{:S(2)}) copy-start(f32[1,1,256,512]{3,2,1,0:T(8,128)} %param.12) | copy-start | bytes 1572868
  43.1 20.3 %copy-start.6 = (f32[608,512]{1,0:T(8,128)}, f32[608,512]{1,0:T(8,128)S(1)}, u32[]{:S(2)}) copy-start(f32[608,512]{1,0:T(8,128)S(1)} %collective-permute-done.refs_9_.refs_3_) | copy-start | bytes 3735556
  43.1 20.3 %copy-start.10 = (f32[608,512]{1,0:T(8,128)S(1)}, f32[608,512]{1,0:T(8,128)}, u32[]{:S(2)}) copy-start(f32[608,512]{1,0:T(8,128)} %get-tuple-element.72.refs_8_.refs_2_) | copy-start | bytes 3735556
  43.2 20.2 %collective-permute-start.7 = (f32[4,96,512]{2,1,0:T(8,128)S(1)}, f32[4,96,512]{2,1,0:T(8,128)S(1)}, u32[]{:S(2)}, u32[]{:S(2)}) collective-permute-start(f32[4,96,512]{2,1,0:T(8,128)S(1)} %pad_maximum_fusion.refs_0_), channel_id=1, source_target_pairs={{0,2},{2,0},{1,3},{3,1},{4,6},{6,4},{5,7},{7,5},{8,10},{10,8},{9,1... | collective-permute-start | bytes 2359304 | tf_op jit(solution)/shard_map/ppermute | solution.py:650
  43.8 4.7 %collective-permute-start.9 = (f32[352,512]{1,0:T(8,128)S(1)}, f32[352,512]{1,0:T(8,128)S(1)}, u32[]{:S(2)}, u32[]{:S(2)}) collective-permute-start(f32[352,512]{1,0:T(8,128)S(1)} %collective-permute-done.5.refs_3_.refs_1_), channel_id=1, source_target_pairs={{0,1},{1,0},{2,3},{3,2},{4,5},{5,4},{6,7},{7,6},{8,9},{9,8},{10,11... | collective-permute-start | bytes 2162696 | tf_op jit(solution)/shard_map/ppermute | solution.py:601
  45.2 28.4 %collective-permute-start.1 = (f32[256,512]{1,0:T(8,128)S(1)}, f32[256,512]{1,0:T(8,128)S(1)}, u32[]{:S(2)}, u32[]{:S(2)}) collective-permute-start(f32[256,512]{1,0:T(8,128)S(1)} %get-tuple-element.74), channel_id=1, source_target_pairs={{0,4},{8,5},{13,8},{1,9},{4,0},{5,1},{9,12},{12,13},{2,6},{10,7},{... | collective-permute-start | bytes 1572872 | tf_op jit(solution)/shard_map/ppermute | solution.py:597
  45.2 28.3 %collective-permute-start.2 = (f32[256,512]{1,0:T(8,128)S(1)}, f32[256,512]{1,0:T(8,128)S(1)}, u32[]{:S(2)}, u32[]{:S(2)}) collective-permute-start(f32[256,512]{1,0:T(8,128)S(1)} %get-tuple-element.75), channel_id=1, source_target_pairs={{8,4},{12,5},{1,8},{5,9},{0,0},{4,1},{9,12},{13,13},{10,6},{14,7},... | collective-permute-start | bytes 1572872 | tf_op jit(solution)/shard_map/ppermute | solution.py:597
  47.2 26.4 %collective-permute-start.3 = (f32[256,512]{1,0:T(8,128)S(1)}, f32[256,512]{1,0:T(8,128)S(1)}, u32[]{:S(2)}, u32[]{:S(2)}) collective-permute-start(f32[256,512]{1,0:T(8,128)S(1)} %get-tuple-element.76), channel_id=1, source_target_pairs={{12,4},{0,5},{5,8},{13,9},{1,0},{4,1},{8,12},{9,13},{14,6},{2,7},{... | collective-permute-start | bytes 1572872 | tf_op jit(solution)/shard_map/ppermute | solution.py:597
  71.0 2.0 %copy-start.11 = (bf16[2,2,512,1024]{3,2,1,0:T(8,128)(2,1)}, bf16[2,2,512,1024]{3,2,1,0:T(8,128)(2,1)S(1)}, u32[]{:S(2)}) copy-start(bf16[2,2,512,1024]{3,2,1,0:T(8,128)(2,1)S(1)} %get-tuple-element.121.turned) | copy-start | bytes 12582916
  73.6 2.8 %collective-permute-start.11 = (f32[512,512]{1,0:T(8,128)S(1)}, f32[512,512]{1,0:T(8,128)S(1)}, u32[]{:S(2)}, u32[]{:S(2)}) collective-permute-start(f32[512,512]{1,0:T(8,128)S(1)} %get-tuple-element.92.refs_3_), channel_id=1, source_target_pairs={{0,1},{1,0},{2,3},{3,2},{4,5},{5,4},{6,7},{7,6},{8,9},{9,8},{10,11... | collective-permute-start | bytes 3145736 | tf_op jit(solution)/shard_map/ppermute | solution.py:602
  74.1 7.3 %collective-permute-start.12 = (f32[256,512]{1,0:T(8,128)S(1)}, f32[256,512]{1,0:T(8,128)S(1)}, u32[]{:S(2)}, u32[]{:S(2)}) collective-permute-start(f32[256,512]{1,0:T(8,128)S(1)} %collective-permute-done.1.refs_0_), channel_id=1, source_target_pairs={{0,1},{1,0},{2,3},{3,2},{4,5},{5,4},{6,7},{7,6},{8,9},{9,8},{10,11... | collective-permute-start | bytes 1572872 | tf_op jit(solution)/shard_map/ppermute | solution.py:601
  74.2 7.2 %collective-permute-start.13 = (f32[256,512]{1,0:T(8,128)S(1)}, f32[256,512]{1,0:T(8,128)S(1)}, u32[]{:S(2)}, u32[]{:S(2)}) collective-permute-start(f32[256,512]{1,0:T(8,128)S(1)} %collective-permute-done.2.refs_1_), channel_id=1, source_target_pairs={{0,1},{1,0},{2,3},{3,2},{4,5},{5,4},{6,7},{7,6},{8,9},{9,8},{10,11... | collective-permute-start | bytes 1572872 | tf_op jit(solution)/shard_map/ppermute | solution.py:601
  74.6 6.8 %collective-permute-start.14 = (f32[256,512]{1,0:T(8,128)S(1)}, f32[256,512]{1,0:T(8,128)S(1)}, u32[]{:S(2)}, u32[]{:S(2)}) collective-permute-start(f32[256,512]{1,0:T(8,128)S(1)} %collective-permute-done.3.refs_2_), channel_id=1, source_target_pairs={{0,1},{1,0},{2,3},{3,2},{4,5},{5,4},{6,7},{7,6},{8,9},{9,8},{10,11... | collective-permute-start | bytes 1572872 | tf_op jit(solution)/shard_map/ppermute | solution.py:601
  88.5 9.4 %collective-permute-start.15 = (f32[512,512]{1,0:T(8,128)S(1)}, f32[512,512]{1,0:T(8,128)S(1)}, u32[]{:S(2)}, u32[]{:S(2)}) collective-permute-start(f32[512,512]{1,0:T(8,128)S(1)} %get-tuple-element.101), channel_id=1, source_target_pairs={{0,1},{1,0},{2,3},{3,2},{4,5},{5,4},{6,7},{7,6},{8,9},{9,8},{10,11... | collective-permute-start | bytes 3145736 | tf_op jit(solution)/shard_map/ppermute | solution.py:748
  88.9 2.4 %copy-start.5 = (f32[352,512]{1,0:T(8,128)S(1)}, f32[352,512]{1,0:T(8,128)}, u32[]{:S(2)}) copy-start(f32[352,512]{1,0:T(8,128)} %copy-done.4) | copy-start | bytes 2162692
  90.1 1.2 copy-start.8
  97.6 1.3 copy-start.13
  97.6 14.0 %collective-permute-start.16 = (f32[512,512]{1,0:T(8,128)S(1)}, f32[512,512]{1,0:T(8,128)}, u32[]{:S(2)}, u32[]{:S(2)}) collective-permute-start(f32[512,512]{1,0:T(8,128)S(1)} %get-tuple-element.110), channel_id=1, source_target_pairs={{0,1},{1,0},{2,3},{3,2},{4,5},{5,4},{6,7},{7,6},{8,9},{9,8},{10,11... | collective-permute-start | bytes 3145736 | tf_op jit(solution)/shard_map/ppermute | solution.py:755
  97.8 6.1 %copy-start.3 = (f32[352,512]{1,0:T(8,128)S(1)}, f32[352,512]{1,0:T(8,128)}, u32[]{:S(2)}) copy-start(f32[352,512]{1,0:T(8,128)} %copy-done.2) | copy-start | bytes 2162692
  97.9 6.1 %copy-start.7 = (f32[608,512]{1,0:T(8,128)S(1)}, f32[608,512]{1,0:T(8,128)}, u32[]{:S(2)}) copy-start(f32[608,512]{1,0:T(8,128)} %copy-done.6) | copy-start | bytes 3735556
  98.9 15.4 %copy-start.25 = (f32[1,1,256]{2,1,0:T(1,128)S(1)}, f32[1,1,256]{2,1,0:T(1,128)}, u32[]{:S(2)}) copy-start(f32[1,1,256]{2,1,0:T(1,128)} %param.11) | copy-start | bytes 3076
  98.9 12.7 %collective-permute-start.17 = (f32[128,512]{1,0:T(8,128)S(1)}, f32[128,512]{1,0:T(8,128)S(1)}, u32[]{:S(2)}, u32[]{:S(2)}) collective-permute-start(f32[128,512]{1,0:T(8,128)S(1)} %get-tuple-element.113), channel_id=1, source_target_pairs={{4,0},{5,8},{8,13},{9,1},{0,4},{1,5},{12,9},{13,12},{6,2},{7,10},{... | collective-permute-start | bytes 786440 | tf_op jit(solution)/shard_map/ppermute | solution.py:616
  98.9 12.7 %collective-permute-start.18 = (f32[128,512]{1,0:T(8,128)S(1)}, f32[128,512]{1,0:T(8,128)S(1)}, u32[]{:S(2)}, u32[]{:S(2)}) collective-permute-start(f32[128,512]{1,0:T(8,128)S(1)} %get-tuple-element.114), channel_id=1, source_target_pairs={{4,8},{5,12},{8,1},{9,5},{0,0},{1,4},{12,9},{13,13},{6,10},{7,14},... | collective-permute-start | bytes 786440 | tf_op jit(solution)/shard_map/ppermute | solution.py:616
  101.0 12.6 %collective-permute-start.19 = (f32[128,512]{1,0:T(8,128)S(1)}, f32[128,512]{1,0:T(8,128)S(1)}, u32[]{:S(2)}, u32[]{:S(2)}) collective-permute-start(f32[128,512]{1,0:T(8,128)S(1)} %get-tuple-element.115), channel_id=1, source_target_pairs={{4,12},{5,0},{8,5},{9,13},{0,1},{1,4},{12,8},{13,9},{6,14},{7,2},{... | collective-permute-start | bytes 786440 | tf_op jit(solution)/shard_map/ppermute | solution.py:616
  110.5 1.1 copy-start.15
  111.6 1.9 %copy-start.19 = (f32[128,512]{1,0:T(8,128)}, f32[128,512]{1,0:T(8,128)S(1)}, u32[]{:S(2)}) copy-start(f32[128,512]{1,0:T(8,128)S(1)} %collective-permute-done.17) | copy-start | bytes 786436
  111.7 1.9 %copy-start.21 = (f32[128,512]{1,0:T(8,128)}, f32[128,512]{1,0:T(8,128)S(1)}, u32[]{:S(2)}) copy-start(f32[128,512]{1,0:T(8,128)S(1)} %collective-permute-done.18) | copy-start | bytes 786436
  113.6 0.7 copy-start.23
  114.3 12.4 %collective-permute-start.20 = (f32[768,512]{1,0:T(8,128)S(1)}, f32[768,512]{1,0:T(8,128)}, u32[]{:S(2)}, u32[]{:S(2)}) collective-permute-start(f32[768,512]{1,0:T(8,128)S(1)} %get-tuple-element.116), channel_id=1, source_target_pairs={{0,1},{1,0},{2,3},{3,2},{4,5},{5,4},{6,7},{7,6},{8,9},{9,8},{10,11... | collective-permute-start | bytes 4718600 | tf_op jit(solution)/shard_map/ppermute | solution.py:606
  114.3 4.7 %copy-start.9 = (f32[3,512,256]{2,1,0:T(8,128)S(1)}, f32[3,512,256]{2,1,0:T(8,128)}, u32[]{:S(2)}) copy-start(f32[3,512,256]{2,1,0:T(8,128)} %copy-done.8) | copy-start | bytes 4718596
  114.3 4.7 %copy-start.14 = (bf16[2,3,512,256]{3,2,1,0:T(8,128)(2,1)S(1)}, bf16[2,3,512,256]{3,2,1,0:T(8,128)(2,1)}, u32[]{:S(2)}) copy-start(bf16[2,3,512,256]{3,2,1,0:T(8,128)(2,1)} %copy-done.13) | copy-start | bytes 4718596
  115.9 16.3 %collective-permute-start.22 = (f32[256,512]{1,0:T(8,128)S(1)}, f32[256,512]{1,0:T(8,128)S(1)}, u32[]{:S(2)}, u32[]{:S(2)}) collective-permute-start(f32[256,512]{1,0:T(8,128)S(1)} %get-tuple-element.130), channel_id=1, source_target_pairs={{4,0},{5,8},{8,13},{9,1},{0,4},{1,5},{12,9},{13,12},{6,2},{7,10},{... | collective-permute-start | bytes 1572872 | tf_op jit(solution)/shard_map/ppermute | solution.py:616
  117.1 16.7 %collective-permute-start.23 = (f32[256,512]{1,0:T(8,128)S(1)}, f32[256,512]{1,0:T(8,128)S(1)}, u32[]{:S(2)}, u32[]{:S(2)}) collective-permute-start(f32[256,512]{1,0:T(8,128)S(1)} %get-tuple-element.131), channel_id=1, source_target_pairs={{4,8},{5,12},{8,1},{9,5},{0,0},{1,4},{12,9},{13,13},{6,10},{7,14},... | collective-permute-start | bytes 1572872 | tf_op jit(solution)/shard_map/ppermute | solution.py:616
  119.0 2.2 %copy-start.12 = (bf16[2,2,512,1024]{3,2,1,0:T(8,128)(2,1)S(1)}, bf16[2,2,512,1024]{3,2,1,0:T(8,128)(2,1)}, u32[]{:S(2)}) copy-start(bf16[2,2,512,1024]{3,2,1,0:T(8,128)(2,1)} %copy-done.11) | copy-start | bytes 12582916
  121.2 1.4 copy-start.16
  122.6 4.0 %copy-start.20 = (f32[128,512]{1,0:T(8,128)S(1)}, f32[128,512]{1,0:T(8,128)}, u32[]{:S(2)}) copy-start(f32[128,512]{1,0:T(8,128)} %copy-done.19) | copy-start | bytes 786436
  122.6 4.0 %copy-start.22 = (f32[128,512]{1,0:T(8,128)S(1)}, f32[128,512]{1,0:T(8,128)}, u32[]{:S(2)}) copy-start(f32[128,512]{1,0:T(8,128)} %copy-done.21) | copy-start | bytes 786436
  122.6 4.0 %copy-start.24 = (f32[128,512]{1,0:T(8,128)S(1)}, f32[128,512]{1,0:T(8,128)}, u32[]{:S(2)}) copy-start(f32[128,512]{1,0:T(8,128)} %copy-done.23) | copy-start | bytes 786436
  126.0 20.2 %collective-permute-start.25 = (f32[4,3,64,256]{3,2,1,0:T(8,128)S(1)}, f32[4,3,64,256]{3,2,1,0:T(8,128)S(1)}, u32[]{:S(2)}, u32[]{:S(2)}) collective-permute-start(f32[4,3,64,256]{3,2,1,0:T(8,128)S(1)} %bitcast.48), channel_id=1, source_target_pairs={{0,2},{2,0},{1,3},{3,1},{4,6},{6,4},{5,7},{7,5},{8,10},{10,8},{9,1... | collective-permute-start | bytes 2359304 | tf_op jit(solution)/shard_map/ppermute | solution.py:795
  127.8 14.3 %collective-permute-start.24 = (f32[256,512]{1,0:T(8,128)S(1)}, f32[256,512]{1,0:T(8,128)S(1)}, u32[]{:S(2)}, u32[]{:S(2)}) collective-permute-start(f32[256,512]{1,0:T(8,128)S(1)} %slice_add_fusion.1), channel_id=1, source_target_pairs={{4,12},{5,0},{8,5},{9,13},{0,1},{1,4},{12,8},{13,9},{6,14},{7,2},{... | collective-permute-start | bytes 1572872 | tf_op jit(solution)/shard_map/ppermute | solution.py:616
  129.7 1.6 copy-start.18
  129.7 1.5 collective-permute-start.21
  146.4 8.3 %collective-permute-start.26 = (f32[3,64,256]{2,1,0:T(8,128)S(1)}, f32[3,64,256]{2,1,0:T(8,128)S(1)}, u32[]{:S(2)}, u32[]{:S(2)}) collective-permute-start(f32[3,64,256]{2,1,0:T(8,128)S(1)} %get-tuple-element.150), channel_id=1, source_target_pairs={{0,1},{1,0},{2,3},{3,2},{4,5},{5,4},{6,7},{7,6},{8,9},{9,8},{10,11... | collective-permute-start | bytes 589832 | tf_op jit(solution)/shard_map/ppermute | solution.py:800
  146.4 8.2 %collective-permute-start.27 = (f32[3,64,256]{2,1,0:T(8,128)S(1)}, f32[3,64,256]{2,1,0:T(8,128)S(1)}, u32[]{:S(2)}, u32[]{:S(2)}) collective-permute-start(f32[3,64,256]{2,1,0:T(8,128)S(1)} %get-tuple-element.153), channel_id=1, source_target_pairs={{4,0},{5,8},{8,13},{9,1},{0,4},{1,5},{12,9},{13,12},{6,2},{7,10},{... | collective-permute-start | bytes 589832 | tf_op jit(solution)/shard_map/ppermute | solution.py:797
  146.5 8.8 %collective-permute-start.28 = (f32[3,64,256]{2,1,0:T(8,128)S(1)}, f32[3,64,256]{2,1,0:T(8,128)S(1)}, u32[]{:S(2)}, u32[]{:S(2)}) collective-permute-start(f32[3,64,256]{2,1,0:T(8,128)S(1)} %get-tuple-element.152), channel_id=1, source_target_pairs={{4,8},{5,12},{8,1},{9,5},{0,0},{1,4},{12,9},{13,13},{6,10},{7,14},... | collective-permute-start | bytes 589832 | tf_op jit(solution)/shard_map/ppermute | solution.py:797
  151.5 7.0 %collective-permute-start.29 = (f32[3,64,256]{2,1,0:T(8,128)S(1)}, f32[3,64,256]{2,1,0:T(8,128)S(1)}, u32[]{:S(2)}, u32[]{:S(2)}) collective-permute-start(f32[3,64,256]{2,1,0:T(8,128)S(1)} %get-tuple-element.151), channel_id=1, source_target_pairs={{4,12},{5,0},{8,5},{9,13},{0,1},{1,4},{12,8},{13,9},{6,14},{7,2},{... | collective-permute-start | bytes 589832 | tf_op jit(solution)/shard_map/ppermute | solution.py:797
  151.9 1.0 copy-start.17
